TPU v7x, 256 devices: a whole 4x4x8 slice. The times are simulated.
256 devices in a mesh: rows: 128 (over x, z, y), cols: 2 (over core).
Axes of the slice: x: 4, y: 4, z: 8, core: 2. Of those that a mesh axis runs over, the one named last changes fastest.
Arguments:
- embeddings: bfloat16 [262144, 384], P('rows')
- test_matrix: bfloat16 [262144, 64], P('rows'), may hold values from -6 to 6
- pair_list: int32 [1024, 2], P(('rows', 'cols')), may hold values from -1 to 255, as said below
Outputs:
- orthonormal_basis: float32 [262144, 64], P(('rows', 'cols'))
- upper_factor: float32 [64, 64], replicated
Inputs may be any that keep to these rules, and one draw needn't show every extreme that they name: `pair_list`: device (r, c) holds 4 entries. Its live entries come first: pairs (i, j) with r * 2 <= i < (r + 1) * 2 and i <= j < min((r + 3) * 2, 256); each pair appears at most once over all devices; its other entries are -1 in both places. The device with c = 0 holds at least one live pair, the two devices of one r hold at most 4 together, and device (0, 0) holds exactly 4.
All inputs are finite; a program needn't handle non-finite values.
Results may differ from a plain program's by a relative error of at most 0.0053.
Values may be sent and summed in bfloat16 or wider, within the bound.
No kernel may reach another device: no remote copies, remote signals or barrier semaphores. Data moves between devices by JAX's collectives and lax.ppermute only.
A program may use at most 64 MiB of HBM per device.

v0:
```python
import jax
import jax.numpy as jnp
from jax import lax
from jax.sharding import PartitionSpec as P

BLK = 1024


SHARPNESS = 6.0
EPSILON = 1e-06


def shifted(value, axis, steps):
    count = lax.axis_size(axis)
    initial, last = (max(0, -steps), min(count, count - steps))
    return lax.ppermute(value, axis, [(source, source + steps) for source in range(initial, last)])


def unit_rows(embeddings):
    widened = embeddings.astype(jnp.float32)
    inverse = lax.rsqrt(jnp.sum(widened * widened, axis=1, keepdims=True) + EPSILON)
    return (widened * inverse).astype(jnp.bfloat16)


def affinity(left_rows, right_rows):
    scores = lax.dot_general(
        left_rows, right_rows, (((1,), (1,)), ((), ())), preferred_element_type=jnp.float32
    )
    return jnp.exp(SHARPNESS * (scores - 1.0)).astype(jnp.bfloat16)


def mirror_product(affinity_tile, vectors):
    return lax.dot_general(
        affinity_tile, vectors, (((0,), (0,)), ((), ())), preferred_element_type=jnp.float32
    )


def block_at(stacked, index):
    return lax.dynamic_index_in_dim(stacked, index, 0, keepdims=False)


def add_block(stacked, index, term):
    return lax.dynamic_update_index_in_dim(stacked, block_at(stacked, index) + term, index, 0)


def count_live(pair_rows):
    return jnp.sum((pair_rows[:, 0] >= 0).astype(jnp.int32))


def orthonormal(sketch_rows, rows_total):
    gram_matrix = lax.dot_general(
        sketch_rows,
        sketch_rows,
        (((0,), (0,)), ((), ())),
        precision=lax.Precision.HIGHEST,
        preferred_element_type=jnp.float32,
    )
    gram_matrix = lax.psum(gram_matrix, ("rows", "cols")) / rows_total
    lower_factor = jnp.linalg.cholesky(gram_matrix)
    solved = lax.linalg.triangular_solve(
        lower_factor, sketch_rows, left_side=False, lower=True, transpose_a=True
    )
    return (solved, lower_factor.T)


def affinity_pass(window_units, own_vectors, my_pairs, base_block):
    blocks_dev = own_vectors.shape[0]
    ahead_vectors = [shifted(own_vectors, "rows", -offset) for offset in (1, 2)]
    window_vectors = jnp.concatenate([own_vectors] + ahead_vectors, axis=0)
    initial = jnp.zeros(window_vectors.shape, jnp.float32)

    def pair_step(slot_index, accumulated):
        entry = my_pairs[slot_index]
        first_block = entry[0] - base_block
        second_block = entry[1] - base_block
        affinity_tile = affinity(
            block_at(window_units, first_block), block_at(window_units, second_block)
        )
        forward = jnp.dot(
            affinity_tile,
            block_at(window_vectors, second_block),
            preferred_element_type=jnp.float32,
        )
        accumulated = add_block(accumulated, first_block, forward)
        mirrored = first_block != second_block

        def add_mirror(current):
            return add_block(
                current,
                second_block,
                mirror_product(affinity_tile, block_at(window_vectors, first_block)),
            )

        return lax.cond(mirrored, add_mirror, lambda unchanged: unchanged, accumulated)

    accumulated = lax.fori_loop(0, count_live(my_pairs), pair_step, initial)
    own_blocks = accumulated[:blocks_dev]
    for offset in (1, 2):
        own_blocks = own_blocks + shifted(
            accumulated[offset * blocks_dev : (offset + 1) * blocks_dev], "rows", offset
        )
    flattened = own_blocks.reshape(-1, own_blocks.shape[2])
    return lax.psum_scatter(flattened, "cols", scatter_dimension=0, tiled=True)


def local(embeddings, test_matrix, pair_list):
    rows_dev = embeddings.shape[0]
    blocks_dev = rows_dev // BLK
    columns = test_matrix.shape[1]
    base_block = lax.axis_index("rows") * blocks_dev
    rows_total = rows_dev * lax.axis_size("rows")
    normed = unit_rows(embeddings).reshape(blocks_dev, BLK, embeddings.shape[1])
    ahead_units = [shifted(normed, "rows", -offset) for offset in (1, 2)]
    window_units = jnp.concatenate([normed] + ahead_units, axis=0)
    sketch_rows = affinity_pass(
        window_units, test_matrix.reshape(blocks_dev, BLK, columns), pair_list, base_block
    )
    panel_rows, _ = orthonormal(sketch_rows, rows_total)
    panel_whole = lax.all_gather(panel_rows.astype(jnp.bfloat16), "cols", axis=0, tiled=True)
    image_rows = affinity_pass(
        window_units, panel_whole.reshape(blocks_dev, BLK, columns), pair_list, base_block
    )
    return orthonormal(image_rows, rows_total)


def solution(mesh):
    in_specs = (P("rows", None), P("rows", None), P(("rows", "cols"), None))
    out_specs = (P(("rows", "cols"), None), P())
    return jax.shard_map(local, mesh=mesh, in_specs=in_specs, out_specs=out_specs, check_vma=False)
```

profile of v0, /device:TPU:1, one launch (start us, length us, event | category | flops | bytes accessed | tf_op | source)
XLA Modules:
  0.0 549.4 jit_solution(13680197383918252103)
XLA Ops:
  7.2 0.0 reduce-scatter.3.cloned.1.call-start
  7.2 1.9 fusion.32
  9.1 0.0 copy-start.1
  9.2 0.0 copy-start.2
  9.2 0.3 fusion.33
  9.5 1.3 collective-permute-start
  10.8 1.3 collective-permute-start.1
  12.1 0.3 copy.14
  12.4 1.3 collective-permute-start.2
  13.7 1.3 collective-permute-start.3
  15.0 0.6 fusion.44
  15.7 85.9 %collective-permute-done.2 = bf16[2,1024,64]{2,1,0:T(8,128)(2,1)S(1)} collective-permute-done((bf16[2,1024,64]{2,1,0:T(8,128)(2,1)S(1)}, bf16[2,1024,64]{2,1,0:T(8,128)(2,1)S(1)}, u32[]{:S(2)}, u32[]{:S(2)}) %collective-permute-start.2) | collective-permute-done | bytes 262176 | tf_op jit(solution)/shard_map/ppermute | solution.py:16
  101.6 0.0 collective-permute-done.3
  101.6 1.5 pad_maximum_fusion.1
  103.1 0.0 collective-permute-done
  103.1 0.0 collective-permute-done.1
  103.1 3.8 pad_maximum_fusion
  106.9 1.3 broadcast.76.clone
  108.3 0.7 while.24
  108.9 1.3 fusion.48
  110.2 6.4 %collective-permute-start.4 = (f32[2,1024,64]{1,2,0:T(8,128)S(1)}, f32[2,1024,64]{1,2,0:T(8,128)S(1)}, u32[]{:S(2)}, u32[]{:S(2)}) collective-permute-start(f32[2,1024,64]{1,2,0:T(8,128)S(1)} %get-tuple-element.272), channel_id=1, source_target_pairs={{0,2},{2,4},{4,6},{6,8},{8,10},{10,12},{12,14},{14,16},{16,18},{18... | collective-permute-start | bytes 1572872 | tf_op jit(solution)/shard_map/ppermute | solution.py:16
  116.6 62.5 %collective-permute-start.5 = (f32[2,1024,64]{1,2,0:T(8,128)S(1)}, f32[2,1024,64]{1,2,0:T(8,128)S(1)}, u32[]{:S(2)}, u32[]{:S(2)}) collective-permute-start(f32[2,1024,64]{1,2,0:T(8,128)S(1)} %get-tuple-element.273), channel_id=1, source_target_pairs={{0,4},{2,6},{4,8},{6,10},{8,12},{10,14},{12,16},{14,18},{16,20},{1... | collective-permute-start | bytes 1572872 | tf_op jit(solution)/shard_map/ppermute | solution.py:16
  179.1 0.0 collective-permute-done.4
  179.1 8.0 %collective-permute-done.5 = f32[2,1024,64]{1,2,0:T(8,128)S(1)} collective-permute-done((f32[2,1024,64]{1,2,0:T(8,128)S(1)}, f32[2,1024,64]{1,2,0:T(8,128)S(1)}, u32[]{:S(2)}, u32[]{:S(2)}) %collective-permute-start.5) | collective-permute-done | bytes 524320 | tf_op jit(solution)/shard_map/ppermute | solution.py:16
  187.2 1.1 add_bitcast_fusion.1
  188.3 0.9 copy.28
  189.2 0.0 reduce-scatter.3.cloned.1.call-update
  189.2 0.0 reduce-scatter.5.cloned.1.call-start
  189.2 45.0 %reduce-scatter.3.cloned.1.call-done = f32[1024,64]{0,1:T(8,128)} async-done(((f32[2048,64]{0,1:T(8,128)}), f32[1024,64]{0,1:T(8,128)}) %reduce-scatter.3.cloned.1.call-update) | async-done | bytes 262160 | tf_op jit(solution)/shard_map/reduce_scatter | solution.py:103
  234.3 1.4 fusion.49
  235.7 77.5 %psum.14 = f32[64,64]{0,1:T(8,128)S(1)} all-reduce(f32[64,64]{0,1:T(8,128)S(1)} %fusion.49), channel_id=1, replica_groups=mesh['rows'=128,'cols'=2] {'rows','cols'}, use_global_device_ids=true, to_apply=%region_7.8 | all-reduce | flops 4096 | bytes 32768 | tf_op jit(solution)/shard_map/psum | solution.py:58
  313.2 0.1 copy.17
  313.3 5.8 %cholesky.44 = f32[64,64]{1,0:T(8,128)S(1)} custom-call(f32[64,64]{1,0:T(8,128)S(1)} %fusion.39), custom_call_target="Cholesky" | custom-call | tf_op jit(solution)/shard_map/jit(cholesky)/cholesky | solution.py:59
  319.2 0.6 compare_reduce_fusion.1
  319.9 0.7 fusion.35
  320.5 4.9 custom-call.6
  325.4 1.4 fusion.34
  326.8 2.5 all_gather.3
  329.3 0.3 copy.27
  329.6 1.3 collective-permute-start.6
  330.9 1.3 collective-permute-start.7
  332.2 22.3 %collective-permute-done.6 = bf16[2,1024,64]{2,1,0:T(8,128)(2,1)S(1)} collective-permute-done((bf16[2,1024,64]{2,1,0:T(8,128)(2,1)S(1)}, bf16[2,1024,64]{2,1,0:T(8,128)(2,1)S(1)}, u32[]{:S(2)}, u32[]{:S(2)}) %collective-permute-start.6) | collective-permute-done | bytes 262176 | tf_op jit(solution)/shard_map/ppermute | solution.py:16
  354.5 0.0 collective-permute-done.7
  354.5 1.5 pad_maximum_fusion.2
  356.0 1.3 broadcast.76
  357.3 0.7 while.25
  358.0 1.3 fusion.47
  359.3 3.7 collective-permute-start.8
  362.9 37.4 %collective-permute-start.9 = (f32[2,1024,64]{1,2,0:T(8,128)S(1)}, f32[2,1024,64]{1,2,0:T(8,128)S(1)}, u32[]{:S(2)}, u32[]{:S(2)}) collective-permute-start(f32[2,1024,64]{1,2,0:T(8,128)S(1)} %get-tuple-element.271), channel_id=1, source_target_pairs={{0,4},{2,6},{4,8},{6,10},{8,12},{10,14},{12,16},{14,18},{16,20},{1... | collective-permute-start | bytes 1572872 | tf_op jit(solution)/shard_map/ppermute | solution.py:16
  400.3 0.0 collective-permute-done.8
  400.4 5.9 %collective-permute-done.9 = f32[2,1024,64]{1,2,0:T(8,128)S(1)} collective-permute-done((f32[2,1024,64]{1,2,0:T(8,128)S(1)}, f32[2,1024,64]{1,2,0:T(8,128)S(1)}, u32[]{:S(2)}, u32[]{:S(2)}) %collective-permute-start.9) | collective-permute-done | bytes 524320 | tf_op jit(solution)/shard_map/ppermute | solution.py:16
  406.2 1.1 add_bitcast_fusion
  407.4 0.8 copy.29
  408.2 0.0 reduce-scatter.5.cloned.1.call-update
  408.2 40.5 %reduce-scatter.5.cloned.1.call-done = f32[1024,64]{0,1:T(8,128)} async-done(((f32[2048,64]{0,1:T(8,128)}), f32[1024,64]{0,1:T(8,128)}) %reduce-scatter.5.cloned.1.call-update) | async-done | bytes 262160 | tf_op jit(solution)/shard_map/reduce_scatter | solution.py:103
  448.7 1.4 fusion.50
  450.1 77.5 %psum.15 = f32[64,64]{0,1:T(8,128)S(1)} all-reduce(f32[64,64]{0,1:T(8,128)S(1)} %fusion.50), channel_id=1, replica_groups=mesh['rows'=128,'cols'=2] {'rows','cols'}, use_global_device_ids=true, to_apply=%region_15.18 | all-reduce | flops 4096 | bytes 32768 | tf_op jit(solution)/shard_map/psum | solution.py:58
  527.6 0.1 copy.23
  527.7 5.8 %cholesky.55 = f32[64,64]{1,0:T(8,128)S(1)} custom-call(f32[64,64]{1,0:T(8,128)S(1)} %fusion.37), custom_call_target="Cholesky" | custom-call | tf_op jit(solution)/shard_map/jit(cholesky)/cholesky | solution.py:59
  533.6 0.6 compare_reduce_fusion
  534.3 0.7 fusion.43
  534.9 4.9 custom-call.7
  539.8 0.7 copy.24
  540.5 2.1 convolution_bitcast_fusion.2
  (11 shorter events, 0.1 us)
Async XLA Ops:
  7.2 2.0 copy-start
  7.2 227.1 %reduce-scatter.3.cloned.1.call-start = ((), (), s32[]{:S(2)}) async-start(), calls=%async_computation.2 | async-start | bytes 786432 | tf_op jit(solution)/shard_map/reduce_scatter | solution.py:103
  9.1 3.0 copy-start.1
  9.2 5.9 %copy-start.2 = (s32[4,2]{0,1:T(2,128)S(1)}, s32[4,2]{0,1:T(2,128)}, u32[]{:S(2)}) copy-start(s32[4,2]{0,1:T(2,128)} %param.16) | copy-start | bytes 100
  9.5 93.6 %collective-permute-start = (bf16[2,1024,384]{2,1,0:T(8,128)(2,1)S(1)}, bf16[2,1024,384]{2,1,0:T(8,128)(2,1)}, u32[]{:S(2)}, u32[]{:S(2)}) collective-permute-start(bf16[2,1024,384]{2,1,0:T(8,128)(2,1)S(1)} %bitcast.145), channel_id=1, source_target_pairs={{2,0},{4,2},{6,4},{8,6},{10,8},{12,10},{14,12},{16,14},{18,16},{20... | collective-permute-start | bytes 4718600 | tf_op jit(solution)/shard_map/ppermute | solution.py:16
  10.8 92.3 %collective-permute-start.1 = (bf16[2,1024,384]{2,1,0:T(8,128)(2,1)S(1)}, bf16[2,1024,384]{2,1,0:T(8,128)(2,1)}, u32[]{:S(2)}, u32[]{:S(2)}) collective-permute-start(bf16[2,1024,384]{2,1,0:T(8,128)(2,1)S(1)} %bitcast.146), channel_id=1, source_target_pairs={{4,0},{6,2},{8,4},{10,6},{12,8},{14,10},{16,12},{18,14},{20,16},{2... | collective-permute-start | bytes 4718600 | tf_op jit(solution)/shard_map/ppermute | solution.py:16
  12.4 89.2 %collective-permute-start.2 = (bf16[2,1024,64]{2,1,0:T(8,128)(2,1)S(1)}, bf16[2,1024,64]{2,1,0:T(8,128)(2,1)S(1)}, u32[]{:S(2)}, u32[]{:S(2)}) collective-permute-start(bf16[2,1024,64]{2,1,0:T(8,128)(2,1)S(1)} %bitcast.150), channel_id=1, source_target_pairs={{2,0},{4,2},{6,4},{8,6},{10,8},{12,10},{14,12},{16,14},{18,16},{20... | collective-permute-start | bytes 786440 | tf_op jit(solution)/shard_map/ppermute | solution.py:16
  13.7 87.9 %collective-permute-start.3 = (bf16[2,1024,64]{2,1,0:T(8,128)(2,1)S(1)}, bf16[2,1024,64]{2,1,0:T(8,128)(2,1)S(1)}, u32[]{:S(2)}, u32[]{:S(2)}) collective-permute-start(bf16[2,1024,64]{2,1,0:T(8,128)(2,1)S(1)} %bitcast.151), channel_id=1, source_target_pairs={{4,0},{6,2},{8,4},{10,6},{12,8},{14,10},{16,12},{18,14},{20,16},{2... | collective-permute-start | bytes 786440 | tf_op jit(solution)/shard_map/ppermute | solution.py:16
  110.2 68.9 %collective-permute-start.4 = (f32[2,1024,64]{1,2,0:T(8,128)S(1)}, f32[2,1024,64]{1,2,0:T(8,128)S(1)}, u32[]{:S(2)}, u32[]{:S(2)}) collective-permute-start(f32[2,1024,64]{1,2,0:T(8,128)S(1)} %get-tuple-element.272), channel_id=1, source_target_pairs={{0,2},{2,4},{4,6},{6,8},{8,10},{10,12},{12,14},{14,16},{16,18},{18... | collective-permute-start | bytes 1572872 | tf_op jit(solution)/shard_map/ppermute | solution.py:16
  116.6 70.5 %collective-permute-start.5 = (f32[2,1024,64]{1,2,0:T(8,128)S(1)}, f32[2,1024,64]{1,2,0:T(8,128)S(1)}, u32[]{:S(2)}, u32[]{:S(2)}) collective-permute-start(f32[2,1024,64]{1,2,0:T(8,128)S(1)} %get-tuple-element.273), channel_id=1, source_target_pairs={{0,4},{2,6},{4,8},{6,10},{8,12},{10,14},{12,16},{14,18},{16,20},{1... | collective-permute-start | bytes 1572872 | tf_op jit(solution)/shard_map/ppermute | solution.py:16
  189.2 259.5 %reduce-scatter.5.cloned.1.call-start = ((), (), s32[]{:S(2)}) async-start(), calls=%async_computation.3 | async-start | bytes 786432 | tf_op jit(solution)/shard_map/reduce_scatter | solution.py:103
  329.6 24.9 %collective-permute-start.6 = (bf16[2,1024,64]{2,1,0:T(8,128)(2,1)S(1)}, bf16[2,1024,64]{2,1,0:T(8,128)(2,1)S(1)}, u32[]{:S(2)}, u32[]{:S(2)}) collective-permute-start(bf16[2,1024,64]{2,1,0:T(8,128)(2,1)S(1)} %bitcast.153), channel_id=1, source_target_pairs={{2,0},{4,2},{6,4},{8,6},{10,8},{12,10},{14,12},{16,14},{18,16},{20... | collective-permute-start | bytes 786440 | tf_op jit(solution)/shard_map/ppermute | solution.py:16
  330.9 23.6 %collective-permute-start.7 = (bf16[2,1024,64]{2,1,0:T(8,128)(2,1)S(1)}, bf16[2,1024,64]{2,1,0:T(8,128)(2,1)S(1)}, u32[]{:S(2)}, u32[]{:S(2)}) collective-permute-start(bf16[2,1024,64]{2,1,0:T(8,128)(2,1)S(1)} %bitcast.154), channel_id=1, source_target_pairs={{4,0},{6,2},{8,4},{10,6},{12,8},{14,10},{16,12},{18,14},{20,16},{2... | collective-permute-start | bytes 786440 | tf_op jit(solution)/shard_map/ppermute | solution.py:16
  359.3 41.1 %collective-permute-start.8 = (f32[2,1024,64]{1,2,0:T(8,128)S(1)}, f32[2,1024,64]{1,2,0:T(8,128)S(1)}, u32[]{:S(2)}, u32[]{:S(2)}) collective-permute-start(f32[2,1024,64]{1,2,0:T(8,128)S(1)} %get-tuple-element.270), channel_id=1, source_target_pairs={{0,2},{2,4},{4,6},{6,8},{8,10},{10,12},{12,14},{14,16},{16,18},{18... | collective-permute-start | bytes 1572872 | tf_op jit(solution)/shard_map/ppermute | solution.py:16
  362.9 43.3 %collective-permute-start.9 = (f32[2,1024,64]{1,2,0:T(8,128)S(1)}, f32[2,1024,64]{1,2,0:T(8,128)S(1)}, u32[]{:S(2)}, u32[]{:S(2)}) collective-permute-start(f32[2,1024,64]{1,2,0:T(8,128)S(1)} %get-tuple-element.271), channel_id=1, source_target_pairs={{0,4},{2,6},{4,8},{6,10},{8,12},{10,14},{12,16},{14,18},{16,20},{1... | collective-permute-start | bytes 1572872 | tf_op jit(solution)/shard_map/ppermute | solution.py:16
Sparse Core Ops, SparseCore 0:
  189.3 44.8 reduce-scatter.2
  408.4 40.2 reduce-scatter.4
where the time goes:
time: 550 us; the launch traced here: 549 us
  waiting for transfers between devices  208 us (38%)
  blocking collectives  158 us (29%)
  starting transfers between devices  118 us (21%)
  other arithmetic  36.2 us (7%)
  between operations  14.3 us (3%)
  local copies, waits for them, and re-layouts  8.38 us (2%)
  matrix products  6.28 us (1%)
    psum x2, blocking collectives, orthonormal(): gram_matrix = lax.psum(gram_matrix, ('rows', 'cols')) / rows_total  155 us
    ppermute x10, waiting for transfers between devices, shifted(): lax.ppermute(value, axis, [(source, source + steps) for source in range(i...  122 us
    ppermute x10, starting transfers between devices, shifted(): lax.ppermute(value, axis, [(source, source + steps) for source in range(i...  118 us
    reduce_scatter x2, waiting for transfers between devices, affinity_pass(): return lax.psum_scatter(flattened, 'cols', scatter_dimension=0, tiled=True)  85.5 us
    another operation x6, other arithmetic, orthonormal(): lower_factor = jnp.linalg.cholesky(gram_matrix)  13 us
  transfers between devices with their start and end apart: 12, of which 6 were waited for; matrix products, arithmetic and copies ran while one was open for 0% of the time, Pallas kernels for 0%

commit v1 on v0

v1 whole, which is shorter than its diff:
```python
import functools

import jax
import jax.numpy as jnp
from jax import lax
from jax.experimental import pallas as pl
from jax.experimental.pallas import tpu as pltpu
from jax.sharding import PartitionSpec as P

BLK = 1024
HALF = 512
SHARPNESS = 6.0
EPSILON = 1e-06
LOG2E = 1.4426950408889634
HIGHEST = lax.Precision.HIGHEST
VMEM = pl.BlockSpec(memory_space=pltpu.VMEM)
SMEM = pl.BlockSpec(memory_space=pltpu.SMEM)
NT = (((1,), (1,)), ((), ()))
NN = (((1,), (0,)), ((), ()))
ACROSS, PLANES, RING = 4, 8, 4


def call(kernel, outs, flops, moved, exps=0):
    return functools.partial(
        pl.pallas_call,
        kernel,
        out_shape=outs,
        out_specs=jax.tree.map(lambda _: VMEM, outs),
        compiler_params=pltpu.CompilerParams(vmem_limit_bytes=48 * 1024 * 1024),
        cost_estimate=pl.CostEstimate(flops=flops, bytes_accessed=moved, transcendentals=exps),
    )


def shape(dims, dtype=jnp.float32):
    return jax.ShapeDtypeStruct(dims, dtype)


def dot(left, right, dims, precision=None):
    return lax.dot_general(
        left, right, dims, precision=precision, preferred_element_type=jnp.float32
    )


def unit_kernel(relative, core_ref, rows_ref, unit_ref):
    core = core_ref[0]
    side = core if relative == 0 else 1 - core
    for block in range(2):
        start = pl.multiple_of(block * BLK + side * HALF, HALF)
        widened = rows_ref[pl.ds(start, HALF), :].astype(jnp.float32)
        inverse = lax.rsqrt(jnp.sum(widened * widened, axis=1, keepdims=True) + EPSILON)
        unit_ref[block] = (widened * inverse).astype(jnp.bfloat16)


def affinity_tile(left, right):
    scores = dot(left, right, NT)
    return jnp.exp2((SHARPNESS * LOG2E) * scores - (SHARPNESS * LOG2E)).astype(jnp.bfloat16)


def fold(product):
    if product.shape[0] == 128:
        return product[:64] + product[64:]
    return product


def make_tiles(left, rights, tile_ref, slot):
    for side in range(2):
        for at in range(0, HALF, 256):
            tile_ref[slot, side, :, at : at + 256] = affinity_tile(
                left, rights[side][at : at + 256]
            )


def use_tiles(tile_ref, slot, ahead, behind, forward_ref, forward_at, mirror_ref, mirror_at, mirror):
    total = fold(dot(ahead[0], tile_ref[slot, 0], NT)) + fold(dot(ahead[1], tile_ref[slot, 1], NT))
    forward_ref[forward_at] += total

    def put_mirror():
        for side in range(2):
            mirror_ref[side, mirror_at] += fold(dot(behind, tile_ref[slot, side], NN))

    if mirror is None:
        put_mirror()
    else:
        pl.when(mirror)(put_mirror)


def local_kernel(make, flags_ref, *refs):
    if make:
        unit0, unit1, vec0, vec1, tile_ref, forward_ref, mirror_ref = refs
    else:
        tile_ref, vec0, vec1, forward_ref, mirror_ref = refs
    forward_ref[...] = jnp.zeros_like(forward_ref)
    mirror_ref[...] = jnp.zeros_like(mirror_ref)

    @pl.loop(0, 3)
    def _(slot):
        first, second = slot // 2, (slot + 1) // 2

        @pl.when(flags_ref[slot] > 0)
        def _():
            if make:
                make_tiles(unit0[first], (unit0.at[second], unit1.at[second]), tile_ref, slot)
            use_tiles(
                tile_ref, slot, (vec0[second], vec1[second]), vec0[first],
                forward_ref, first, mirror_ref, second, slot == 1,
            )


def near_kernel(make, flags_ref, *refs):
    if make:
        (unit0, unit_prev, next0, next1, vec0, vec_prev, vnext0, vnext1, started,
         tile_ref, forward_ref, before_ref, mirror_ref) = refs
    else:
        (tile_ref, vec0, vec_prev, vnext0, vnext1, started,
         forward_ref, before_ref, mirror_ref) = refs
    forward_ref[...] = started[...]
    before_ref[...] = jnp.zeros_like(before_ref)
    mirror_ref[...] = jnp.zeros_like(mirror_ref)
    for kind in range(2):

        @pl.loop(0, 4)
        def _(index):
            first, second = index // 2, index % 2
            slot = kind * 4 + index

            @pl.when(flags_ref[3 + slot] > 0)
            def _():
                if make:
                    left = (unit0, unit_prev)[kind][first]
                    make_tiles(left, (next0.at[second], next1.at[second]), tile_ref, slot)
                use_tiles(
                    tile_ref, slot, (vnext0[second], vnext1[second]), (vec0, vec_prev)[kind][first],
                    (forward_ref, before_ref)[kind], first, mirror_ref, second, None,
                )


def total_kernel(forward, mirror_mine, mirror_other, from_next, from_prev, sum_ref, pair_ref=None):
    for block in range(2):
        value = (
            forward[block] + mirror_mine[0, block] + mirror_other[block]
            + from_next[block] + from_prev[block]
        )
        sum_ref[block] = value
        if pair_ref is not None:
            high = value.astype(jnp.bfloat16)
            pair_ref[block, :64] = high
            pair_ref[block, 64:] = (value - high.astype(jnp.float32)).astype(jnp.bfloat16)


def gram_of(value_ref, scale):
    gram = dot(value_ref[0], value_ref[0], NT, HIGHEST) + dot(value_ref[1], value_ref[1], NT, HIGHEST)
    gram = gram * scale
    return jnp.concatenate([gram[:32], gram[32:]], axis=1)


def gram_kernel(scale, value_ref, gram_ref):
    gram_ref[...] = gram_of(value_ref, scale)


def second_gram_kernel(scale, core_ref, first_ref, value_ref, keep_ref, give_ref, swap_ref):
    second = gram_of(value_ref, scale)
    first = first_ref[...]
    lead = core_ref[0] == 0
    keep_ref[...] = jnp.where(lead, first, second)
    give_ref[...] = jnp.where(lead, second, first)
    swap_ref[...] = value_ref[1 - core_ref[0]]


def eliminate(packed):
    lanes = lax.broadcasted_iota(jnp.int32, (8, 64), 1)
    subs = lax.broadcasted_iota(jnp.int32, (8, 64), 0)
    sub1 = lax.broadcasted_iota(jnp.int32, (8, 1), 0)
    states = []
    for matrix in packed:
        whole = jnp.concatenate([matrix[:, :64], matrix[:, 64:]], axis=0)
        states.append([
            jnp.concatenate(
                [whole[8 * b : 8 * b + 8], (lanes == subs + 8 * b).astype(jnp.float32)], axis=1
            )
            for b in range(8)
        ])
    for k in range(64):
        at, sub = k // 8, k % 8
        for state in states:
            row = state[at][sub : sub + 1, :]
            scaled = row / state[at][sub : sub + 1, k : k + 1]
            for b in range(at, 8):
                column = state[b][:, k : k + 1]
                if b == at:
                    column = jnp.where(sub1 > sub, column, 0.0)
                state[b] = state[b] - column * scaled
    uppers, inverses = [], []
    for state in states:
        rows = []
        for b in range(8):
            diagonal = jnp.sum(
                jnp.where(lanes == subs + 8 * b, state[b][:, :64], 0.0), axis=1, keepdims=True
            )
            rows.append(state[b] * lax.rsqrt(diagonal))
        whole = jnp.concatenate(rows, axis=0)
        uppers.append(whole[:, :64])
        inverses.append(whole[:, 64:])
    return uppers, inverses


def finish_kernel(core_ref, mine_ref, other_ref, value_ref, got_ref, basis_ref, factor_ref):
    core = core_ref[0]
    lead = core == 0
    mine, other = mine_ref[...], other_ref[...]
    first, second = jnp.where(lead, mine, other), jnp.where(lead, other, mine)
    uppers, inverses = eliminate([first, second])
    factor = dot(uppers[1], inverses[0], NT, HIGHEST)
    wide = lax.broadcasted_iota(jnp.int32, (64, 64), 1)
    tall = lax.broadcasted_iota(jnp.int32, (64, 64), 0)
    factor_ref[...] = jnp.where(wide >= tall, factor, 0.0)
    low = jnp.where(wide <= tall, inverses[1], 0.0)
    here = pl.multiple_of(core * HALF, HALF)
    there = pl.multiple_of((1 - core) * HALF, HALF)
    basis_ref[:, pl.ds(here, HALF)] = dot(low, value_ref[core], NN, HIGHEST)
    basis_ref[:, pl.ds(there, HALF)] = dot(low, got_ref[...], NN, HIGHEST)


def step_rows(value, steps):
    count = lax.axis_size("rows")
    return lax.ppermute(value, "rows", [(r, (r + steps) % count) for r in range(count)])


def swap(value):
    return lax.ppermute(value, "cols", [(0, 1), (1, 0)])


def live_flags(pair_list, base):
    own = jnp.concatenate([pair_list, swap(pair_list)], axis=0)
    before = step_rows(own, 1)

    def any_of(entries, pairs):
        table = jnp.array(pairs, jnp.int32) + base
        hit = (entries[None, :, :] == table[:, None, :]).all(axis=2)
        live = entries[None, :, 0] >= 0
        return jnp.any(hit & live, axis=1)

    ours = [(0, 0), (0, 1), (1, 1), (0, 2), (0, 3), (1, 2), (1, 3)]
    across = [(-2, 2), (-2, 3), (-1, 2), (-1, 3)]
    return jnp.concatenate([any_of(own, ours), any_of(before, across)]).astype(jnp.int32)


def spread(forward, before, mirror_own, mirror_next):
    from_next = step_rows(before, -1)
    other_own = swap(mirror_own[1])
    other_next = swap(mirror_next[1])
    from_prev = step_rows(mirror_next[0] + other_next, 1)
    return forward, mirror_own, other_own, from_next, from_prev


def sum_over_chips(value):
    count = lax.axis_size("rows")
    planes = [[(x * PLANES + z) * RING + y for x in range(ACROSS) for y in range(RING)] for z in range(PLANES)]
    lines = [[(x * PLANES + z) * RING + y for z in range(PLANES)] for x in range(ACROSS) for y in range(RING)]
    for groups in (planes, lines):
        size = len(groups[0])
        copies = jnp.broadcast_to(value[None], (size,) + value.shape)
        value = lax.all_to_all(copies, "rows", 0, 0, axis_index_groups=groups, tiled=True).sum(0)
    return value


def local(embeddings, test_matrix, pair_list):
    rows_dev = embeddings.shape[0]
    columns = test_matrix.shape[1]
    bf16, f32 = jnp.bfloat16, jnp.float32
    core = lax.axis_index("cols").astype(jnp.int32)
    core_ref = core.reshape(1)
    base = (lax.axis_index("rows") * 2).astype(jnp.int32)
    scale = 1.0 / (rows_dev * lax.axis_size("rows"))

    def unit(relative):
        return call(
            functools.partial(unit_kernel, relative), shape((2, HALF, 384), bf16), 2**20, 2**21
        )(in_specs=[SMEM, VMEM])(core_ref, embeddings)

    unit0 = unit(0)
    unit_prev = step_rows(unit0, 1)
    next0 = step_rows(unit0, -1)
    flags = live_flags(pair_list, base)
    turned = test_matrix.T.reshape(columns, 2, 2, HALF).transpose(2, 1, 0, 3)
    vec0 = lax.dynamic_index_in_dim(turned, core, 0, keepdims=False)
    vec1 = lax.dynamic_index_in_dim(turned, 1 - core, 0, keepdims=False)
    vec_prev = step_rows(vec0, 1)
    vnext0 = step_rows(vec0, -1)
    vnext1 = swap(vnext0)
    unit1 = unit(1)
    next1 = swap(next0)

    sum_shape, mirror_shape = shape((2, 64, HALF)), shape((2, 2, 64, HALF))
    tiles_own, forward, mirror_own = call(
        functools.partial(local_kernel, True),
        (shape((3, 2, HALF, HALF), bf16), sum_shape, mirror_shape),
        2 * 10**9, 4 * 10**6, 10**6,
    )(in_specs=[SMEM] + [VMEM] * 4)(flags, unit0, unit1, vec0, vec1)
    tiles_near, forward, before, mirror_next = call(
        functools.partial(near_kernel, True),
        (shape((8, 2, HALF, HALF), bf16), sum_shape, sum_shape, mirror_shape),
        4 * 10**9, 8 * 10**6, 2 * 10**6,
    )(in_specs=[SMEM] + [VMEM] * 9)(
        flags, unit0, unit_prev, next0, next1, vec0, vec_prev, vnext0, vnext1, forward
    )
    sketch, pair0 = call(total_kernel, (sum_shape, shape((2, 128, HALF), bf16)), 10**6, 2 * 10**6)(
        in_specs=[VMEM] * 5
    )(*spread(forward, before, mirror_own, mirror_next))

    pair_prev = step_rows(pair0, 1)
    pnext0 = step_rows(pair0, -1)
    pair1 = swap(pair0)
    pnext1 = swap(pnext0)
    gram_shape = shape((32, 128))
    first_gram = call(functools.partial(gram_kernel, scale), gram_shape, 10**8, 10**6)(
        in_specs=[VMEM]
    )(sketch)
    forward, mirror_own = call(
        functools.partial(local_kernel, False), (sum_shape, mirror_shape), 10**9, 3 * 10**6
    )(in_specs=[SMEM] + [VMEM] * 3)(flags, tiles_own, pair0, pair1)
    forward, before, mirror_next = call(
        functools.partial(near_kernel, False), (sum_shape, sum_shape, mirror_shape), 10**9, 8 * 10**6
    )(in_specs=[SMEM] + [VMEM] * 6)(flags, tiles_near, pair0, pair_prev, pnext0, pnext1, forward)
    image = call(total_kernel, sum_shape, 10**6, 2 * 10**6)(in_specs=[VMEM] * 5)(
        *spread(forward, before, mirror_own, mirror_next)
    )
    keep, give, half = call(
        functools.partial(second_gram_kernel, scale),
        (gram_shape, gram_shape, shape((64, HALF))),
        10**8, 10**6,
    )(in_specs=[SMEM, VMEM, VMEM])(core_ref, first_gram, image)
    got = swap(half)
    mine = sum_over_chips(keep + swap(give))
    other = swap(mine)
    basis, factor = call(finish_kernel, (shape((64, BLK)), shape((64, 64))), 10**8, 10**6)(
        in_specs=[SMEM] + [VMEM] * 4
    )(core_ref, mine, other, image, got)
    return basis.T, factor


def solution(mesh):
    in_specs = (P("rows", None), P("rows", None), P(("rows", "cols"), None))
    out_specs = (P(("rows", "cols"), None), P())
    return jax.shard_map(local, mesh=mesh, in_specs=in_specs, out_specs=out_specs, check_vma=False)
```

time: 550 us -> 143 us (0.26)
  waiting for transfers between devices: 208 us -> 59.4 us
  blocking collectives: 158 us -> 10.3 us
  starting transfers between devices: 118 us -> 42 us
  other arithmetic: 36.2 us -> 0.69 us
  Pallas kernels: 0 us -> 25.6 us
  between operations: 14.3 us -> 0.87 us
  matrix products: 6.28 us -> 0 us
    psum x2 -> x0, blocking collectives: 155 us -> none  [orthonormal(): gram_matrix = lax.psum(gram_matrix, ('rows', 'cols')) / rows_total]
    reduce_scatter x2 -> x0, waiting for transfers between devices: 85.5 us -> none  [affinity_pass(): return lax.psum_scatter(flattened, 'cols', scatter_dimension=0, tiled=True)]
    ppermute x10 -> x23, starting transfers between devices: 118 us -> 38.6 us  [the longest x11 21.8 us: step_rows(): lax.ppermute(value, 'rows', [(r, (r + steps) % count) for r in range(coun...]
    ppermute x10 -> x23, waiting for transfers between devices: 122 us -> 53.3 us  [the longest x11 50.3 us: step_rows(): lax.ppermute(value, 'rows', [(r, (r + steps) % count) for r in range(coun...]
    pallas_call x0 -> x11, Pallas kernels: none -> 25.6 us  [the longest x1 7.44 us: local(): call(functools.partial(near_kernel, True), (shape((8, 2, HALF, HALF), bf1...]
    another operation x9 -> x0, other arithmetic: 23.5 us -> none  [the longest x6 13 us: orthonormal(): lower_factor = jnp.linalg.cholesky(gram_matrix)]
    all_to_all x0 -> x1, blocking collectives: none -> 10.3 us  [sum_over_chips(): lax.all_to_all(copies, 'rows', 0, 0, axis_index_groups=groups, tiled=True)]
    concatenate x3 -> x1, other arithmetic: 6.85 us -> 0.08 us  [live_flags(): own = jnp.concatenate([pair_list, swap(pair_list)], axis=0)]
  transfers between devices with their start and end apart: 12 -> 24, of which waited for: 6 -> 13; matrix products, arithmetic and copies ran while one was open for 0% -> 1% of each run, Pallas kernels for 0% -> 4%
where the time goes in v1:
time: 143 us; the launch traced here: 145 us
  waiting for transfers between devices  59.4 us (42%)
  starting transfers between devices  42 us (29%)
  Pallas kernels  25.6 us (18%)
  blocking collectives  10.3 us (7%)
  local copies, waits for them, and re-layouts  5.74 us (4%)
    ppermute x11, waiting for transfers between devices, step_rows(): lax.ppermute(value, 'rows', [(r, (r + steps) % count) for r in range(coun...  50.3 us
    ppermute x11, starting transfers between devices, step_rows(): lax.ppermute(value, 'rows', [(r, (r + steps) % count) for r in range(coun...  21.8 us
    ppermute x12, starting transfers between devices, swap(): return lax.ppermute(value, 'cols', [(0, 1), (1, 0)])  16.8 us
    all_to_all x1, blocking collectives, sum_over_chips(): lax.all_to_all(copies, 'rows', 0, 0, axis_index_groups=groups, tiled=True)  10.3 us
    pallas_call x1, Pallas kernels, local(): call(functools.partial(near_kernel, True), (shape((8, 2, HALF, HALF), bf1...  7.44 us
    pallas_call x1, Pallas kernels, local(): call(finish_kernel, (shape((64, BLK)), shape((64, 64))), 10 ** 8, 10 ** 6)  6.68 us
    all_to_all x1, waiting for transfers between devices, sum_over_chips(): lax.all_to_all(copies, 'rows', 0, 0, axis_index_groups=groups, tiled=True)  6.06 us
    pallas_call x1, Pallas kernels, local(): call(functools.partial(near_kernel, False), (sum_shape, sum_shape, mirror...  4.85 us
  transfers between devices with their start and end apart: 24, of which 13 were waited for; matrix products, arithmetic and copies ran while one was open for 1% of the time, Pallas kernels for 4%

profile of v1, /device:TPU:1, one launch (start us, length us, event | category | flops | bytes accessed | tf_op | source)
XLA Modules:
  0.0 144.7 jit_solution(6395310247513621479)
XLA Ops:
  0.6 0.0 copy-start.1
  0.7 1.3 reshape.35
  1.9 0.0 copy-start.4
  1.9 0.0 copy-start.3
  1.9 1.3 constant_dynamic-slice_fusion
  3.2 11.1 %collective-permute-start.6 = (bf16[2,64,512]{2,1,0:T(8,128)(2,1)S(1)}, bf16[2,64,512]{2,1,0:T(8,128)(2,1)S(1)}, u32[]{:S(2)}, u32[]{:S(2)}) collective-permute-start(bf16[2,64,512]{2,1,0:T(8,128)(2,1)S(1)} %bitcast.29), channel_id=1, source_target_pairs={{0,254},{2,0},{4,2},{6,4},{8,6},{10,8},{12,10},{14,12},{16,14},{18... | collective-permute-start | bytes 393224 | tf_op jit(solution)/shard_map/ppermute | solution.py:225
  14.4 1.4 copy-done
  15.8 0.3 shard_map.68.refs_0_
  16.1 7.0 %collective-permute-start.3 = (bf16[2,512,384]{2,1,0:T(8,128)(2,1)S(1)}, bf16[2,512,384]{2,1,0:T(8,128)(2,1)}, u32[]{:S(2)}, u32[]{:S(2)}) collective-permute-start(bf16[2,512,384]{2,1,0:T(8,128)(2,1)S(1)} %shard_map.68.refs_0_), channel_id=1, source_target_pairs={{0,254},{2,0},{4,2},{6,4},{8,6},{10,8},{12,10},{14,12},{16,14},{18... | collective-permute-start | bytes 2359304 | tf_op jit(solution)/shard_map/ppermute | solution.py:225
  23.0 0.0 collective-permute-start.2
  23.0 1.5 %collective-permute-start = (s32[4,2]{0,1:T(2,128)S(1)}, s32[4,2]{0,1:T(2,128)S(1)}, u32[]{:S(2)}, u32[]{:S(2)}) collective-permute-start(s32[4,2]{0,1:T(2,128)S(1)} %copy-done.2), channel_id=1, source_target_pairs={{0,1},{1,0},{2,3},{3,2},{4,5},{5,4},{6,7},{7,6},{8,9},{9,8},{10,11... | collective-permute-start | bytes 104 | tf_op jit(solution)/shard_map/ppermute | solution.py:229
  24.6 0.3 shard_map.69.refs_1_
  24.8 1.0 copy.19
  25.9 0.1 pad_add_fusion
  26.0 0.0 collective-permute-start.1
  26.0 0.1 compare_reduce_fusion
  26.1 12.5 %collective-permute-done.3.refs_2_ = bf16[2,512,384]{2,1,0:T(8,128)(2,1)} collective-permute-done((bf16[2,512,384]{2,1,0:T(8,128)(2,1)S(1)}, bf16[2,512,384]{2,1,0:T(8,128)(2,1)}, u32[]{:S(2)}, u32[]{:S(2)}) %collective-permute-start.3) | collective-permute-done | bytes 786464 | tf_op jit(solution)/shard_map/ppermute | solution.py:225
  38.6 2.2 %collective-permute-start.4 = (bf16[2,512,384]{2,1,0:T(8,128)(2,1)}, bf16[2,512,384]{2,1,0:T(8,128)(2,1)S(1)}, u32[]{:S(2)}, u32[]{:S(2)}) collective-permute-start(bf16[2,512,384]{2,1,0:T(8,128)(2,1)} %collective-permute-done.3.refs_2_), channel_id=1, source_target_pairs={{0,1},{1,0},{2,3},{3,2},{4,5},{5,4},{6,7},{7,6},{8,9},{9,8},{10,11... | collective-permute-start | bytes 2359304 | tf_op jit(solution)/shard_map/ppermute | solution.py:229
  40.8 0.1 and_reduce_fusion
  40.9 5.2 %collective-permute-done.1 = s32[8,2]{0,1:T(2,128)S(1)} collective-permute-done((s32[8,2]{0,1:T(2,128)S(1)}, s32[8,2]{0,1:T(2,128)S(1)}, u32[]{:S(2)}, u32[]{:S(2)}) %collective-permute-start.1) | collective-permute-done | bytes 96 | tf_op jit(solution)/shard_map/ppermute | solution.py:225
  46.1 0.1 compare_reduce_fusion.1
  46.2 0.1 and_reduce_fusion.1
  46.3 0.1 add_convert_fusion.flags_ref
  46.4 0.0 collective-permute-done.6.refs_6_
  46.4 2.5 %collective-permute-start.7 = (bf16[2,64,512]{2,1,0:T(8,128)(2,1)S(1)}, bf16[2,64,512]{2,1,0:T(8,128)(2,1)S(1)}, u32[]{:S(2)}, u32[]{:S(2)}) collective-permute-start(bf16[2,64,512]{2,1,0:T(8,128)(2,1)S(1)} %collective-permute-done.6.refs_6_), channel_id=1, source_target_pairs={{0,1},{1,0},{2,3},{3,2},{4,5},{5,4},{6,7},{7,6},{8,9},{9,8},{10,11... | collective-permute-start | bytes 393224 | tf_op jit(solution)/shard_map/ppermute | solution.py:229
  48.9 3.2 %shard_map.70 = (bf16[3,2,512,512]{3,2,1,0:T(8,128)(2,1)S(1)}, f32[2,64,512]{2,1,0:T(8,128)S(1)}, f32[2,2,64,512]{3,2,1,0:T(8,128)S(1)}) custom-call(s32[11]{0:T(128)S(1)} %add_convert_fusion.flags_ref, bf16[2,512,384]{2,1,0:T(8,128)(2,1)S(1)} %shard_map.68.refs_0_, bf16[2,512,384]{2,1,0:T(8,128)(2,1)S(1)} %shard_map.69.refs_1_, ...), custom_call_target="tpu_custom_call" | custom-call | flops 2000000000 | bytes 4000000 | tf_op jit(solution)/shard_map/pallas_call | solution.py:294
  52.1 0.0 collective-permute-done.2.refs_1_
  52.1 0.0 collective-permute-done.4.refs_3_
  52.1 7.4 %shard_map.71 = (bf16[8,2,512,512]{3,2,1,0:T(8,128)(2,1)}, f32[2,64,512]{2,1,0:T(8,128)S(1)}, f32[2,64,512]{2,1,0:T(8,128)S(1)}, f32[2,2,64,512]{3,2,1,0:T(8,128)S(1)}) custom-call(s32[11]{0:T(128)S(1)} %add_convert_fusion.flags_ref, bf16[2,512,384]{2,1,0:T(8,128)(2,1)S(1)} %shard_map.68.refs_0_, bf16[2,512,384]{2,1,0:T(8,128)(2,1)} %collective-permute-done.2.refs_1_, ...), custom_call_target="tpu_custom_call" | custom-call | flops 4000000000 | bytes 8000000 | tf_op jit(solution)/shard_map/pallas_call | solution.py:299
  59.6 0.1 collective-permute-start.10
  59.7 0.6 collective-permute-start.8
  60.3 0.9 collective-permute-done.10
  61.2 0.8 collective-permute-start.11
  62.1 6.1 %collective-permute-done.9.from_next = f32[2,64,512]{2,1,0:T(8,128)S(1)} collective-permute-done((f32[2,64,512]{2,1,0:T(8,128)S(1)}, f32[2,64,512]{2,1,0:T(8,128)S(1)}, u32[]{:S(2)}, u32[]{:S(2)}) %collective-permute-start.9) | collective-permute-done | bytes 262176 | tf_op jit(solution)/shard_map/ppermute | solution.py:225
  68.1 6.5 %collective-permute-done.11.from_prev = f32[2,64,512]{2,1,0:T(8,128)S(1)} collective-permute-done((f32[2,64,512]{2,1,0:T(8,128)S(1)}, f32[2,64,512]{2,1,0:T(8,128)S(1)}, u32[]{:S(2)}, u32[]{:S(2)}) %collective-permute-start.11) | collective-permute-done | bytes 262176 | tf_op jit(solution)/shard_map/ppermute | solution.py:225
  74.7 0.1 shard_map.72
  74.8 0.1 collective-permute-start.13
  74.9 1.0 collective-permute-start.15
  75.9 1.6 %collective-permute-start.12 = (bf16[2,128,512]{2,1,0:T(8,128)(2,1)S(1)}, bf16[2,128,512]{2,1,0:T(8,128)(2,1)S(1)}, u32[]{:S(2)}, u32[]{:S(2)}) collective-permute-start(bf16[2,128,512]{2,1,0:T(8,128)(2,1)S(1)} %get-tuple-element.28.refs_1_), channel_id=1, source_target_pairs={{0,2},{2,4},{4,6},{6,8},{8,10},{10,12},{12,14},{14,16},{16,18},{18... | collective-permute-start | bytes 786440 | tf_op jit(solution)/shard_map/ppermute | solution.py:225
  77.6 4.2 %collective-permute-done.13.refs_3_ = bf16[2,128,512]{2,1,0:T(8,128)(2,1)S(1)} collective-permute-done((bf16[2,128,512]{2,1,0:T(8,128)(2,1)S(1)}, bf16[2,128,512]{2,1,0:T(8,128)(2,1)S(1)}, u32[]{:S(2)}, u32[]{:S(2)}) %collective-permute-start.13) | collective-permute-done | bytes 262176 | tf_op jit(solution)/shard_map/ppermute | solution.py:225
  81.7 1.9 %collective-permute-start.14 = (bf16[2,128,512]{2,1,0:T(8,128)(2,1)S(1)}, bf16[2,128,512]{2,1,0:T(8,128)(2,1)S(1)}, u32[]{:S(2)}, u32[]{:S(2)}) collective-permute-start(bf16[2,128,512]{2,1,0:T(8,128)(2,1)S(1)} %collective-permute-done.13.refs_3_), channel_id=1, source_target_pairs={{0,1},{1,0},{2,3},{3,2},{4,5},{5,4},{6,7},{7,6},{8,9},{9,8},{10,11... | collective-permute-start | bytes 786440 | tf_op jit(solution)/shard_map/ppermute | solution.py:229
  83.6 1.9 %shard_map.74 = (f32[2,64,512]{2,1,0:T(8,128)S(1)}, f32[2,2,64,512]{3,2,1,0:T(8,128)S(1)}) custom-call(s32[11]{0:T(128)S(1)} %add_convert_fusion.flags_ref, bf16[3,2,512,512]{3,2,1,0:T(8,128)(2,1)S(1)} %get-tuple-element.29.refs_0_, bf16[2,128,512]{2,1,0:T(8,128)(2,1)S(1)} %get-tuple-element.28.refs_1_, bf16[2,128,512]{2,1,0:T(8,128)(2,1)S(1)} %collective-permute-done.15.refs_2_), custom_call_target="tpu_custom_call" | custom-call | flops 1000000000 | bytes 3000000 | tf_op jit(solution)/shard_map/pallas_call | solution.py:318
  85.5 3.7 %collective-permute-done.12.refs_2_ = bf16[2,128,512]{2,1,0:T(8,128)(2,1)S(1)} collective-permute-done((bf16[2,128,512]{2,1,0:T(8,128)(2,1)S(1)}, bf16[2,128,512]{2,1,0:T(8,128)(2,1)S(1)}, u32[]{:S(2)}, u32[]{:S(2)}) %collective-permute-start.12) | collective-permute-done | bytes 262176 | tf_op jit(solution)/shard_map/ppermute | solution.py:225
  89.2 4.9 %shard_map.75 = (f32[2,64,512]{2,1,0:T(8,128)S(1)}, f32[2,64,512]{2,1,0:T(8,128)S(1)}, f32[2,2,64,512]{3,2,1,0:T(8,128)S(1)}) custom-call(s32[11]{0:T(128)S(1)} %add_convert_fusion.flags_ref, bf16[8,2,512,512]{3,2,1,0:T(8,128)(2,1)} %get-tuple-element.27.refs_0_, bf16[2,128,512]{2,1,0:T(8,128)(2,1)S(1)} %get-tuple-element.28.refs_1_, ...), custom_call_target="tpu_custom_call" | custom-call | flops 1000000000 | bytes 8000000 | tf_op jit(solution)/shard_map/pallas_call | solution.py:321
  94.1 1.0 collective-permute-start.18
  95.1 0.1 collective-permute-start.16
  95.2 0.6 collective-permute-start.17
  95.8 0.5 collective-permute-done.18
  96.3 0.6 collective-permute-start.19
  96.9 0.4 shard_map.73.first_ref
  97.3 5.4 %collective-permute-done.17.from_next = f32[2,64,512]{2,1,0:T(8,128)S(1)} collective-permute-done((f32[2,64,512]{2,1,0:T(8,128)S(1)}, f32[2,64,512]{2,1,0:T(8,128)S(1)}, u32[]{:S(2)}, u32[]{:S(2)}) %collective-permute-start.17) | collective-permute-done | bytes 262176 | tf_op jit(solution)/shard_map/ppermute | solution.py:225
  102.7 6.6 %collective-permute-done.19.from_prev = f32[2,64,512]{2,1,0:T(8,128)S(1)} collective-permute-done((f32[2,64,512]{2,1,0:T(8,128)S(1)}, f32[2,64,512]{2,1,0:T(8,128)S(1)}, u32[]{:S(2)}, u32[]{:S(2)}) %collective-permute-start.19) | collective-permute-done | bytes 262176 | tf_op jit(solution)/shard_map/ppermute | solution.py:225
  109.3 0.1 shard_map.76.value_ref
  109.4 0.4 shard_map.77
  109.8 1.3 collective-permute-start.20
  111.1 0.8 collective-permute-done.20
  111.9 10.3 %all_to_all.10 = f32[16,32,128]{2,1,0:T(8,128)S(1)} all-to-all(f32[16,32,128]{2,1,0:T(8,128)S(1)} %broadcast_in_dim.4), channel_id=1, replica_groups={{0,2,4,6,64,66,68,70,128,130,132,134,192,194,196,198},{8,10,12,14,72,74..., dimensions={0} | all-to-all | bytes 524288 | tf_op jit(solution)/shard_map/all_to_all | solution.py:262
  122.3 0.7 broadcast_in_dim.5
  123.0 3.4 %all-to-all-start.1 = ((f32[8,32,128]{2,1,0:T(8,128)}), f32[8,32,128]{2,1,0:T(8,128)S(1)}, u32[]{:S(2)}, u32[]{:S(2)}) async-start(f32[8,32,128]{2,1,0:T(8,128)} %broadcast_in_dim.5), calls=%async_computation.1 | async-start | bytes 262144 | tf_op jit(solution)/shard_map/all_to_all | solution.py:262
  126.3 1.8 %collective-permute-start.22 = (f32[64,512]{1,0:T(8,128)S(1)}, f32[64,512]{1,0:T(8,128)S(1)}, u32[]{:S(2)}, u32[]{:S(2)}) collective-permute-start(f32[64,512]{1,0:T(8,128)S(1)} %get-tuple-element.37), channel_id=1, source_target_pairs={{0,1},{1,0},{2,3},{3,2},{4,5},{5,4},{6,7},{7,6},{8,9},{9,8},{10,11... | collective-permute-start | bytes 393224 | tf_op jit(solution)/shard_map/ppermute | solution.py:229
  128.1 6.1 %all-to-all-done.1 = f32[8,32,128]{2,1,0:T(8,128)S(1)} async-done(((f32[8,32,128]{2,1,0:T(8,128)}), f32[8,32,128]{2,1,0:T(8,128)S(1)}, u32[]{:S(2)}, u32[]{:S(2)}) %all-to-all-start.1) | async-done | bytes 131104 | tf_op jit(solution)/shard_map/all_to_all | solution.py:262
  134.2 2.9 %collective-permute-start.21 = (f32[32,128]{1,0:T(8,128)S(1)}, f32[32,128]{1,0:T(8,128)S(1)}, u32[]{:S(2)}, u32[]{:S(2)}) collective-permute-start(f32[32,128]{1,0:T(8,128)S(1)} %reduce_sum.19.mine_ref), channel_id=1, source_target_pairs={{0,1},{1,0},{2,3},{3,2},{4,5},{5,4},{6,7},{7,6},{8,9},{9,8},{10,11... | collective-permute-start | bytes 49160 | tf_op jit(solution)/shard_map/ppermute | solution.py:229
  137.1 0.8 collective-permute-done.21.other_ref
  138.0 6.7 %shard_map.78 = (f32[64,1024]{1,0:T(8,128)}, f32[64,64]{1,0:T(8,128)}) custom-call(s32[1]{0:T(128)} %bitcast.core_ref, f32[32,128]{1,0:T(8,128)S(1)} %reduce_sum.19.mine_ref, f32[32,128]{1,0:T(8,128)S(1)} %collective-permute-done.21.other_ref, f32[2,64,512]{2,1,0:T(8,128)S(1)} %shard_map.76.value_ref, f32[64,512]{1,0:T(8,128)S(1)} %collective-permute-done.22.got_ref), custom_call_target="tpu_custom_call" | custom-call | flops 100000000 | bytes 1000000 | tf_op jit(solution)/shard_map/pallas_call | solution.py:335
  (31 shorter events, 0.3 us)
Async XLA Ops:
  0.6 23.9 %copy-start.1 = (bf16[2048,384]{1,0:T(8,128)(2,1)S(1)}, bf16[2048,384]{1,0:T(8,128)(2,1)}, u32[]{:S(2)}) copy-start(bf16[2048,384]{1,0:T(8,128)(2,1)} %rows_ref.3) | copy-start | bytes 4718596
  0.6 22.4 %copy-start.2 = (s32[4,2]{0,1:T(2,128)S(1)}, s32[4,2]{0,1:T(2,128)}, u32[]{:S(2)}) copy-start(s32[4,2]{0,1:T(2,128)} %param.7) | copy-start | bytes 100
  1.9 23.9 %copy-start.4 = (s32[4,2]{0,1:T(2,128)S(1)}, s32[4,2]{0,1:T(2,128)}, u32[]{:S(2)}) copy-start(s32[4,2]{0,1:T(2,128)} %constant.33.clone) | copy-start | bytes 100
  1.9 23.9 %copy-start.3 = (s32[7,2]{0,1:T(2,128)S(1)}, s32[7,2]{0,1:T(2,128)}, u32[]{:S(2)}) copy-start(s32[7,2]{0,1:T(2,128)} %constant.32.clone) | copy-start | bytes 172
  3.2 43.1 %collective-permute-start.6 = (bf16[2,64,512]{2,1,0:T(8,128)(2,1)S(1)}, bf16[2,64,512]{2,1,0:T(8,128)(2,1)S(1)}, u32[]{:S(2)}, u32[]{:S(2)}) collective-permute-start(bf16[2,64,512]{2,1,0:T(8,128)(2,1)S(1)} %bitcast.29), channel_id=1, source_target_pairs={{0,254},{2,0},{4,2},{6,4},{8,6},{10,8},{12,10},{14,12},{16,14},{18... | collective-permute-start | bytes 393224 | tf_op jit(solution)/shard_map/ppermute | solution.py:225
  14.4 37.7 %collective-permute-start.5 = (bf16[2,64,512]{2,1,0:T(8,128)(2,1)S(1)}, bf16[2,64,512]{2,1,0:T(8,128)(2,1)S(1)}, u32[]{:S(2)}, u32[]{:S(2)}) collective-permute-start(bf16[2,64,512]{2,1,0:T(8,128)(2,1)S(1)} %bitcast.30), channel_id=1, source_target_pairs={{0,2},{2,4},{4,6},{6,8},{8,10},{10,12},{12,14},{14,16},{16,18},{18... | collective-permute-start | bytes 393224 | tf_op jit(solution)/shard_map/ppermute | solution.py:225
  14.4 1.4 copy-start
  16.1 22.6 %collective-permute-start.3 = (bf16[2,512,384]{2,1,0:T(8,128)(2,1)S(1)}, bf16[2,512,384]{2,1,0:T(8,128)(2,1)}, u32[]{:S(2)}, u32[]{:S(2)}) collective-permute-start(bf16[2,512,384]{2,1,0:T(8,128)(2,1)S(1)} %shard_map.68.refs_0_), channel_id=1, source_target_pairs={{0,254},{2,0},{4,2},{6,4},{8,6},{10,8},{12,10},{14,12},{16,14},{18... | collective-permute-start | bytes 2359304 | tf_op jit(solution)/shard_map/ppermute | solution.py:225
  23.0 29.1 %collective-permute-start.2 = (bf16[2,512,384]{2,1,0:T(8,128)(2,1)S(1)}, bf16[2,512,384]{2,1,0:T(8,128)(2,1)}, u32[]{:S(2)}, u32[]{:S(2)}) collective-permute-start(bf16[2,512,384]{2,1,0:T(8,128)(2,1)S(1)} %shard_map.68.refs_0_), channel_id=1, source_target_pairs={{0,2},{2,4},{4,6},{6,8},{8,10},{10,12},{12,14},{14,16},{16,18},{18... | collective-permute-start | bytes 2359304 | tf_op jit(solution)/shard_map/ppermute | solution.py:225
  23.0 2.8 %collective-permute-start = (s32[4,2]{0,1:T(2,128)S(1)}, s32[4,2]{0,1:T(2,128)S(1)}, u32[]{:S(2)}, u32[]{:S(2)}) collective-permute-start(s32[4,2]{0,1:T(2,128)S(1)} %copy-done.2), channel_id=1, source_target_pairs={{0,1},{1,0},{2,3},{3,2},{4,5},{5,4},{6,7},{7,6},{8,9},{9,8},{10,11... | collective-permute-start | bytes 104 | tf_op jit(solution)/shard_map/ppermute | solution.py:229
  26.0 20.1 %collective-permute-start.1 = (s32[8,2]{0,1:T(2,128)S(1)}, s32[8,2]{0,1:T(2,128)S(1)}, u32[]{:S(2)}, u32[]{:S(2)}) collective-permute-start(s32[8,2]{0,1:T(2,128)S(1)} %pad_add_fusion), channel_id=1, source_target_pairs={{0,2},{2,4},{4,6},{6,8},{8,10},{10,12},{12,14},{14,16},{16,18},{18... | collective-permute-start | bytes 200 | tf_op jit(solution)/shard_map/ppermute | solution.py:225
  38.6 13.5 %collective-permute-start.4 = (bf16[2,512,384]{2,1,0:T(8,128)(2,1)}, bf16[2,512,384]{2,1,0:T(8,128)(2,1)S(1)}, u32[]{:S(2)}, u32[]{:S(2)}) collective-permute-start(bf16[2,512,384]{2,1,0:T(8,128)(2,1)} %collective-permute-done.3.refs_2_), channel_id=1, source_target_pairs={{0,1},{1,0},{2,3},{3,2},{4,5},{5,4},{6,7},{7,6},{8,9},{9,8},{10,11... | collective-permute-start | bytes 2359304 | tf_op jit(solution)/shard_map/ppermute | solution.py:229
  46.4 5.7 %collective-permute-start.7 = (bf16[2,64,512]{2,1,0:T(8,128)(2,1)S(1)}, bf16[2,64,512]{2,1,0:T(8,128)(2,1)S(1)}, u32[]{:S(2)}, u32[]{:S(2)}) collective-permute-start(bf16[2,64,512]{2,1,0:T(8,128)(2,1)S(1)} %collective-permute-done.6.refs_6_), channel_id=1, source_target_pairs={{0,1},{1,0},{2,3},{3,2},{4,5},{5,4},{6,7},{7,6},{8,9},{9,8},{10,11... | collective-permute-start | bytes 393224 | tf_op jit(solution)/shard_map/ppermute | solution.py:229
  59.6 1.6 %collective-permute-start.10 = (f32[2,64,512]{2,1,0:T(8,128)S(1)}, f32[2,64,512]{2,1,0:T(8,128)S(1)}, u32[]{:S(2)}, u32[]{:S(2)}) collective-permute-start(f32[2,64,512]{2,1,0:T(8,128)S(1)} %slice_bitcast_fusion.2), channel_id=1, source_target_pairs={{0,1},{1,0},{2,3},{3,2},{4,5},{5,4},{6,7},{7,6},{8,9},{9,8},{10,11... | collective-permute-start | bytes 786440 | tf_op jit(solution)/shard_map/ppermute | solution.py:229
  59.7 2.4 %collective-permute-start.8 = (f32[2,64,512]{2,1,0:T(8,128)S(1)}, f32[2,64,512]{2,1,0:T(8,128)S(1)}, u32[]{:S(2)}, u32[]{:S(2)}) collective-permute-start(f32[2,64,512]{2,1,0:T(8,128)S(1)} %slice_bitcast_fusion.3), channel_id=1, source_target_pairs={{0,1},{1,0},{2,3},{3,2},{4,5},{5,4},{6,7},{7,6},{8,9},{9,8},{10,11... | collective-permute-start | bytes 786440 | tf_op jit(solution)/shard_map/ppermute | solution.py:229
  60.3 7.9 %collective-permute-start.9 = (f32[2,64,512]{2,1,0:T(8,128)S(1)}, f32[2,64,512]{2,1,0:T(8,128)S(1)}, u32[]{:S(2)}, u32[]{:S(2)}) collective-permute-start(f32[2,64,512]{2,1,0:T(8,128)S(1)} %get-tuple-element.24), channel_id=1, source_target_pairs={{0,254},{2,0},{4,2},{6,4},{8,6},{10,8},{12,10},{14,12},{16,14},{18... | collective-permute-start | bytes 786440 | tf_op jit(solution)/shard_map/ppermute | solution.py:225
  61.2 13.5 %collective-permute-start.11 = (f32[2,64,512]{2,1,0:T(8,128)S(1)}, f32[2,64,512]{2,1,0:T(8,128)S(1)}, u32[]{:S(2)}, u32[]{:S(2)}) collective-permute-start(f32[2,64,512]{2,1,0:T(8,128)S(1)} %bitcast_add_fusion.1), channel_id=1, source_target_pairs={{0,2},{2,4},{4,6},{6,8},{8,10},{10,12},{12,14},{14,16},{16,18},{18... | collective-permute-start | bytes 786440 | tf_op jit(solution)/shard_map/ppermute | solution.py:225
  74.8 6.9 %collective-permute-start.13 = (bf16[2,128,512]{2,1,0:T(8,128)(2,1)S(1)}, bf16[2,128,512]{2,1,0:T(8,128)(2,1)S(1)}, u32[]{:S(2)}, u32[]{:S(2)}) collective-permute-start(bf16[2,128,512]{2,1,0:T(8,128)(2,1)S(1)} %get-tuple-element.28.refs_1_), channel_id=1, source_target_pairs={{0,254},{2,0},{4,2},{6,4},{8,6},{10,8},{12,10},{14,12},{16,14},{18... | collective-permute-start | bytes 786440 | tf_op jit(solution)/shard_map/ppermute | solution.py:225
  74.9 8.7 %collective-permute-start.15 = (bf16[2,128,512]{2,1,0:T(8,128)(2,1)S(1)}, bf16[2,128,512]{2,1,0:T(8,128)(2,1)S(1)}, u32[]{:S(2)}, u32[]{:S(2)}) collective-permute-start(bf16[2,128,512]{2,1,0:T(8,128)(2,1)S(1)} %get-tuple-element.28.refs_1_), channel_id=1, source_target_pairs={{0,1},{1,0},{2,3},{3,2},{4,5},{5,4},{6,7},{7,6},{8,9},{9,8},{10,11... | collective-permute-start | bytes 786440 | tf_op jit(solution)/shard_map/ppermute | solution.py:229
  75.9 13.3 %collective-permute-start.12 = (bf16[2,128,512]{2,1,0:T(8,128)(2,1)S(1)}, bf16[2,128,512]{2,1,0:T(8,128)(2,1)S(1)}, u32[]{:S(2)}, u32[]{:S(2)}) collective-permute-start(bf16[2,128,512]{2,1,0:T(8,128)(2,1)S(1)} %get-tuple-element.28.refs_1_), channel_id=1, source_target_pairs={{0,2},{2,4},{4,6},{6,8},{8,10},{10,12},{12,14},{14,16},{16,18},{18... | collective-permute-start | bytes 786440 | tf_op jit(solution)/shard_map/ppermute | solution.py:225
  81.7 7.5 %collective-permute-start.14 = (bf16[2,128,512]{2,1,0:T(8,128)(2,1)S(1)}, bf16[2,128,512]{2,1,0:T(8,128)(2,1)S(1)}, u32[]{:S(2)}, u32[]{:S(2)}) collective-permute-start(bf16[2,128,512]{2,1,0:T(8,128)(2,1)S(1)} %collective-permute-done.13.refs_3_), channel_id=1, source_target_pairs={{0,1},{1,0},{2,3},{3,2},{4,5},{5,4},{6,7},{7,6},{8,9},{9,8},{10,11... | collective-permute-start | bytes 786440 | tf_op jit(solution)/shard_map/ppermute | solution.py:229
  94.1 2.1 %collective-permute-start.18 = (f32[2,64,512]{2,1,0:T(8,128)S(1)}, f32[2,64,512]{2,1,0:T(8,128)S(1)}, u32[]{:S(2)}, u32[]{:S(2)}) collective-permute-start(f32[2,64,512]{2,1,0:T(8,128)S(1)} %slice_bitcast_fusion), channel_id=1, source_target_pairs={{0,1},{1,0},{2,3},{3,2},{4,5},{5,4},{6,7},{7,6},{8,9},{9,8},{10,11... | collective-permute-start | bytes 786440 | tf_op jit(solution)/shard_map/ppermute | solution.py:229
  95.1 2.2 %collective-permute-start.16 = (f32[2,64,512]{2,1,0:T(8,128)S(1)}, f32[2,64,512]{2,1,0:T(8,128)S(1)}, u32[]{:S(2)}, u32[]{:S(2)}) collective-permute-start(f32[2,64,512]{2,1,0:T(8,128)S(1)} %slice_bitcast_fusion.1), channel_id=1, source_target_pairs={{0,1},{1,0},{2,3},{3,2},{4,5},{5,4},{6,7},{7,6},{8,9},{9,8},{10,11... | collective-permute-start | bytes 786440 | tf_op jit(solution)/shard_map/ppermute | solution.py:229
  95.2 7.5 %collective-permute-start.17 = (f32[2,64,512]{2,1,0:T(8,128)S(1)}, f32[2,64,512]{2,1,0:T(8,128)S(1)}, u32[]{:S(2)}, u32[]{:S(2)}) collective-permute-start(f32[2,64,512]{2,1,0:T(8,128)S(1)} %get-tuple-element.33), channel_id=1, source_target_pairs={{0,254},{2,0},{4,2},{6,4},{8,6},{10,8},{12,10},{14,12},{16,14},{18... | collective-permute-start | bytes 786440 | tf_op jit(solution)/shard_map/ppermute | solution.py:225
  96.3 13.0 %collective-permute-start.19 = (f32[2,64,512]{2,1,0:T(8,128)S(1)}, f32[2,64,512]{2,1,0:T(8,128)S(1)}, u32[]{:S(2)}, u32[]{:S(2)}) collective-permute-start(f32[2,64,512]{2,1,0:T(8,128)S(1)} %bitcast_add_fusion), channel_id=1, source_target_pairs={{0,2},{2,4},{4,6},{6,8},{8,10},{10,12},{12,14},{14,16},{16,18},{18... | collective-permute-start | bytes 786440 | tf_op jit(solution)/shard_map/ppermute | solution.py:225
  109.8 2.1 %collective-permute-start.20 = (f32[32,128]{1,0:T(8,128)S(1)}, f32[32,128]{1,0:T(8,128)S(1)}, u32[]{:S(2)}, u32[]{:S(2)}) collective-permute-start(f32[32,128]{1,0:T(8,128)S(1)} %get-tuple-element.36), channel_id=1, source_target_pairs={{0,1},{1,0},{2,3},{3,2},{4,5},{5,4},{6,7},{7,6},{8,9},{9,8},{10,11... | collective-permute-start | bytes 49160 | tf_op jit(solution)/shard_map/ppermute | solution.py:229
  123.0 11.2 %all-to-all-start.1 = ((f32[8,32,128]{2,1,0:T(8,128)}), f32[8,32,128]{2,1,0:T(8,128)S(1)}, u32[]{:S(2)}, u32[]{:S(2)}) async-start(f32[8,32,128]{2,1,0:T(8,128)} %broadcast_in_dim.5), calls=%async_computation.1 | async-start | bytes 262144 | tf_op jit(solution)/shard_map/all_to_all | solution.py:262
  126.3 10.8 %collective-permute-start.22 = (f32[64,512]{1,0:T(8,128)S(1)}, f32[64,512]{1,0:T(8,128)S(1)}, u32[]{:S(2)}, u32[]{:S(2)}) collective-permute-start(f32[64,512]{1,0:T(8,128)S(1)} %get-tuple-element.37), channel_id=1, source_target_pairs={{0,1},{1,0},{2,3},{3,2},{4,5},{5,4},{6,7},{7,6},{8,9},{9,8},{10,11... | collective-permute-start | bytes 393224 | tf_op jit(solution)/shard_map/ppermute | solution.py:229
  134.2 3.8 %collective-permute-start.21 = (f32[32,128]{1,0:T(8,128)S(1)}, f32[32,128]{1,0:T(8,128)S(1)}, u32[]{:S(2)}, u32[]{:S(2)}) collective-permute-start(f32[32,128]{1,0:T(8,128)S(1)} %reduce_sum.19.mine_ref), channel_id=1, source_target_pairs={{0,1},{1,0},{2,3},{3,2},{4,5},{5,4},{6,7},{7,6},{8,9},{9,8},{10,11... | collective-permute-start | bytes 49160 | tf_op jit(solution)/shard_map/ppermute | solution.py:229

commit v2 on v1

--- a/solution.py
+++ b/solution.py
@@ -14,19 +14,20 @@
 LOG2E = 1.4426950408889634
 HIGHEST = lax.Precision.HIGHEST
 VMEM = pl.BlockSpec(memory_space=pltpu.VMEM)
+HBM = pl.BlockSpec(memory_space=pltpu.HBM)
 SMEM = pl.BlockSpec(memory_space=pltpu.SMEM)
 NT = (((1,), (1,)), ((), ()))
 NN = (((1,), (0,)), ((), ()))
 ACROSS, PLANES, RING = 4, 8, 4
 
 
-def call(kernel, outs, flops, moved, exps=0):
+def call(kernel, outs, flops, moved, exps=0, room=16):
     return functools.partial(
         pl.pallas_call,
         kernel,
         out_shape=outs,
         out_specs=jax.tree.map(lambda _: VMEM, outs),
-        compiler_params=pltpu.CompilerParams(vmem_limit_bytes=48 * 1024 * 1024),
+        compiler_params=pltpu.CompilerParams(vmem_limit_bytes=room * 1024 * 1024),
         cost_estimate=pl.CostEstimate(flops=flops, bytes_accessed=moved, transcendentals=exps),
     )
 
@@ -41,14 +42,41 @@
     )
 
 
-def unit_kernel(relative, core_ref, rows_ref, unit_ref):
-    core = core_ref[0]
-    side = core if relative == 0 else 1 - core
+def packet_kernel(relative, core_ref, rows_ref, columns_ref, packet_ref, raw_ref, vec_ref, sems):
+    side = core_ref[0] if relative == 0 else 1 - core_ref[0]
+    copies = []
     for block in range(2):
         start = pl.multiple_of(block * BLK + side * HALF, HALF)
-        widened = rows_ref[pl.ds(start, HALF), :].astype(jnp.float32)
+        copies.append((
+            pltpu.make_async_copy(rows_ref.at[pl.ds(start, HALF), :], raw_ref.at[block], sems.at[block]),
+            pltpu.make_async_copy(
+                columns_ref.at[:, pl.ds(start, HALF)], vec_ref.at[block], sems.at[2 + block]
+            ),
+        ))
+        for copy in copies[-1]:
+            copy.start()
+    for block in range(2):
+        for copy in copies[block]:
+            copy.wait()
+        widened = raw_ref[block].astype(jnp.float32)
         inverse = lax.rsqrt(jnp.sum(widened * widened, axis=1, keepdims=True) + EPSILON)
-        unit_ref[block] = (widened * inverse).astype(jnp.bfloat16)
+        unit = (widened * inverse).astype(jnp.bfloat16)
+        for tile in range(3):
+            packet_ref[block, HALF * tile : HALF * (tile + 1)] = unit[:, 128 * tile : 128 * (tile + 1)]
+        for tile in range(4):
+            packet_ref[block, 1536 + 64 * tile : 1600 + 64 * tile] = vec_ref[
+                block, :, 128 * tile : 128 * (tile + 1)
+            ]
+
+
+def unit_rows(packet, start, count):
+    return jnp.concatenate(
+        [packet[HALF * tile + start : HALF * tile + start + count] for tile in range(3)], axis=1
+    )
+
+
+def vectors(packet):
+    return jnp.concatenate([packet[1536 + 64 * tile : 1600 + 64 * tile] for tile in range(4)], axis=1)
 
 
 def affinity_tile(left, right):
@@ -63,20 +91,21 @@
 
 
 def make_tiles(left, rights, tile_ref, slot):
+    whole = unit_rows(left, 0, HALF)
     for side in range(2):
         for at in range(0, HALF, 256):
             tile_ref[slot, side, :, at : at + 256] = affinity_tile(
-                left, rights[side][at : at + 256]
+                whole, unit_rows(rights[side], at, 256)
             )
 
 
-def use_tiles(tile_ref, slot, ahead, behind, forward_ref, forward_at, mirror_ref, mirror_at, mirror):
+def use_tiles(tile_ref, slot, ahead, behind, forward_ref, forward_at, mirror_refs, mirror_at, mirror):
     total = fold(dot(ahead[0], tile_ref[slot, 0], NT)) + fold(dot(ahead[1], tile_ref[slot, 1], NT))
     forward_ref[forward_at] += total
 
     def put_mirror():
         for side in range(2):
-            mirror_ref[side, mirror_at] += fold(dot(behind, tile_ref[slot, side], NN))
+            mirror_refs[side][mirror_at] += fold(dot(behind, tile_ref[slot, side], NN))
 
     if mirror is None:
         put_mirror()
@@ -86,11 +115,12 @@
 
 def local_kernel(make, flags_ref, *refs):
     if make:
-        unit0, unit1, vec0, vec1, tile_ref, forward_ref, mirror_ref = refs
+        own0, own1, tile_ref, forward_ref, mirror0, mirror1 = refs
     else:
-        tile_ref, vec0, vec1, forward_ref, mirror_ref = refs
-    forward_ref[...] = jnp.zeros_like(forward_ref)
-    mirror_ref[...] = jnp.zeros_like(mirror_ref)
+        tile_ref, own0, own1, forward_ref, mirror0, mirror1 = refs
+    for ref in (forward_ref, mirror0, mirror1):
+        ref[...] = jnp.zeros_like(ref)
+    take = vectors if make else (lambda ref: ref[...])
 
     @pl.loop(0, 3)
     def _(slot):
@@ -99,45 +129,45 @@
         @pl.when(flags_ref[slot] > 0)
         def _():
             if make:
-                make_tiles(unit0[first], (unit0.at[second], unit1.at[second]), tile_ref, slot)
+                make_tiles(own0.at[first], (own0.at[second], own1.at[second]), tile_ref, slot)
             use_tiles(
-                tile_ref, slot, (vec0[second], vec1[second]), vec0[first],
-                forward_ref, first, mirror_ref, second, slot == 1,
+                tile_ref, slot, (take(own0.at[second]), take(own1.at[second])), take(own0.at[first]),
+                forward_ref, first, (mirror0, mirror1), second, slot == 1,
             )
 
 
 def near_kernel(make, flags_ref, *refs):
     if make:
-        (unit0, unit_prev, next0, next1, vec0, vec_prev, vnext0, vnext1, started,
-         tile_ref, forward_ref, before_ref, mirror_ref) = refs
+        own0, prev, next0, next1, started, tile_ref, forward_ref, before_ref, mirror0, mirror1 = refs
     else:
-        (tile_ref, vec0, vec_prev, vnext0, vnext1, started,
-         forward_ref, before_ref, mirror_ref) = refs
+        tile_ref, own0, prev, next0, next1, started, forward_ref, before_ref, mirror0, mirror1 = refs
     forward_ref[...] = started[...]
-    before_ref[...] = jnp.zeros_like(before_ref)
-    mirror_ref[...] = jnp.zeros_like(mirror_ref)
+    for ref in (before_ref, mirror0, mirror1):
+        ref[...] = jnp.zeros_like(ref)
+    take = vectors if make else (lambda ref: ref[...])
     for kind in range(2):
 
         @pl.loop(0, 4)
         def _(index):
             first, second = index // 2, index % 2
             slot = kind * 4 + index
+            left = (own0, prev)[kind]
 
             @pl.when(flags_ref[3 + slot] > 0)
             def _():
                 if make:
-                    left = (unit0, unit_prev)[kind][first]
-                    make_tiles(left, (next0.at[second], next1.at[second]), tile_ref, slot)
+                    make_tiles(left.at[first], (next0.at[second], next1.at[second]), tile_ref, slot)
                 use_tiles(
-                    tile_ref, slot, (vnext0[second], vnext1[second]), (vec0, vec_prev)[kind][first],
-                    (forward_ref, before_ref)[kind], first, mirror_ref, second, None,
+                    tile_ref, slot, (take(next0.at[second]), take(next1.at[second])),
+                    take(left.at[first]), (forward_ref, before_ref)[kind], first,
+                    (mirror0, mirror1), second, None,
                 )
 
 
 def total_kernel(forward, mirror_mine, mirror_other, from_next, from_prev, sum_ref, pair_ref=None):
     for block in range(2):
         value = (
-            forward[block] + mirror_mine[0, block] + mirror_other[block]
+            forward[block] + mirror_mine[block] + mirror_other[block]
             + from_next[block] + from_prev[block]
         )
         sum_ref[block] = value
@@ -222,7 +252,18 @@
 
 def step_rows(value, steps):
     count = lax.axis_size("rows")
-    return lax.ppermute(value, "rows", [(r, (r + steps) % count) for r in range(count)])
+    return lax.ppermute(
+        value, "rows", [(r, r + steps) for r in range(count) if 0 <= r + steps < count]
+    )
+
+
+def cross_rows(value):
+    count = lax.axis_size("rows")
+    return lax.ppermute(
+        value,
+        ("rows", "cols"),
+        [(2 * r + c, 2 * (r + 1) + 1 - c) for r in range(count - 1) for c in range(2)],
+    )
 
 
 def swap(value):
@@ -230,26 +271,22 @@
 
 
 def live_flags(pair_list, base):
-    own = jnp.concatenate([pair_list, swap(pair_list)], axis=0)
-    before = step_rows(own, 1)
-
-    def any_of(entries, pairs):
-        table = jnp.array(pairs, jnp.int32) + base
-        hit = (entries[None, :, :] == table[:, None, :]).all(axis=2)
-        live = entries[None, :, 0] >= 0
-        return jnp.any(hit & live, axis=1)
-
+    pairs = jnp.concatenate(
+        [pair_list, swap(pair_list), step_rows(pair_list, 1), cross_rows(pair_list)], axis=0
+    )
+    from_prev = lax.broadcasted_iota(jnp.int32, (16,), 0) >= 8
+    codes = (pairs[:, 0] - base) * 8 + (pairs[:, 1] - base) + jnp.where(from_prev, 1000, 0)
     ours = [(0, 0), (0, 1), (1, 1), (0, 2), (0, 3), (1, 2), (1, 3)]
     across = [(-2, 2), (-2, 3), (-1, 2), (-1, 3)]
-    return jnp.concatenate([any_of(own, ours), any_of(before, across)]).astype(jnp.int32)
-
-
-def spread(forward, before, mirror_own, mirror_next):
+    wanted = [8 * i + j for i, j in ours] + [1000 + 8 * i + j for i, j in across]
+    hit = codes[None, :] == jnp.array(wanted, jnp.int32)[:, None]
+    return jnp.any(hit & (pairs[None, :, 0] >= 0), axis=1).astype(jnp.int32)
+
+
+def spread(forward, before, own0, other_own, next0, next1):
     from_next = step_rows(before, -1)
-    other_own = swap(mirror_own[1])
-    other_next = swap(mirror_next[1])
-    from_prev = step_rows(mirror_next[0] + other_next, 1)
-    return forward, mirror_own, other_own, from_next, from_prev
+    from_prev = step_rows(next0 + swap(next1), 1)
+    return forward, own0, other_own, from_next, from_prev
 
 
 def sum_over_chips(value):
@@ -272,57 +309,62 @@
     base = (lax.axis_index("rows") * 2).astype(jnp.int32)
     scale = 1.0 / (rows_dev * lax.axis_size("rows"))
 
-    def unit(relative):
+    test_columns = pltpu.with_memory_space_constraint(test_matrix.T, pltpu.HBM)
+    embeddings = pltpu.with_memory_space_constraint(embeddings, pltpu.HBM)
+
+    def packet(relative):
         return call(
-            functools.partial(unit_kernel, relative), shape((2, HALF, 384), bf16), 2**20, 2**21
-        )(in_specs=[SMEM, VMEM])(core_ref, embeddings)
-
-    unit0 = unit(0)
-    unit_prev = step_rows(unit0, 1)
-    next0 = step_rows(unit0, -1)
+            functools.partial(packet_kernel, relative), shape((2, 1792, 128), bf16), 10**4, 10**4,
+        )(
+            in_specs=[SMEM, HBM, HBM],
+            scratch_shapes=[
+                pltpu.VMEM((2, HALF, 384), bf16),
+                pltpu.VMEM((2, columns, HALF), bf16),
+                pltpu.SemaphoreType.DMA((4,)),
+            ],
+        )(core_ref, embeddings, test_columns)
+
+    own0 = packet(0)
+    next0 = step_rows(own0, -1)
+    prev = step_rows(own0, 1)
+    own1, pair_list = lax.optimization_barrier((packet(1), pair_list))
     flags = live_flags(pair_list, base)
-    turned = test_matrix.T.reshape(columns, 2, 2, HALF).transpose(2, 1, 0, 3)
-    vec0 = lax.dynamic_index_in_dim(turned, core, 0, keepdims=False)
-    vec1 = lax.dynamic_index_in_dim(turned, 1 - core, 0, keepdims=False)
-    vec_prev = step_rows(vec0, 1)
-    vnext0 = step_rows(vec0, -1)
-    vnext1 = swap(vnext0)
-    unit1 = unit(1)
+
+    sum_shape = shape((2, 64, HALF))
+    tiles_own, forward, mirror_own, mirror1 = call(
+        functools.partial(local_kernel, True),
+        (shape((3, 2, HALF, HALF), bf16),) + 3 * (sum_shape,),
+        10**4, 10**4,
+    )(in_specs=[SMEM] + [VMEM] * 2)(flags, own0, own1)
+    mirror1, next0, prev = lax.optimization_barrier((mirror1, next0, prev))
     next1 = swap(next0)
-
-    sum_shape, mirror_shape = shape((2, 64, HALF)), shape((2, 2, 64, HALF))
-    tiles_own, forward, mirror_own = call(
-        functools.partial(local_kernel, True),
-        (shape((3, 2, HALF, HALF), bf16), sum_shape, mirror_shape),
-        2 * 10**9, 4 * 10**6, 10**6,
-    )(in_specs=[SMEM] + [VMEM] * 4)(flags, unit0, unit1, vec0, vec1)
-    tiles_near, forward, before, mirror_next = call(
+    other_own = swap(mirror1)
+    tiles_near, forward, before, mirror0, mirror1 = call(
         functools.partial(near_kernel, True),
-        (shape((8, 2, HALF, HALF), bf16), sum_shape, sum_shape, mirror_shape),
+        (shape((8, 2, HALF, HALF), bf16),) + 4 * (sum_shape,),
         4 * 10**9, 8 * 10**6, 2 * 10**6,
-    )(in_specs=[SMEM] + [VMEM] * 9)(
-        flags, unit0, unit_prev, next0, next1, vec0, vec_prev, vnext0, vnext1, forward
-    )
+    )(in_specs=[SMEM] + [VMEM] * 5)(flags, own0, prev, next0, next1, forward)
     sketch, pair0 = call(total_kernel, (sum_shape, shape((2, 128, HALF), bf16)), 10**6, 2 * 10**6)(
         in_specs=[VMEM] * 5
-    )(*spread(forward, before, mirror_own, mirror_next))
-
+    )(*spread(forward, before, mirror_own, other_own, mirror0, mirror1))
+
+    pnext0 = step_rows(pair0, -1)
     pair_prev = step_rows(pair0, 1)
-    pnext0 = step_rows(pair0, -1)
     pair1 = swap(pair0)
     pnext1 = swap(pnext0)
     gram_shape = shape((32, 128))
     first_gram = call(functools.partial(gram_kernel, scale), gram_shape, 10**8, 10**6)(
         in_specs=[VMEM]
     )(sketch)
-    forward, mirror_own = call(
-        functools.partial(local_kernel, False), (sum_shape, mirror_shape), 10**9, 3 * 10**6
+    forward, mirror_own, mirror1 = call(
+        functools.partial(local_kernel, False), 3 * (sum_shape,), 10**9, 3 * 10**6
     )(in_specs=[SMEM] + [VMEM] * 3)(flags, tiles_own, pair0, pair1)
-    forward, before, mirror_next = call(
-        functools.partial(near_kernel, False), (sum_shape, sum_shape, mirror_shape), 10**9, 8 * 10**6
+    other_own = swap(mirror1)
+    forward, before, mirror0, mirror1 = call(
+        functools.partial(near_kernel, False), 4 * (sum_shape,), 10**9, 8 * 10**6
     )(in_specs=[SMEM] + [VMEM] * 6)(flags, tiles_near, pair0, pair_prev, pnext0, pnext1, forward)
     image = call(total_kernel, sum_shape, 10**6, 2 * 10**6)(in_specs=[VMEM] * 5)(
-        *spread(forward, before, mirror_own, mirror_next)
+        *spread(forward, before, mirror_own, other_own, mirror0, mirror1)
     )
     keep, give, half = call(
         functools.partial(second_gram_kernel, scale),

time: 143 us -> 138 us (0.965); the launches traced: 145 us -> 138 us
  waiting for transfers between devices: 59.4 us -> 31.7 us
  blocking collectives: 10.3 us -> 32.8 us
  starting transfers between devices: 42 us -> 53.1 us
  Pallas kernels: 25.6 us -> 18 us
  local copies, waits for them, and re-layouts: 5.74 us -> 0.7 us
    ppermute x11 -> x10, waiting for transfers between devices: 50.3 us -> 21.9 us  [the longest x9 14 us: step_rows(): lax.ppermute(value, 'rows', [(r, r + steps) for r in range(count) if 0 <=...]
    all_to_all x1, blocking collectives: 10.3 us -> 32.8 us  [sum_over_chips(): lax.all_to_all(copies, 'rows', 0, 0, axis_index_groups=groups, tiled=True)]
    ppermute x11 -> x10, starting transfers between devices: 21.8 us -> 36.5 us  [the longest x9 31.4 us: step_rows(): lax.ppermute(value, 'rows', [(r, r + steps) for r in range(count) if 0 <=...]
    pallas_call x1, Pallas kernels: 7.44 us -> 2.7 us  [local(): call(functools.partial(near_kernel, True), (shape((8, 2, HALF, HALF), bf1...]
    ppermute x12 -> x11, starting transfers between devices: 16.8 us -> 13.2 us  [swap(): return lax.ppermute(value, 'cols', [(0, 1), (1, 0)])]
    unnamed x12 -> x4, local copies, waits for them, and re-layouts: 2.47 us -> 0.01 us
    pallas_call x4, Pallas kernels: 7.29 us -> 5.55 us  [the longest x2 2.75 us: packet(): call(functools.partial(packet_kernel, relative), shape((2, 1792, 128), bf...]
    ppermute x12 -> x11, waiting for transfers between devices: 3.07 us -> 4.01 us  [swap(): return lax.ppermute(value, 'cols', [(0, 1), (1, 0)])]
  transfers between devices with their start and end apart: 24 -> 22, of which waited for: 13 -> 12; matrix products, arithmetic and copies ran while one was open for 1% -> 0% of each run, Pallas kernels for 4% -> 4%
where the time goes in v2:
time: 138 us
  starting transfers between devices  53.1 us (38%)
  blocking collectives  32.8 us (24%)
  waiting for transfers between devices  31.7 us (23%)
  Pallas kernels  18 us (13%)
    all_to_all x1, blocking collectives, sum_over_chips(): lax.all_to_all(copies, 'rows', 0, 0, axis_index_groups=groups, tiled=True)  32.8 us
    ppermute x9, starting transfers between devices, step_rows(): lax.ppermute(value, 'rows', [(r, r + steps) for r in range(count) if 0 <=...  31.4 us
    ppermute x9, waiting for transfers between devices, step_rows(): lax.ppermute(value, 'rows', [(r, r + steps) for r in range(count) if 0 <=...  14 us
    ppermute x11, starting transfers between devices, swap(): return lax.ppermute(value, 'cols', [(0, 1), (1, 0)])  13.2 us
    ppermute x1, waiting for transfers between devices, cross_rows(): lax.ppermute(value, ('rows', 'cols'), [(2 * r + c, 2 * (r + 1) + 1 - c) f...  7.89 us
    pallas_call x1, Pallas kernels, local(): call(finish_kernel, (shape((64, BLK)), shape((64, 64))), 10 ** 8, 10 ** 6)  6.68 us
    all_to_all x1, waiting for transfers between devices, sum_over_chips(): lax.all_to_all(copies, 'rows', 0, 0, axis_index_groups=groups, tiled=True)  5.73 us
    ppermute x1, starting transfers between devices, cross_rows(): lax.ppermute(value, ('rows', 'cols'), [(2 * r + c, 2 * (r + 1) + 1 - c) f...  5.11 us
  transfers between devices with their start and end apart: 22, of which 12 were waited for; matrix products, arithmetic and copies ran while one was open for 0% of the time, Pallas kernels for 4%

profile of v2, /device:TPU:1, one launch (start us, length us, event | category | flops | bytes accessed | tf_op | source)
XLA Modules:
  0.0 137.6 jit_solution(3890320839928908414)
XLA Ops:
  0.6 0.0 copy-start.1
  0.6 0.0 copy-start
  0.7 1.4 %shard_map.60.refs_0_ = bf16[2,1792,128]{2,1,0:T(8,128)(2,1)S(1)} custom-call(s32[1]{0:T(128)} %bitcast.core_ref, bf16[2048,384]{1,0:T(8,128)(2,1)} %rows_ref.3, bf16[64,2048]{1,0:T(8,128)(2,1)} %bitcast.7), custom_call_target="tpu_custom_call" | custom-call | flops 10000 | bytes 10000 | tf_op jit(solution)/shard_map/pallas_call | solution.py:316
  2.0 4.1 %collective-permute-start.4 = (bf16[2,1792,128]{2,1,0:T(8,128)(2,1)S(1)}, bf16[2,1792,128]{2,1,0:T(8,128)(2,1)S(1)}, u32[]{:S(2)}, u32[]{:S(2)}) collective-permute-start(bf16[2,1792,128]{2,1,0:T(8,128)(2,1)S(1)} %shard_map.60.refs_0_), channel_id=1, source_target_pairs={{0,2},{2,4},{4,6},{6,8},{8,10},{10,12},{12,14},{14,16},{16,18},{18... | collective-permute-start | bytes 2752520 | tf_op jit(solution)/shard_map/ppermute | solution.py:255
  6.1 1.3 collective-permute-start.3
  7.4 1.4 %shard_map.59.refs_1_ = bf16[2,1792,128]{2,1,0:T(8,128)(2,1)S(1)} custom-call(s32[1]{0:T(128)} %bitcast.core_ref, bf16[2048,384]{1,0:T(8,128)(2,1)} %rows_ref.3, bf16[64,2048]{1,0:T(8,128)(2,1)} %bitcast.8), custom_call_target="tpu_custom_call" | custom-call | flops 10000 | bytes 10000 | tf_op jit(solution)/shard_map/pallas_call | solution.py:316
  8.8 0.0 copy-done
  8.8 5.1 %collective-permute-start.2 = (s32[4,2]{0,1:T(2,128)S(1)}, s32[4,2]{0,1:T(2,128)S(1)}, u32[]{:S(2)}, u32[]{:S(2)}) collective-permute-start(s32[4,2]{0,1:T(2,128)S(1)} %copy-done), channel_id=1, source_target_pairs={{0,3},{1,2},{2,5},{3,4},{4,7},{5,6},{6,9},{7,8},{8,11},{9,10},{10,... | collective-permute-start | bytes 104 | tf_op jit(solution)/shard_map/ppermute | solution.py:262
  13.9 3.2 %collective-permute-start.1 = (s32[4,2]{0,1:T(2,128)S(1)}, s32[4,2]{0,1:T(2,128)S(1)}, u32[]{:S(2)}, u32[]{:S(2)}) collective-permute-start(s32[4,2]{0,1:T(2,128)S(1)} %copy-done), channel_id=1, source_target_pairs={{0,2},{2,4},{4,6},{6,8},{8,10},{10,12},{12,14},{14,16},{16,18},{18... | collective-permute-start | bytes 104 | tf_op jit(solution)/shard_map/ppermute | solution.py:255
  17.1 0.1 collective-permute-start
  17.2 7.9 %collective-permute-done.2 = s32[4,2]{0,1:T(2,128)S(1)} collective-permute-done((s32[4,2]{0,1:T(2,128)S(1)}, s32[4,2]{0,1:T(2,128)S(1)}, u32[]{:S(2)}, u32[]{:S(2)}) %collective-permute-start.2) | collective-permute-done | bytes 64 | tf_op jit(solution)/shard_map/ppermute | solution.py:262
  25.1 0.0 collective-permute-done.1
  25.1 0.0 collective-permute-done
  25.1 0.1 pad_add_fusion
  25.2 0.0 copy-done.1
  25.2 0.2 and_reduce_fusion
  25.4 2.1 %shard_map.61 = (bf16[3,2,512,512]{3,2,1,0:T(8,128)(2,1)S(1)}, f32[2,64,512]{2,1,0:T(8,128)S(1)}, f32[2,64,512]{2,1,0:T(8,128)S(1)}, f32[2,64,512]{2,1,0:T(8,128)S(1)}) custom-call(s32[11]{0:T(128)S(1)} %convert_element_type.3.flags_ref, bf16[2,1792,128]{2,1,0:T(8,128)(2,1)S(1)} %shard_map.60.refs_0_, bf16[2,1792,128]{2,1,0:T(8,128)(2,1)S(1)} %shard_map.59.refs_1_), custom_call_target="tpu_custom_call" | custom-call | flops 10000 | bytes 10000 | tf_op jit(solution)/shard_map/pallas_call | solution.py:334
  27.5 0.0 collective-permute-done.4.refs_1_
  27.5 1.5 %collective-permute-done.3.refs_2_ = bf16[2,1792,128]{2,1,0:T(8,128)(2,1)} collective-permute-done((bf16[2,1792,128]{2,1,0:T(8,128)(2,1)S(1)}, bf16[2,1792,128]{2,1,0:T(8,128)(2,1)}, u32[]{:S(2)}, u32[]{:S(2)}) %collective-permute-start.3) | collective-permute-done | bytes 917536 | tf_op jit(solution)/shard_map/ppermute | solution.py:255
  29.0 1.9 %collective-permute-start.5 = (bf16[2,1792,128]{2,1,0:T(8,128)(2,1)}, bf16[2,1792,128]{2,1,0:T(8,128)(2,1)S(1)}, u32[]{:S(2)}, u32[]{:S(2)}) collective-permute-start(bf16[2,1792,128]{2,1,0:T(8,128)(2,1)} %collective-permute-done.3.refs_2_), channel_id=1, source_target_pairs={{0,1},{1,0},{2,3},{3,2},{4,5},{5,4},{6,7},{7,6},{8,9},{9,8},{10,11... | collective-permute-start | bytes 2752520 | tf_op jit(solution)/shard_map/ppermute | solution.py:270
  30.9 2.3 %collective-permute-done.5.refs_3_ = bf16[2,1792,128]{2,1,0:T(8,128)(2,1)S(1)} collective-permute-done((bf16[2,1792,128]{2,1,0:T(8,128)(2,1)}, bf16[2,1792,128]{2,1,0:T(8,128)(2,1)S(1)}, u32[]{:S(2)}, u32[]{:S(2)}) %collective-permute-start.5) | collective-permute-done | bytes 917536 | tf_op jit(solution)/shard_map/ppermute | solution.py:270
  33.2 2.7 %shard_map.62 = (bf16[8,2,512,512]{3,2,1,0:T(8,128)(2,1)S(1)}, f32[2,64,512]{2,1,0:T(8,128)S(1)}, f32[2,64,512]{2,1,0:T(8,128)S(1)}, f32[2,64,512]{2,1,0:T(8,128)S(1)}, f32[2,64,512]{2,1,0:T(8,128)S(1)}) custom-call(s32[11]{0:T(128)S(1)} %convert_element_type.3.flags_ref, bf16[2,1792,128]{2,1,0:T(8,128)(2,1)S(1)} %shard_map.60.refs_0_, ...), custom_call_target="tpu_custom_call" | custom-call | flops 4000000000 | bytes 8000000 | tf_op jit(solution)/shard_map/pallas_call | solution.py:342
  35.9 0.5 collective-permute-start.8
  36.4 0.1 collective-permute-start.6
  36.5 1.3 collective-permute-start.7
  37.8 0.0 collective-permute-done.8
  37.9 7.7 %collective-permute-start.9 = (f32[2,64,512]{2,1,0:T(8,128)S(1)}, f32[2,64,512]{2,1,0:T(8,128)S(1)}, u32[]{:S(2)}, u32[]{:S(2)}) collective-permute-start(f32[2,64,512]{2,1,0:T(8,128)S(1)} %add.29), channel_id=1, source_target_pairs={{0,2},{2,4},{4,6},{6,8},{8,10},{10,12},{12,14},{14,16},{16,18},{18... | collective-permute-start | bytes 786440 | tf_op jit(solution)/shard_map/ppermute | solution.py:255
  45.6 0.0 collective-permute-done.6.mirror_other
  45.6 4.3 %collective-permute-done.7.from_next = f32[2,64,512]{2,1,0:T(8,128)S(1)} collective-permute-done((f32[2,64,512]{2,1,0:T(8,128)S(1)}, f32[2,64,512]{2,1,0:T(8,128)S(1)}, u32[]{:S(2)}, u32[]{:S(2)}) %collective-permute-start.7) | collective-permute-done | bytes 262176 | tf_op jit(solution)/shard_map/ppermute | solution.py:255
  49.9 0.9 collective-permute-done.9.from_prev
  50.8 0.1 shard_map.63
  50.9 1.3 collective-permute-start.11
  52.2 1.3 collective-permute-start.13
  53.5 4.7 %collective-permute-start.10 = (bf16[2,128,512]{2,1,0:T(8,128)(2,1)S(1)}, bf16[2,128,512]{2,1,0:T(8,128)(2,1)S(1)}, u32[]{:S(2)}, u32[]{:S(2)}) collective-permute-start(bf16[2,128,512]{2,1,0:T(8,128)(2,1)S(1)} %get-tuple-element.44.refs_1_), channel_id=1, source_target_pairs={{0,2},{2,4},{4,6},{6,8},{8,10},{10,12},{12,14},{14,16},{16,18},{18... | collective-permute-start | bytes 786440 | tf_op jit(solution)/shard_map/ppermute | solution.py:255
  58.3 2.2 %collective-permute-done.11.refs_3_ = bf16[2,128,512]{2,1,0:T(8,128)(2,1)S(1)} collective-permute-done((bf16[2,128,512]{2,1,0:T(8,128)(2,1)S(1)}, bf16[2,128,512]{2,1,0:T(8,128)(2,1)S(1)}, u32[]{:S(2)}, u32[]{:S(2)}) %collective-permute-start.11) | collective-permute-done | bytes 262176 | tf_op jit(solution)/shard_map/ppermute | solution.py:255
  60.4 1.8 %collective-permute-start.12 = (bf16[2,128,512]{2,1,0:T(8,128)(2,1)S(1)}, bf16[2,128,512]{2,1,0:T(8,128)(2,1)S(1)}, u32[]{:S(2)}, u32[]{:S(2)}) collective-permute-start(bf16[2,128,512]{2,1,0:T(8,128)(2,1)S(1)} %collective-permute-done.11.refs_3_), channel_id=1, source_target_pairs={{0,1},{1,0},{2,3},{3,2},{4,5},{5,4},{6,7},{7,6},{8,9},{9,8},{10,11... | collective-permute-start | bytes 786440 | tf_op jit(solution)/shard_map/ppermute | solution.py:270
  62.3 0.0 collective-permute-done.13.refs_2_
  62.3 1.4 %shard_map.65 = (f32[2,64,512]{2,1,0:T(8,128)S(1)}, f32[2,64,512]{2,1,0:T(8,128)S(1)}, f32[2,64,512]{2,1,0:T(8,128)S(1)}) custom-call(s32[11]{0:T(128)S(1)} %convert_element_type.3.flags_ref, bf16[3,2,512,512]{3,2,1,0:T(8,128)(2,1)S(1)} %get-tuple-element.45.refs_0_, bf16[2,128,512]{2,1,0:T(8,128)(2,1)S(1)} %get-tuple-element.44.refs_1_, ...), custom_call_target="tpu_custom_call" | custom-call | flops 1000000000 | bytes 3000000 | tf_op jit(solution)/shard_map/pallas_call | solution.py:359
  63.7 0.2 collective-permute-done.10.refs_2_
  64.0 0.0 collective-permute-done.12.refs_4_
  64.0 1.4 shard_map.66
  65.3 0.9 collective-permute-start.16
  66.2 0.1 collective-permute-start.14
  66.3 1.3 collective-permute-start.15
  67.6 0.0 collective-permute-done.16
  67.7 6.6 %collective-permute-start.17 = (f32[2,64,512]{2,1,0:T(8,128)S(1)}, f32[2,64,512]{2,1,0:T(8,128)S(1)}, u32[]{:S(2)}, u32[]{:S(2)}) collective-permute-start(f32[2,64,512]{2,1,0:T(8,128)S(1)} %add.30), channel_id=1, source_target_pairs={{0,2},{2,4},{4,6},{6,8},{8,10},{10,12},{12,14},{14,16},{16,18},{18... | collective-permute-start | bytes 786440 | tf_op jit(solution)/shard_map/ppermute | solution.py:255
  74.3 0.4 shard_map.64.first_ref
  74.7 0.0 collective-permute-done.14.mirror_other
  74.7 3.9 %collective-permute-done.15.from_next = f32[2,64,512]{2,1,0:T(8,128)S(1)} collective-permute-done((f32[2,64,512]{2,1,0:T(8,128)S(1)}, f32[2,64,512]{2,1,0:T(8,128)S(1)}, u32[]{:S(2)}, u32[]{:S(2)}) %collective-permute-start.15) | collective-permute-done | bytes 262176 | tf_op jit(solution)/shard_map/ppermute | solution.py:255
  78.6 0.9 collective-permute-done.17.from_prev
  79.5 0.1 shard_map.67.value_ref
  79.6 0.4 shard_map.68
  80.0 1.3 collective-permute-start.18
  81.3 0.8 collective-permute-done.18
  82.2 32.8 %all_to_all.10 = f32[16,32,128]{2,1,0:T(8,128)S(1)} all-to-all(f32[16,32,128]{2,1,0:T(8,128)S(1)} %broadcast_in_dim.27), channel_id=1, replica_groups={{0,2,4,6,64,66,68,70,128,130,132,134,192,194,196,198},{8,10,12,14,72,74..., dimensions={0} | all-to-all | bytes 524288 | tf_op jit(solution)/shard_map/all_to_all | solution.py:299
  115.0 0.7 broadcast_in_dim.28
  115.7 3.4 %all-to-all-start.1 = ((f32[8,32,128]{2,1,0:T(8,128)}), f32[8,32,128]{2,1,0:T(8,128)S(1)}, u32[]{:S(2)}, u32[]{:S(2)}) async-start(f32[8,32,128]{2,1,0:T(8,128)} %broadcast_in_dim.28), calls=%async_computation.1 | async-start | bytes 262144 | tf_op jit(solution)/shard_map/all_to_all | solution.py:299
  119.1 2.1 %collective-permute-start.20 = (f32[64,512]{1,0:T(8,128)S(1)}, f32[64,512]{1,0:T(8,128)S(1)}, u32[]{:S(2)}, u32[]{:S(2)}) collective-permute-start(f32[64,512]{1,0:T(8,128)S(1)} %get-tuple-element.55), channel_id=1, source_target_pairs={{0,1},{1,0},{2,3},{3,2},{4,5},{5,4},{6,7},{7,6},{8,9},{9,8},{10,11... | collective-permute-start | bytes 393224 | tf_op jit(solution)/shard_map/ppermute | solution.py:270
  121.2 5.7 %all-to-all-done.1 = f32[8,32,128]{2,1,0:T(8,128)S(1)} async-done(((f32[8,32,128]{2,1,0:T(8,128)}), f32[8,32,128]{2,1,0:T(8,128)S(1)}, u32[]{:S(2)}, u32[]{:S(2)}) %all-to-all-start.1) | async-done | bytes 131104 | tf_op jit(solution)/shard_map/all_to_all | solution.py:299
  127.0 3.1 %collective-permute-start.19 = (f32[32,128]{1,0:T(8,128)S(1)}, f32[32,128]{1,0:T(8,128)S(1)}, u32[]{:S(2)}, u32[]{:S(2)}) collective-permute-start(f32[32,128]{1,0:T(8,128)S(1)} %reduce_sum.19.mine_ref), channel_id=1, source_target_pairs={{0,1},{1,0},{2,3},{3,2},{4,5},{5,4},{6,7},{7,6},{8,9},{9,8},{10,11... | collective-permute-start | bytes 49160 | tf_op jit(solution)/shard_map/ppermute | solution.py:270
  130.0 0.0 collective-permute-done.20.got_ref
  130.0 0.8 collective-permute-done.19.other_ref
  130.9 6.7 %shard_map.69 = (f32[64,1024]{1,0:T(8,128)}, f32[64,64]{1,0:T(8,128)}) custom-call(s32[1]{0:T(128)} %bitcast.core_ref, f32[32,128]{1,0:T(8,128)S(1)} %reduce_sum.19.mine_ref, f32[32,128]{1,0:T(8,128)S(1)} %collective-permute-done.19.other_ref, f32[2,64,512]{2,1,0:T(8,128)S(1)} %shard_map.67.value_ref, f32[64,512]{1,0:T(8,128)S(1)} %collective-permute-done.20.got_ref), custom_call_target="tpu_custom_call" | custom-call | flops 100000000 | bytes 1000000 | tf_op jit(solution)/shard_map/pallas_call | solution.py:377
  (9 shorter events, 0.2 us)
Async XLA Ops:
  0.6 24.6 %copy-start.1 = (s32[11]{0:T(128)S(1)}, s32[11]{0:T(128)}, u32[]{:S(2)}) copy-start(s32[11]{0:T(128)} %constant.23.clone) | copy-start | bytes 136
  0.6 8.2 %copy-start = (s32[4,2]{0,1:T(2,128)S(1)}, s32[4,2]{0,1:T(2,128)}, u32[]{:S(2)}) copy-start(s32[4,2]{0,1:T(2,128)} %param.6) | copy-start | bytes 100
  2.0 25.4 %collective-permute-start.4 = (bf16[2,1792,128]{2,1,0:T(8,128)(2,1)S(1)}, bf16[2,1792,128]{2,1,0:T(8,128)(2,1)S(1)}, u32[]{:S(2)}, u32[]{:S(2)}) collective-permute-start(bf16[2,1792,128]{2,1,0:T(8,128)(2,1)S(1)} %shard_map.60.refs_0_), channel_id=1, source_target_pairs={{0,2},{2,4},{4,6},{6,8},{8,10},{10,12},{12,14},{14,16},{16,18},{18... | collective-permute-start | bytes 2752520 | tf_op jit(solution)/shard_map/ppermute | solution.py:255
  6.1 22.9 %collective-permute-start.3 = (bf16[2,1792,128]{2,1,0:T(8,128)(2,1)S(1)}, bf16[2,1792,128]{2,1,0:T(8,128)(2,1)}, u32[]{:S(2)}, u32[]{:S(2)}) collective-permute-start(bf16[2,1792,128]{2,1,0:T(8,128)(2,1)S(1)} %shard_map.60.refs_0_), channel_id=1, source_target_pairs={{2,0},{4,2},{6,4},{8,6},{10,8},{12,10},{14,12},{16,14},{18,16},{20... | collective-permute-start | bytes 2752520 | tf_op jit(solution)/shard_map/ppermute | solution.py:255
  8.8 16.3 %collective-permute-start.2 = (s32[4,2]{0,1:T(2,128)S(1)}, s32[4,2]{0,1:T(2,128)S(1)}, u32[]{:S(2)}, u32[]{:S(2)}) collective-permute-start(s32[4,2]{0,1:T(2,128)S(1)} %copy-done), channel_id=1, source_target_pairs={{0,3},{1,2},{2,5},{3,4},{4,7},{5,6},{6,9},{7,8},{8,11},{9,10},{10,... | collective-permute-start | bytes 104 | tf_op jit(solution)/shard_map/ppermute | solution.py:262
  13.9 11.2 %collective-permute-start.1 = (s32[4,2]{0,1:T(2,128)S(1)}, s32[4,2]{0,1:T(2,128)S(1)}, u32[]{:S(2)}, u32[]{:S(2)}) collective-permute-start(s32[4,2]{0,1:T(2,128)S(1)} %copy-done), channel_id=1, source_target_pairs={{0,2},{2,4},{4,6},{6,8},{8,10},{10,12},{12,14},{14,16},{16,18},{18... | collective-permute-start | bytes 104 | tf_op jit(solution)/shard_map/ppermute | solution.py:255
  17.1 8.0 %collective-permute-start = (s32[4,2]{0,1:T(2,128)S(1)}, s32[4,2]{0,1:T(2,128)S(1)}, u32[]{:S(2)}, u32[]{:S(2)}) collective-permute-start(s32[4,2]{0,1:T(2,128)S(1)} %copy-done), channel_id=1, source_target_pairs={{0,1},{1,0},{2,3},{3,2},{4,5},{5,4},{6,7},{7,6},{8,9},{9,8},{10,11... | collective-permute-start | bytes 104 | tf_op jit(solution)/shard_map/ppermute | solution.py:270
  29.0 4.2 %collective-permute-start.5 = (bf16[2,1792,128]{2,1,0:T(8,128)(2,1)}, bf16[2,1792,128]{2,1,0:T(8,128)(2,1)S(1)}, u32[]{:S(2)}, u32[]{:S(2)}) collective-permute-start(bf16[2,1792,128]{2,1,0:T(8,128)(2,1)} %collective-permute-done.3.refs_2_), channel_id=1, source_target_pairs={{0,1},{1,0},{2,3},{3,2},{4,5},{5,4},{6,7},{7,6},{8,9},{9,8},{10,11... | collective-permute-start | bytes 2752520 | tf_op jit(solution)/shard_map/ppermute | solution.py:270
  35.9 1.9 %collective-permute-start.8 = (f32[2,64,512]{2,1,0:T(8,128)S(1)}, f32[2,64,512]{2,1,0:T(8,128)S(1)}, u32[]{:S(2)}, u32[]{:S(2)}) collective-permute-start(f32[2,64,512]{2,1,0:T(8,128)S(1)} %get-tuple-element.41), channel_id=1, source_target_pairs={{0,1},{1,0},{2,3},{3,2},{4,5},{5,4},{6,7},{7,6},{8,9},{9,8},{10,11... | collective-permute-start | bytes 786440 | tf_op jit(solution)/shard_map/ppermute | solution.py:270
  36.4 9.2 %collective-permute-start.6 = (f32[2,64,512]{2,1,0:T(8,128)S(1)}, f32[2,64,512]{2,1,0:T(8,128)S(1)}, u32[]{:S(2)}, u32[]{:S(2)}) collective-permute-start(f32[2,64,512]{2,1,0:T(8,128)S(1)} %get-tuple-element.38), channel_id=1, source_target_pairs={{0,1},{1,0},{2,3},{3,2},{4,5},{5,4},{6,7},{7,6},{8,9},{9,8},{10,11... | collective-permute-start | bytes 786440 | tf_op jit(solution)/shard_map/ppermute | solution.py:270
  36.5 13.4 %collective-permute-start.7 = (f32[2,64,512]{2,1,0:T(8,128)S(1)}, f32[2,64,512]{2,1,0:T(8,128)S(1)}, u32[]{:S(2)}, u32[]{:S(2)}) collective-permute-start(f32[2,64,512]{2,1,0:T(8,128)S(1)} %get-tuple-element.39), channel_id=1, source_target_pairs={{2,0},{4,2},{6,4},{8,6},{10,8},{12,10},{14,12},{16,14},{18,16},{20... | collective-permute-start | bytes 786440 | tf_op jit(solution)/shard_map/ppermute | solution.py:255
  37.9 13.0 %collective-permute-start.9 = (f32[2,64,512]{2,1,0:T(8,128)S(1)}, f32[2,64,512]{2,1,0:T(8,128)S(1)}, u32[]{:S(2)}, u32[]{:S(2)}) collective-permute-start(f32[2,64,512]{2,1,0:T(8,128)S(1)} %add.29), channel_id=1, source_target_pairs={{0,2},{2,4},{4,6},{6,8},{8,10},{10,12},{12,14},{14,16},{16,18},{18... | collective-permute-start | bytes 786440 | tf_op jit(solution)/shard_map/ppermute | solution.py:255
  50.9 9.5 %collective-permute-start.11 = (bf16[2,128,512]{2,1,0:T(8,128)(2,1)S(1)}, bf16[2,128,512]{2,1,0:T(8,128)(2,1)S(1)}, u32[]{:S(2)}, u32[]{:S(2)}) collective-permute-start(bf16[2,128,512]{2,1,0:T(8,128)(2,1)S(1)} %get-tuple-element.44.refs_1_), channel_id=1, source_target_pairs={{2,0},{4,2},{6,4},{8,6},{10,8},{12,10},{14,12},{16,14},{18,16},{20... | collective-permute-start | bytes 786440 | tf_op jit(solution)/shard_map/ppermute | solution.py:255
  52.2 10.1 %collective-permute-start.13 = (bf16[2,128,512]{2,1,0:T(8,128)(2,1)S(1)}, bf16[2,128,512]{2,1,0:T(8,128)(2,1)S(1)}, u32[]{:S(2)}, u32[]{:S(2)}) collective-permute-start(bf16[2,128,512]{2,1,0:T(8,128)(2,1)S(1)} %get-tuple-element.44.refs_1_), channel_id=1, source_target_pairs={{0,1},{1,0},{2,3},{3,2},{4,5},{5,4},{6,7},{7,6},{8,9},{9,8},{10,11... | collective-permute-start | bytes 786440 | tf_op jit(solution)/shard_map/ppermute | solution.py:270
  53.5 10.4 %collective-permute-start.10 = (bf16[2,128,512]{2,1,0:T(8,128)(2,1)S(1)}, bf16[2,128,512]{2,1,0:T(8,128)(2,1)S(1)}, u32[]{:S(2)}, u32[]{:S(2)}) collective-permute-start(bf16[2,128,512]{2,1,0:T(8,128)(2,1)S(1)} %get-tuple-element.44.refs_1_), channel_id=1, source_target_pairs={{0,2},{2,4},{4,6},{6,8},{8,10},{10,12},{12,14},{14,16},{16,18},{18... | collective-permute-start | bytes 786440 | tf_op jit(solution)/shard_map/ppermute | solution.py:255
  60.4 3.5 %collective-permute-start.12 = (bf16[2,128,512]{2,1,0:T(8,128)(2,1)S(1)}, bf16[2,128,512]{2,1,0:T(8,128)(2,1)S(1)}, u32[]{:S(2)}, u32[]{:S(2)}) collective-permute-start(bf16[2,128,512]{2,1,0:T(8,128)(2,1)S(1)} %collective-permute-done.11.refs_3_), channel_id=1, source_target_pairs={{0,1},{1,0},{2,3},{3,2},{4,5},{5,4},{6,7},{7,6},{8,9},{9,8},{10,11... | collective-permute-start | bytes 786440 | tf_op jit(solution)/shard_map/ppermute | solution.py:270
  65.3 2.3 %collective-permute-start.16 = (f32[2,64,512]{2,1,0:T(8,128)S(1)}, f32[2,64,512]{2,1,0:T(8,128)S(1)}, u32[]{:S(2)}, u32[]{:S(2)}) collective-permute-start(f32[2,64,512]{2,1,0:T(8,128)S(1)} %get-tuple-element.52), channel_id=1, source_target_pairs={{0,1},{1,0},{2,3},{3,2},{4,5},{5,4},{6,7},{7,6},{8,9},{9,8},{10,11... | collective-permute-start | bytes 786440 | tf_op jit(solution)/shard_map/ppermute | solution.py:270
  66.2 8.5 %collective-permute-start.14 = (f32[2,64,512]{2,1,0:T(8,128)S(1)}, f32[2,64,512]{2,1,0:T(8,128)S(1)}, u32[]{:S(2)}, u32[]{:S(2)}) collective-permute-start(f32[2,64,512]{2,1,0:T(8,128)S(1)} %get-tuple-element.49), channel_id=1, source_target_pairs={{0,1},{1,0},{2,3},{3,2},{4,5},{5,4},{6,7},{7,6},{8,9},{9,8},{10,11... | collective-permute-start | bytes 786440 | tf_op jit(solution)/shard_map/ppermute | solution.py:270
  66.3 12.3 %collective-permute-start.15 = (f32[2,64,512]{2,1,0:T(8,128)S(1)}, f32[2,64,512]{2,1,0:T(8,128)S(1)}, u32[]{:S(2)}, u32[]{:S(2)}) collective-permute-start(f32[2,64,512]{2,1,0:T(8,128)S(1)} %get-tuple-element.50), channel_id=1, source_target_pairs={{2,0},{4,2},{6,4},{8,6},{10,8},{12,10},{14,12},{16,14},{18,16},{20... | collective-permute-start | bytes 786440 | tf_op jit(solution)/shard_map/ppermute | solution.py:255
  67.7 11.9 %collective-permute-start.17 = (f32[2,64,512]{2,1,0:T(8,128)S(1)}, f32[2,64,512]{2,1,0:T(8,128)S(1)}, u32[]{:S(2)}, u32[]{:S(2)}) collective-permute-start(f32[2,64,512]{2,1,0:T(8,128)S(1)} %add.30), channel_id=1, source_target_pairs={{0,2},{2,4},{4,6},{6,8},{8,10},{10,12},{12,14},{14,16},{16,18},{18... | collective-permute-start | bytes 786440 | tf_op jit(solution)/shard_map/ppermute | solution.py:255
  80.0 2.1 %collective-permute-start.18 = (f32[32,128]{1,0:T(8,128)S(1)}, f32[32,128]{1,0:T(8,128)S(1)}, u32[]{:S(2)}, u32[]{:S(2)}) collective-permute-start(f32[32,128]{1,0:T(8,128)S(1)} %get-tuple-element.54), channel_id=1, source_target_pairs={{0,1},{1,0},{2,3},{3,2},{4,5},{5,4},{6,7},{7,6},{8,9},{9,8},{10,11... | collective-permute-start | bytes 49160 | tf_op jit(solution)/shard_map/ppermute | solution.py:270
  115.7 11.3 %all-to-all-start.1 = ((f32[8,32,128]{2,1,0:T(8,128)}), f32[8,32,128]{2,1,0:T(8,128)S(1)}, u32[]{:S(2)}, u32[]{:S(2)}) async-start(f32[8,32,128]{2,1,0:T(8,128)} %broadcast_in_dim.28), calls=%async_computation.1 | async-start | bytes 262144 | tf_op jit(solution)/shard_map/all_to_all | solution.py:299
  119.1 11.0 %collective-permute-start.20 = (f32[64,512]{1,0:T(8,128)S(1)}, f32[64,512]{1,0:T(8,128)S(1)}, u32[]{:S(2)}, u32[]{:S(2)}) collective-permute-start(f32[64,512]{1,0:T(8,128)S(1)} %get-tuple-element.55), channel_id=1, source_target_pairs={{0,1},{1,0},{2,3},{3,2},{4,5},{5,4},{6,7},{7,6},{8,9},{9,8},{10,11... | collective-permute-start | bytes 393224 | tf_op jit(solution)/shard_map/ppermute | solution.py:270
  127.0 3.9 %collective-permute-start.19 = (f32[32,128]{1,0:T(8,128)S(1)}, f32[32,128]{1,0:T(8,128)S(1)}, u32[]{:S(2)}, u32[]{:S(2)}) collective-permute-start(f32[32,128]{1,0:T(8,128)S(1)} %reduce_sum.19.mine_ref), channel_id=1, source_target_pairs={{0,1},{1,0},{2,3},{3,2},{4,5},{5,4},{6,7},{7,6},{8,9},{9,8},{10,11... | collective-permute-start | bytes 49160 | tf_op jit(solution)/shard_map/ppermute | solution.py:270

commit v3 on v2

--- a/solution.py
+++ b/solution.py
@@ -99,28 +99,37 @@
             )
 
 
-def use_tiles(tile_ref, slot, ahead, behind, forward_ref, forward_at, mirror_refs, mirror_at, mirror):
-    total = fold(dot(ahead[0], tile_ref[slot, 0], NT)) + fold(dot(ahead[1], tile_ref[slot, 1], NT))
-    forward_ref[forward_at] += total
-
-    def put_mirror():
+def use_tiles(tile_ref, slot, rights, left, done_ref, done_at, part_refs, part_at, partial):
+    total = fold(dot(rights[0], tile_ref[slot, 0], NT)) + fold(dot(rights[1], tile_ref[slot, 1], NT))
+    done_ref[done_at] += total
+
+    def put_part():
         for side in range(2):
-            mirror_refs[side][mirror_at] += fold(dot(behind, tile_ref[slot, side], NN))
-
-    if mirror is None:
-        put_mirror()
+            part_refs[side][part_at] += fold(dot(left, tile_ref[slot, side], NN))
+
+    if partial is None:
+        put_part()
     else:
-        pl.when(mirror)(put_mirror)
+        pl.when(partial)(put_part)
+
+
+def one_pair(make, tile_ref, slot, left, rights, done_ref, done_at, part_refs, part_at, partial=None):
+    take = vectors if make else (lambda ref: ref[...])
+    if make:
+        make_tiles(left, rights, tile_ref, slot)
+    use_tiles(
+        tile_ref, slot, (take(rights[0]), take(rights[1])), take(left),
+        done_ref, done_at, part_refs, part_at, partial,
+    )
 
 
 def local_kernel(make, flags_ref, *refs):
     if make:
-        own0, own1, tile_ref, forward_ref, mirror0, mirror1 = refs
+        own0, own1, tile_ref, done_ref, part0, part1 = refs
     else:
-        tile_ref, own0, own1, forward_ref, mirror0, mirror1 = refs
-    for ref in (forward_ref, mirror0, mirror1):
+        tile_ref, own0, own1, done_ref, part0, part1 = refs
+    for ref in (done_ref, part0, part1):
         ref[...] = jnp.zeros_like(ref)
-    take = vectors if make else (lambda ref: ref[...])
 
     @pl.loop(0, 3)
     def _(slot):
@@ -128,47 +137,63 @@
 
         @pl.when(flags_ref[slot] > 0)
         def _():
-            if make:
-                make_tiles(own0.at[first], (own0.at[second], own1.at[second]), tile_ref, slot)
-            use_tiles(
-                tile_ref, slot, (take(own0.at[second]), take(own1.at[second])), take(own0.at[first]),
-                forward_ref, first, (mirror0, mirror1), second, slot == 1,
+            one_pair(
+                make, tile_ref, slot, own0.at[first], (own0.at[second], own1.at[second]),
+                done_ref, first, (part0, part1), second, slot == 1,
             )
 
 
-def near_kernel(make, flags_ref, *refs):
+def odd_kernel(make, flags_ref, *refs):
     if make:
-        own0, prev, next0, next1, started, tile_ref, forward_ref, before_ref, mirror0, mirror1 = refs
+        odd0, own0, own1, in0, in1, tile_ref, done_ref, part0, part1 = refs
     else:
-        tile_ref, own0, prev, next0, next1, started, forward_ref, before_ref, mirror0, mirror1 = refs
-    forward_ref[...] = started[...]
-    for ref in (before_ref, mirror0, mirror1):
+        tile_ref, odd0, own0, own1, in0, in1, done_ref, part0, part1 = refs
+    done_ref[...] = jnp.zeros_like(done_ref)
+    part0[...] = in0[...]
+    part1[...] = in1[...]
+
+    @pl.loop(0, 4)
+    def _(slot):
+        left, right = slot // 2, slot % 2
+
+        @pl.when(flags_ref[7 + slot] > 0)
+        def _():
+            one_pair(
+                make, tile_ref, slot, odd0.at[left], (own0.at[right], own1.at[right]),
+                done_ref, left, (part0, part1), right,
+            )
+
+
+def even_kernel(make, flags_ref, far_ref, *refs):
+    if make:
+        own0, odd0, even0, even1, own_in, odd_in, tile_ref, *refs = refs
+    else:
+        tile_ref, own0, odd0, even0, even1, own_in, odd_in, *refs = refs
+    own_done, odd_done, part0, part1 = refs
+    own_done[...] = own_in[...]
+    odd_done[...] = odd_in[...]
+    for ref in (part0, part1):
         ref[...] = jnp.zeros_like(ref)
-    take = vectors if make else (lambda ref: ref[...])
     for kind in range(2):
+        lefts, done_ref = ((own0, own_done), (odd0, odd_done))[kind]
+        flag_ref, flag_at = ((flags_ref, 3), (far_ref, 0))[kind]
 
         @pl.loop(0, 4)
         def _(index):
-            first, second = index // 2, index % 2
-            slot = kind * 4 + index
-            left = (own0, prev)[kind]
-
-            @pl.when(flags_ref[3 + slot] > 0)
+            left, right = index // 2, index % 2
+
+            @pl.when(flag_ref[flag_at + index] > 0)
             def _():
-                if make:
-                    make_tiles(left.at[first], (next0.at[second], next1.at[second]), tile_ref, slot)
-                use_tiles(
-                    tile_ref, slot, (take(next0.at[second]), take(next1.at[second])),
-                    take(left.at[first]), (forward_ref, before_ref)[kind], first,
-                    (mirror0, mirror1), second, None,
+                one_pair(
+                    make, tile_ref, kind * 4 + index, lefts.at[left],
+                    (even0.at[right], even1.at[right]), done_ref, left, (part0, part1), right,
                 )
 
 
-def total_kernel(forward, mirror_mine, mirror_other, from_next, from_prev, sum_ref, pair_ref=None):
+def total_kernel(done, part_mine, part_other, from_odd, from_even, sum_ref, pair_ref=None):
     for block in range(2):
         value = (
-            forward[block] + mirror_mine[block] + mirror_other[block]
-            + from_next[block] + from_prev[block]
+            done[block] + part_mine[block] + part_other[block] + from_odd[block] + from_even[block]
         )
         sum_ref[block] = value
         if pair_ref is not None:
@@ -250,43 +275,65 @@
     basis_ref[:, pl.ds(there, HALF)] = dot(low, got_ref[...], NN, HIGHEST)
 
 
-def step_rows(value, steps):
-    count = lax.axis_size("rows")
-    return lax.ppermute(
-        value, "rows", [(r, r + steps) for r in range(count) if 0 <= r + steps < count]
-    )
-
-
-def cross_rows(value):
-    count = lax.axis_size("rows")
-    return lax.ppermute(
-        value,
-        ("rows", "cols"),
-        [(2 * r + c, 2 * (r + 1) + 1 - c) for r in range(count - 1) for c in range(2)],
-    )
+def exchange(value, start):
+    links = []
+    for r in range(start, lax.axis_size("rows") - 1, 2):
+        links += [(r, r + 1), (r + 1, r)]
+    return lax.ppermute(value, "rows", links)
+
+
+def to_even(value):
+    return exchange(value, 0)
+
+
+def to_odd(value):
+    return exchange(value, 1)
 
 
 def swap(value):
     return lax.ppermute(value, "cols", [(0, 1), (1, 0)])
 
 
-def live_flags(pair_list, base):
-    pairs = jnp.concatenate(
-        [pair_list, swap(pair_list), step_rows(pair_list, 1), cross_rows(pair_list)], axis=0
-    )
-    from_prev = lax.broadcasted_iota(jnp.int32, (16,), 0) >= 8
-    codes = (pairs[:, 0] - base) * 8 + (pairs[:, 1] - base) + jnp.where(from_prev, 1000, 0)
-    ours = [(0, 0), (0, 1), (1, 1), (0, 2), (0, 3), (1, 2), (1, 3)]
-    across = [(-2, 2), (-2, 3), (-1, 2), (-1, 3)]
-    wanted = [8 * i + j for i, j in ours] + [1000 + 8 * i + j for i, j in across]
-    hit = codes[None, :] == jnp.array(wanted, jnp.int32)[:, None]
-    return jnp.any(hit & (pairs[None, :, 0] >= 0), axis=1).astype(jnp.int32)
-
-
-def spread(forward, before, own0, other_own, next0, next1):
-    from_next = step_rows(before, -1)
-    from_prev = step_rows(next0 + swap(next1), 1)
-    return forward, own0, other_own, from_next, from_prev
+def live_flags(pairs, base, even_codes, odd_codes):
+    none = (100, 100)
+
+    def table(entries):
+        return jnp.array([64 * i + j for i, j in (none if e is None else e for e in entries)], jnp.int32)
+
+    even_row = lax.axis_index("rows") % 2 == 0
+    wanted = jnp.where(even_row, table(even_codes), table(odd_codes))
+    codes = (pairs[:, 0] - base) * 64 + (pairs[:, 1] - base)
+    hit = (codes[None, :] == wanted[:, None]) & (pairs[None, :, 0] >= 0)
+    return jnp.any(hit, axis=1).astype(jnp.int32)
+
+
+SLOTS = [(0, 0), (0, 1), (1, 0), (1, 1)]
+
+
+def own_flags_and_list(pair_list, base):
+    own = jnp.concatenate([pair_list, swap(pair_list)], axis=0)
+    before = lax.ppermute(own, "rows", [(r, r + 1) for r in range(lax.axis_size("rows") - 1)])
+    within, idle = [(0, 0), (0, 1), (1, 1)], [None] * 4
+    flags = live_flags(
+        own, base,
+        within + [(left, 2 + right) for left, right in SLOTS] + idle,
+        within + idle + [(right, 2 + left) for left, right in SLOTS],
+    )
+    return flags, before
+
+
+def flags_of_far(before, base):
+    return live_flags(
+        before, base,
+        [(left - 2, 2 + right) for left, right in SLOTS],
+        [(right - 2, 2 + left) for left, right in SLOTS],
+    )
+
+
+def spread(done, own0, own1, out_odd, even0, even1):
+    from_odd = to_odd(out_odd)
+    from_even = to_even(even0 + swap(even1))
+    return done, own0, swap(own1), from_odd, from_even
 
 
 def sum_over_chips(value):
@@ -325,46 +372,54 @@
         )(core_ref, embeddings, test_columns)
 
     own0 = packet(0)
-    next0 = step_rows(own0, -1)
-    prev = step_rows(own0, 1)
+    even0 = to_even(own0)
+    odd0 = to_odd(own0)
     own1, pair_list = lax.optimization_barrier((packet(1), pair_list))
-    flags = live_flags(pair_list, base)
+    flags, before = own_flags_and_list(pair_list, base)
 
     sum_shape = shape((2, 64, HALF))
-    tiles_own, forward, mirror_own, mirror1 = call(
-        functools.partial(local_kernel, True),
-        (shape((3, 2, HALF, HALF), bf16),) + 3 * (sum_shape,),
-        10**4, 10**4,
+
+    def tiles(count):
+        return shape((count, 2, HALF, HALF), bf16)
+
+    tiles_own, done, own_part0, own_part1 = call(
+        functools.partial(local_kernel, True), (tiles(3),) + 3 * (sum_shape,), 10**4, 10**4
     )(in_specs=[SMEM] + [VMEM] * 2)(flags, own0, own1)
-    mirror1, next0, prev = lax.optimization_barrier((mirror1, next0, prev))
-    next1 = swap(next0)
-    other_own = swap(mirror1)
-    tiles_near, forward, before, mirror0, mirror1 = call(
-        functools.partial(near_kernel, True),
-        (shape((8, 2, HALF, HALF), bf16),) + 4 * (sum_shape,),
-        4 * 10**9, 8 * 10**6, 2 * 10**6,
-    )(in_specs=[SMEM] + [VMEM] * 5)(flags, own0, prev, next0, next1, forward)
+    done, even0, odd0, before = lax.optimization_barrier((done, even0, odd0, before))
+    even1 = swap(even0)
+    far_flags = flags_of_far(before, base)
+    tiles_odd, out_odd, own_part0, own_part1 = call(
+        functools.partial(odd_kernel, True), (tiles(4),) + 3 * (sum_shape,), 10**4, 10**4
+    )(in_specs=[SMEM] + [VMEM] * 5)(flags, odd0, own0, own1, own_part0, own_part1)
+    tiles_even, done, out_odd, even_part0, even_part1 = call(
+        functools.partial(even_kernel, True), (tiles(8),) + 4 * (sum_shape,), 10**9, 10**6
+    )(in_specs=[SMEM] * 2 + [VMEM] * 6)(flags, far_flags, own0, odd0, even0, even1, done, out_odd)
     sketch, pair0 = call(total_kernel, (sum_shape, shape((2, 128, HALF), bf16)), 10**6, 2 * 10**6)(
         in_specs=[VMEM] * 5
-    )(*spread(forward, before, mirror_own, other_own, mirror0, mirror1))
-
-    pnext0 = step_rows(pair0, -1)
-    pair_prev = step_rows(pair0, 1)
+    )(*spread(done, own_part0, own_part1, out_odd, even_part0, even_part1))
+
+    even0 = to_even(pair0)
+    odd0 = to_odd(pair0)
     pair1 = swap(pair0)
-    pnext1 = swap(pnext0)
     gram_shape = shape((32, 128))
     first_gram = call(functools.partial(gram_kernel, scale), gram_shape, 10**8, 10**6)(
         in_specs=[VMEM]
     )(sketch)
-    forward, mirror_own, mirror1 = call(
-        functools.partial(local_kernel, False), 3 * (sum_shape,), 10**9, 3 * 10**6
+    done, own_part0, own_part1 = call(
+        functools.partial(local_kernel, False), 3 * (sum_shape,), 10**4, 10**4
     )(in_specs=[SMEM] + [VMEM] * 3)(flags, tiles_own, pair0, pair1)
-    other_own = swap(mirror1)
-    forward, before, mirror0, mirror1 = call(
-        functools.partial(near_kernel, False), 4 * (sum_shape,), 10**9, 8 * 10**6
-    )(in_specs=[SMEM] + [VMEM] * 6)(flags, tiles_near, pair0, pair_prev, pnext0, pnext1, forward)
+    done, even0, odd0 = lax.optimization_barrier((done, even0, odd0))
+    even1 = swap(even0)
+    out_odd, own_part0, own_part1 = call(
+        functools.partial(odd_kernel, False), 3 * (sum_shape,), 10**4, 10**4
+    )(in_specs=[SMEM] + [VMEM] * 6)(flags, tiles_odd, odd0, pair0, pair1, own_part0, own_part1)
+    done, out_odd, even_part0, even_part1 = call(
+        functools.partial(even_kernel, False), 4 * (sum_shape,), 10**9, 10**6
+    )(in_specs=[SMEM] * 2 + [VMEM] * 7)(
+        flags, far_flags, tiles_even, pair0, odd0, even0, even1, done, out_odd
+    )
     image = call(total_kernel, sum_shape, 10**6, 2 * 10**6)(in_specs=[VMEM] * 5)(
-        *spread(forward, before, mirror_own, other_own, mirror0, mirror1)
+        *spread(done, own_part0, own_part1, out_odd, even_part0, even_part1)
     )
     keep, give, half = call(
         functools.partial(second_gram_kernel, scale),

time: 138 us -> 131 us (0.949)
  starting transfers between devices: 53.1 us -> 38.8 us
  waiting for transfers between devices: 31.7 us -> 40.7 us
  blocking collectives: 32.8 us -> 25.4 us
  Pallas kernels: 18 us -> 22.6 us
    ppermute x10 -> x9, starting transfers between devices: 36.5 us -> 22.3 us  [the longest x8 20.7 us: exchange(): return lax.ppermute(value, 'rows', links)]
    ppermute x10 -> x9, waiting for transfers between devices: 21.9 us -> 29.7 us  [the longest x8 18.1 us: exchange(): return lax.ppermute(value, 'rows', links)]
    all_to_all x1, blocking collectives: 32.8 us -> 25.4 us  [sum_over_chips(): lax.all_to_all(copies, 'rows', 0, 0, axis_index_groups=groups, tiled=True)]
    pallas_call x4 -> x6, Pallas kernels: 7.55 us -> 12.1 us  [the longest x1 5.27 us: local(): call(functools.partial(even_kernel, True), (tiles(8),) + 4 * (sum_shape,)...]
  transfers between devices with their start and end apart: 22 -> 21, of which waited for: 12 -> 13; matrix products, arithmetic and copies ran while one was open for 0% -> 0% of each run, Pallas kernels for 4% -> 5%
where the time goes in v3:
time: 131 us; the launch traced here: 130 us
  waiting for transfers between devices  40.7 us (31%)
  starting transfers between devices  38.8 us (30%)
  blocking collectives  25.4 us (19%)
  Pallas kernels  22.6 us (17%)
    all_to_all x1, blocking collectives, sum_over_chips(): lax.all_to_all(copies, 'rows', 0, 0, axis_index_groups=groups, tiled=True)  25.4 us
    ppermute x8, starting transfers between devices, exchange(): return lax.ppermute(value, 'rows', links)  20.7 us
    ppermute x8, waiting for transfers between devices, exchange(): return lax.ppermute(value, 'rows', links)  18.1 us
    ppermute x11, starting transfers between devices, swap(): return lax.ppermute(value, 'cols', [(0, 1), (1, 0)])  13.1 us
    ppermute x1, waiting for transfers between devices, own_flags_and_list(): lax.ppermute(own, 'rows', [(r, r + 1) for r in range(lax.axis_size('rows'...  11.6 us
    pallas_call x1, Pallas kernels, local(): call(finish_kernel, (shape((64, BLK)), shape((64, 64))), 10 ** 8, 10 ** 6)  6.68 us
    all_to_all x1, waiting for transfers between devices, sum_over_chips(): lax.all_to_all(copies, 'rows', 0, 0, axis_index_groups=groups, tiled=True)  5.87 us
    pallas_call x1, Pallas kernels, local(): call(functools.partial(even_kernel, True), (tiles(8),) + 4 * (sum_shape,)...  5.27 us
  transfers between devices with their start and end apart: 21, of which 13 were waited for; matrix products, arithmetic and copies ran while one was open for 0% of the time, Pallas kernels for 5%

profile of v3, /device:TPU:1, one launch (start us, length us, event | category | flops | bytes accessed | tf_op | source)
XLA Modules:
  0.0 129.6 jit_solution(204969835909179033)
XLA Ops:
  0.6 0.0 copy-start.3
  0.6 0.0 copy-start.4
  0.7 0.0 copy-start.1
  0.7 0.0 copy-start.2
  0.7 1.4 %shard_map.87.refs_0_.refs_1_ = bf16[2,1792,128]{2,1,0:T(8,128)(2,1)S(1)} custom-call(s32[1]{0:T(128)} %bitcast.core_ref, bf16[2048,384]{1,0:T(8,128)(2,1)} %rows_ref.3, bf16[64,2048]{1,0:T(8,128)(2,1)} %bitcast.11), custom_call_target="tpu_custom_call" | custom-call | flops 10000 | bytes 10000 | tf_op jit(solution)/shard_map/pallas_call | solution.py:363
  2.1 0.7 collective-permute-start.2
  2.8 4.7 %collective-permute-start.1 = (bf16[2,1792,128]{2,1,0:T(8,128)(2,1)S(1)}, bf16[2,1792,128]{2,1,0:T(8,128)(2,1)}, u32[]{:S(2)}, u32[]{:S(2)}) collective-permute-start(bf16[2,1792,128]{2,1,0:T(8,128)(2,1)S(1)} %shard_map.87.refs_0_.refs_1_), channel_id=1, source_target_pairs={{0,2},{2,0},{4,6},{6,4},{8,10},{10,8},{12,14},{14,12},{16,18},{18,... | collective-permute-start | bytes 2752520 | tf_op jit(solution)/shard_map/ppermute | solution.py:282
  7.5 1.4 %shard_map.86.refs_1_.refs_2_ = bf16[2,1792,128]{2,1,0:T(8,128)(2,1)S(1)} custom-call(s32[1]{0:T(128)} %bitcast.core_ref, bf16[2048,384]{1,0:T(8,128)(2,1)} %rows_ref.3, bf16[64,2048]{1,0:T(8,128)(2,1)} %bitcast.12), custom_call_target="tpu_custom_call" | custom-call | flops 10000 | bytes 10000 | tf_op jit(solution)/shard_map/pallas_call | solution.py:363
  8.9 1.3 %collective-permute-start = (s32[4,2]{0,1:T(2,128)S(1)}, s32[4,2]{0,1:T(2,128)S(1)}, u32[]{:S(2)}, u32[]{:S(2)}) collective-permute-start(s32[4,2]{0,1:T(2,128)S(1)} %copy-done), channel_id=1, source_target_pairs={{0,1},{1,0},{2,3},{3,2},{4,5},{5,4},{6,7},{7,6},{8,9},{9,8},{10,11... | collective-permute-start | bytes 104 | tf_op jit(solution)/shard_map/ppermute | solution.py:294
  10.2 0.8 collective-permute-done
  11.0 0.1 pad_add_fusion
  11.1 1.6 %collective-permute-start.3 = (s32[8,2]{0,1:T(2,128)S(1)}, s32[8,2]{0,1:T(2,128)S(1)}, u32[]{:S(2)}, u32[]{:S(2)}) collective-permute-start(s32[8,2]{0,1:T(2,128)S(1)} %pad_add_fusion), channel_id=1, source_target_pairs={{0,2},{2,4},{4,6},{6,8},{8,10},{10,12},{12,14},{14,16},{16,18},{18... | collective-permute-start | bytes 200 | tf_op jit(solution)/shard_map/ppermute | solution.py:315
  12.8 0.1 and_reduce_fusion
  12.9 1.8 %shard_map.88 = (bf16[3,2,512,512]{3,2,1,0:T(8,128)(2,1)S(1)}, f32[2,64,512]{2,1,0:T(8,128)S(1)}, f32[2,64,512]{2,1,0:T(8,128)S(1)}, f32[2,64,512]{2,1,0:T(8,128)S(1)}) custom-call(s32[11]{0:T(128)S(1)} %convert_element_type.6.flags_ref, bf16[2,1792,128]{2,1,0:T(8,128)(2,1)S(1)} %shard_map.87.refs_0_.refs_1_, bf16[2,1792,128]{2,1,0:T(8,128)(2,1)S(1)} %shard_map.86.refs_1_.refs_2_), custom_call_target="tpu_custom_call" | custom-call | flops 10000 | bytes 10000 | tf_op jit(solution)/shard_map/pallas_call | solution.py:385
  14.7 11.6 %collective-permute-done.3 = s32[8,2]{0,1:T(2,128)S(1)} collective-permute-done((s32[8,2]{0,1:T(2,128)S(1)}, s32[8,2]{0,1:T(2,128)S(1)}, u32[]{:S(2)}, u32[]{:S(2)}) %collective-permute-start.3) | collective-permute-done | bytes 96 | tf_op jit(solution)/shard_map/ppermute | solution.py:315
  26.2 0.0 collective-permute-done.2.refs_0_.refs_1_
  26.2 1.1 collective-permute-done.1.refs_2_
  27.4 1.5 %collective-permute-start.4 = (bf16[2,1792,128]{2,1,0:T(8,128)(2,1)}, bf16[2,1792,128]{2,1,0:T(8,128)(2,1)S(1)}, u32[]{:S(2)}, u32[]{:S(2)}) collective-permute-start(bf16[2,1792,128]{2,1,0:T(8,128)(2,1)} %collective-permute-done.1.refs_2_), channel_id=1, source_target_pairs={{0,1},{1,0},{2,3},{3,2},{4,5},{5,4},{6,7},{7,6},{8,9},{9,8},{10,11... | collective-permute-start | bytes 2752520 | tf_op jit(solution)/shard_map/ppermute | solution.py:294
  28.9 0.7 shard_map.89
  29.6 0.2 and_reduce_fusion.1
  29.8 1.4 %collective-permute-done.4.refs_3_ = bf16[2,1792,128]{2,1,0:T(8,128)(2,1)S(1)} collective-permute-done((bf16[2,1792,128]{2,1,0:T(8,128)(2,1)}, bf16[2,1792,128]{2,1,0:T(8,128)(2,1)S(1)}, u32[]{:S(2)}, u32[]{:S(2)}) %collective-permute-start.4) | collective-permute-done | bytes 917536 | tf_op jit(solution)/shard_map/ppermute | solution.py:294
  31.2 5.3 %shard_map.90 = (bf16[8,2,512,512]{3,2,1,0:T(8,128)(2,1)S(1)}, f32[2,64,512]{2,1,0:T(8,128)S(1)}, f32[2,64,512]{2,1,0:T(8,128)S(1)}, f32[2,64,512]{2,1,0:T(8,128)S(1)}, f32[2,64,512]{2,1,0:T(8,128)S(1)}) custom-call(s32[11]{0:T(128)S(1)} %convert_element_type.6.flags_ref, s32[4]{0:T(128)S(1)} %convert_element_type.7.far_ref, ...), custom_call_target="tpu_custom_call" | custom-call | flops 1000000000 | bytes 1000000 | tf_op jit(solution)/shard_map/pallas_call | solution.py:394
  36.5 0.5 collective-permute-start.7
  37.0 0.1 collective-permute-start.5
  37.1 0.7 collective-permute-start.6
  37.8 0.4 collective-permute-done.7
  38.2 4.6 %collective-permute-start.8 = (f32[2,64,512]{2,1,0:T(8,128)S(1)}, f32[2,64,512]{2,1,0:T(8,128)S(1)}, u32[]{:S(2)}, u32[]{:S(2)}) collective-permute-start(f32[2,64,512]{2,1,0:T(8,128)S(1)} %add.39), channel_id=1, source_target_pairs={{0,2},{2,0},{4,6},{6,4},{8,10},{10,8},{12,14},{14,12},{16,18},{18,... | collective-permute-start | bytes 786440 | tf_op jit(solution)/shard_map/ppermute | solution.py:282
  42.8 0.0 collective-permute-done.5.part_other
  42.8 0.0 collective-permute-done.6.from_odd
  42.8 6.1 %collective-permute-done.8.from_even = f32[2,64,512]{2,1,0:T(8,128)S(1)} collective-permute-done((f32[2,64,512]{2,1,0:T(8,128)S(1)}, f32[2,64,512]{2,1,0:T(8,128)S(1)}, u32[]{:S(2)}, u32[]{:S(2)}) %collective-permute-start.8) | collective-permute-done | bytes 262176 | tf_op jit(solution)/shard_map/ppermute | solution.py:282
  48.8 0.1 shard_map.91
  48.9 1.3 collective-permute-start.9
  50.2 0.7 collective-permute-start.11
  50.9 2.8 %collective-permute-start.10 = (bf16[2,128,512]{2,1,0:T(8,128)(2,1)S(1)}, bf16[2,128,512]{2,1,0:T(8,128)(2,1)S(1)}, u32[]{:S(2)}, u32[]{:S(2)}) collective-permute-start(bf16[2,128,512]{2,1,0:T(8,128)(2,1)S(1)} %get-tuple-element.59.refs_1_.refs_2_), channel_id=1, source_target_pairs={{0,2},{2,0},{4,6},{6,4},{8,10},{10,8},{12,14},{14,12},{16,18},{18,... | collective-permute-start | bytes 786440 | tf_op jit(solution)/shard_map/ppermute | solution.py:282
  53.6 0.0 collective-permute-done.9.refs_2_.refs_3_
  53.6 1.1 shard_map.93
  54.8 0.0 collective-permute-done.11.refs_1_.refs_2_
  54.8 5.3 %collective-permute-done.10.refs_3_ = bf16[2,128,512]{2,1,0:T(8,128)(2,1)S(1)} collective-permute-done((bf16[2,128,512]{2,1,0:T(8,128)(2,1)S(1)}, bf16[2,128,512]{2,1,0:T(8,128)(2,1)S(1)}, u32[]{:S(2)}, u32[]{:S(2)}) %collective-permute-start.10) | collective-permute-done | bytes 262176 | tf_op jit(solution)/shard_map/ppermute | solution.py:282
  60.1 0.8 collective-permute-start.12
  60.9 0.7 shard_map.94
  61.6 0.5 collective-permute-done.12.refs_4_
  62.1 2.6 %shard_map.95 = (f32[2,64,512]{2,1,0:T(8,128)S(1)}, f32[2,64,512]{2,1,0:T(8,128)S(1)}, f32[2,64,512]{2,1,0:T(8,128)S(1)}, f32[2,64,512]{2,1,0:T(8,128)S(1)}) custom-call(s32[11]{0:T(128)S(1)} %convert_element_type.6.flags_ref, s32[4]{0:T(128)S(1)} %convert_element_type.7.far_ref, bf16[8,2,512,512]{3,2,1,0:T(8,128)(2,1)S(1)} %get-tuple-element.58.refs_0_, ...), custom_call_target="tpu_custom_call" | custom-call | flops 1000000000 | bytes 1000000 | tf_op jit(solution)/shard_map/pallas_call | solution.py:416
  64.7 0.6 collective-permute-start.15
  65.3 0.1 collective-permute-start.13
  65.5 0.7 collective-permute-start.14
  66.1 0.4 collective-permute-done.15
  66.5 5.9 %collective-permute-start.16 = (f32[2,64,512]{2,1,0:T(8,128)S(1)}, f32[2,64,512]{2,1,0:T(8,128)S(1)}, u32[]{:S(2)}, u32[]{:S(2)}) collective-permute-start(f32[2,64,512]{2,1,0:T(8,128)S(1)} %add.40), channel_id=1, source_target_pairs={{0,2},{2,0},{4,6},{6,4},{8,10},{10,8},{12,14},{14,12},{16,18},{18,... | collective-permute-start | bytes 786440 | tf_op jit(solution)/shard_map/ppermute | solution.py:282
  72.4 0.4 shard_map.92.first_ref
  72.8 0.0 collective-permute-done.13.part_other
  72.8 0.0 collective-permute-done.14.from_odd
  72.9 5.6 %collective-permute-done.16.from_even = f32[2,64,512]{2,1,0:T(8,128)S(1)} collective-permute-done((f32[2,64,512]{2,1,0:T(8,128)S(1)}, f32[2,64,512]{2,1,0:T(8,128)S(1)}, u32[]{:S(2)}, u32[]{:S(2)}) %collective-permute-start.16) | collective-permute-done | bytes 262176 | tf_op jit(solution)/shard_map/ppermute | solution.py:282
  78.5 0.1 shard_map.96.value_ref
  78.6 0.4 shard_map.97
  79.0 1.3 collective-permute-start.17
  80.3 0.8 collective-permute-done.17
  81.1 25.4 %all_to_all.10 = f32[16,32,128]{2,1,0:T(8,128)S(1)} all-to-all(f32[16,32,128]{2,1,0:T(8,128)S(1)} %broadcast_in_dim.4), channel_id=1, replica_groups={{0,2,4,6,64,66,68,70,128,130,132,134,192,194,196,198},{8,10,12,14,72,74..., dimensions={0} | all-to-all | bytes 524288 | tf_op jit(solution)/shard_map/all_to_all | solution.py:346
  106.6 0.7 broadcast_in_dim.5
  107.2 3.5 %all-to-all-start.1 = ((f32[8,32,128]{2,1,0:T(8,128)}), f32[8,32,128]{2,1,0:T(8,128)S(1)}, u32[]{:S(2)}, u32[]{:S(2)}) async-start(f32[8,32,128]{2,1,0:T(8,128)} %broadcast_in_dim.5), calls=%async_computation.1 | async-start | bytes 262144 | tf_op jit(solution)/shard_map/all_to_all | solution.py:346
  110.7 2.2 %collective-permute-start.19 = (f32[64,512]{1,0:T(8,128)S(1)}, f32[64,512]{1,0:T(8,128)S(1)}, u32[]{:S(2)}, u32[]{:S(2)}) collective-permute-start(f32[64,512]{1,0:T(8,128)S(1)} %get-tuple-element.77), channel_id=1, source_target_pairs={{0,1},{1,0},{2,3},{3,2},{4,5},{5,4},{6,7},{7,6},{8,9},{9,8},{10,11... | collective-permute-start | bytes 393224 | tf_op jit(solution)/shard_map/ppermute | solution.py:294
  112.9 5.9 %all-to-all-done.1 = f32[8,32,128]{2,1,0:T(8,128)S(1)} async-done(((f32[8,32,128]{2,1,0:T(8,128)}), f32[8,32,128]{2,1,0:T(8,128)S(1)}, u32[]{:S(2)}, u32[]{:S(2)}) %all-to-all-start.1) | async-done | bytes 131104 | tf_op jit(solution)/shard_map/all_to_all | solution.py:346
  118.8 3.3 %collective-permute-start.18 = (f32[32,128]{1,0:T(8,128)S(1)}, f32[32,128]{1,0:T(8,128)S(1)}, u32[]{:S(2)}, u32[]{:S(2)}) collective-permute-start(f32[32,128]{1,0:T(8,128)S(1)} %reduce_sum.19.mine_ref), channel_id=1, source_target_pairs={{0,1},{1,0},{2,3},{3,2},{4,5},{5,4},{6,7},{7,6},{8,9},{9,8},{10,11... | collective-permute-start | bytes 49160 | tf_op jit(solution)/shard_map/ppermute | solution.py:294
  122.1 0.0 collective-permute-done.19.got_ref
  122.1 0.8 collective-permute-done.18.other_ref
  122.9 6.7 %shard_map.98 = (f32[64,1024]{1,0:T(8,128)}, f32[64,64]{1,0:T(8,128)}) custom-call(s32[1]{0:T(128)} %bitcast.core_ref, f32[32,128]{1,0:T(8,128)S(1)} %reduce_sum.19.mine_ref, f32[32,128]{1,0:T(8,128)S(1)} %collective-permute-done.18.other_ref, f32[2,64,512]{2,1,0:T(8,128)S(1)} %shard_map.96.value_ref, f32[64,512]{1,0:T(8,128)S(1)} %collective-permute-done.19.got_ref), custom_call_target="tpu_custom_call" | custom-call | flops 100000000 | bytes 1000000 | tf_op jit(solution)/shard_map/pallas_call | solution.py:432
  (20 shorter events, 0.2 us)
Async XLA Ops:
  0.6 9.6 %copy-start.3 = (s32[11]{0:T(128)S(1)}, s32[11]{0:T(128)}, u32[]{:S(2)}) copy-start(s32[11]{0:T(128)} %constant.40.clone) | copy-start | bytes 136
  0.6 9.6 %copy-start.4 = (s32[11]{0:T(128)S(1)}, s32[11]{0:T(128)}, u32[]{:S(2)}) copy-start(s32[11]{0:T(128)} %constant.39.clone) | copy-start | bytes 136
  0.7 28.3 %copy-start.1 = (s32[4]{0:T(128)S(1)}, s32[4]{0:T(128)}, u32[]{:S(2)}) copy-start(s32[4]{0:T(128)} %constant.42.clone) | copy-start | bytes 52
  0.7 28.3 %copy-start.2 = (s32[4]{0:T(128)S(1)}, s32[4]{0:T(128)}, u32[]{:S(2)}) copy-start(s32[4]{0:T(128)} %constant.41.clone) | copy-start | bytes 52
  0.7 8.2 %copy-start = (s32[4,2]{0,1:T(2,128)S(1)}, s32[4,2]{0,1:T(2,128)}, u32[]{:S(2)}) copy-start(s32[4,2]{0,1:T(2,128)} %param.9) | copy-start | bytes 100
  2.1 24.2 %collective-permute-start.2 = (bf16[2,1792,128]{2,1,0:T(8,128)(2,1)S(1)}, bf16[2,1792,128]{2,1,0:T(8,128)(2,1)S(1)}, u32[]{:S(2)}, u32[]{:S(2)}) collective-permute-start(bf16[2,1792,128]{2,1,0:T(8,128)(2,1)S(1)} %shard_map.87.refs_0_.refs_1_), channel_id=1, source_target_pairs={{2,4},{4,2},{6,8},{8,6},{10,12},{12,10},{14,16},{16,14},{18,20},{2... | collective-permute-start | bytes 2752520 | tf_op jit(solution)/shard_map/ppermute | solution.py:282
  2.8 24.6 %collective-permute-start.1 = (bf16[2,1792,128]{2,1,0:T(8,128)(2,1)S(1)}, bf16[2,1792,128]{2,1,0:T(8,128)(2,1)}, u32[]{:S(2)}, u32[]{:S(2)}) collective-permute-start(bf16[2,1792,128]{2,1,0:T(8,128)(2,1)S(1)} %shard_map.87.refs_0_.refs_1_), channel_id=1, source_target_pairs={{0,2},{2,0},{4,6},{6,4},{8,10},{10,8},{12,14},{14,12},{16,18},{18,... | collective-permute-start | bytes 2752520 | tf_op jit(solution)/shard_map/ppermute | solution.py:282
  8.9 2.1 %collective-permute-start = (s32[4,2]{0,1:T(2,128)S(1)}, s32[4,2]{0,1:T(2,128)S(1)}, u32[]{:S(2)}, u32[]{:S(2)}) collective-permute-start(s32[4,2]{0,1:T(2,128)S(1)} %copy-done), channel_id=1, source_target_pairs={{0,1},{1,0},{2,3},{3,2},{4,5},{5,4},{6,7},{7,6},{8,9},{9,8},{10,11... | collective-permute-start | bytes 104 | tf_op jit(solution)/shard_map/ppermute | solution.py:294
  11.1 15.1 %collective-permute-start.3 = (s32[8,2]{0,1:T(2,128)S(1)}, s32[8,2]{0,1:T(2,128)S(1)}, u32[]{:S(2)}, u32[]{:S(2)}) collective-permute-start(s32[8,2]{0,1:T(2,128)S(1)} %pad_add_fusion), channel_id=1, source_target_pairs={{0,2},{2,4},{4,6},{6,8},{8,10},{10,12},{12,14},{14,16},{16,18},{18... | collective-permute-start | bytes 200 | tf_op jit(solution)/shard_map/ppermute | solution.py:315
  27.4 3.9 %collective-permute-start.4 = (bf16[2,1792,128]{2,1,0:T(8,128)(2,1)}, bf16[2,1792,128]{2,1,0:T(8,128)(2,1)S(1)}, u32[]{:S(2)}, u32[]{:S(2)}) collective-permute-start(bf16[2,1792,128]{2,1,0:T(8,128)(2,1)} %collective-permute-done.1.refs_2_), channel_id=1, source_target_pairs={{0,1},{1,0},{2,3},{3,2},{4,5},{5,4},{6,7},{7,6},{8,9},{9,8},{10,11... | collective-permute-start | bytes 2752520 | tf_op jit(solution)/shard_map/ppermute | solution.py:294
  36.5 1.6 %collective-permute-start.7 = (f32[2,64,512]{2,1,0:T(8,128)S(1)}, f32[2,64,512]{2,1,0:T(8,128)S(1)}, u32[]{:S(2)}, u32[]{:S(2)}) collective-permute-start(f32[2,64,512]{2,1,0:T(8,128)S(1)} %get-tuple-element.56), channel_id=1, source_target_pairs={{0,1},{1,0},{2,3},{3,2},{4,5},{5,4},{6,7},{7,6},{8,9},{9,8},{10,11... | collective-permute-start | bytes 786440 | tf_op jit(solution)/shard_map/ppermute | solution.py:294
  37.0 5.8 %collective-permute-start.5 = (f32[2,64,512]{2,1,0:T(8,128)S(1)}, f32[2,64,512]{2,1,0:T(8,128)S(1)}, u32[]{:S(2)}, u32[]{:S(2)}) collective-permute-start(f32[2,64,512]{2,1,0:T(8,128)S(1)} %get-tuple-element.53), channel_id=1, source_target_pairs={{0,1},{1,0},{2,3},{3,2},{4,5},{5,4},{6,7},{7,6},{8,9},{9,8},{10,11... | collective-permute-start | bytes 786440 | tf_op jit(solution)/shard_map/ppermute | solution.py:294
  37.1 5.6 %collective-permute-start.6 = (f32[2,64,512]{2,1,0:T(8,128)S(1)}, f32[2,64,512]{2,1,0:T(8,128)S(1)}, u32[]{:S(2)}, u32[]{:S(2)}) collective-permute-start(f32[2,64,512]{2,1,0:T(8,128)S(1)} %get-tuple-element.54), channel_id=1, source_target_pairs={{2,4},{4,2},{6,8},{8,6},{10,12},{12,10},{14,16},{16,14},{18,20},{2... | collective-permute-start | bytes 786440 | tf_op jit(solution)/shard_map/ppermute | solution.py:282
  38.2 10.6 %collective-permute-start.8 = (f32[2,64,512]{2,1,0:T(8,128)S(1)}, f32[2,64,512]{2,1,0:T(8,128)S(1)}, u32[]{:S(2)}, u32[]{:S(2)}) collective-permute-start(f32[2,64,512]{2,1,0:T(8,128)S(1)} %add.39), channel_id=1, source_target_pairs={{0,2},{2,0},{4,6},{6,4},{8,10},{10,8},{12,14},{14,12},{16,18},{18,... | collective-permute-start | bytes 786440 | tf_op jit(solution)/shard_map/ppermute | solution.py:282
  48.9 4.8 %collective-permute-start.9 = (bf16[2,128,512]{2,1,0:T(8,128)(2,1)S(1)}, bf16[2,128,512]{2,1,0:T(8,128)(2,1)S(1)}, u32[]{:S(2)}, u32[]{:S(2)}) collective-permute-start(bf16[2,128,512]{2,1,0:T(8,128)(2,1)S(1)} %get-tuple-element.59.refs_1_.refs_2_), channel_id=1, source_target_pairs={{0,1},{1,0},{2,3},{3,2},{4,5},{5,4},{6,7},{7,6},{8,9},{9,8},{10,11... | collective-permute-start | bytes 786440 | tf_op jit(solution)/shard_map/ppermute | solution.py:294
  50.2 4.6 %collective-permute-start.11 = (bf16[2,128,512]{2,1,0:T(8,128)(2,1)S(1)}, bf16[2,128,512]{2,1,0:T(8,128)(2,1)S(1)}, u32[]{:S(2)}, u32[]{:S(2)}) collective-permute-start(bf16[2,128,512]{2,1,0:T(8,128)(2,1)S(1)} %get-tuple-element.59.refs_1_.refs_2_), channel_id=1, source_target_pairs={{2,4},{4,2},{6,8},{8,6},{10,12},{12,10},{14,16},{16,14},{18,20},{2... | collective-permute-start | bytes 786440 | tf_op jit(solution)/shard_map/ppermute | solution.py:282
  50.9 9.2 %collective-permute-start.10 = (bf16[2,128,512]{2,1,0:T(8,128)(2,1)S(1)}, bf16[2,128,512]{2,1,0:T(8,128)(2,1)S(1)}, u32[]{:S(2)}, u32[]{:S(2)}) collective-permute-start(bf16[2,128,512]{2,1,0:T(8,128)(2,1)S(1)} %get-tuple-element.59.refs_1_.refs_2_), channel_id=1, source_target_pairs={{0,2},{2,0},{4,6},{6,4},{8,10},{10,8},{12,14},{14,12},{16,18},{18,... | collective-permute-start | bytes 786440 | tf_op jit(solution)/shard_map/ppermute | solution.py:282
  60.1 2.0 %collective-permute-start.12 = (bf16[2,128,512]{2,1,0:T(8,128)(2,1)S(1)}, bf16[2,128,512]{2,1,0:T(8,128)(2,1)S(1)}, u32[]{:S(2)}, u32[]{:S(2)}) collective-permute-start(bf16[2,128,512]{2,1,0:T(8,128)(2,1)S(1)} %collective-permute-done.10.refs_3_), channel_id=1, source_target_pairs={{0,1},{1,0},{2,3},{3,2},{4,5},{5,4},{6,7},{7,6},{8,9},{9,8},{10,11... | collective-permute-start | bytes 786440 | tf_op jit(solution)/shard_map/ppermute | solution.py:294
  64.7 1.8 %collective-permute-start.15 = (f32[2,64,512]{2,1,0:T(8,128)S(1)}, f32[2,64,512]{2,1,0:T(8,128)S(1)}, u32[]{:S(2)}, u32[]{:S(2)}) collective-permute-start(f32[2,64,512]{2,1,0:T(8,128)S(1)} %get-tuple-element.74), channel_id=1, source_target_pairs={{0,1},{1,0},{2,3},{3,2},{4,5},{5,4},{6,7},{7,6},{8,9},{9,8},{10,11... | collective-permute-start | bytes 786440 | tf_op jit(solution)/shard_map/ppermute | solution.py:294
  65.3 7.5 %collective-permute-start.13 = (f32[2,64,512]{2,1,0:T(8,128)S(1)}, f32[2,64,512]{2,1,0:T(8,128)S(1)}, u32[]{:S(2)}, u32[]{:S(2)}) collective-permute-start(f32[2,64,512]{2,1,0:T(8,128)S(1)} %get-tuple-element.71), channel_id=1, source_target_pairs={{0,1},{1,0},{2,3},{3,2},{4,5},{5,4},{6,7},{7,6},{8,9},{9,8},{10,11... | collective-permute-start | bytes 786440 | tf_op jit(solution)/shard_map/ppermute | solution.py:294
  65.5 7.4 %collective-permute-start.14 = (f32[2,64,512]{2,1,0:T(8,128)S(1)}, f32[2,64,512]{2,1,0:T(8,128)S(1)}, u32[]{:S(2)}, u32[]{:S(2)}) collective-permute-start(f32[2,64,512]{2,1,0:T(8,128)S(1)} %get-tuple-element.72), channel_id=1, source_target_pairs={{2,4},{4,2},{6,8},{8,6},{10,12},{12,10},{14,16},{16,14},{18,20},{2... | collective-permute-start | bytes 786440 | tf_op jit(solution)/shard_map/ppermute | solution.py:282
  66.5 11.9 %collective-permute-start.16 = (f32[2,64,512]{2,1,0:T(8,128)S(1)}, f32[2,64,512]{2,1,0:T(8,128)S(1)}, u32[]{:S(2)}, u32[]{:S(2)}) collective-permute-start(f32[2,64,512]{2,1,0:T(8,128)S(1)} %add.40), channel_id=1, source_target_pairs={{0,2},{2,0},{4,6},{6,4},{8,10},{10,8},{12,14},{14,12},{16,18},{18,... | collective-permute-start | bytes 786440 | tf_op jit(solution)/shard_map/ppermute | solution.py:282
  79.0 2.1 %collective-permute-start.17 = (f32[32,128]{1,0:T(8,128)S(1)}, f32[32,128]{1,0:T(8,128)S(1)}, u32[]{:S(2)}, u32[]{:S(2)}) collective-permute-start(f32[32,128]{1,0:T(8,128)S(1)} %get-tuple-element.76), channel_id=1, source_target_pairs={{0,1},{1,0},{2,3},{3,2},{4,5},{5,4},{6,7},{7,6},{8,9},{9,8},{10,11... | collective-permute-start | bytes 49160 | tf_op jit(solution)/shard_map/ppermute | solution.py:294
  107.2 11.5 %all-to-all-start.1 = ((f32[8,32,128]{2,1,0:T(8,128)}), f32[8,32,128]{2,1,0:T(8,128)S(1)}, u32[]{:S(2)}, u32[]{:S(2)}) async-start(f32[8,32,128]{2,1,0:T(8,128)} %broadcast_in_dim.5), calls=%async_computation.1 | async-start | bytes 262144 | tf_op jit(solution)/shard_map/all_to_all | solution.py:346
  110.7 11.3 %collective-permute-start.19 = (f32[64,512]{1,0:T(8,128)S(1)}, f32[64,512]{1,0:T(8,128)S(1)}, u32[]{:S(2)}, u32[]{:S(2)}) collective-permute-start(f32[64,512]{1,0:T(8,128)S(1)} %get-tuple-element.77), channel_id=1, source_target_pairs={{0,1},{1,0},{2,3},{3,2},{4,5},{5,4},{6,7},{7,6},{8,9},{9,8},{10,11... | collective-permute-start | bytes 393224 | tf_op jit(solution)/shard_map/ppermute | solution.py:294
  118.8 4.1 %collective-permute-start.18 = (f32[32,128]{1,0:T(8,128)S(1)}, f32[32,128]{1,0:T(8,128)S(1)}, u32[]{:S(2)}, u32[]{:S(2)}) collective-permute-start(f32[32,128]{1,0:T(8,128)S(1)} %reduce_sum.19.mine_ref), channel_id=1, source_target_pairs={{0,1},{1,0},{2,3},{3,2},{4,5},{5,4},{6,7},{7,6},{8,9},{9,8},{10,11... | collective-permute-start | bytes 49160 | tf_op jit(solution)/shard_map/ppermute | solution.py:294

commit v4 on v3

--- a/solution.py
+++ b/solution.py
@@ -143,40 +143,41 @@
             )
 
 
-def odd_kernel(make, flags_ref, *refs):
+def early_kernel(make, flags_ref, *refs):
     if make:
-        odd0, own0, own1, in0, in1, tile_ref, done_ref, part0, part1 = refs
+        own0, even0, even1, started, tile_ref, done_ref, part0, part1 = refs
     else:
-        tile_ref, odd0, own0, own1, in0, in1, done_ref, part0, part1 = refs
-    done_ref[...] = jnp.zeros_like(done_ref)
-    part0[...] = in0[...]
-    part1[...] = in1[...]
+        tile_ref, own0, even0, even1, started, done_ref, part0, part1 = refs
+    done_ref[...] = started[...]
+    for ref in (part0, part1):
+        ref[...] = jnp.zeros_like(ref)
 
     @pl.loop(0, 4)
     def _(slot):
         left, right = slot // 2, slot % 2
 
-        @pl.when(flags_ref[7 + slot] > 0)
+        @pl.when(flags_ref[3 + slot] > 0)
         def _():
             one_pair(
-                make, tile_ref, slot, odd0.at[left], (own0.at[right], own1.at[right]),
+                make, tile_ref, slot, own0.at[left], (even0.at[right], even1.at[right]),
                 done_ref, left, (part0, part1), right,
             )
 
 
-def even_kernel(make, flags_ref, far_ref, *refs):
+def late_kernel(make, flags_ref, far_ref, *refs):
     if make:
-        own0, odd0, even0, even1, own_in, odd_in, tile_ref, *refs = refs
+        odd0, own0, own1, even0, even1, *ins = refs[:9]
+        tile_ref, done_ref, *parts = refs[9:]
     else:
-        tile_ref, own0, odd0, even0, even1, own_in, odd_in, *refs = refs
-    own_done, odd_done, part0, part1 = refs
-    own_done[...] = own_in[...]
-    odd_done[...] = odd_in[...]
-    for ref in (part0, part1):
-        ref[...] = jnp.zeros_like(ref)
+        tile_ref, odd0, own0, own1, even0, even1, *ins = refs[:10]
+        done_ref, *parts = refs[10:]
+    done_ref[...] = jnp.zeros_like(done_ref)
+    for ref, value in zip(parts, ins):
+        ref[...] = value[...]
     for kind in range(2):
-        lefts, done_ref = ((own0, own_done), (odd0, odd_done))[kind]
-        flag_ref, flag_at = ((flags_ref, 3), (far_ref, 0))[kind]
+        rights = ((own0, own1), (even0, even1))[kind]
+        part_refs = (parts[:2], parts[2:])[kind]
+        flag_ref, flag_at = ((flags_ref, 7), (far_ref, 0))[kind]
 
         @pl.loop(0, 4)
         def _(index):
@@ -185,8 +186,8 @@
             @pl.when(flag_ref[flag_at + index] > 0)
             def _():
                 one_pair(
-                    make, tile_ref, kind * 4 + index, lefts.at[left],
-                    (even0.at[right], even1.at[right]), done_ref, left, (part0, part1), right,
+                    make, tile_ref, kind * 4 + index, odd0.at[left],
+                    (rights[0].at[right], rights[1].at[right]), done_ref, left, part_refs, right,
                 )
 
 
@@ -294,6 +295,10 @@
     return lax.ppermute(value, "cols", [(0, 1), (1, 0)])
 
 
+def swap_blocks(value):
+    return jnp.stack([swap(value[block]) for block in range(2)])
+
+
 def live_flags(pairs, base, even_codes, odd_codes):
     none = (100, 100)
 
@@ -385,38 +390,42 @@
     tiles_own, done, own_part0, own_part1 = call(
         functools.partial(local_kernel, True), (tiles(3),) + 3 * (sum_shape,), 10**4, 10**4
     )(in_specs=[SMEM] + [VMEM] * 2)(flags, own0, own1)
-    done, even0, odd0, before = lax.optimization_barrier((done, even0, odd0, before))
-    even1 = swap(even0)
+    done, even0 = lax.optimization_barrier((done, even0))
+    even1 = swap_blocks(even0)
+    tiles_early, done, even_part0, even_part1 = call(
+        functools.partial(early_kernel, True), (tiles(4),) + 3 * (sum_shape,), 10**4, 10**4
+    )(in_specs=[SMEM] + [VMEM] * 4)(flags, own0, even0, even1, done)
+    done, odd0, before = lax.optimization_barrier((done, odd0, before))
     far_flags = flags_of_far(before, base)
-    tiles_odd, out_odd, own_part0, own_part1 = call(
-        functools.partial(odd_kernel, True), (tiles(4),) + 3 * (sum_shape,), 10**4, 10**4
-    )(in_specs=[SMEM] + [VMEM] * 5)(flags, odd0, own0, own1, own_part0, own_part1)
-    tiles_even, done, out_odd, even_part0, even_part1 = call(
-        functools.partial(even_kernel, True), (tiles(8),) + 4 * (sum_shape,), 10**9, 10**6
-    )(in_specs=[SMEM] * 2 + [VMEM] * 6)(flags, far_flags, own0, odd0, even0, even1, done, out_odd)
+    tiles_late, out_odd, own_part0, own_part1, even_part0, even_part1 = call(
+        functools.partial(late_kernel, True), (tiles(8),) + 5 * (sum_shape,), 10**9, 10**6
+    )(in_specs=[SMEM] * 2 + [VMEM] * 9)(
+        flags, far_flags, odd0, own0, own1, even0, even1, own_part0, own_part1, even_part0, even_part1
+    )
     sketch, pair0 = call(total_kernel, (sum_shape, shape((2, 128, HALF), bf16)), 10**6, 2 * 10**6)(
         in_specs=[VMEM] * 5
     )(*spread(done, own_part0, own_part1, out_odd, even_part0, even_part1))
 
     even0 = to_even(pair0)
     odd0 = to_odd(pair0)
-    pair1 = swap(pair0)
     gram_shape = shape((32, 128))
-    first_gram = call(functools.partial(gram_kernel, scale), gram_shape, 10**8, 10**6)(
+    first_gram = call(functools.partial(gram_kernel, scale), gram_shape, 10**4, 10**4)(
         in_specs=[VMEM]
     )(sketch)
+    pair1 = swap(pair0)
     done, own_part0, own_part1 = call(
         functools.partial(local_kernel, False), 3 * (sum_shape,), 10**4, 10**4
     )(in_specs=[SMEM] + [VMEM] * 3)(flags, tiles_own, pair0, pair1)
-    done, even0, odd0 = lax.optimization_barrier((done, even0, odd0))
-    even1 = swap(even0)
-    out_odd, own_part0, own_part1 = call(
-        functools.partial(odd_kernel, False), 3 * (sum_shape,), 10**4, 10**4
-    )(in_specs=[SMEM] + [VMEM] * 6)(flags, tiles_odd, odd0, pair0, pair1, own_part0, own_part1)
-    done, out_odd, even_part0, even_part1 = call(
-        functools.partial(even_kernel, False), 4 * (sum_shape,), 10**9, 10**6
-    )(in_specs=[SMEM] * 2 + [VMEM] * 7)(
-        flags, far_flags, tiles_even, pair0, odd0, even0, even1, done, out_odd
+    even1 = swap_blocks(even0)
+    done, even_part0, even_part1 = call(
+        functools.partial(early_kernel, False), 3 * (sum_shape,), 10**4, 10**4
+    )(in_specs=[SMEM] + [VMEM] * 5)(flags, tiles_early, pair0, even0, even1, done)
+    done, odd0 = lax.optimization_barrier((done, odd0))
+    out_odd, own_part0, own_part1, even_part0, even_part1 = call(
+        functools.partial(late_kernel, False), 5 * (sum_shape,), 10**9, 10**6
+    )(in_specs=[SMEM] * 2 + [VMEM] * 10)(
+        flags, far_flags, tiles_late, odd0, pair0, pair1, even0, even1,
+        own_part0, own_part1, even_part0, even_part1,
     )
     image = call(total_kernel, sum_shape, 10**6, 2 * 10**6)(in_specs=[VMEM] * 5)(
         *spread(done, own_part0, own_part1, out_odd, even_part0, even_part1)

time: 131 us -> 129 us (0.985); the launches traced: 130 us -> 126 us
  waiting for transfers between devices: 40.7 us -> 36.6 us
  starting transfers between devices: 38.8 us -> 41.4 us
  Pallas kernels: 22.6 us -> 20.8 us
    ppermute x1, waiting for transfers between devices: 11.6 us -> 0.01 us  [own_flags_and_list(): lax.ppermute(own, 'rows', [(r, r + 1) for r in range(lax.axis_size('rows'...]
    ppermute x8, waiting for transfers between devices: 18.1 us -> 27.5 us  [exchange(): return lax.ppermute(value, 'rows', links)]
    ppermute x8, starting transfers between devices: 20.7 us -> 17.1 us  [exchange(): return lax.ppermute(value, 'rows', links)]
    ppermute x11 -> x13, starting transfers between devices: 13.1 us -> 15.6 us  [swap(): return lax.ppermute(value, 'cols', [(0, 1), (1, 0)])]
    ppermute x11 -> x13, waiting for transfers between devices: 5.1 us -> 3.24 us  [swap(): return lax.ppermute(value, 'cols', [(0, 1), (1, 0)])]
    all_to_all x1, starting transfers between devices: 3.49 us -> 5.33 us  [sum_over_chips(): lax.all_to_all(copies, 'rows', 0, 0, axis_index_groups=groups, tiled=True)]
    pallas_call x5, Pallas kernels: 9.63 us -> 7.79 us  [the longest x1 3.27 us: local(): call(functools.partial(early_kernel, True), (tiles(4),) + 3 * (sum_shape,...]
    ppermute x1, starting transfers between devices: 1.63 us -> 3.36 us  [own_flags_and_list(): lax.ppermute(own, 'rows', [(r, r + 1) for r in range(lax.axis_size('rows'...]
  transfers between devices with their start and end apart: 21 -> 23, of which waited for: 13 -> 10; matrix products, arithmetic and copies ran while one was open for 0% -> 0% of each run, Pallas kernels for 5% -> 8%
where the time goes in v4:
time: 129 us; the launch traced here: 126 us
  starting transfers between devices  41.4 us (32%)
  waiting for transfers between devices  36.6 us (28%)
  blocking collectives  25.1 us (19%)
  Pallas kernels  20.8 us (16%)
    ppermute x8, waiting for transfers between devices, exchange(): return lax.ppermute(value, 'rows', links)  27.5 us
    all_to_all x1, blocking collectives, sum_over_chips(): lax.all_to_all(copies, 'rows', 0, 0, axis_index_groups=groups, tiled=True)  25.1 us
    ppermute x8, starting transfers between devices, exchange(): return lax.ppermute(value, 'rows', links)  17.1 us
    ppermute x13, starting transfers between devices, swap(): return lax.ppermute(value, 'cols', [(0, 1), (1, 0)])  15.6 us
    pallas_call x1, Pallas kernels, local(): call(finish_kernel, (shape((64, BLK)), shape((64, 64))), 10 ** 8, 10 ** 6)  6.68 us
    all_to_all x1, waiting for transfers between devices, sum_over_chips(): lax.all_to_all(copies, 'rows', 0, 0, axis_index_groups=groups, tiled=True)  5.87 us
    all_to_all x1, starting transfers between devices, sum_over_chips(): lax.all_to_all(copies, 'rows', 0, 0, axis_index_groups=groups, tiled=True)  5.33 us
    ppermute x1, starting transfers between devices, own_flags_and_list(): lax.ppermute(own, 'rows', [(r, r + 1) for r in range(lax.axis_size('rows'...  3.36 us
  transfers between devices with their start and end apart: 23, of which 10 were waited for; matrix products, arithmetic and copies ran while one was open for 0% of the time, Pallas kernels for 8%

profile of v4, /device:TPU:1, one launch (start us, length us, event | category | flops | bytes accessed | tf_op | source)
XLA Modules:
  0.0 126.3 jit_solution(6811200034246074799)
XLA Ops:
  0.6 0.0 copy-start.3
  0.6 0.0 copy-start.4
  0.7 0.0 copy-start.1
  0.7 0.0 copy-start.2
  0.7 1.4 %shard_map.87.refs_0_.refs_1_ = bf16[2,1792,128]{2,1,0:T(8,128)(2,1)S(1)} custom-call(s32[1]{0:T(128)} %bitcast.core_ref, bf16[2048,384]{1,0:T(8,128)(2,1)} %rows_ref.3, bf16[64,2048]{1,0:T(8,128)(2,1)} %bitcast.23), custom_call_target="tpu_custom_call" | custom-call | flops 10000 | bytes 10000 | tf_op jit(solution)/shard_map/pallas_call | solution.py:368
  2.1 2.2 %collective-permute-start.1 = (bf16[2,1792,128]{2,1,0:T(8,128)(2,1)S(1)}, bf16[2,1792,128]{2,1,0:T(8,128)(2,1)S(1)}, u32[]{:S(2)}, u32[]{:S(2)}) collective-permute-start(bf16[2,1792,128]{2,1,0:T(8,128)(2,1)S(1)} %shard_map.87.refs_0_.refs_1_), channel_id=1, source_target_pairs={{0,2},{2,0},{4,6},{6,4},{8,10},{10,8},{12,14},{14,12},{16,18},{18,... | collective-permute-start | bytes 2752520 | tf_op jit(solution)/shard_map/ppermute | solution.py:283
  4.3 1.6 %collective-permute-start.4 = (bf16[2,1792,128]{2,1,0:T(8,128)(2,1)S(1)}, bf16[2,1792,128]{2,1,0:T(8,128)(2,1)}, u32[]{:S(2)}, u32[]{:S(2)}) collective-permute-start(bf16[2,1792,128]{2,1,0:T(8,128)(2,1)S(1)} %shard_map.87.refs_0_.refs_1_), channel_id=1, source_target_pairs={{2,4},{4,2},{6,8},{8,6},{10,12},{12,10},{14,16},{16,14},{18,20},{2... | collective-permute-start | bytes 2752520 | tf_op jit(solution)/shard_map/ppermute | solution.py:283
  5.9 1.4 %shard_map.86.refs_1_.refs_2_ = bf16[2,1792,128]{2,1,0:T(8,128)(2,1)S(1)} custom-call(s32[1]{0:T(128)} %bitcast.core_ref, bf16[2048,384]{1,0:T(8,128)(2,1)} %rows_ref.3, bf16[64,2048]{1,0:T(8,128)(2,1)} %bitcast.24), custom_call_target="tpu_custom_call" | custom-call | flops 10000 | bytes 10000 | tf_op jit(solution)/shard_map/pallas_call | solution.py:368
  7.3 1.2 collective-permute-start
  8.6 0.8 collective-permute-done
  9.4 0.1 pad_add_fusion
  9.5 0.1 and_reduce_fusion
  9.6 1.8 %shard_map.88 = (bf16[3,2,512,512]{3,2,1,0:T(8,128)(2,1)S(1)}, f32[2,64,512]{2,1,0:T(8,128)S(1)}, f32[2,64,512]{2,1,0:T(8,128)S(1)}, f32[2,64,512]{2,1,0:T(8,128)S(1)}) custom-call(s32[11]{0:T(128)S(1)} %convert_element_type.6.flags_ref, bf16[2,1792,128]{2,1,0:T(8,128)(2,1)S(1)} %shard_map.87.refs_0_.refs_1_, bf16[2,1792,128]{2,1,0:T(8,128)(2,1)S(1)} %shard_map.86.refs_1_.refs_2_), custom_call_target="tpu_custom_call" | custom-call | flops 10000 | bytes 10000 | tf_op jit(solution)/shard_map/pallas_call | solution.py:390
  11.3 11.8 %collective-permute-done.1.refs_1_.refs_3_ = bf16[2,1792,128]{2,1,0:T(8,128)(2,1)S(1)} collective-permute-done((bf16[2,1792,128]{2,1,0:T(8,128)(2,1)S(1)}, bf16[2,1792,128]{2,1,0:T(8,128)(2,1)S(1)}, u32[]{:S(2)}, u32[]{:S(2)}) %collective-permute-start.1) | collective-permute-done | bytes 917536 | tf_op jit(solution)/shard_map/ppermute | solution.py:283
  23.1 0.1 slice_bitcast_fusion.1
  23.2 2.6 %collective-permute-start.2 = (bf16[1792,128]{1,0:T(8,128)(2,1)S(1)}, bf16[1792,128]{1,0:T(8,128)(2,1)S(1)}, u32[]{:S(2)}, u32[]{:S(2)}) collective-permute-start(bf16[1792,128]{1,0:T(8,128)(2,1)S(1)} %get-tuple-element.84), channel_id=1, source_target_pairs={{0,1},{1,0},{2,3},{3,2},{4,5},{5,4},{6,7},{7,6},{8,9},{9,8},{10,11... | collective-permute-start | bytes 1376264 | tf_op jit(solution)/shard_map/ppermute | solution.py:295
  25.8 0.1 collective-permute-start.3
  25.9 3.4 %collective-permute-start.5 = (s32[8,2]{0,1:T(2,128)S(1)}, s32[8,2]{0,1:T(2,128)S(1)}, u32[]{:S(2)}, u32[]{:S(2)}) collective-permute-start(s32[8,2]{0,1:T(2,128)S(1)} %pad_add_fusion), channel_id=1, source_target_pairs={{0,2},{2,4},{4,6},{6,8},{8,10},{10,12},{12,14},{14,16},{16,18},{18... | collective-permute-start | bytes 200 | tf_op jit(solution)/shard_map/ppermute | solution.py:320
  29.3 0.0 collective-permute-done.2
  29.3 0.1 pad_maximum_fusion.refs_2_.refs_4_
  29.4 3.3 %shard_map.89 = (bf16[4,2,512,512]{3,2,1,0:T(8,128)(2,1)S(1)}, f32[2,64,512]{2,1,0:T(8,128)S(1)}, f32[2,64,512]{2,1,0:T(8,128)S(1)}, f32[2,64,512]{2,1,0:T(8,128)S(1)}) custom-call(s32[11]{0:T(128)S(1)} %convert_element_type.6.flags_ref, bf16[2,1792,128]{2,1,0:T(8,128)(2,1)S(1)} %shard_map.87.refs_0_.refs_1_, ...), custom_call_target="tpu_custom_call" | custom-call | flops 10000 | bytes 10000 | tf_op jit(solution)/shard_map/pallas_call | solution.py:395
  32.7 0.2 and_reduce_fusion.1
  32.9 1.4 %shard_map.90 = (bf16[8,2,512,512]{3,2,1,0:T(8,128)(2,1)S(1)}, f32[2,64,512]{2,1,0:T(8,128)S(1)}, f32[2,64,512]{2,1,0:T(8,128)S(1)}, f32[2,64,512]{2,1,0:T(8,128...) custom-call(s32[11]{0:T(128)S(1)} %convert_element_type.6.flags_ref, s32[4]{0:T(128)S(1)} %convert_element_type.7.far_ref, ...), custom_call_target="tpu_custom_call" | custom-call | flops 1000000000 | bytes 1000000 | tf_op jit(solution)/shard_map/pallas_call | solution.py:400
  34.3 0.8 collective-permute-start.8
  35.1 0.1 collective-permute-start.6
  35.2 0.7 collective-permute-start.7
  35.9 0.4 collective-permute-done.8
  36.3 6.0 %collective-permute-start.9 = (f32[2,64,512]{2,1,0:T(8,128)S(1)}, f32[2,64,512]{2,1,0:T(8,128)S(1)}, u32[]{:S(2)}, u32[]{:S(2)}) collective-permute-start(f32[2,64,512]{2,1,0:T(8,128)S(1)} %add.39), channel_id=1, source_target_pairs={{0,2},{2,0},{4,6},{6,4},{8,10},{10,8},{12,14},{14,12},{16,18},{18,... | collective-permute-start | bytes 786440 | tf_op jit(solution)/shard_map/ppermute | solution.py:283
  42.3 0.0 collective-permute-done.6.part_other
  42.3 6.3 %collective-permute-done.9.from_even = f32[2,64,512]{2,1,0:T(8,128)S(1)} collective-permute-done((f32[2,64,512]{2,1,0:T(8,128)S(1)}, f32[2,64,512]{2,1,0:T(8,128)S(1)}, u32[]{:S(2)}, u32[]{:S(2)}) %collective-permute-start.9) | collective-permute-done | bytes 262176 | tf_op jit(solution)/shard_map/ppermute | solution.py:283
  48.6 0.1 shard_map.91
  48.7 1.2 collective-permute-start.10
  49.9 0.7 collective-permute-start.14
  50.6 1.6 %collective-permute-start.13 = (bf16[2,128,512]{2,1,0:T(8,128)(2,1)S(1)}, bf16[2,128,512]{2,1,0:T(8,128)(2,1)S(1)}, u32[]{:S(2)}, u32[]{:S(2)}) collective-permute-start(bf16[2,128,512]{2,1,0:T(8,128)(2,1)S(1)} %get-tuple-element.63.refs_1_.refs_2_), channel_id=1, source_target_pairs={{0,1},{1,0},{2,3},{3,2},{4,5},{5,4},{6,7},{7,6},{8,9},{9,8},{10,11... | collective-permute-start | bytes 786440 | tf_op jit(solution)/shard_map/ppermute | solution.py:295
  52.2 3.5 %collective-permute-done.10.refs_2_.refs_4_ = bf16[2,128,512]{2,1,0:T(8,128)(2,1)S(1)} collective-permute-done((bf16[2,128,512]{2,1,0:T(8,128)(2,1)S(1)}, bf16[2,128,512]{2,1,0:T(8,128)(2,1)S(1)}, u32[]{:S(2)}, u32[]{:S(2)}) %collective-permute-start.10) | collective-permute-done | bytes 262176 | tf_op jit(solution)/shard_map/ppermute | solution.py:283
  55.7 1.9 %collective-permute-start.11 = (bf16[128,512]{1,0:T(8,128)(2,1)S(1)}, bf16[128,512]{1,0:T(8,128)(2,1)S(1)}, u32[]{:S(2)}, u32[]{:S(2)}) collective-permute-start(bf16[128,512]{1,0:T(8,128)(2,1)S(1)} %get-tuple-element.86), channel_id=1, source_target_pairs={{0,1},{1,0},{2,3},{3,2},{4,5},{5,4},{6,7},{7,6},{8,9},{9,8},{10,11... | collective-permute-start | bytes 393224 | tf_op jit(solution)/shard_map/ppermute | solution.py:295
  57.6 0.3 collective-permute-start.12
  57.9 1.1 shard_map.93
  59.0 0.0 collective-permute-done.11
  59.1 1.9 %shard_map.94 = (f32[2,64,512]{2,1,0:T(8,128)S(1)}, f32[2,64,512]{2,1,0:T(8,128)S(1)}, f32[2,64,512]{2,1,0:T(8,128)S(1)}) custom-call(s32[11]{0:T(128)S(1)} %convert_element_type.6.flags_ref, bf16[4,2,512,512]{3,2,1,0:T(8,128)(2,1)S(1)} %get-tuple-element.62.refs_0_, bf16[2,128,512]{2,1,0:T(8,128)(2,1)S(1)} %get-tuple-element.63.refs_1_.refs_2_, ...), custom_call_target="tpu_custom_call" | custom-call | flops 10000 | bytes 10000 | tf_op jit(solution)/shard_map/pallas_call | solution.py:420
  61.0 0.0 collective-permute-done.14.refs_1_
  61.0 0.8 shard_map.95
  61.8 0.3 collective-permute-start.17
  62.1 0.3 collective-permute-start.15
  62.4 0.7 collective-permute-start.16
  63.1 0.4 collective-permute-done.17
  63.5 4.1 %collective-permute-start.18 = (f32[2,64,512]{2,1,0:T(8,128)S(1)}, f32[2,64,512]{2,1,0:T(8,128)S(1)}, u32[]{:S(2)}, u32[]{:S(2)}) collective-permute-start(f32[2,64,512]{2,1,0:T(8,128)S(1)} %add.40), channel_id=1, source_target_pairs={{0,2},{2,0},{4,6},{6,4},{8,10},{10,8},{12,14},{14,12},{16,18},{18,... | collective-permute-start | bytes 786440 | tf_op jit(solution)/shard_map/ppermute | solution.py:283
  67.6 0.4 shard_map.92.first_ref
  68.0 0.0 collective-permute-done.15.part_other
  68.0 0.0 collective-permute-done.16.from_odd
  68.0 5.9 %collective-permute-done.18.from_even = f32[2,64,512]{2,1,0:T(8,128)S(1)} collective-permute-done((f32[2,64,512]{2,1,0:T(8,128)S(1)}, f32[2,64,512]{2,1,0:T(8,128)S(1)}, u32[]{:S(2)}, u32[]{:S(2)}) %collective-permute-start.18) | collective-permute-done | bytes 262176 | tf_op jit(solution)/shard_map/ppermute | solution.py:283
  73.9 0.1 shard_map.96.value_ref
  74.0 0.4 shard_map.97
  74.4 1.0 collective-permute-start.19
  75.4 0.8 collective-permute-done.19
  76.3 25.1 %all_to_all.10 = f32[16,32,128]{2,1,0:T(8,128)S(1)} all-to-all(f32[16,32,128]{2,1,0:T(8,128)S(1)} %broadcast_in_dim.4), channel_id=1, replica_groups={{0,2,4,6,64,66,68,70,128,130,132,134,192,194,196,198},{8,10,12,14,72,74..., dimensions={0} | all-to-all | bytes 524288 | tf_op jit(solution)/shard_map/all_to_all | solution.py:351
  101.4 0.7 broadcast_in_dim.5
  102.1 5.3 %all-to-all-start.1 = ((f32[8,32,128]{2,1,0:T(8,128)}), f32[8,32,128]{2,1,0:T(8,128)S(1)}, u32[]{:S(2)}, u32[]{:S(2)}) async-start(f32[8,32,128]{2,1,0:T(8,128)} %broadcast_in_dim.5), calls=%async_computation.1 | async-start | bytes 262144 | tf_op jit(solution)/shard_map/all_to_all | solution.py:351
  107.4 2.2 %collective-permute-start.21 = (f32[64,512]{1,0:T(8,128)S(1)}, f32[64,512]{1,0:T(8,128)S(1)}, u32[]{:S(2)}, u32[]{:S(2)}) collective-permute-start(f32[64,512]{1,0:T(8,128)S(1)} %get-tuple-element.81), channel_id=1, source_target_pairs={{0,1},{1,0},{2,3},{3,2},{4,5},{5,4},{6,7},{7,6},{8,9},{9,8},{10,11... | collective-permute-start | bytes 393224 | tf_op jit(solution)/shard_map/ppermute | solution.py:295
  109.6 5.9 %all-to-all-done.1 = f32[8,32,128]{2,1,0:T(8,128)S(1)} async-done(((f32[8,32,128]{2,1,0:T(8,128)}), f32[8,32,128]{2,1,0:T(8,128)S(1)}, u32[]{:S(2)}, u32[]{:S(2)}) %all-to-all-start.1) | async-done | bytes 131104 | tf_op jit(solution)/shard_map/all_to_all | solution.py:351
  115.4 3.3 %collective-permute-start.20 = (f32[32,128]{1,0:T(8,128)S(1)}, f32[32,128]{1,0:T(8,128)S(1)}, u32[]{:S(2)}, u32[]{:S(2)}) collective-permute-start(f32[32,128]{1,0:T(8,128)S(1)} %reduce_sum.19.mine_ref), channel_id=1, source_target_pairs={{0,1},{1,0},{2,3},{3,2},{4,5},{5,4},{6,7},{7,6},{8,9},{9,8},{10,11... | collective-permute-start | bytes 49160 | tf_op jit(solution)/shard_map/ppermute | solution.py:295
  118.7 0.0 collective-permute-done.21.got_ref
  118.7 0.8 collective-permute-done.20.other_ref
  119.6 6.7 %shard_map.98 = (f32[64,1024]{1,0:T(8,128)}, f32[64,64]{1,0:T(8,128)}) custom-call(s32[1]{0:T(128)} %bitcast.core_ref, f32[32,128]{1,0:T(8,128)S(1)} %reduce_sum.19.mine_ref, f32[32,128]{1,0:T(8,128)S(1)} %collective-permute-done.20.other_ref, f32[2,64,512]{2,1,0:T(8,128)S(1)} %shard_map.96.value_ref, f32[64,512]{1,0:T(8,128)S(1)} %collective-permute-done.21.got_ref), custom_call_target="tpu_custom_call" | custom-call | flops 100000000 | bytes 1000000 | tf_op jit(solution)/shard_map/pallas_call | solution.py:441
  (28 shorter events, 0.3 us)
Async XLA Ops:
  0.6 7.9 %copy-start.3 = (s32[11]{0:T(128)S(1)}, s32[11]{0:T(128)}, u32[]{:S(2)}) copy-start(s32[11]{0:T(128)} %constant.40.clone) | copy-start | bytes 136
  0.6 7.9 %copy-start.4 = (s32[11]{0:T(128)S(1)}, s32[11]{0:T(128)}, u32[]{:S(2)}) copy-start(s32[11]{0:T(128)} %constant.39.clone) | copy-start | bytes 136
  0.7 6.7 %copy-start = (s32[4,2]{0,1:T(2,128)S(1)}, s32[4,2]{0,1:T(2,128)}, u32[]{:S(2)}) copy-start(s32[4,2]{0,1:T(2,128)} %param.9) | copy-start | bytes 100
  0.7 25.2 %copy-start.1 = (s32[4]{0:T(128)S(1)}, s32[4]{0:T(128)}, u32[]{:S(2)}) copy-start(s32[4]{0:T(128)} %constant.42.clone) | copy-start | bytes 52
  0.7 25.2 %copy-start.2 = (s32[4]{0:T(128)S(1)}, s32[4]{0:T(128)}, u32[]{:S(2)}) copy-start(s32[4]{0:T(128)} %constant.41.clone) | copy-start | bytes 52
  2.1 21.0 %collective-permute-start.1 = (bf16[2,1792,128]{2,1,0:T(8,128)(2,1)S(1)}, bf16[2,1792,128]{2,1,0:T(8,128)(2,1)S(1)}, u32[]{:S(2)}, u32[]{:S(2)}) collective-permute-start(bf16[2,1792,128]{2,1,0:T(8,128)(2,1)S(1)} %shard_map.87.refs_0_.refs_1_), channel_id=1, source_target_pairs={{0,2},{2,0},{4,6},{6,4},{8,10},{10,8},{12,14},{14,12},{16,18},{18,... | collective-permute-start | bytes 2752520 | tf_op jit(solution)/shard_map/ppermute | solution.py:283
  4.3 28.3 %collective-permute-start.4 = (bf16[2,1792,128]{2,1,0:T(8,128)(2,1)S(1)}, bf16[2,1792,128]{2,1,0:T(8,128)(2,1)}, u32[]{:S(2)}, u32[]{:S(2)}) collective-permute-start(bf16[2,1792,128]{2,1,0:T(8,128)(2,1)S(1)} %shard_map.87.refs_0_.refs_1_), channel_id=1, source_target_pairs={{2,4},{4,2},{6,8},{8,6},{10,12},{12,10},{14,16},{16,14},{18,20},{2... | collective-permute-start | bytes 2752520 | tf_op jit(solution)/shard_map/ppermute | solution.py:283
  7.3 2.0 %collective-permute-start = (s32[4,2]{0,1:T(2,128)S(1)}, s32[4,2]{0,1:T(2,128)S(1)}, u32[]{:S(2)}, u32[]{:S(2)}) collective-permute-start(s32[4,2]{0,1:T(2,128)S(1)} %copy-done), channel_id=1, source_target_pairs={{0,1},{1,0},{2,3},{3,2},{4,5},{5,4},{6,7},{7,6},{8,9},{9,8},{10,11... | collective-permute-start | bytes 104 | tf_op jit(solution)/shard_map/ppermute | solution.py:295
  23.2 6.1 %collective-permute-start.2 = (bf16[1792,128]{1,0:T(8,128)(2,1)S(1)}, bf16[1792,128]{1,0:T(8,128)(2,1)S(1)}, u32[]{:S(2)}, u32[]{:S(2)}) collective-permute-start(bf16[1792,128]{1,0:T(8,128)(2,1)S(1)} %get-tuple-element.84), channel_id=1, source_target_pairs={{0,1},{1,0},{2,3},{3,2},{4,5},{5,4},{6,7},{7,6},{8,9},{9,8},{10,11... | collective-permute-start | bytes 1376264 | tf_op jit(solution)/shard_map/ppermute | solution.py:295
  25.8 3.5 %collective-permute-start.3 = (bf16[1792,128]{1,0:T(8,128)(2,1)S(1)}, bf16[1792,128]{1,0:T(8,128)(2,1)S(1)}, u32[]{:S(2)}, u32[]{:S(2)}) collective-permute-start(bf16[1792,128]{1,0:T(8,128)(2,1)S(1)} %get-tuple-element.85), channel_id=1, source_target_pairs={{0,1},{1,0},{2,3},{3,2},{4,5},{5,4},{6,7},{7,6},{8,9},{9,8},{10,11... | collective-permute-start | bytes 1376264 | tf_op jit(solution)/shard_map/ppermute | solution.py:295
  25.9 6.8 %collective-permute-start.5 = (s32[8,2]{0,1:T(2,128)S(1)}, s32[8,2]{0,1:T(2,128)S(1)}, u32[]{:S(2)}, u32[]{:S(2)}) collective-permute-start(s32[8,2]{0,1:T(2,128)S(1)} %pad_add_fusion), channel_id=1, source_target_pairs={{0,2},{2,4},{4,6},{6,8},{8,10},{10,12},{12,14},{14,16},{16,18},{18... | collective-permute-start | bytes 200 | tf_op jit(solution)/shard_map/ppermute | solution.py:320
  34.3 1.9 %collective-permute-start.8 = (f32[2,64,512]{2,1,0:T(8,128)S(1)}, f32[2,64,512]{2,1,0:T(8,128)S(1)}, u32[]{:S(2)}, u32[]{:S(2)}) collective-permute-start(f32[2,64,512]{2,1,0:T(8,128)S(1)} %get-tuple-element.60), channel_id=1, source_target_pairs={{0,1},{1,0},{2,3},{3,2},{4,5},{5,4},{6,7},{7,6},{8,9},{9,8},{10,11... | collective-permute-start | bytes 786440 | tf_op jit(solution)/shard_map/ppermute | solution.py:295
  35.1 7.2 %collective-permute-start.6 = (f32[2,64,512]{2,1,0:T(8,128)S(1)}, f32[2,64,512]{2,1,0:T(8,128)S(1)}, u32[]{:S(2)}, u32[]{:S(2)}) collective-permute-start(f32[2,64,512]{2,1,0:T(8,128)S(1)} %get-tuple-element.57), channel_id=1, source_target_pairs={{0,1},{1,0},{2,3},{3,2},{4,5},{5,4},{6,7},{7,6},{8,9},{9,8},{10,11... | collective-permute-start | bytes 786440 | tf_op jit(solution)/shard_map/ppermute | solution.py:295
  35.2 7.1 %collective-permute-start.7 = (f32[2,64,512]{2,1,0:T(8,128)S(1)}, f32[2,64,512]{2,1,0:T(8,128)S(1)}, u32[]{:S(2)}, u32[]{:S(2)}) collective-permute-start(f32[2,64,512]{2,1,0:T(8,128)S(1)} %get-tuple-element.58), channel_id=1, source_target_pairs={{2,4},{4,2},{6,8},{8,6},{10,12},{12,10},{14,16},{16,14},{18,20},{2... | collective-permute-start | bytes 786440 | tf_op jit(solution)/shard_map/ppermute | solution.py:283
  36.3 12.3 %collective-permute-start.9 = (f32[2,64,512]{2,1,0:T(8,128)S(1)}, f32[2,64,512]{2,1,0:T(8,128)S(1)}, u32[]{:S(2)}, u32[]{:S(2)}) collective-permute-start(f32[2,64,512]{2,1,0:T(8,128)S(1)} %add.39), channel_id=1, source_target_pairs={{0,2},{2,0},{4,6},{6,4},{8,10},{10,8},{12,14},{14,12},{16,18},{18,... | collective-permute-start | bytes 786440 | tf_op jit(solution)/shard_map/ppermute | solution.py:283
  48.7 7.0 %collective-permute-start.10 = (bf16[2,128,512]{2,1,0:T(8,128)(2,1)S(1)}, bf16[2,128,512]{2,1,0:T(8,128)(2,1)S(1)}, u32[]{:S(2)}, u32[]{:S(2)}) collective-permute-start(bf16[2,128,512]{2,1,0:T(8,128)(2,1)S(1)} %get-tuple-element.63.refs_1_.refs_2_), channel_id=1, source_target_pairs={{0,2},{2,0},{4,6},{6,4},{8,10},{10,8},{12,14},{14,12},{16,18},{18,... | collective-permute-start | bytes 786440 | tf_op jit(solution)/shard_map/ppermute | solution.py:283
  49.9 11.1 %collective-permute-start.14 = (bf16[2,128,512]{2,1,0:T(8,128)(2,1)S(1)}, bf16[2,128,512]{2,1,0:T(8,128)(2,1)S(1)}, u32[]{:S(2)}, u32[]{:S(2)}) collective-permute-start(bf16[2,128,512]{2,1,0:T(8,128)(2,1)S(1)} %get-tuple-element.63.refs_1_.refs_2_), channel_id=1, source_target_pairs={{2,4},{4,2},{6,8},{8,6},{10,12},{12,10},{14,16},{16,14},{18,20},{2... | collective-permute-start | bytes 786440 | tf_op jit(solution)/shard_map/ppermute | solution.py:283
  50.6 7.3 %collective-permute-start.13 = (bf16[2,128,512]{2,1,0:T(8,128)(2,1)S(1)}, bf16[2,128,512]{2,1,0:T(8,128)(2,1)S(1)}, u32[]{:S(2)}, u32[]{:S(2)}) collective-permute-start(bf16[2,128,512]{2,1,0:T(8,128)(2,1)S(1)} %get-tuple-element.63.refs_1_.refs_2_), channel_id=1, source_target_pairs={{0,1},{1,0},{2,3},{3,2},{4,5},{5,4},{6,7},{7,6},{8,9},{9,8},{10,11... | collective-permute-start | bytes 786440 | tf_op jit(solution)/shard_map/ppermute | solution.py:295
  55.7 3.3 %collective-permute-start.11 = (bf16[128,512]{1,0:T(8,128)(2,1)S(1)}, bf16[128,512]{1,0:T(8,128)(2,1)S(1)}, u32[]{:S(2)}, u32[]{:S(2)}) collective-permute-start(bf16[128,512]{1,0:T(8,128)(2,1)S(1)} %get-tuple-element.86), channel_id=1, source_target_pairs={{0,1},{1,0},{2,3},{3,2},{4,5},{5,4},{6,7},{7,6},{8,9},{9,8},{10,11... | collective-permute-start | bytes 393224 | tf_op jit(solution)/shard_map/ppermute | solution.py:295
  57.6 1.4 %collective-permute-start.12 = (bf16[128,512]{1,0:T(8,128)(2,1)S(1)}, bf16[128,512]{1,0:T(8,128)(2,1)S(1)}, u32[]{:S(2)}, u32[]{:S(2)}) collective-permute-start(bf16[128,512]{1,0:T(8,128)(2,1)S(1)} %get-tuple-element.87), channel_id=1, source_target_pairs={{0,1},{1,0},{2,3},{3,2},{4,5},{5,4},{6,7},{7,6},{8,9},{9,8},{10,11... | collective-permute-start | bytes 393224 | tf_op jit(solution)/shard_map/ppermute | solution.py:295
  61.8 1.6 %collective-permute-start.17 = (f32[2,64,512]{2,1,0:T(8,128)S(1)}, f32[2,64,512]{2,1,0:T(8,128)S(1)}, u32[]{:S(2)}, u32[]{:S(2)}) collective-permute-start(f32[2,64,512]{2,1,0:T(8,128)S(1)} %get-tuple-element.78), channel_id=1, source_target_pairs={{0,1},{1,0},{2,3},{3,2},{4,5},{5,4},{6,7},{7,6},{8,9},{9,8},{10,11... | collective-permute-start | bytes 786440 | tf_op jit(solution)/shard_map/ppermute | solution.py:295
  62.1 5.9 %collective-permute-start.15 = (f32[2,64,512]{2,1,0:T(8,128)S(1)}, f32[2,64,512]{2,1,0:T(8,128)S(1)}, u32[]{:S(2)}, u32[]{:S(2)}) collective-permute-start(f32[2,64,512]{2,1,0:T(8,128)S(1)} %get-tuple-element.75), channel_id=1, source_target_pairs={{0,1},{1,0},{2,3},{3,2},{4,5},{5,4},{6,7},{7,6},{8,9},{9,8},{10,11... | collective-permute-start | bytes 786440 | tf_op jit(solution)/shard_map/ppermute | solution.py:295
  62.4 5.6 %collective-permute-start.16 = (f32[2,64,512]{2,1,0:T(8,128)S(1)}, f32[2,64,512]{2,1,0:T(8,128)S(1)}, u32[]{:S(2)}, u32[]{:S(2)}) collective-permute-start(f32[2,64,512]{2,1,0:T(8,128)S(1)} %get-tuple-element.76), channel_id=1, source_target_pairs={{2,4},{4,2},{6,8},{8,6},{10,12},{12,10},{14,16},{16,14},{18,20},{2... | collective-permute-start | bytes 786440 | tf_op jit(solution)/shard_map/ppermute | solution.py:283
  63.5 10.4 %collective-permute-start.18 = (f32[2,64,512]{2,1,0:T(8,128)S(1)}, f32[2,64,512]{2,1,0:T(8,128)S(1)}, u32[]{:S(2)}, u32[]{:S(2)}) collective-permute-start(f32[2,64,512]{2,1,0:T(8,128)S(1)} %add.40), channel_id=1, source_target_pairs={{0,2},{2,0},{4,6},{6,4},{8,10},{10,8},{12,14},{14,12},{16,18},{18,... | collective-permute-start | bytes 786440 | tf_op jit(solution)/shard_map/ppermute | solution.py:283
  74.4 1.8 %collective-permute-start.19 = (f32[32,128]{1,0:T(8,128)S(1)}, f32[32,128]{1,0:T(8,128)S(1)}, u32[]{:S(2)}, u32[]{:S(2)}) collective-permute-start(f32[32,128]{1,0:T(8,128)S(1)} %get-tuple-element.80), channel_id=1, source_target_pairs={{0,1},{1,0},{2,3},{3,2},{4,5},{5,4},{6,7},{7,6},{8,9},{9,8},{10,11... | collective-permute-start | bytes 49160 | tf_op jit(solution)/shard_map/ppermute | solution.py:295
  102.1 13.4 %all-to-all-start.1 = ((f32[8,32,128]{2,1,0:T(8,128)}), f32[8,32,128]{2,1,0:T(8,128)S(1)}, u32[]{:S(2)}, u32[]{:S(2)}) async-start(f32[8,32,128]{2,1,0:T(8,128)} %broadcast_in_dim.5), calls=%async_computation.1 | async-start | bytes 262144 | tf_op jit(solution)/shard_map/all_to_all | solution.py:351
  107.4 11.3 %collective-permute-start.21 = (f32[64,512]{1,0:T(8,128)S(1)}, f32[64,512]{1,0:T(8,128)S(1)}, u32[]{:S(2)}, u32[]{:S(2)}) collective-permute-start(f32[64,512]{1,0:T(8,128)S(1)} %get-tuple-element.81), channel_id=1, source_target_pairs={{0,1},{1,0},{2,3},{3,2},{4,5},{5,4},{6,7},{7,6},{8,9},{9,8},{10,11... | collective-permute-start | bytes 393224 | tf_op jit(solution)/shard_map/ppermute | solution.py:295
  115.4 4.1 %collective-permute-start.20 = (f32[32,128]{1,0:T(8,128)S(1)}, f32[32,128]{1,0:T(8,128)S(1)}, u32[]{:S(2)}, u32[]{:S(2)}) collective-permute-start(f32[32,128]{1,0:T(8,128)S(1)} %reduce_sum.19.mine_ref), channel_id=1, source_target_pairs={{0,1},{1,0},{2,3},{3,2},{4,5},{5,4},{6,7},{7,6},{8,9},{9,8},{10,11... | collective-permute-start | bytes 49160 | tf_op jit(solution)/shard_map/ppermute | solution.py:295

commit v5 on v4

--- a/solution.py
+++ b/solution.py
@@ -164,7 +164,7 @@
             )
 
 
-def late_kernel(make, flags_ref, far_ref, *refs):
+def late_kernel(make, flags_ref, list_ref, *refs):
     if make:
         odd0, own0, own1, even0, even1, *ins = refs[:9]
         tile_ref, done_ref, *parts = refs[9:]
@@ -174,16 +174,28 @@
     done_ref[...] = jnp.zeros_like(done_ref)
     for ref, value in zip(parts, ins):
         ref[...] = value[...]
+    base, even = flags_ref[11], flags_ref[12] > 0
+
+    def far_is_live(left, right):
+        first = base - 2 + jnp.where(even, left, right)
+        second = base + 2 + jnp.where(even, right, left)
+        hits = [
+            (list_ref[0, at] == first) & (list_ref[1, at] == second)
+            for at in range(list_ref.shape[1])
+        ]
+        return functools.reduce(jnp.logical_or, hits)
+
     for kind in range(2):
         rights = ((own0, own1), (even0, even1))[kind]
         part_refs = (parts[:2], parts[2:])[kind]
-        flag_ref, flag_at = ((flags_ref, 7), (far_ref, 0))[kind]
 
         @pl.loop(0, 4)
         def _(index):
             left, right = index // 2, index % 2
 
-            @pl.when(flag_ref[flag_at + index] > 0)
+            live = far_is_live(left, right) if kind else flags_ref[7 + index] > 0
+
+            @pl.when(live)
             def _():
                 one_pair(
                     make, tile_ref, kind * 4 + index, odd0.at[left],
@@ -225,7 +237,7 @@
 def eliminate(packed):
     lanes = lax.broadcasted_iota(jnp.int32, (8, 64), 1)
     subs = lax.broadcasted_iota(jnp.int32, (8, 64), 0)
-    sub1 = lax.broadcasted_iota(jnp.int32, (8, 1), 0)
+    deep = lax.broadcasted_iota(jnp.int32, (8, 128), 0)
     states = []
     for matrix in packed:
         whole = jnp.concatenate([matrix[:, :64], matrix[:, 64:]], axis=0)
@@ -235,28 +247,48 @@
             )
             for b in range(8)
         ])
-    for k in range(64):
-        at, sub = k // 8, k % 8
-        for state in states:
-            row = state[at][sub : sub + 1, :]
-            scaled = row / state[at][sub : sub + 1, k : k + 1]
-            for b in range(at, 8):
-                column = state[b][:, k : k + 1]
-                if b == at:
-                    column = jnp.where(sub1 > sub, column, 0.0)
-                state[b] = state[b] - column * scaled
+    scales = [[] for _ in states]
+    for at in range(8):
+        spreads = [
+            {
+                b: [jnp.broadcast_to(state[b][:, k : k + 1], (8, 128)) for k in range(8 * at, 8 * at + 8)]
+                for b in range(at, 8)
+            }
+            for state in states
+        ]
+        pivots = [jnp.zeros((8, 128), jnp.float32) for _ in states]
+        for sub in range(8):
+            for n, (state, spread_of) in enumerate(zip(states, spreads)):
+                pivot = spread_of[at][sub][sub : sub + 1, :]
+                inverse = 1.0 / pivot
+                pivots[n] = jnp.where(deep == sub, pivot, pivots[n])
+                row = state[at][sub : sub + 1, :] * inverse
+                ahead = {j: spread_of[at][j][sub : sub + 1, :] * inverse for j in range(sub + 1, 8)}
+                for b in range(at, 8):
+                    column = spread_of[b][sub]
+                    if b == at:
+                        column = jnp.where(deep > sub, column, 0.0)
+                    for j, value in ahead.items():
+                        spread_of[b][j] = spread_of[b][j] - column * value
+                    state[b] = state[b] - column * row
+        for n, pivot in enumerate(pivots):
+            scales[n].append(lax.rsqrt(pivot))
     uppers, inverses = [], []
-    for state in states:
-        rows = []
-        for b in range(8):
-            diagonal = jnp.sum(
-                jnp.where(lanes == subs + 8 * b, state[b][:, :64], 0.0), axis=1, keepdims=True
-            )
-            rows.append(state[b] * lax.rsqrt(diagonal))
-        whole = jnp.concatenate(rows, axis=0)
+    for state, scale in zip(states, scales):
+        whole = jnp.concatenate([rows * by for rows, by in zip(state, scale)], axis=0)
         uppers.append(whole[:, :64])
         inverses.append(whole[:, 64:])
     return uppers, inverses
+
+
+def copies_kernel(*refs):
+    *value_refs, copies_ref = refs
+    total = None
+    for ref in value_refs:
+        value = ref[...] if len(ref.shape) == 2 else jnp.sum(ref[...], axis=0)
+        total = value if total is None else total + value
+    for at in range(copies_ref.shape[0]):
+        copies_ref[at] = total
 
 
 def finish_kernel(core_ref, mine_ref, other_ref, value_ref, got_ref, basis_ref, factor_ref):
@@ -299,40 +331,27 @@
     return jnp.stack([swap(value[block]) for block in range(2)])
 
 
-def live_flags(pairs, base, even_codes, odd_codes):
-    none = (100, 100)
+SLOTS = [(0, 0), (0, 1), (1, 0), (1, 1)]
+
+
+def own_flags_and_list(pair_list, base):
+    own = jnp.concatenate([pair_list.T, swap(pair_list.T)], axis=1)
+    before = lax.ppermute(own, "rows", [(r, r + 1) for r in range(lax.axis_size("rows") - 1)])
+    within, idle = [(0, 0), (0, 1), (1, 1)], [(100, 100)] * 4
 
     def table(entries):
-        return jnp.array([64 * i + j for i, j in (none if e is None else e for e in entries)], jnp.int32)
-
-    even_row = lax.axis_index("rows") % 2 == 0
-    wanted = jnp.where(even_row, table(even_codes), table(odd_codes))
-    codes = (pairs[:, 0] - base) * 64 + (pairs[:, 1] - base)
-    hit = (codes[None, :] == wanted[:, None]) & (pairs[None, :, 0] >= 0)
-    return jnp.any(hit, axis=1).astype(jnp.int32)
-
-
-SLOTS = [(0, 0), (0, 1), (1, 0), (1, 1)]
-
-
-def own_flags_and_list(pair_list, base):
-    own = jnp.concatenate([pair_list, swap(pair_list)], axis=0)
-    before = lax.ppermute(own, "rows", [(r, r + 1) for r in range(lax.axis_size("rows") - 1)])
-    within, idle = [(0, 0), (0, 1), (1, 1)], [None] * 4
-    flags = live_flags(
-        own, base,
-        within + [(left, 2 + right) for left, right in SLOTS] + idle,
-        within + idle + [(right, 2 + left) for left, right in SLOTS],
-    )
-    return flags, before
-
-
-def flags_of_far(before, base):
-    return live_flags(
-        before, base,
-        [(left - 2, 2 + right) for left, right in SLOTS],
-        [(right - 2, 2 + left) for left, right in SLOTS],
-    )
+        return jnp.array([64 * i + j for i, j in entries], jnp.int32)
+
+    even = lax.axis_index("rows") % 2 == 0
+    wanted = jnp.where(
+        even,
+        table(within + [(left, 2 + right) for left, right in SLOTS] + idle),
+        table(within + idle + [(right, 2 + left) for left, right in SLOTS]),
+    )
+    codes = (own[0] - base) * 64 + (own[1] - base)
+    hit = (codes[None, :] == wanted[:, None]) & (own[0][None, :] >= 0)
+    flags = jnp.any(hit, axis=1).astype(jnp.int32)
+    return jnp.concatenate([flags, base[None], even.astype(jnp.int32)[None]]), before
 
 
 def spread(done, own0, own1, out_odd, even0, even1):
@@ -341,15 +360,17 @@
     return done, own0, swap(own1), from_odd, from_even
 
 
-def sum_over_chips(value):
-    count = lax.axis_size("rows")
+def sum_over_chips(*values):
     planes = [[(x * PLANES + z) * RING + y for x in range(ACROSS) for y in range(RING)] for z in range(PLANES)]
     lines = [[(x * PLANES + z) * RING + y for z in range(PLANES)] for x in range(ACROSS) for y in range(RING)]
     for groups in (planes, lines):
-        size = len(groups[0])
-        copies = jnp.broadcast_to(value[None], (size,) + value.shape)
-        value = lax.all_to_all(copies, "rows", 0, 0, axis_index_groups=groups, tiled=True).sum(0)
-    return value
+        copies = call(copies_kernel, shape((len(groups[0]), 32, 128)), 10**5, 10**5)(
+            in_specs=[VMEM] * len(values)
+        )(*values)
+        values = [
+            lax.all_to_all(copies, "rows", 0, 0, axis_index_groups=groups, tiled=True)
+        ]
+    return values[0].sum(0)
 
 
 def local(embeddings, test_matrix, pair_list):
@@ -396,11 +417,10 @@
         functools.partial(early_kernel, True), (tiles(4),) + 3 * (sum_shape,), 10**4, 10**4
     )(in_specs=[SMEM] + [VMEM] * 4)(flags, own0, even0, even1, done)
     done, odd0, before = lax.optimization_barrier((done, odd0, before))
-    far_flags = flags_of_far(before, base)
     tiles_late, out_odd, own_part0, own_part1, even_part0, even_part1 = call(
         functools.partial(late_kernel, True), (tiles(8),) + 5 * (sum_shape,), 10**9, 10**6
     )(in_specs=[SMEM] * 2 + [VMEM] * 9)(
-        flags, far_flags, odd0, own0, own1, even0, even1, own_part0, own_part1, even_part0, even_part1
+        flags, before, odd0, own0, own1, even0, even1, own_part0, own_part1, even_part0, even_part1
     )
     sketch, pair0 = call(total_kernel, (sum_shape, shape((2, 128, HALF), bf16)), 10**6, 2 * 10**6)(
         in_specs=[VMEM] * 5
@@ -424,7 +444,7 @@
     out_odd, own_part0, own_part1, even_part0, even_part1 = call(
         functools.partial(late_kernel, False), 5 * (sum_shape,), 10**9, 10**6
     )(in_specs=[SMEM] * 2 + [VMEM] * 10)(
-        flags, far_flags, tiles_late, odd0, pair0, pair1, even0, even1,
+        flags, before, tiles_late, odd0, pair0, pair1, even0, even1,
         own_part0, own_part1, even_part0, even_part1,
     )
     image = call(total_kernel, sum_shape, 10**6, 2 * 10**6)(in_specs=[VMEM] * 5)(
@@ -436,7 +456,7 @@
         10**8, 10**6,
     )(in_specs=[SMEM, VMEM, VMEM])(core_ref, first_gram, image)
     got = swap(half)
-    mine = sum_over_chips(keep + swap(give))
+    mine = sum_over_chips(keep, swap(give))
     other = swap(mine)
     basis, factor = call(finish_kernel, (shape((64, BLK)), shape((64, 64))), 10**8, 10**6)(
         in_specs=[SMEM] + [VMEM] * 4

time: 129 us -> 128 us (level)
  Pallas kernels: 20.8 us -> 18.2 us
  starting transfers between devices: 41.4 us -> 43.4 us
    ppermute x8, starting transfers between devices: 17.1 us -> 21.7 us  [exchange(): return lax.ppermute(value, 'rows', links)]
    pallas_call x1, Pallas kernels: 6.68 us -> 3 us  [local(): call(finish_kernel, (shape((64, BLK)), shape((64, 64))), 10 ** 8, 10 ** 6)]
    all_to_all x1, starting transfers between devices: 5.33 us -> 3.37 us  [sum_over_chips(): lax.all_to_all(copies, 'rows', 0, 0, axis_index_groups=groups, tiled=True)]
    pallas_call x1, Pallas kernels: 1.77 us -> 3.17 us  [local(): call(functools.partial(local_kernel, True), (tiles(3),) + 3 * (sum_shape,...]
    pallas_call x1, Pallas kernels: 3.27 us -> 1.97 us  [local(): call(functools.partial(early_kernel, True), (tiles(4),) + 3 * (sum_shape,...]
where the time goes in v5:
time: 128 us; the launch traced here: 126 us
  starting transfers between devices  43.4 us (34%)
  waiting for transfers between devices  37.1 us (29%)
  blocking collectives  26.3 us (21%)
  Pallas kernels  18.2 us (14%)
    ppermute x8, waiting for transfers between devices, exchange(): return lax.ppermute(value, 'rows', links)  27.9 us
    all_to_all x1, blocking collectives, sum_over_chips(): lax.all_to_all(copies, 'rows', 0, 0, axis_index_groups=groups, tiled=True)  26.3 us
    ppermute x8, starting transfers between devices, exchange(): return lax.ppermute(value, 'rows', links)  21.7 us
    ppermute x13, starting transfers between devices, swap(): return lax.ppermute(value, 'cols', [(0, 1), (1, 0)])  15 us
    all_to_all x1, waiting for transfers between devices, sum_over_chips(): lax.all_to_all(copies, 'rows', 0, 0, axis_index_groups=groups, tiled=True)  5.95 us
    all_to_all x1, starting transfers between devices, sum_over_chips(): lax.all_to_all(copies, 'rows', 0, 0, axis_index_groups=groups, tiled=True)  3.37 us
    ppermute x1, starting transfers between devices, own_flags_and_list(): lax.ppermute(own, 'rows', [(r, r + 1) for r in range(lax.axis_size('rows'...  3.35 us
    ppermute x13, waiting for transfers between devices, swap(): return lax.ppermute(value, 'cols', [(0, 1), (1, 0)])  3.24 us
  transfers between devices with their start and end apart: 23, of which 10 were waited for; matrix products, arithmetic and copies ran while one was open for 0% of the time, Pallas kernels for 8%

profile of v5, /device:TPU:1, one launch (start us, length us, event | category | flops | bytes accessed | tf_op | source)
XLA Modules:
  0.0 126.4 jit_solution(4590946743827730608)
XLA Ops:
  0.6 0.0 copy-start.1
  0.6 0.0 copy-start.2
  0.7 1.4 %shard_map.69.refs_0_.refs_1_ = bf16[2,1792,128]{2,1,0:T(8,128)(2,1)S(1)} custom-call(s32[1]{0:T(128)} %bitcast.core_ref, bf16[2048,384]{1,0:T(8,128)(2,1)} %rows_ref.3, bf16[64,2048]{1,0:T(8,128)(2,1)} %bitcast.22), custom_call_target="tpu_custom_call" | custom-call | flops 10000 | bytes 10000 | tf_op jit(solution)/shard_map/pallas_call | solution.py:389
  2.1 1.6 %collective-permute-start.4 = (bf16[2,1792,128]{2,1,0:T(8,128)(2,1)S(1)}, bf16[2,1792,128]{2,1,0:T(8,128)(2,1)}, u32[]{:S(2)}, u32[]{:S(2)}) collective-permute-start(bf16[2,1792,128]{2,1,0:T(8,128)(2,1)S(1)} %shard_map.69.refs_0_.refs_1_), channel_id=1, source_target_pairs={{2,4},{4,2},{6,8},{8,6},{10,12},{12,10},{14,16},{16,14},{18,20},{2... | collective-permute-start | bytes 2752520 | tf_op jit(solution)/shard_map/ppermute | solution.py:315
  3.7 3.8 %collective-permute-start.1 = (bf16[2,1792,128]{2,1,0:T(8,128)(2,1)S(1)}, bf16[2,1792,128]{2,1,0:T(8,128)(2,1)S(1)}, u32[]{:S(2)}, u32[]{:S(2)}) collective-permute-start(bf16[2,1792,128]{2,1,0:T(8,128)(2,1)S(1)} %shard_map.69.refs_0_.refs_1_), channel_id=1, source_target_pairs={{0,2},{2,0},{4,6},{6,4},{8,10},{10,8},{12,14},{14,12},{16,18},{18,... | collective-permute-start | bytes 2752520 | tf_op jit(solution)/shard_map/ppermute | solution.py:315
  7.5 1.4 %shard_map.68.refs_1_.refs_2_ = bf16[2,1792,128]{2,1,0:T(8,128)(2,1)S(1)} custom-call(s32[1]{0:T(128)} %bitcast.core_ref, bf16[2048,384]{1,0:T(8,128)(2,1)} %rows_ref.3, bf16[64,2048]{1,0:T(8,128)(2,1)} %bitcast.23), custom_call_target="tpu_custom_call" | custom-call | flops 10000 | bytes 10000 | tf_op jit(solution)/shard_map/pallas_call | solution.py:389
  8.9 1.3 %collective-permute-start = (s32[2,4]{1,0:T(2,128)S(1)}, s32[2,4]{1,0:T(2,128)S(1)}, u32[]{:S(2)}, u32[]{:S(2)}) collective-permute-start(s32[2,4]{1,0:T(2,128)S(1)} %bitcast.28), channel_id=1, source_target_pairs={{0,1},{1,0},{2,3},{3,2},{4,5},{5,4},{6,7},{7,6},{8,9},{9,8},{10,11... | collective-permute-start | bytes 104 | tf_op jit(solution)/shard_map/ppermute | solution.py:327
  10.2 0.8 collective-permute-done
  11.0 0.1 pad_add_fusion
  11.1 0.1 and_reduce_fusion
  11.2 0.1 pad_add_fusion.1.flags_ref
  11.3 3.2 %shard_map.70 = (bf16[3,2,512,512]{3,2,1,0:T(8,128)(2,1)S(1)}, f32[2,64,512]{2,1,0:T(8,128)S(1)}, f32[2,64,512]{2,1,0:T(8,128)S(1)}, f32[2,64,512]{2,1,0:T(8,128)S(1)}) custom-call(s32[13]{0:T(128)S(1)} %pad_add_fusion.1.flags_ref, bf16[2,1792,128]{2,1,0:T(8,128)(2,1)S(1)} %shard_map.69.refs_0_.refs_1_, bf16[2,1792,128]{2,1,0:T(8,128)(2,1)S(1)} %shard_map.68.refs_1_.refs_2_), custom_call_target="tpu_custom_call" | custom-call | flops 10000 | bytes 10000 | tf_op jit(solution)/shard_map/pallas_call | solution.py:411
  14.5 12.5 %collective-permute-done.1.refs_1_.refs_3_ = bf16[2,1792,128]{2,1,0:T(8,128)(2,1)S(1)} collective-permute-done((bf16[2,1792,128]{2,1,0:T(8,128)(2,1)S(1)}, bf16[2,1792,128]{2,1,0:T(8,128)(2,1)S(1)}, u32[]{:S(2)}, u32[]{:S(2)}) %collective-permute-start.1) | collective-permute-done | bytes 917536 | tf_op jit(solution)/shard_map/ppermute | solution.py:315
  27.0 0.1 slice_bitcast_fusion.1
  27.1 1.9 %collective-permute-start.2 = (bf16[1792,128]{1,0:T(8,128)(2,1)S(1)}, bf16[1792,128]{1,0:T(8,128)(2,1)S(1)}, u32[]{:S(2)}, u32[]{:S(2)}) collective-permute-start(bf16[1792,128]{1,0:T(8,128)(2,1)S(1)} %get-tuple-element.84), channel_id=1, source_target_pairs={{0,1},{1,0},{2,3},{3,2},{4,5},{5,4},{6,7},{7,6},{8,9},{9,8},{10,11... | collective-permute-start | bytes 1376264 | tf_op jit(solution)/shard_map/ppermute | solution.py:327
  28.9 0.1 collective-permute-start.3
  29.0 3.4 %collective-permute-start.5 = (s32[2,8]{1,0:T(2,128)S(1)}, s32[2,8]{1,0:T(2,128)S(1)}, u32[]{:S(2)}, u32[]{:S(2)}) collective-permute-start(s32[2,8]{1,0:T(2,128)S(1)} %pad_add_fusion), channel_id=1, source_target_pairs={{0,2},{2,4},{4,6},{6,8},{8,10},{10,12},{12,14},{14,16},{16,18},{18... | collective-permute-start | bytes 200 | tf_op jit(solution)/shard_map/ppermute | solution.py:339
  32.4 0.0 collective-permute-done.2
  32.4 0.0 collective-permute-done.3
  32.4 0.1 pad_maximum_fusion.refs_2_.refs_4_
  32.5 2.0 %shard_map.71 = (bf16[4,2,512,512]{3,2,1,0:T(8,128)(2,1)S(1)}, f32[2,64,512]{2,1,0:T(8,128)S(1)}, f32[2,64,512]{2,1,0:T(8,128)S(1)}, f32[2,64,512]{2,1,0:T(8,128)S(1)}) custom-call(s32[13]{0:T(128)S(1)} %pad_add_fusion.1.flags_ref, bf16[2,1792,128]{2,1,0:T(8,128)(2,1)S(1)} %shard_map.69.refs_0_.refs_1_, ...), custom_call_target="tpu_custom_call" | custom-call | flops 10000 | bytes 10000 | tf_op jit(solution)/shard_map/pallas_call | solution.py:416
  34.5 0.0 collective-permute-done.5.list_ref
  34.5 0.0 collective-permute-done.4.refs_0_
  34.5 1.5 %shard_map.72 = (bf16[8,2,512,512]{3,2,1,0:T(8,128)(2,1)S(1)}, f32[2,64,512]{2,1,0:T(8,128)S(1)}, f32[2,64,512]{2,1,0:T(8,128)S(1)}, f32[2,64,512]{2,1,0:T(8,128...) custom-call(s32[13]{0:T(128)S(1)} %pad_add_fusion.1.flags_ref, s32[2,8]{1,0:T(2,128)S(1)} %collective-permute-done.5.list_ref, ...), custom_call_target="tpu_custom_call" | custom-call | flops 1000000000 | bytes 1000000 | tf_op jit(solution)/shard_map/pallas_call | solution.py:420
  36.0 0.8 collective-permute-start.8
  36.8 0.1 collective-permute-start.6
  36.9 0.7 collective-permute-start.7
  37.6 0.4 collective-permute-done.8
  38.0 4.7 %collective-permute-start.9 = (f32[2,64,512]{2,1,0:T(8,128)S(1)}, f32[2,64,512]{2,1,0:T(8,128)S(1)}, u32[]{:S(2)}, u32[]{:S(2)}) collective-permute-start(f32[2,64,512]{2,1,0:T(8,128)S(1)} %add.16), channel_id=1, source_target_pairs={{0,2},{2,0},{4,6},{6,4},{8,10},{10,8},{12,14},{14,12},{16,18},{18,... | collective-permute-start | bytes 786440 | tf_op jit(solution)/shard_map/ppermute | solution.py:315
  42.7 6.3 %collective-permute-done.9.from_even = f32[2,64,512]{2,1,0:T(8,128)S(1)} collective-permute-done((f32[2,64,512]{2,1,0:T(8,128)S(1)}, f32[2,64,512]{2,1,0:T(8,128)S(1)}, u32[]{:S(2)}, u32[]{:S(2)}) %collective-permute-start.9) | collective-permute-done | bytes 262176 | tf_op jit(solution)/shard_map/ppermute | solution.py:315
  49.0 0.1 shard_map.73
  49.1 1.2 collective-permute-start.10
  50.4 0.7 collective-permute-start.14
  51.0 1.6 %collective-permute-start.13 = (bf16[2,128,512]{2,1,0:T(8,128)(2,1)S(1)}, bf16[2,128,512]{2,1,0:T(8,128)(2,1)S(1)}, u32[]{:S(2)}, u32[]{:S(2)}) collective-permute-start(bf16[2,128,512]{2,1,0:T(8,128)(2,1)S(1)} %get-tuple-element.63.refs_1_.refs_2_), channel_id=1, source_target_pairs={{0,1},{1,0},{2,3},{3,2},{4,5},{5,4},{6,7},{7,6},{8,9},{9,8},{10,11... | collective-permute-start | bytes 786440 | tf_op jit(solution)/shard_map/ppermute | solution.py:327
  52.6 3.5 %collective-permute-done.10.refs_2_.refs_4_ = bf16[2,128,512]{2,1,0:T(8,128)(2,1)S(1)} collective-permute-done((bf16[2,128,512]{2,1,0:T(8,128)(2,1)S(1)}, bf16[2,128,512]{2,1,0:T(8,128)(2,1)S(1)}, u32[]{:S(2)}, u32[]{:S(2)}) %collective-permute-start.10) | collective-permute-done | bytes 262176 | tf_op jit(solution)/shard_map/ppermute | solution.py:315
  56.1 1.9 %collective-permute-start.11 = (bf16[128,512]{1,0:T(8,128)(2,1)S(1)}, bf16[128,512]{1,0:T(8,128)(2,1)S(1)}, u32[]{:S(2)}, u32[]{:S(2)}) collective-permute-start(bf16[128,512]{1,0:T(8,128)(2,1)S(1)} %get-tuple-element.86), channel_id=1, source_target_pairs={{0,1},{1,0},{2,3},{3,2},{4,5},{5,4},{6,7},{7,6},{8,9},{9,8},{10,11... | collective-permute-start | bytes 393224 | tf_op jit(solution)/shard_map/ppermute | solution.py:327
  58.0 0.3 collective-permute-start.12
  58.3 1.9 %shard_map.75 = (f32[2,64,512]{2,1,0:T(8,128)S(1)}, f32[2,64,512]{2,1,0:T(8,128)S(1)}, f32[2,64,512]{2,1,0:T(8,128)S(1)}) custom-call(s32[13]{0:T(128)S(1)} %pad_add_fusion.1.flags_ref, bf16[3,2,512,512]{3,2,1,0:T(8,128)(2,1)S(1)} %get-tuple-element.64.refs_0_, bf16[2,128,512]{2,1,0:T(8,128)(2,1)S(1)} %get-tuple-element.63.refs_1_.refs_2_, ...), custom_call_target="tpu_custom_call" | custom-call | flops 10000 | bytes 10000 | tf_op jit(solution)/shard_map/pallas_call | solution.py:436
  60.2 0.0 collective-permute-done.11
  60.2 0.0 collective-permute-done.12
  60.3 1.3 %shard_map.76 = (f32[2,64,512]{2,1,0:T(8,128)S(1)}, f32[2,64,512]{2,1,0:T(8,128)S(1)}, f32[2,64,512]{2,1,0:T(8,128)S(1)}) custom-call(s32[13]{0:T(128)S(1)} %pad_add_fusion.1.flags_ref, bf16[4,2,512,512]{3,2,1,0:T(8,128)(2,1)S(1)} %get-tuple-element.62.refs_0_, bf16[2,128,512]{2,1,0:T(8,128)(2,1)S(1)} %get-tuple-element.63.refs_1_.refs_2_, ...), custom_call_target="tpu_custom_call" | custom-call | flops 10000 | bytes 10000 | tf_op jit(solution)/shard_map/pallas_call | solution.py:440
  61.6 0.0 collective-permute-done.14.refs_1_
  61.6 0.9 shard_map.77
  62.4 0.3 collective-permute-start.17
  62.8 0.3 collective-permute-start.15
  63.0 0.7 collective-permute-start.16
  63.7 0.4 collective-permute-done.17
  64.1 8.3 %collective-permute-start.18 = (f32[2,64,512]{2,1,0:T(8,128)S(1)}, f32[2,64,512]{2,1,0:T(8,128)S(1)}, u32[]{:S(2)}, u32[]{:S(2)}) collective-permute-start(f32[2,64,512]{2,1,0:T(8,128)S(1)} %add.17), channel_id=1, source_target_pairs={{0,2},{2,0},{4,6},{6,4},{8,10},{10,8},{12,14},{14,12},{16,18},{18,... | collective-permute-start | bytes 786440 | tf_op jit(solution)/shard_map/ppermute | solution.py:315
  72.4 0.4 shard_map.74.first_ref
  72.9 0.0 collective-permute-done.16.from_odd
  72.9 5.6 %collective-permute-done.18.from_even = f32[2,64,512]{2,1,0:T(8,128)S(1)} collective-permute-done((f32[2,64,512]{2,1,0:T(8,128)S(1)}, f32[2,64,512]{2,1,0:T(8,128)S(1)}, u32[]{:S(2)}, u32[]{:S(2)}) %collective-permute-start.18) | collective-permute-done | bytes 262176 | tf_op jit(solution)/shard_map/ppermute | solution.py:315
  78.5 0.1 shard_map.78.value_ref
  78.6 0.4 shard_map.79
  79.0 1.3 %collective-permute-start.19 = (f32[32,128]{1,0:T(8,128)S(1)}, f32[32,128]{1,0:T(8,128)S(1)}, u32[]{:S(2)}, u32[]{:S(2)}) collective-permute-start(f32[32,128]{1,0:T(8,128)S(1)} %get-tuple-element.80), channel_id=1, source_target_pairs={{0,1},{1,0},{2,3},{3,2},{4,5},{5,4},{6,7},{7,6},{8,9},{9,8},{10,11... | collective-permute-start | bytes 49160 | tf_op jit(solution)/shard_map/ppermute | solution.py:327
  80.3 0.8 collective-permute-done.19.refs_1_
  81.2 26.3 %all_to_all.10.refs_0_ = f32[16,32,128]{2,1,0:T(8,128)S(1)} all-to-all(f32[16,32,128]{2,1,0:T(8,128)S(1)} %shard_map.80), channel_id=1, replica_groups={{0,2,4,6,64,66,68,70,128,130,132,134,192,194,196,198},{8,10,12,14,72,74..., dimensions={0} | all-to-all | bytes 524288 | tf_op jit(solution)/shard_map/all_to_all | solution.py:371
  107.4 0.7 shard_map.81
  108.1 3.4 %all-to-all-start.1 = ((f32[8,32,128]{2,1,0:T(8,128)}), f32[8,32,128]{2,1,0:T(8,128)S(1)}, u32[]{:S(2)}, u32[]{:S(2)}) async-start(f32[8,32,128]{2,1,0:T(8,128)} %shard_map.81), calls=%async_computation.1 | async-start | bytes 262144 | tf_op jit(solution)/shard_map/all_to_all | solution.py:371
  111.5 2.0 %collective-permute-start.21 = (f32[64,512]{1,0:T(8,128)S(1)}, f32[64,512]{1,0:T(8,128)S(1)}, u32[]{:S(2)}, u32[]{:S(2)}) collective-permute-start(f32[64,512]{1,0:T(8,128)S(1)} %get-tuple-element.81), channel_id=1, source_target_pairs={{0,1},{1,0},{2,3},{3,2},{4,5},{5,4},{6,7},{7,6},{8,9},{9,8},{10,11... | collective-permute-start | bytes 393224 | tf_op jit(solution)/shard_map/ppermute | solution.py:327
  113.5 5.9 %all-to-all-done.1 = f32[8,32,128]{2,1,0:T(8,128)S(1)} async-done(((f32[8,32,128]{2,1,0:T(8,128)}), f32[8,32,128]{2,1,0:T(8,128)S(1)}, u32[]{:S(2)}, u32[]{:S(2)}) %all-to-all-start.1) | async-done | bytes 131104 | tf_op jit(solution)/shard_map/all_to_all | solution.py:371
  119.4 3.2 %collective-permute-start.20 = (f32[32,128]{1,0:T(8,128)S(1)}, f32[32,128]{1,0:T(8,128)S(1)}, u32[]{:S(2)}, u32[]{:S(2)}) collective-permute-start(f32[32,128]{1,0:T(8,128)S(1)} %reduce_sum.9.mine_ref), channel_id=1, source_target_pairs={{0,1},{1,0},{2,3},{3,2},{4,5},{5,4},{6,7},{7,6},{8,9},{9,8},{10,11... | collective-permute-start | bytes 49160 | tf_op jit(solution)/shard_map/ppermute | solution.py:327
  122.6 0.0 collective-permute-done.21.got_ref
  122.6 0.8 collective-permute-done.20.other_ref
  123.4 3.0 %shard_map.82 = (f32[64,1024]{1,0:T(8,128)}, f32[64,64]{1,0:T(8,128)}) custom-call(s32[1]{0:T(128)} %bitcast.core_ref, f32[32,128]{1,0:T(8,128)S(1)} %reduce_sum.9.mine_ref, f32[32,128]{1,0:T(8,128)S(1)} %collective-permute-done.20.other_ref, f32[2,64,512]{2,1,0:T(8,128)S(1)} %shard_map.78.value_ref, f32[64,512]{1,0:T(8,128)S(1)} %collective-permute-done.21.got_ref), custom_call_target="tpu_custom_call" | custom-call | flops 100000000 | bytes 1000000 | tf_op jit(solution)/shard_map/pallas_call | solution.py:461
  (18 shorter events, 0.2 us)
Async XLA Ops:
  0.6 9.6 %copy-start.1 = (s32[11]{0:T(128)S(1)}, s32[11]{0:T(128)}, u32[]{:S(2)}) copy-start(s32[11]{0:T(128)} %constant.34.clone) | copy-start | bytes 136
  0.6 9.6 %copy-start.2 = (s32[11]{0:T(128)S(1)}, s32[11]{0:T(128)}, u32[]{:S(2)}) copy-start(s32[11]{0:T(128)} %constant.33.clone) | copy-start | bytes 136
  0.7 8.2 %copy-start = (s32[4,2]{0,1:T(2,128)S(1)}, s32[4,2]{0,1:T(2,128)}, u32[]{:S(2)}) copy-start(s32[4,2]{0,1:T(2,128)} %param.7) | copy-start | bytes 100
  2.1 32.4 %collective-permute-start.4 = (bf16[2,1792,128]{2,1,0:T(8,128)(2,1)S(1)}, bf16[2,1792,128]{2,1,0:T(8,128)(2,1)}, u32[]{:S(2)}, u32[]{:S(2)}) collective-permute-start(bf16[2,1792,128]{2,1,0:T(8,128)(2,1)S(1)} %shard_map.69.refs_0_.refs_1_), channel_id=1, source_target_pairs={{2,4},{4,2},{6,8},{8,6},{10,12},{12,10},{14,16},{16,14},{18,20},{2... | collective-permute-start | bytes 2752520 | tf_op jit(solution)/shard_map/ppermute | solution.py:315
  3.7 23.3 %collective-permute-start.1 = (bf16[2,1792,128]{2,1,0:T(8,128)(2,1)S(1)}, bf16[2,1792,128]{2,1,0:T(8,128)(2,1)S(1)}, u32[]{:S(2)}, u32[]{:S(2)}) collective-permute-start(bf16[2,1792,128]{2,1,0:T(8,128)(2,1)S(1)} %shard_map.69.refs_0_.refs_1_), channel_id=1, source_target_pairs={{0,2},{2,0},{4,6},{6,4},{8,10},{10,8},{12,14},{14,12},{16,18},{18,... | collective-permute-start | bytes 2752520 | tf_op jit(solution)/shard_map/ppermute | solution.py:315
  8.9 2.1 %collective-permute-start = (s32[2,4]{1,0:T(2,128)S(1)}, s32[2,4]{1,0:T(2,128)S(1)}, u32[]{:S(2)}, u32[]{:S(2)}) collective-permute-start(s32[2,4]{1,0:T(2,128)S(1)} %bitcast.28), channel_id=1, source_target_pairs={{0,1},{1,0},{2,3},{3,2},{4,5},{5,4},{6,7},{7,6},{8,9},{9,8},{10,11... | collective-permute-start | bytes 104 | tf_op jit(solution)/shard_map/ppermute | solution.py:327
  27.1 5.3 %collective-permute-start.2 = (bf16[1792,128]{1,0:T(8,128)(2,1)S(1)}, bf16[1792,128]{1,0:T(8,128)(2,1)S(1)}, u32[]{:S(2)}, u32[]{:S(2)}) collective-permute-start(bf16[1792,128]{1,0:T(8,128)(2,1)S(1)} %get-tuple-element.84), channel_id=1, source_target_pairs={{0,1},{1,0},{2,3},{3,2},{4,5},{5,4},{6,7},{7,6},{8,9},{9,8},{10,11... | collective-permute-start | bytes 1376264 | tf_op jit(solution)/shard_map/ppermute | solution.py:327
  28.9 3.5 %collective-permute-start.3 = (bf16[1792,128]{1,0:T(8,128)(2,1)S(1)}, bf16[1792,128]{1,0:T(8,128)(2,1)S(1)}, u32[]{:S(2)}, u32[]{:S(2)}) collective-permute-start(bf16[1792,128]{1,0:T(8,128)(2,1)S(1)} %get-tuple-element.85), channel_id=1, source_target_pairs={{0,1},{1,0},{2,3},{3,2},{4,5},{5,4},{6,7},{7,6},{8,9},{9,8},{10,11... | collective-permute-start | bytes 1376264 | tf_op jit(solution)/shard_map/ppermute | solution.py:327
  29.0 5.5 %collective-permute-start.5 = (s32[2,8]{1,0:T(2,128)S(1)}, s32[2,8]{1,0:T(2,128)S(1)}, u32[]{:S(2)}, u32[]{:S(2)}) collective-permute-start(s32[2,8]{1,0:T(2,128)S(1)} %pad_add_fusion), channel_id=1, source_target_pairs={{0,2},{2,4},{4,6},{6,8},{8,10},{10,12},{12,14},{14,16},{16,18},{18... | collective-permute-start | bytes 200 | tf_op jit(solution)/shard_map/ppermute | solution.py:339
  36.0 1.9 %collective-permute-start.8 = (f32[2,64,512]{2,1,0:T(8,128)S(1)}, f32[2,64,512]{2,1,0:T(8,128)S(1)}, u32[]{:S(2)}, u32[]{:S(2)}) collective-permute-start(f32[2,64,512]{2,1,0:T(8,128)S(1)} %get-tuple-element.60), channel_id=1, source_target_pairs={{0,1},{1,0},{2,3},{3,2},{4,5},{5,4},{6,7},{7,6},{8,9},{9,8},{10,11... | collective-permute-start | bytes 786440 | tf_op jit(solution)/shard_map/ppermute | solution.py:327
  36.8 5.9 %collective-permute-start.6 = (f32[2,64,512]{2,1,0:T(8,128)S(1)}, f32[2,64,512]{2,1,0:T(8,128)S(1)}, u32[]{:S(2)}, u32[]{:S(2)}) collective-permute-start(f32[2,64,512]{2,1,0:T(8,128)S(1)} %get-tuple-element.57), channel_id=1, source_target_pairs={{0,1},{1,0},{2,3},{3,2},{4,5},{5,4},{6,7},{7,6},{8,9},{9,8},{10,11... | collective-permute-start | bytes 786440 | tf_op jit(solution)/shard_map/ppermute | solution.py:327
  36.9 5.8 %collective-permute-start.7 = (f32[2,64,512]{2,1,0:T(8,128)S(1)}, f32[2,64,512]{2,1,0:T(8,128)S(1)}, u32[]{:S(2)}, u32[]{:S(2)}) collective-permute-start(f32[2,64,512]{2,1,0:T(8,128)S(1)} %get-tuple-element.58), channel_id=1, source_target_pairs={{2,4},{4,2},{6,8},{8,6},{10,12},{12,10},{14,16},{16,14},{18,20},{2... | collective-permute-start | bytes 786440 | tf_op jit(solution)/shard_map/ppermute | solution.py:315
  38.0 11.0 %collective-permute-start.9 = (f32[2,64,512]{2,1,0:T(8,128)S(1)}, f32[2,64,512]{2,1,0:T(8,128)S(1)}, u32[]{:S(2)}, u32[]{:S(2)}) collective-permute-start(f32[2,64,512]{2,1,0:T(8,128)S(1)} %add.16), channel_id=1, source_target_pairs={{0,2},{2,0},{4,6},{6,4},{8,10},{10,8},{12,14},{14,12},{16,18},{18,... | collective-permute-start | bytes 786440 | tf_op jit(solution)/shard_map/ppermute | solution.py:315
  49.1 7.0 %collective-permute-start.10 = (bf16[2,128,512]{2,1,0:T(8,128)(2,1)S(1)}, bf16[2,128,512]{2,1,0:T(8,128)(2,1)S(1)}, u32[]{:S(2)}, u32[]{:S(2)}) collective-permute-start(bf16[2,128,512]{2,1,0:T(8,128)(2,1)S(1)} %get-tuple-element.63.refs_1_.refs_2_), channel_id=1, source_target_pairs={{0,2},{2,0},{4,6},{6,4},{8,10},{10,8},{12,14},{14,12},{16,18},{18,... | collective-permute-start | bytes 786440 | tf_op jit(solution)/shard_map/ppermute | solution.py:315
  50.4 11.2 %collective-permute-start.14 = (bf16[2,128,512]{2,1,0:T(8,128)(2,1)S(1)}, bf16[2,128,512]{2,1,0:T(8,128)(2,1)S(1)}, u32[]{:S(2)}, u32[]{:S(2)}) collective-permute-start(bf16[2,128,512]{2,1,0:T(8,128)(2,1)S(1)} %get-tuple-element.63.refs_1_.refs_2_), channel_id=1, source_target_pairs={{2,4},{4,2},{6,8},{8,6},{10,12},{12,10},{14,16},{16,14},{18,20},{2... | collective-permute-start | bytes 786440 | tf_op jit(solution)/shard_map/ppermute | solution.py:315
  51.0 7.3 %collective-permute-start.13 = (bf16[2,128,512]{2,1,0:T(8,128)(2,1)S(1)}, bf16[2,128,512]{2,1,0:T(8,128)(2,1)S(1)}, u32[]{:S(2)}, u32[]{:S(2)}) collective-permute-start(bf16[2,128,512]{2,1,0:T(8,128)(2,1)S(1)} %get-tuple-element.63.refs_1_.refs_2_), channel_id=1, source_target_pairs={{0,1},{1,0},{2,3},{3,2},{4,5},{5,4},{6,7},{7,6},{8,9},{9,8},{10,11... | collective-permute-start | bytes 786440 | tf_op jit(solution)/shard_map/ppermute | solution.py:327
  56.1 4.1 %collective-permute-start.11 = (bf16[128,512]{1,0:T(8,128)(2,1)S(1)}, bf16[128,512]{1,0:T(8,128)(2,1)S(1)}, u32[]{:S(2)}, u32[]{:S(2)}) collective-permute-start(bf16[128,512]{1,0:T(8,128)(2,1)S(1)} %get-tuple-element.86), channel_id=1, source_target_pairs={{0,1},{1,0},{2,3},{3,2},{4,5},{5,4},{6,7},{7,6},{8,9},{9,8},{10,11... | collective-permute-start | bytes 393224 | tf_op jit(solution)/shard_map/ppermute | solution.py:327
  58.0 2.2 %collective-permute-start.12 = (bf16[128,512]{1,0:T(8,128)(2,1)S(1)}, bf16[128,512]{1,0:T(8,128)(2,1)S(1)}, u32[]{:S(2)}, u32[]{:S(2)}) collective-permute-start(bf16[128,512]{1,0:T(8,128)(2,1)S(1)} %get-tuple-element.87), channel_id=1, source_target_pairs={{0,1},{1,0},{2,3},{3,2},{4,5},{5,4},{6,7},{7,6},{8,9},{9,8},{10,11... | collective-permute-start | bytes 393224 | tf_op jit(solution)/shard_map/ppermute | solution.py:327
  62.4 1.6 %collective-permute-start.17 = (f32[2,64,512]{2,1,0:T(8,128)S(1)}, f32[2,64,512]{2,1,0:T(8,128)S(1)}, u32[]{:S(2)}, u32[]{:S(2)}) collective-permute-start(f32[2,64,512]{2,1,0:T(8,128)S(1)} %get-tuple-element.78), channel_id=1, source_target_pairs={{0,1},{1,0},{2,3},{3,2},{4,5},{5,4},{6,7},{7,6},{8,9},{9,8},{10,11... | collective-permute-start | bytes 786440 | tf_op jit(solution)/shard_map/ppermute | solution.py:327
  62.8 10.1 %collective-permute-start.15 = (f32[2,64,512]{2,1,0:T(8,128)S(1)}, f32[2,64,512]{2,1,0:T(8,128)S(1)}, u32[]{:S(2)}, u32[]{:S(2)}) collective-permute-start(f32[2,64,512]{2,1,0:T(8,128)S(1)} %get-tuple-element.75), channel_id=1, source_target_pairs={{0,1},{1,0},{2,3},{3,2},{4,5},{5,4},{6,7},{7,6},{8,9},{9,8},{10,11... | collective-permute-start | bytes 786440 | tf_op jit(solution)/shard_map/ppermute | solution.py:327
  63.0 9.8 %collective-permute-start.16 = (f32[2,64,512]{2,1,0:T(8,128)S(1)}, f32[2,64,512]{2,1,0:T(8,128)S(1)}, u32[]{:S(2)}, u32[]{:S(2)}) collective-permute-start(f32[2,64,512]{2,1,0:T(8,128)S(1)} %get-tuple-element.76), channel_id=1, source_target_pairs={{2,4},{4,2},{6,8},{8,6},{10,12},{12,10},{14,16},{16,14},{18,20},{2... | collective-permute-start | bytes 786440 | tf_op jit(solution)/shard_map/ppermute | solution.py:315
  64.1 14.4 %collective-permute-start.18 = (f32[2,64,512]{2,1,0:T(8,128)S(1)}, f32[2,64,512]{2,1,0:T(8,128)S(1)}, u32[]{:S(2)}, u32[]{:S(2)}) collective-permute-start(f32[2,64,512]{2,1,0:T(8,128)S(1)} %add.17), channel_id=1, source_target_pairs={{0,2},{2,0},{4,6},{6,4},{8,10},{10,8},{12,14},{14,12},{16,18},{18,... | collective-permute-start | bytes 786440 | tf_op jit(solution)/shard_map/ppermute | solution.py:315
  79.0 2.1 %collective-permute-start.19 = (f32[32,128]{1,0:T(8,128)S(1)}, f32[32,128]{1,0:T(8,128)S(1)}, u32[]{:S(2)}, u32[]{:S(2)}) collective-permute-start(f32[32,128]{1,0:T(8,128)S(1)} %get-tuple-element.80), channel_id=1, source_target_pairs={{0,1},{1,0},{2,3},{3,2},{4,5},{5,4},{6,7},{7,6},{8,9},{9,8},{10,11... | collective-permute-start | bytes 49160 | tf_op jit(solution)/shard_map/ppermute | solution.py:327
  108.1 11.3 %all-to-all-start.1 = ((f32[8,32,128]{2,1,0:T(8,128)}), f32[8,32,128]{2,1,0:T(8,128)S(1)}, u32[]{:S(2)}, u32[]{:S(2)}) async-start(f32[8,32,128]{2,1,0:T(8,128)} %shard_map.81), calls=%async_computation.1 | async-start | bytes 262144 | tf_op jit(solution)/shard_map/all_to_all | solution.py:371
  111.5 11.1 %collective-permute-start.21 = (f32[64,512]{1,0:T(8,128)S(1)}, f32[64,512]{1,0:T(8,128)S(1)}, u32[]{:S(2)}, u32[]{:S(2)}) collective-permute-start(f32[64,512]{1,0:T(8,128)S(1)} %get-tuple-element.81), channel_id=1, source_target_pairs={{0,1},{1,0},{2,3},{3,2},{4,5},{5,4},{6,7},{7,6},{8,9},{9,8},{10,11... | collective-permute-start | bytes 393224 | tf_op jit(solution)/shard_map/ppermute | solution.py:327
  119.4 4.0 %collective-permute-start.20 = (f32[32,128]{1,0:T(8,128)S(1)}, f32[32,128]{1,0:T(8,128)S(1)}, u32[]{:S(2)}, u32[]{:S(2)}) collective-permute-start(f32[32,128]{1,0:T(8,128)S(1)} %reduce_sum.9.mine_ref), channel_id=1, source_target_pairs={{0,1},{1,0},{2,3},{3,2},{4,5},{5,4},{6,7},{7,6},{8,9},{9,8},{10,11... | collective-permute-start | bytes 49160 | tf_op jit(solution)/shard_map/ppermute | solution.py:327

commit v6 on v5

--- a/solution.py
+++ b/solution.py
@@ -164,7 +164,7 @@
             )
 
 
-def late_kernel(make, flags_ref, list_ref, *refs):
+def late_kernel(make, flags_ref, far_ref, *refs):
     if make:
         odd0, own0, own1, even0, even1, *ins = refs[:9]
         tile_ref, done_ref, *parts = refs[9:]
@@ -174,28 +174,16 @@
     done_ref[...] = jnp.zeros_like(done_ref)
     for ref, value in zip(parts, ins):
         ref[...] = value[...]
-    base, even = flags_ref[11], flags_ref[12] > 0
-
-    def far_is_live(left, right):
-        first = base - 2 + jnp.where(even, left, right)
-        second = base + 2 + jnp.where(even, right, left)
-        hits = [
-            (list_ref[0, at] == first) & (list_ref[1, at] == second)
-            for at in range(list_ref.shape[1])
-        ]
-        return functools.reduce(jnp.logical_or, hits)
-
     for kind in range(2):
         rights = ((own0, own1), (even0, even1))[kind]
         part_refs = (parts[:2], parts[2:])[kind]
+        flag_ref, flag_at = ((flags_ref, 7), (far_ref, 0))[kind]
 
         @pl.loop(0, 4)
         def _(index):
             left, right = index // 2, index % 2
 
-            live = far_is_live(left, right) if kind else flags_ref[7 + index] > 0
-
-            @pl.when(live)
+            @pl.when(flag_ref[flag_at + index] > 0)
             def _():
                 one_pair(
                     make, tile_ref, kind * 4 + index, odd0.at[left],
@@ -331,27 +319,40 @@
     return jnp.stack([swap(value[block]) for block in range(2)])
 
 
+def live_flags(pairs, base, even_codes, odd_codes):
+    none = (100, 100)
+
+    def table(entries):
+        return jnp.array([64 * i + j for i, j in (none if e is None else e for e in entries)], jnp.int32)
+
+    even_row = lax.axis_index("rows") % 2 == 0
+    wanted = jnp.where(even_row, table(even_codes), table(odd_codes))
+    codes = (pairs[:, 0] - base) * 64 + (pairs[:, 1] - base)
+    hit = (codes[None, :] == wanted[:, None]) & (pairs[None, :, 0] >= 0)
+    return jnp.any(hit, axis=1).astype(jnp.int32)
+
+
 SLOTS = [(0, 0), (0, 1), (1, 0), (1, 1)]
 
 
 def own_flags_and_list(pair_list, base):
-    own = jnp.concatenate([pair_list.T, swap(pair_list.T)], axis=1)
+    own = jnp.concatenate([pair_list, swap(pair_list)], axis=0)
     before = lax.ppermute(own, "rows", [(r, r + 1) for r in range(lax.axis_size("rows") - 1)])
-    within, idle = [(0, 0), (0, 1), (1, 1)], [(100, 100)] * 4
-
-    def table(entries):
-        return jnp.array([64 * i + j for i, j in entries], jnp.int32)
-
-    even = lax.axis_index("rows") % 2 == 0
-    wanted = jnp.where(
-        even,
-        table(within + [(left, 2 + right) for left, right in SLOTS] + idle),
-        table(within + idle + [(right, 2 + left) for left, right in SLOTS]),
-    )
-    codes = (own[0] - base) * 64 + (own[1] - base)
-    hit = (codes[None, :] == wanted[:, None]) & (own[0][None, :] >= 0)
-    flags = jnp.any(hit, axis=1).astype(jnp.int32)
-    return jnp.concatenate([flags, base[None], even.astype(jnp.int32)[None]]), before
+    within, idle = [(0, 0), (0, 1), (1, 1)], [None] * 4
+    flags = live_flags(
+        own, base,
+        within + [(left, 2 + right) for left, right in SLOTS] + idle,
+        within + idle + [(right, 2 + left) for left, right in SLOTS],
+    )
+    return flags, before
+
+
+def flags_of_far(before, base):
+    return live_flags(
+        before, base,
+        [(left - 2, 2 + right) for left, right in SLOTS],
+        [(right - 2, 2 + left) for left, right in SLOTS],
+    )
 
 
 def spread(done, own0, own1, out_odd, even0, even1):
@@ -417,10 +418,11 @@
         functools.partial(early_kernel, True), (tiles(4),) + 3 * (sum_shape,), 10**4, 10**4
     )(in_specs=[SMEM] + [VMEM] * 4)(flags, own0, even0, even1, done)
     done, odd0, before = lax.optimization_barrier((done, odd0, before))
+    far_flags = flags_of_far(before, base)
     tiles_late, out_odd, own_part0, own_part1, even_part0, even_part1 = call(
         functools.partial(late_kernel, True), (tiles(8),) + 5 * (sum_shape,), 10**9, 10**6
     )(in_specs=[SMEM] * 2 + [VMEM] * 9)(
-        flags, before, odd0, own0, own1, even0, even1, own_part0, own_part1, even_part0, even_part1
+        flags, far_flags, odd0, own0, own1, even0, even1, own_part0, own_part1, even_part0, even_part1
     )
     sketch, pair0 = call(total_kernel, (sum_shape, shape((2, 128, HALF), bf16)), 10**6, 2 * 10**6)(
         in_specs=[VMEM] * 5
@@ -444,7 +446,7 @@
     out_odd, own_part0, own_part1, even_part0, even_part1 = call(
         functools.partial(late_kernel, False), 5 * (sum_shape,), 10**9, 10**6
     )(in_specs=[SMEM] * 2 + [VMEM] * 10)(
-        flags, before, tiles_late, odd0, pair0, pair1, even0, even1,
+        flags, far_flags, tiles_late, odd0, pair0, pair1, even0, even1,
         own_part0, own_part1, even_part0, even_part1,
     )
     image = call(total_kernel, sum_shape, 10**6, 2 * 10**6)(in_specs=[VMEM] * 5)(

time: 128 us -> 124 us (0.969); the launches traced: 126 us -> 124 us
  waiting for transfers between devices: 37.1 us -> 34.1 us
  blocking collectives: 26.3 us -> 27.6 us
    ppermute x8, starting transfers between devices: 21.7 us -> 18 us  [exchange(): return lax.ppermute(value, 'rows', links)]
    ppermute x8, waiting for transfers between devices: 27.9 us -> 25 us  [exchange(): return lax.ppermute(value, 'rows', links)]
    all_to_all x1, starting transfers between devices: 3.37 us -> 5.33 us  [sum_over_chips(): lax.all_to_all(copies, 'rows', 0, 0, axis_index_groups=groups, tiled=True)]
    ppermute x13, starting transfers between devices: 15 us -> 16.4 us  [swap(): return lax.ppermute(value, 'cols', [(0, 1), (1, 0)])]
    all_to_all x1, blocking collectives: 26.3 us -> 27.6 us  [sum_over_chips(): lax.all_to_all(copies, 'rows', 0, 0, axis_index_groups=groups, tiled=True)]
where the time goes in v6:
time: 124 us
  starting transfers between devices  43.1 us (35%)
  waiting for transfers between devices  34.1 us (28%)
  blocking collectives  27.6 us (22%)
  Pallas kernels  18 us (15%)
    all_to_all x1, blocking collectives, sum_over_chips(): lax.all_to_all(copies, 'rows', 0, 0, axis_index_groups=groups, tiled=True)  27.6 us
    ppermute x8, waiting for transfers between devices, exchange(): return lax.ppermute(value, 'rows', links)  25 us
    ppermute x8, starting transfers between devices, exchange(): return lax.ppermute(value, 'rows', links)  18 us
    ppermute x13, starting transfers between devices, swap(): return lax.ppermute(value, 'cols', [(0, 1), (1, 0)])  16.4 us
    all_to_all x1, waiting for transfers between devices, sum_over_chips(): lax.all_to_all(copies, 'rows', 0, 0, axis_index_groups=groups, tiled=True)  5.87 us
    all_to_all x1, starting transfers between devices, sum_over_chips(): lax.all_to_all(copies, 'rows', 0, 0, axis_index_groups=groups, tiled=True)  5.33 us
    ppermute x1, starting transfers between devices, own_flags_and_list(): lax.ppermute(own, 'rows', [(r, r + 1) for r in range(lax.axis_size('rows'...  3.36 us
    ppermute x13, waiting for transfers between devices, swap(): return lax.ppermute(value, 'cols', [(0, 1), (1, 0)])  3.24 us
  transfers between devices with their start and end apart: 23, of which 10 were waited for; matrix products, arithmetic and copies ran while one was open for 0% of the time, Pallas kernels for 8%

profile of v6, /device:TPU:1, one launch (start us, length us, event | category | flops | bytes accessed | tf_op | source)
XLA Modules:
  0.0 124.5 jit_solution(279870854433079338)
XLA Ops:
  0.6 0.0 copy-start.3
  0.6 0.0 copy-start.4
  0.7 0.0 copy-start.1
  0.7 0.0 copy-start.2
  0.7 1.4 %shard_map.87.refs_0_.refs_1_ = bf16[2,1792,128]{2,1,0:T(8,128)(2,1)S(1)} custom-call(s32[1]{0:T(128)} %bitcast.core_ref, bf16[2048,384]{1,0:T(8,128)(2,1)} %rows_ref.3, bf16[64,2048]{1,0:T(8,128)(2,1)} %bitcast.23), custom_call_target="tpu_custom_call" | custom-call | flops 10000 | bytes 10000 | tf_op jit(solution)/shard_map/pallas_call | solution.py:390
  2.1 2.2 %collective-permute-start.1 = (bf16[2,1792,128]{2,1,0:T(8,128)(2,1)S(1)}, bf16[2,1792,128]{2,1,0:T(8,128)(2,1)S(1)}, u32[]{:S(2)}, u32[]{:S(2)}) collective-permute-start(bf16[2,1792,128]{2,1,0:T(8,128)(2,1)S(1)} %shard_map.87.refs_0_.refs_1_), channel_id=1, source_target_pairs={{0,2},{2,0},{4,6},{6,4},{8,10},{10,8},{12,14},{14,12},{16,18},{18,... | collective-permute-start | bytes 2752520 | tf_op jit(solution)/shard_map/ppermute | solution.py:303
  4.3 1.6 %collective-permute-start.4 = (bf16[2,1792,128]{2,1,0:T(8,128)(2,1)S(1)}, bf16[2,1792,128]{2,1,0:T(8,128)(2,1)}, u32[]{:S(2)}, u32[]{:S(2)}) collective-permute-start(bf16[2,1792,128]{2,1,0:T(8,128)(2,1)S(1)} %shard_map.87.refs_0_.refs_1_), channel_id=1, source_target_pairs={{2,4},{4,2},{6,8},{8,6},{10,12},{12,10},{14,16},{16,14},{18,20},{2... | collective-permute-start | bytes 2752520 | tf_op jit(solution)/shard_map/ppermute | solution.py:303
  5.9 1.4 %shard_map.86.refs_1_.refs_2_ = bf16[2,1792,128]{2,1,0:T(8,128)(2,1)S(1)} custom-call(s32[1]{0:T(128)} %bitcast.core_ref, bf16[2048,384]{1,0:T(8,128)(2,1)} %rows_ref.3, bf16[64,2048]{1,0:T(8,128)(2,1)} %bitcast.24), custom_call_target="tpu_custom_call" | custom-call | flops 10000 | bytes 10000 | tf_op jit(solution)/shard_map/pallas_call | solution.py:390
  7.3 1.2 collective-permute-start
  8.5 0.8 collective-permute-done
  9.4 0.1 pad_add_fusion
  9.4 0.1 and_reduce_fusion
  9.5 3.2 %shard_map.88 = (bf16[3,2,512,512]{3,2,1,0:T(8,128)(2,1)S(1)}, f32[2,64,512]{2,1,0:T(8,128)S(1)}, f32[2,64,512]{2,1,0:T(8,128)S(1)}, f32[2,64,512]{2,1,0:T(8,128)S(1)}) custom-call(s32[11]{0:T(128)S(1)} %convert_element_type.6.flags_ref, bf16[2,1792,128]{2,1,0:T(8,128)(2,1)S(1)} %shard_map.87.refs_0_.refs_1_, bf16[2,1792,128]{2,1,0:T(8,128)(2,1)S(1)} %shard_map.86.refs_1_.refs_2_), custom_call_target="tpu_custom_call" | custom-call | flops 10000 | bytes 10000 | tf_op jit(solution)/shard_map/pallas_call | solution.py:412
  12.7 10.4 %collective-permute-done.1.refs_1_.refs_3_ = bf16[2,1792,128]{2,1,0:T(8,128)(2,1)S(1)} collective-permute-done((bf16[2,1792,128]{2,1,0:T(8,128)(2,1)S(1)}, bf16[2,1792,128]{2,1,0:T(8,128)(2,1)S(1)}, u32[]{:S(2)}, u32[]{:S(2)}) %collective-permute-start.1) | collective-permute-done | bytes 917536 | tf_op jit(solution)/shard_map/ppermute | solution.py:303
  23.1 0.1 slice_bitcast_fusion.1
  23.2 2.6 %collective-permute-start.2 = (bf16[1792,128]{1,0:T(8,128)(2,1)S(1)}, bf16[1792,128]{1,0:T(8,128)(2,1)S(1)}, u32[]{:S(2)}, u32[]{:S(2)}) collective-permute-start(bf16[1792,128]{1,0:T(8,128)(2,1)S(1)} %get-tuple-element.84), channel_id=1, source_target_pairs={{0,1},{1,0},{2,3},{3,2},{4,5},{5,4},{6,7},{7,6},{8,9},{9,8},{10,11... | collective-permute-start | bytes 1376264 | tf_op jit(solution)/shard_map/ppermute | solution.py:315
  25.8 0.1 collective-permute-start.3
  25.9 3.4 %collective-permute-start.5 = (s32[8,2]{0,1:T(2,128)S(1)}, s32[8,2]{0,1:T(2,128)S(1)}, u32[]{:S(2)}, u32[]{:S(2)}) collective-permute-start(s32[8,2]{0,1:T(2,128)S(1)} %pad_add_fusion), channel_id=1, source_target_pairs={{0,2},{2,4},{4,6},{6,8},{8,10},{10,12},{12,14},{14,16},{16,18},{18... | collective-permute-start | bytes 200 | tf_op jit(solution)/shard_map/ppermute | solution.py:340
  29.3 0.0 collective-permute-done.2
  29.3 0.0 collective-permute-done.3
  29.3 0.1 pad_maximum_fusion.refs_2_.refs_4_
  29.4 2.0 %shard_map.89 = (bf16[4,2,512,512]{3,2,1,0:T(8,128)(2,1)S(1)}, f32[2,64,512]{2,1,0:T(8,128)S(1)}, f32[2,64,512]{2,1,0:T(8,128)S(1)}, f32[2,64,512]{2,1,0:T(8,128)S(1)}) custom-call(s32[11]{0:T(128)S(1)} %convert_element_type.6.flags_ref, bf16[2,1792,128]{2,1,0:T(8,128)(2,1)S(1)} %shard_map.87.refs_0_.refs_1_, ...), custom_call_target="tpu_custom_call" | custom-call | flops 10000 | bytes 10000 | tf_op jit(solution)/shard_map/pallas_call | solution.py:417
  31.4 0.0 collective-permute-done.5
  31.4 0.0 collective-permute-done.4.refs_0_
  31.4 0.2 and_reduce_fusion.1
  31.6 1.4 %shard_map.90 = (bf16[8,2,512,512]{3,2,1,0:T(8,128)(2,1)S(1)}, f32[2,64,512]{2,1,0:T(8,128)S(1)}, f32[2,64,512]{2,1,0:T(8,128)S(1)}, f32[2,64,512]{2,1,0:T(8,128...) custom-call(s32[11]{0:T(128)S(1)} %convert_element_type.6.flags_ref, s32[4]{0:T(128)S(1)} %convert_element_type.7.far_ref, ...), custom_call_target="tpu_custom_call" | custom-call | flops 1000000000 | bytes 1000000 | tf_op jit(solution)/shard_map/pallas_call | solution.py:422
  33.0 0.8 collective-permute-start.8
  33.8 0.1 collective-permute-start.6
  33.9 0.7 collective-permute-start.7
  34.6 0.4 collective-permute-done.8
  35.0 4.6 %collective-permute-start.9 = (f32[2,64,512]{2,1,0:T(8,128)S(1)}, f32[2,64,512]{2,1,0:T(8,128)S(1)}, u32[]{:S(2)}, u32[]{:S(2)}) collective-permute-start(f32[2,64,512]{2,1,0:T(8,128)S(1)} %add.36), channel_id=1, source_target_pairs={{0,2},{2,0},{4,6},{6,4},{8,10},{10,8},{12,14},{14,12},{16,18},{18,... | collective-permute-start | bytes 786440 | tf_op jit(solution)/shard_map/ppermute | solution.py:303
  39.6 6.0 %collective-permute-done.9.from_even = f32[2,64,512]{2,1,0:T(8,128)S(1)} collective-permute-done((f32[2,64,512]{2,1,0:T(8,128)S(1)}, f32[2,64,512]{2,1,0:T(8,128)S(1)}, u32[]{:S(2)}, u32[]{:S(2)}) %collective-permute-start.9) | collective-permute-done | bytes 262176 | tf_op jit(solution)/shard_map/ppermute | solution.py:303
  45.6 0.1 shard_map.91
  45.7 1.2 collective-permute-start.10
  46.9 0.7 collective-permute-start.14
  47.6 1.9 %collective-permute-start.13 = (bf16[2,128,512]{2,1,0:T(8,128)(2,1)S(1)}, bf16[2,128,512]{2,1,0:T(8,128)(2,1)S(1)}, u32[]{:S(2)}, u32[]{:S(2)}) collective-permute-start(bf16[2,128,512]{2,1,0:T(8,128)(2,1)S(1)} %get-tuple-element.63.refs_1_.refs_2_), channel_id=1, source_target_pairs={{0,1},{1,0},{2,3},{3,2},{4,5},{5,4},{6,7},{7,6},{8,9},{9,8},{10,11... | collective-permute-start | bytes 786440 | tf_op jit(solution)/shard_map/ppermute | solution.py:315
  49.5 2.8 %collective-permute-done.10.refs_2_.refs_4_ = bf16[2,128,512]{2,1,0:T(8,128)(2,1)S(1)} collective-permute-done((bf16[2,128,512]{2,1,0:T(8,128)(2,1)S(1)}, bf16[2,128,512]{2,1,0:T(8,128)(2,1)S(1)}, u32[]{:S(2)}, u32[]{:S(2)}) %collective-permute-start.10) | collective-permute-done | bytes 262176 | tf_op jit(solution)/shard_map/ppermute | solution.py:303
  52.3 2.3 %collective-permute-start.11 = (bf16[128,512]{1,0:T(8,128)(2,1)S(1)}, bf16[128,512]{1,0:T(8,128)(2,1)S(1)}, u32[]{:S(2)}, u32[]{:S(2)}) collective-permute-start(bf16[128,512]{1,0:T(8,128)(2,1)S(1)} %get-tuple-element.86), channel_id=1, source_target_pairs={{0,1},{1,0},{2,3},{3,2},{4,5},{5,4},{6,7},{7,6},{8,9},{9,8},{10,11... | collective-permute-start | bytes 393224 | tf_op jit(solution)/shard_map/ppermute | solution.py:315
  54.6 0.3 collective-permute-start.12
  54.9 1.9 %shard_map.93 = (f32[2,64,512]{2,1,0:T(8,128)S(1)}, f32[2,64,512]{2,1,0:T(8,128)S(1)}, f32[2,64,512]{2,1,0:T(8,128)S(1)}) custom-call(s32[11]{0:T(128)S(1)} %convert_element_type.6.flags_ref, bf16[3,2,512,512]{3,2,1,0:T(8,128)(2,1)S(1)} %get-tuple-element.64.refs_0_, bf16[2,128,512]{2,1,0:T(8,128)(2,1)S(1)} %get-tuple-element.63.refs_1_.refs_2_, ...), custom_call_target="tpu_custom_call" | custom-call | flops 10000 | bytes 10000 | tf_op jit(solution)/shard_map/pallas_call | solution.py:438
  56.8 0.0 collective-permute-done.12
  56.8 1.3 %shard_map.94 = (f32[2,64,512]{2,1,0:T(8,128)S(1)}, f32[2,64,512]{2,1,0:T(8,128)S(1)}, f32[2,64,512]{2,1,0:T(8,128)S(1)}) custom-call(s32[11]{0:T(128)S(1)} %convert_element_type.6.flags_ref, bf16[4,2,512,512]{3,2,1,0:T(8,128)(2,1)S(1)} %get-tuple-element.62.refs_0_, bf16[2,128,512]{2,1,0:T(8,128)(2,1)S(1)} %get-tuple-element.63.refs_1_.refs_2_, ...), custom_call_target="tpu_custom_call" | custom-call | flops 10000 | bytes 10000 | tf_op jit(solution)/shard_map/pallas_call | solution.py:442
  58.1 0.0 collective-permute-done.14.refs_1_
  58.1 0.8 shard_map.95
  58.9 0.3 collective-permute-start.17
  59.2 0.3 collective-permute-start.15
  59.5 0.7 collective-permute-start.16
  60.2 0.4 collective-permute-done.17
  60.6 6.4 %collective-permute-start.18 = (f32[2,64,512]{2,1,0:T(8,128)S(1)}, f32[2,64,512]{2,1,0:T(8,128)S(1)}, u32[]{:S(2)}, u32[]{:S(2)}) collective-permute-start(f32[2,64,512]{2,1,0:T(8,128)S(1)} %add.37), channel_id=1, source_target_pairs={{0,2},{2,0},{4,6},{6,4},{8,10},{10,8},{12,14},{14,12},{16,18},{18,... | collective-permute-start | bytes 786440 | tf_op jit(solution)/shard_map/ppermute | solution.py:303
  67.0 0.4 shard_map.92.first_ref
  67.4 5.7 %collective-permute-done.18.from_even = f32[2,64,512]{2,1,0:T(8,128)S(1)} collective-permute-done((f32[2,64,512]{2,1,0:T(8,128)S(1)}, f32[2,64,512]{2,1,0:T(8,128)S(1)}, u32[]{:S(2)}, u32[]{:S(2)}) %collective-permute-start.18) | collective-permute-done | bytes 262176 | tf_op jit(solution)/shard_map/ppermute | solution.py:303
  73.2 0.1 shard_map.96.value_ref
  73.3 0.4 shard_map.97
  73.7 1.1 collective-permute-start.19
  74.8 0.8 collective-permute-done.19.refs_1_
  75.7 27.6 %all_to_all.10.refs_0_ = f32[16,32,128]{2,1,0:T(8,128)S(1)} all-to-all(f32[16,32,128]{2,1,0:T(8,128)S(1)} %shard_map.98), channel_id=1, replica_groups={{0,2,4,6,64,66,68,70,128,130,132,134,192,194,196,198},{8,10,12,14,72,74..., dimensions={0} | all-to-all | bytes 524288 | tf_op jit(solution)/shard_map/all_to_all | solution.py:372
  103.3 0.7 shard_map.99
  104.0 5.3 %all-to-all-start.1 = ((f32[8,32,128]{2,1,0:T(8,128)}), f32[8,32,128]{2,1,0:T(8,128)S(1)}, u32[]{:S(2)}, u32[]{:S(2)}) async-start(f32[8,32,128]{2,1,0:T(8,128)} %shard_map.99), calls=%async_computation.1 | async-start | bytes 262144 | tf_op jit(solution)/shard_map/all_to_all | solution.py:372
  109.3 2.2 %collective-permute-start.21 = (f32[64,512]{1,0:T(8,128)S(1)}, f32[64,512]{1,0:T(8,128)S(1)}, u32[]{:S(2)}, u32[]{:S(2)}) collective-permute-start(f32[64,512]{1,0:T(8,128)S(1)} %get-tuple-element.81), channel_id=1, source_target_pairs={{0,1},{1,0},{2,3},{3,2},{4,5},{5,4},{6,7},{7,6},{8,9},{9,8},{10,11... | collective-permute-start | bytes 393224 | tf_op jit(solution)/shard_map/ppermute | solution.py:315
  111.5 5.9 %all-to-all-done.1 = f32[8,32,128]{2,1,0:T(8,128)S(1)} async-done(((f32[8,32,128]{2,1,0:T(8,128)}), f32[8,32,128]{2,1,0:T(8,128)S(1)}, u32[]{:S(2)}, u32[]{:S(2)}) %all-to-all-start.1) | async-done | bytes 131104 | tf_op jit(solution)/shard_map/all_to_all | solution.py:372
  117.4 3.3 %collective-permute-start.20 = (f32[32,128]{1,0:T(8,128)S(1)}, f32[32,128]{1,0:T(8,128)S(1)}, u32[]{:S(2)}, u32[]{:S(2)}) collective-permute-start(f32[32,128]{1,0:T(8,128)S(1)} %reduce_sum.9.mine_ref), channel_id=1, source_target_pairs={{0,1},{1,0},{2,3},{3,2},{4,5},{5,4},{6,7},{7,6},{8,9},{9,8},{10,11... | collective-permute-start | bytes 49160 | tf_op jit(solution)/shard_map/ppermute | solution.py:315
  120.7 0.0 collective-permute-done.21.got_ref
  120.7 0.8 collective-permute-done.20.other_ref
  121.5 3.0 %shard_map.100 = (f32[64,1024]{1,0:T(8,128)}, f32[64,64]{1,0:T(8,128)}) custom-call(s32[1]{0:T(128)} %bitcast.core_ref, f32[32,128]{1,0:T(8,128)S(1)} %reduce_sum.9.mine_ref, f32[32,128]{1,0:T(8,128)S(1)} %collective-permute-done.20.other_ref, f32[2,64,512]{2,1,0:T(8,128)S(1)} %shard_map.96.value_ref, f32[64,512]{1,0:T(8,128)S(1)} %collective-permute-done.21.got_ref), custom_call_target="tpu_custom_call" | custom-call | flops 100000000 | bytes 1000000 | tf_op jit(solution)/shard_map/pallas_call | solution.py:463
  (26 shorter events, 0.2 us)
Async XLA Ops:
  0.6 7.9 %copy-start.3 = (s32[11]{0:T(128)S(1)}, s32[11]{0:T(128)}, u32[]{:S(2)}) copy-start(s32[11]{0:T(128)} %constant.40.clone) | copy-start | bytes 136
  0.6 7.9 %copy-start.4 = (s32[11]{0:T(128)S(1)}, s32[11]{0:T(128)}, u32[]{:S(2)}) copy-start(s32[11]{0:T(128)} %constant.39.clone) | copy-start | bytes 136
  0.7 6.6 %copy-start = (s32[4,2]{0,1:T(2,128)S(1)}, s32[4,2]{0,1:T(2,128)}, u32[]{:S(2)}) copy-start(s32[4,2]{0,1:T(2,128)} %param.9) | copy-start | bytes 100
  0.7 25.2 %copy-start.1 = (s32[4]{0:T(128)S(1)}, s32[4]{0:T(128)}, u32[]{:S(2)}) copy-start(s32[4]{0:T(128)} %constant.42.clone) | copy-start | bytes 52
  0.7 25.2 %copy-start.2 = (s32[4]{0:T(128)S(1)}, s32[4]{0:T(128)}, u32[]{:S(2)}) copy-start(s32[4]{0:T(128)} %constant.41.clone) | copy-start | bytes 52
  2.1 21.0 %collective-permute-start.1 = (bf16[2,1792,128]{2,1,0:T(8,128)(2,1)S(1)}, bf16[2,1792,128]{2,1,0:T(8,128)(2,1)S(1)}, u32[]{:S(2)}, u32[]{:S(2)}) collective-permute-start(bf16[2,1792,128]{2,1,0:T(8,128)(2,1)S(1)} %shard_map.87.refs_0_.refs_1_), channel_id=1, source_target_pairs={{0,2},{2,0},{4,6},{6,4},{8,10},{10,8},{12,14},{14,12},{16,18},{18,... | collective-permute-start | bytes 2752520 | tf_op jit(solution)/shard_map/ppermute | solution.py:303
  4.3 27.0 %collective-permute-start.4 = (bf16[2,1792,128]{2,1,0:T(8,128)(2,1)S(1)}, bf16[2,1792,128]{2,1,0:T(8,128)(2,1)}, u32[]{:S(2)}, u32[]{:S(2)}) collective-permute-start(bf16[2,1792,128]{2,1,0:T(8,128)(2,1)S(1)} %shard_map.87.refs_0_.refs_1_), channel_id=1, source_target_pairs={{2,4},{4,2},{6,8},{8,6},{10,12},{12,10},{14,16},{16,14},{18,20},{2... | collective-permute-start | bytes 2752520 | tf_op jit(solution)/shard_map/ppermute | solution.py:303
  7.3 2.0 %collective-permute-start = (s32[4,2]{0,1:T(2,128)S(1)}, s32[4,2]{0,1:T(2,128)S(1)}, u32[]{:S(2)}, u32[]{:S(2)}) collective-permute-start(s32[4,2]{0,1:T(2,128)S(1)} %copy-done), channel_id=1, source_target_pairs={{0,1},{1,0},{2,3},{3,2},{4,5},{5,4},{6,7},{7,6},{8,9},{9,8},{10,11... | collective-permute-start | bytes 104 | tf_op jit(solution)/shard_map/ppermute | solution.py:315
  23.2 6.1 %collective-permute-start.2 = (bf16[1792,128]{1,0:T(8,128)(2,1)S(1)}, bf16[1792,128]{1,0:T(8,128)(2,1)S(1)}, u32[]{:S(2)}, u32[]{:S(2)}) collective-permute-start(bf16[1792,128]{1,0:T(8,128)(2,1)S(1)} %get-tuple-element.84), channel_id=1, source_target_pairs={{0,1},{1,0},{2,3},{3,2},{4,5},{5,4},{6,7},{7,6},{8,9},{9,8},{10,11... | collective-permute-start | bytes 1376264 | tf_op jit(solution)/shard_map/ppermute | solution.py:315
  25.8 3.5 %collective-permute-start.3 = (bf16[1792,128]{1,0:T(8,128)(2,1)S(1)}, bf16[1792,128]{1,0:T(8,128)(2,1)S(1)}, u32[]{:S(2)}, u32[]{:S(2)}) collective-permute-start(bf16[1792,128]{1,0:T(8,128)(2,1)S(1)} %get-tuple-element.85), channel_id=1, source_target_pairs={{0,1},{1,0},{2,3},{3,2},{4,5},{5,4},{6,7},{7,6},{8,9},{9,8},{10,11... | collective-permute-start | bytes 1376264 | tf_op jit(solution)/shard_map/ppermute | solution.py:315
  25.9 5.5 %collective-permute-start.5 = (s32[8,2]{0,1:T(2,128)S(1)}, s32[8,2]{0,1:T(2,128)S(1)}, u32[]{:S(2)}, u32[]{:S(2)}) collective-permute-start(s32[8,2]{0,1:T(2,128)S(1)} %pad_add_fusion), channel_id=1, source_target_pairs={{0,2},{2,4},{4,6},{6,8},{8,10},{10,12},{12,14},{14,16},{16,18},{18... | collective-permute-start | bytes 200 | tf_op jit(solution)/shard_map/ppermute | solution.py:340
  33.0 1.9 %collective-permute-start.8 = (f32[2,64,512]{2,1,0:T(8,128)S(1)}, f32[2,64,512]{2,1,0:T(8,128)S(1)}, u32[]{:S(2)}, u32[]{:S(2)}) collective-permute-start(f32[2,64,512]{2,1,0:T(8,128)S(1)} %get-tuple-element.60), channel_id=1, source_target_pairs={{0,1},{1,0},{2,3},{3,2},{4,5},{5,4},{6,7},{7,6},{8,9},{9,8},{10,11... | collective-permute-start | bytes 786440 | tf_op jit(solution)/shard_map/ppermute | solution.py:315
  33.8 5.8 %collective-permute-start.6 = (f32[2,64,512]{2,1,0:T(8,128)S(1)}, f32[2,64,512]{2,1,0:T(8,128)S(1)}, u32[]{:S(2)}, u32[]{:S(2)}) collective-permute-start(f32[2,64,512]{2,1,0:T(8,128)S(1)} %get-tuple-element.57), channel_id=1, source_target_pairs={{0,1},{1,0},{2,3},{3,2},{4,5},{5,4},{6,7},{7,6},{8,9},{9,8},{10,11... | collective-permute-start | bytes 786440 | tf_op jit(solution)/shard_map/ppermute | solution.py:315
  33.9 5.7 %collective-permute-start.7 = (f32[2,64,512]{2,1,0:T(8,128)S(1)}, f32[2,64,512]{2,1,0:T(8,128)S(1)}, u32[]{:S(2)}, u32[]{:S(2)}) collective-permute-start(f32[2,64,512]{2,1,0:T(8,128)S(1)} %get-tuple-element.58), channel_id=1, source_target_pairs={{2,4},{4,2},{6,8},{8,6},{10,12},{12,10},{14,16},{16,14},{18,20},{2... | collective-permute-start | bytes 786440 | tf_op jit(solution)/shard_map/ppermute | solution.py:303
  35.0 10.6 %collective-permute-start.9 = (f32[2,64,512]{2,1,0:T(8,128)S(1)}, f32[2,64,512]{2,1,0:T(8,128)S(1)}, u32[]{:S(2)}, u32[]{:S(2)}) collective-permute-start(f32[2,64,512]{2,1,0:T(8,128)S(1)} %add.36), channel_id=1, source_target_pairs={{0,2},{2,0},{4,6},{6,4},{8,10},{10,8},{12,14},{14,12},{16,18},{18,... | collective-permute-start | bytes 786440 | tf_op jit(solution)/shard_map/ppermute | solution.py:303
  45.7 6.6 %collective-permute-start.10 = (bf16[2,128,512]{2,1,0:T(8,128)(2,1)S(1)}, bf16[2,128,512]{2,1,0:T(8,128)(2,1)S(1)}, u32[]{:S(2)}, u32[]{:S(2)}) collective-permute-start(bf16[2,128,512]{2,1,0:T(8,128)(2,1)S(1)} %get-tuple-element.63.refs_1_.refs_2_), channel_id=1, source_target_pairs={{0,2},{2,0},{4,6},{6,4},{8,10},{10,8},{12,14},{14,12},{16,18},{18,... | collective-permute-start | bytes 786440 | tf_op jit(solution)/shard_map/ppermute | solution.py:303
  46.9 11.2 %collective-permute-start.14 = (bf16[2,128,512]{2,1,0:T(8,128)(2,1)S(1)}, bf16[2,128,512]{2,1,0:T(8,128)(2,1)S(1)}, u32[]{:S(2)}, u32[]{:S(2)}) collective-permute-start(bf16[2,128,512]{2,1,0:T(8,128)(2,1)S(1)} %get-tuple-element.63.refs_1_.refs_2_), channel_id=1, source_target_pairs={{2,4},{4,2},{6,8},{8,6},{10,12},{12,10},{14,16},{16,14},{18,20},{2... | collective-permute-start | bytes 786440 | tf_op jit(solution)/shard_map/ppermute | solution.py:303
  47.6 7.3 %collective-permute-start.13 = (bf16[2,128,512]{2,1,0:T(8,128)(2,1)S(1)}, bf16[2,128,512]{2,1,0:T(8,128)(2,1)S(1)}, u32[]{:S(2)}, u32[]{:S(2)}) collective-permute-start(bf16[2,128,512]{2,1,0:T(8,128)(2,1)S(1)} %get-tuple-element.63.refs_1_.refs_2_), channel_id=1, source_target_pairs={{0,1},{1,0},{2,3},{3,2},{4,5},{5,4},{6,7},{7,6},{8,9},{9,8},{10,11... | collective-permute-start | bytes 786440 | tf_op jit(solution)/shard_map/ppermute | solution.py:315
  52.3 4.4 %collective-permute-start.11 = (bf16[128,512]{1,0:T(8,128)(2,1)S(1)}, bf16[128,512]{1,0:T(8,128)(2,1)S(1)}, u32[]{:S(2)}, u32[]{:S(2)}) collective-permute-start(bf16[128,512]{1,0:T(8,128)(2,1)S(1)} %get-tuple-element.86), channel_id=1, source_target_pairs={{0,1},{1,0},{2,3},{3,2},{4,5},{5,4},{6,7},{7,6},{8,9},{9,8},{10,11... | collective-permute-start | bytes 393224 | tf_op jit(solution)/shard_map/ppermute | solution.py:315
  54.6 2.2 %collective-permute-start.12 = (bf16[128,512]{1,0:T(8,128)(2,1)S(1)}, bf16[128,512]{1,0:T(8,128)(2,1)S(1)}, u32[]{:S(2)}, u32[]{:S(2)}) collective-permute-start(bf16[128,512]{1,0:T(8,128)(2,1)S(1)} %get-tuple-element.87), channel_id=1, source_target_pairs={{0,1},{1,0},{2,3},{3,2},{4,5},{5,4},{6,7},{7,6},{8,9},{9,8},{10,11... | collective-permute-start | bytes 393224 | tf_op jit(solution)/shard_map/ppermute | solution.py:315
  58.9 1.6 %collective-permute-start.17 = (f32[2,64,512]{2,1,0:T(8,128)S(1)}, f32[2,64,512]{2,1,0:T(8,128)S(1)}, u32[]{:S(2)}, u32[]{:S(2)}) collective-permute-start(f32[2,64,512]{2,1,0:T(8,128)S(1)} %get-tuple-element.78), channel_id=1, source_target_pairs={{0,1},{1,0},{2,3},{3,2},{4,5},{5,4},{6,7},{7,6},{8,9},{9,8},{10,11... | collective-permute-start | bytes 786440 | tf_op jit(solution)/shard_map/ppermute | solution.py:315
  59.2 8.2 %collective-permute-start.15 = (f32[2,64,512]{2,1,0:T(8,128)S(1)}, f32[2,64,512]{2,1,0:T(8,128)S(1)}, u32[]{:S(2)}, u32[]{:S(2)}) collective-permute-start(f32[2,64,512]{2,1,0:T(8,128)S(1)} %get-tuple-element.75), channel_id=1, source_target_pairs={{0,1},{1,0},{2,3},{3,2},{4,5},{5,4},{6,7},{7,6},{8,9},{9,8},{10,11... | collective-permute-start | bytes 786440 | tf_op jit(solution)/shard_map/ppermute | solution.py:315
  59.5 7.9 %collective-permute-start.16 = (f32[2,64,512]{2,1,0:T(8,128)S(1)}, f32[2,64,512]{2,1,0:T(8,128)S(1)}, u32[]{:S(2)}, u32[]{:S(2)}) collective-permute-start(f32[2,64,512]{2,1,0:T(8,128)S(1)} %get-tuple-element.76), channel_id=1, source_target_pairs={{2,4},{4,2},{6,8},{8,6},{10,12},{12,10},{14,16},{16,14},{18,20},{2... | collective-permute-start | bytes 786440 | tf_op jit(solution)/shard_map/ppermute | solution.py:303
  60.6 12.6 %collective-permute-start.18 = (f32[2,64,512]{2,1,0:T(8,128)S(1)}, f32[2,64,512]{2,1,0:T(8,128)S(1)}, u32[]{:S(2)}, u32[]{:S(2)}) collective-permute-start(f32[2,64,512]{2,1,0:T(8,128)S(1)} %add.37), channel_id=1, source_target_pairs={{0,2},{2,0},{4,6},{6,4},{8,10},{10,8},{12,14},{14,12},{16,18},{18,... | collective-permute-start | bytes 786440 | tf_op jit(solution)/shard_map/ppermute | solution.py:303
  73.7 2.0 %collective-permute-start.19 = (f32[32,128]{1,0:T(8,128)S(1)}, f32[32,128]{1,0:T(8,128)S(1)}, u32[]{:S(2)}, u32[]{:S(2)}) collective-permute-start(f32[32,128]{1,0:T(8,128)S(1)} %get-tuple-element.80), channel_id=1, source_target_pairs={{0,1},{1,0},{2,3},{3,2},{4,5},{5,4},{6,7},{7,6},{8,9},{9,8},{10,11... | collective-permute-start | bytes 49160 | tf_op jit(solution)/shard_map/ppermute | solution.py:315
  104.0 13.4 %all-to-all-start.1 = ((f32[8,32,128]{2,1,0:T(8,128)}), f32[8,32,128]{2,1,0:T(8,128)S(1)}, u32[]{:S(2)}, u32[]{:S(2)}) async-start(f32[8,32,128]{2,1,0:T(8,128)} %shard_map.99), calls=%async_computation.1 | async-start | bytes 262144 | tf_op jit(solution)/shard_map/all_to_all | solution.py:372
  109.3 11.3 %collective-permute-start.21 = (f32[64,512]{1,0:T(8,128)S(1)}, f32[64,512]{1,0:T(8,128)S(1)}, u32[]{:S(2)}, u32[]{:S(2)}) collective-permute-start(f32[64,512]{1,0:T(8,128)S(1)} %get-tuple-element.81), channel_id=1, source_target_pairs={{0,1},{1,0},{2,3},{3,2},{4,5},{5,4},{6,7},{7,6},{8,9},{9,8},{10,11... | collective-permute-start | bytes 393224 | tf_op jit(solution)/shard_map/ppermute | solution.py:315
  117.4 4.1 %collective-permute-start.20 = (f32[32,128]{1,0:T(8,128)S(1)}, f32[32,128]{1,0:T(8,128)S(1)}, u32[]{:S(2)}, u32[]{:S(2)}) collective-permute-start(f32[32,128]{1,0:T(8,128)S(1)} %reduce_sum.9.mine_ref), channel_id=1, source_target_pairs={{0,1},{1,0},{2,3},{3,2},{4,5},{5,4},{6,7},{7,6},{8,9},{9,8},{10,11... | collective-permute-start | bytes 49160 | tf_op jit(solution)/shard_map/ppermute | solution.py:315

commit v7 on v6

--- a/solution.py
+++ b/solution.py
@@ -9,6 +9,7 @@
 
 BLK = 1024
 HALF = 512
+QUARTER = 256
 SHARPNESS = 6.0
 EPSILON = 1e-06
 LOG2E = 1.4426950408889634
@@ -47,22 +48,33 @@
     copies = []
     for block in range(2):
         start = pl.multiple_of(block * BLK + side * HALF, HALF)
-        copies.append((
-            pltpu.make_async_copy(rows_ref.at[pl.ds(start, HALF), :], raw_ref.at[block], sems.at[block]),
+        for part in range(2):
+            rows = pl.ds(pl.multiple_of(start + part * QUARTER, QUARTER), QUARTER)
+            copies.append(
+                pltpu.make_async_copy(
+                    rows_ref.at[rows, :],
+                    raw_ref.at[block, pl.ds(part * QUARTER, QUARTER)],
+                    sems.at[2 * block + part],
+                )
+            )
+        copies.append(
             pltpu.make_async_copy(
-                columns_ref.at[:, pl.ds(start, HALF)], vec_ref.at[block], sems.at[2 + block]
-            ),
-        ))
-        for copy in copies[-1]:
-            copy.start()
+                columns_ref.at[:, pl.ds(start, HALF)], vec_ref.at[block], sems.at[4 + block]
+            )
+        )
+    for copy in copies:
+        copy.start()
     for block in range(2):
-        for copy in copies[block]:
-            copy.wait()
-        widened = raw_ref[block].astype(jnp.float32)
-        inverse = lax.rsqrt(jnp.sum(widened * widened, axis=1, keepdims=True) + EPSILON)
-        unit = (widened * inverse).astype(jnp.bfloat16)
-        for tile in range(3):
-            packet_ref[block, HALF * tile : HALF * (tile + 1)] = unit[:, 128 * tile : 128 * (tile + 1)]
+        for part in range(2):
+            copies[3 * block + part].wait()
+            here = slice(part * QUARTER, (part + 1) * QUARTER)
+            widened = raw_ref[block, here].astype(jnp.float32)
+            inverse = lax.rsqrt(jnp.sum(widened * widened, axis=1, keepdims=True) + EPSILON)
+            unit = (widened * inverse).astype(jnp.bfloat16)
+            for tile in range(3):
+                first = HALF * tile + part * QUARTER
+                packet_ref[block, first : first + QUARTER] = unit[:, 128 * tile : 128 * (tile + 1)]
+        copies[3 * block + 2].wait()
         for tile in range(4):
             packet_ref[block, 1536 + 64 * tile : 1600 + 64 * tile] = vec_ref[
                 block, :, 128 * tile : 128 * (tile + 1)
@@ -91,12 +103,13 @@
 
 
 def make_tiles(left, rights, tile_ref, slot):
-    whole = unit_rows(left, 0, HALF)
     for side in range(2):
         for at in range(0, HALF, 256):
-            tile_ref[slot, side, :, at : at + 256] = affinity_tile(
-                whole, unit_rows(rights[side], at, 256)
-            )
+            right = unit_rows(rights[side], at, 256)
+            for row in range(0, HALF, 256):
+                tile_ref[slot, side, row : row + 256, at : at + 256] = affinity_tile(
+                    unit_rows(left, row, 256), right
+                )
 
 
 def use_tiles(tile_ref, slot, rights, left, done_ref, done_at, part_refs, part_at, partial):
@@ -167,10 +180,11 @@
 def late_kernel(make, flags_ref, far_ref, *refs):
     if make:
         odd0, own0, own1, even0, even1, *ins = refs[:9]
-        tile_ref, done_ref, *parts = refs[9:]
+        tile_ref, done_ref, own_part, even_part, give_ref = refs[9:]
     else:
         tile_ref, odd0, own0, own1, even0, even1, *ins = refs[:10]
-        done_ref, *parts = refs[10:]
+        done_ref, own_part, even_part, give_ref = refs[10:]
+    parts = (own_part, give_ref.at[0], even_part, give_ref.at[1])
     done_ref[...] = jnp.zeros_like(done_ref)
     for ref, value in zip(parts, ins):
         ref[...] = value[...]
@@ -191,10 +205,10 @@
                 )
 
 
-def total_kernel(done, part_mine, part_other, from_odd, from_even, sum_ref, pair_ref=None):
+def total_kernel(done, part_mine, parts_other, from_odd, from_even, sum_ref, pair_ref=None):
     for block in range(2):
         value = (
-            done[block] + part_mine[block] + part_other[block] + from_odd[block] + from_even[block]
+            done[block] + part_mine[block] + parts_other[0, block] + from_odd[block] + from_even[block]
         )
         sum_ref[block] = value
         if pair_ref is not None:
@@ -355,10 +369,11 @@
     )
 
 
-def spread(done, own0, own1, out_odd, even0, even1):
+def spread(done, own0, out_odd, even0, give):
     from_odd = to_odd(out_odd)
-    from_even = to_even(even0 + swap(even1))
-    return done, own0, swap(own1), from_odd, from_even
+    got = swap(give)
+    from_even = to_even(even0 + got[1])
+    return done, own0, got, from_odd, from_even
 
 
 def sum_over_chips(*values):
@@ -394,7 +409,7 @@
             scratch_shapes=[
                 pltpu.VMEM((2, HALF, 384), bf16),
                 pltpu.VMEM((2, columns, HALF), bf16),
-                pltpu.SemaphoreType.DMA((4,)),
+                pltpu.SemaphoreType.DMA((6,)),
             ],
         )(core_ref, embeddings, test_columns)
 
@@ -419,14 +434,15 @@
     )(in_specs=[SMEM] + [VMEM] * 4)(flags, own0, even0, even1, done)
     done, odd0, before = lax.optimization_barrier((done, odd0, before))
     far_flags = flags_of_far(before, base)
-    tiles_late, out_odd, own_part0, own_part1, even_part0, even_part1 = call(
-        functools.partial(late_kernel, True), (tiles(8),) + 5 * (sum_shape,), 10**9, 10**6
+    give_shape = shape((2, 2, 64, HALF))
+    tiles_late, out_odd, own_part0, even_part0, give = call(
+        functools.partial(late_kernel, True), (tiles(8),) + 3 * (sum_shape,) + (give_shape,), 10**9, 10**6
     )(in_specs=[SMEM] * 2 + [VMEM] * 9)(
         flags, far_flags, odd0, own0, own1, even0, even1, own_part0, own_part1, even_part0, even_part1
     )
     sketch, pair0 = call(total_kernel, (sum_shape, shape((2, 128, HALF), bf16)), 10**6, 2 * 10**6)(
         in_specs=[VMEM] * 5
-    )(*spread(done, own_part0, own_part1, out_odd, even_part0, even_part1))
+    )(*spread(done, own_part0, out_odd, even_part0, give))
 
     even0 = to_even(pair0)
     odd0 = to_odd(pair0)
@@ -443,22 +459,22 @@
         functools.partial(early_kernel, False), 3 * (sum_shape,), 10**4, 10**4
     )(in_specs=[SMEM] + [VMEM] * 5)(flags, tiles_early, pair0, even0, even1, done)
     done, odd0 = lax.optimization_barrier((done, odd0))
-    out_odd, own_part0, own_part1, even_part0, even_part1 = call(
-        functools.partial(late_kernel, False), 5 * (sum_shape,), 10**9, 10**6
+    out_odd, own_part0, even_part0, give = call(
+        functools.partial(late_kernel, False), 3 * (sum_shape,) + (give_shape,), 10**9, 10**6
     )(in_specs=[SMEM] * 2 + [VMEM] * 10)(
         flags, far_flags, tiles_late, odd0, pair0, pair1, even0, even1,
         own_part0, own_part1, even_part0, even_part1,
     )
     image = call(total_kernel, sum_shape, 10**6, 2 * 10**6)(in_specs=[VMEM] * 5)(
-        *spread(done, own_part0, own_part1, out_odd, even_part0, even_part1)
-    )
-    keep, give, half = call(
+        *spread(done, own_part0, out_odd, even_part0, give)
+    )
+    keep, gram_give, half = call(
         functools.partial(second_gram_kernel, scale),
         (gram_shape, gram_shape, shape((64, HALF))),
         10**8, 10**6,
     )(in_specs=[SMEM, VMEM, VMEM])(core_ref, first_gram, image)
     got = swap(half)
-    mine = sum_over_chips(keep, swap(give))
+    mine = sum_over_chips(keep, swap(gram_give))
     other = swap(mine)
     basis, factor = call(finish_kernel, (shape((64, BLK)), shape((64, 64))), 10**8, 10**6)(
         in_specs=[SMEM] + [VMEM] * 4

time: 124 us -> 125 us (level)
  starting transfers between devices: 43.1 us -> 37.3 us
  waiting for transfers between devices: 34.1 us -> 39.6 us
  blocking collectives: 27.6 us -> 29.8 us
    ppermute x8, starting transfers between devices: 18 us -> 13.6 us  [exchange(): return lax.ppermute(value, 'rows', links)]
    ppermute x8, waiting for transfers between devices: 25 us -> 29 us  [exchange(): return lax.ppermute(value, 'rows', links)]
    pallas_call x1, Pallas kernels: 3.17 us -> 0.65 us  [local(): call(functools.partial(local_kernel, True), (tiles(3),) + 3 * (sum_shape,...]
    pallas_call x1, Pallas kernels: 1.96 us -> 4.34 us  [local(): call(functools.partial(early_kernel, True), (tiles(4),) + 3 * (sum_shape,...]
    all_to_all x1, blocking collectives: 27.6 us -> 29.8 us  [sum_over_chips(): lax.all_to_all(copies, 'rows', 0, 0, axis_index_groups=groups, tiled=True)]
    ppermute x13 -> x11, starting transfers between devices: 16.4 us -> 15 us  [swap(): return lax.ppermute(value, 'cols', [(0, 1), (1, 0)])]
    ppermute x13 -> x11, waiting for transfers between devices: 3.24 us -> 4.71 us  [swap(): return lax.ppermute(value, 'cols', [(0, 1), (1, 0)])]
  transfers between devices with their start and end apart: 23 -> 21, of which waited for: 10 -> 11; matrix products, arithmetic and copies ran while one was open for 0% -> 0% of each run, Pallas kernels for 8% -> 8%
where the time goes in v7:
time: 125 us; the launch traced here: 126 us
  waiting for transfers between devices  39.6 us (32%)
  starting transfers between devices  37.3 us (30%)
  blocking collectives  29.8 us (24%)
  Pallas kernels  18.1 us (14%)
    all_to_all x1, blocking collectives, sum_over_chips(): lax.all_to_all(copies, 'rows', 0, 0, axis_index_groups=groups, tiled=True)  29.8 us
    ppermute x8, waiting for transfers between devices, exchange(): return lax.ppermute(value, 'rows', links)  29 us
    ppermute x11, starting transfers between devices, swap(): return lax.ppermute(value, 'cols', [(0, 1), (1, 0)])  15 us
    ppermute x8, starting transfers between devices, exchange(): return lax.ppermute(value, 'rows', links)  13.6 us
    all_to_all x1, waiting for transfers between devices, sum_over_chips(): lax.all_to_all(copies, 'rows', 0, 0, axis_index_groups=groups, tiled=True)  5.87 us
    all_to_all x1, starting transfers between devices, sum_over_chips(): lax.all_to_all(copies, 'rows', 0, 0, axis_index_groups=groups, tiled=True)  5.32 us
    ppermute x11, waiting for transfers between devices, swap(): return lax.ppermute(value, 'cols', [(0, 1), (1, 0)])  4.71 us
    pallas_call x1, Pallas kernels, local(): call(functools.partial(early_kernel, True), (tiles(4),) + 3 * (sum_shape,...  4.34 us
  transfers between devices with their start and end apart: 21, of which 11 were waited for; matrix products, arithmetic and copies ran while one was open for 0% of the time, Pallas kernels for 8%

profile of v7, /device:TPU:1, one launch (start us, length us, event | category | flops | bytes accessed | tf_op | source)
XLA Modules:
  0.0 126.4 jit_solution(13122691942469237379)
XLA Ops:
  0.6 0.0 copy-start.3
  0.6 0.0 copy-start.4
  0.7 0.0 copy-start.1
  0.7 0.0 copy-start.2
  0.7 1.5 %shard_map.87.refs_0_.refs_1_ = bf16[2,1792,128]{2,1,0:T(8,128)(2,1)S(1)} custom-call(s32[1]{0:T(128)} %bitcast.core_ref, bf16[2048,384]{1,0:T(8,128)(2,1)} %rows_ref.3, bf16[64,2048]{1,0:T(8,128)(2,1)} %bitcast.31), custom_call_target="tpu_custom_call" | custom-call | flops 10000 | bytes 10000 | tf_op jit(solution)/shard_map/pallas_call | solution.py:405
  2.2 2.2 %collective-permute-start.1 = (bf16[2,1792,128]{2,1,0:T(8,128)(2,1)S(1)}, bf16[2,1792,128]{2,1,0:T(8,128)(2,1)S(1)}, u32[]{:S(2)}, u32[]{:S(2)}) collective-permute-start(bf16[2,1792,128]{2,1,0:T(8,128)(2,1)S(1)} %shard_map.87.refs_0_.refs_1_), channel_id=1, source_target_pairs={{0,2},{2,0},{4,6},{6,4},{8,10},{10,8},{12,14},{14,12},{16,18},{18,... | collective-permute-start | bytes 2752520 | tf_op jit(solution)/shard_map/ppermute | solution.py:317
  4.4 1.6 %collective-permute-start.4 = (bf16[2,1792,128]{2,1,0:T(8,128)(2,1)S(1)}, bf16[2,1792,128]{2,1,0:T(8,128)(2,1)}, u32[]{:S(2)}, u32[]{:S(2)}) collective-permute-start(bf16[2,1792,128]{2,1,0:T(8,128)(2,1)S(1)} %shard_map.87.refs_0_.refs_1_), channel_id=1, source_target_pairs={{2,4},{4,2},{6,8},{8,6},{10,12},{12,10},{14,16},{16,14},{18,20},{2... | collective-permute-start | bytes 2752520 | tf_op jit(solution)/shard_map/ppermute | solution.py:317
  6.0 1.5 %shard_map.86.refs_1_.refs_2_ = bf16[2,1792,128]{2,1,0:T(8,128)(2,1)S(1)} custom-call(s32[1]{0:T(128)} %bitcast.core_ref, bf16[2048,384]{1,0:T(8,128)(2,1)} %rows_ref.3, bf16[64,2048]{1,0:T(8,128)(2,1)} %bitcast.32), custom_call_target="tpu_custom_call" | custom-call | flops 10000 | bytes 10000 | tf_op jit(solution)/shard_map/pallas_call | solution.py:405
  7.6 1.2 collective-permute-start
  8.8 0.8 collective-permute-done
  9.6 0.1 pad_add_fusion
  9.7 0.1 and_reduce_fusion
  9.8 0.6 shard_map.88
  10.4 12.8 %collective-permute-done.1.refs_1_.refs_3_ = bf16[2,1792,128]{2,1,0:T(8,128)(2,1)S(1)} collective-permute-done((bf16[2,1792,128]{2,1,0:T(8,128)(2,1)S(1)}, bf16[2,1792,128]{2,1,0:T(8,128)(2,1)S(1)}, u32[]{:S(2)}, u32[]{:S(2)}) %collective-permute-start.1) | collective-permute-done | bytes 917536 | tf_op jit(solution)/shard_map/ppermute | solution.py:317
  23.3 0.1 slice_bitcast_fusion.1
  23.3 2.6 %collective-permute-start.2 = (bf16[1792,128]{1,0:T(8,128)(2,1)S(1)}, bf16[1792,128]{1,0:T(8,128)(2,1)S(1)}, u32[]{:S(2)}, u32[]{:S(2)}) collective-permute-start(bf16[1792,128]{1,0:T(8,128)(2,1)S(1)} %get-tuple-element.80), channel_id=1, source_target_pairs={{0,1},{1,0},{2,3},{3,2},{4,5},{5,4},{6,7},{7,6},{8,9},{9,8},{10,11... | collective-permute-start | bytes 1376264 | tf_op jit(solution)/shard_map/ppermute | solution.py:329
  25.9 0.1 collective-permute-start.3
  26.0 3.4 %collective-permute-start.5 = (s32[8,2]{0,1:T(2,128)S(1)}, s32[8,2]{0,1:T(2,128)S(1)}, u32[]{:S(2)}, u32[]{:S(2)}) collective-permute-start(s32[8,2]{0,1:T(2,128)S(1)} %pad_add_fusion), channel_id=1, source_target_pairs={{0,2},{2,4},{4,6},{6,8},{8,10},{10,12},{12,14},{14,16},{16,18},{18... | collective-permute-start | bytes 200 | tf_op jit(solution)/shard_map/ppermute | solution.py:354
  29.4 0.0 collective-permute-done.2
  29.4 0.0 collective-permute-done.3
  29.4 0.1 pad_maximum_fusion.refs_2_.refs_4_
  29.5 4.3 %shard_map.89 = (bf16[4,2,512,512]{3,2,1,0:T(8,128)(2,1)S(1)}, f32[2,64,512]{2,1,0:T(8,128)S(1)}, f32[2,64,512]{2,1,0:T(8,128)S(1)}, f32[2,64,512]{2,1,0:T(8,128)S(1)}) custom-call(s32[11]{0:T(128)S(1)} %convert_element_type.6.flags_ref, bf16[2,1792,128]{2,1,0:T(8,128)(2,1)S(1)} %shard_map.87.refs_0_.refs_1_, ...), custom_call_target="tpu_custom_call" | custom-call | flops 10000 | bytes 10000 | tf_op jit(solution)/shard_map/pallas_call | solution.py:432
  33.9 0.0 collective-permute-done.5
  33.9 0.0 collective-permute-done.4.refs_0_
  33.9 0.2 and_reduce_fusion.1
  34.1 1.4 %shard_map.90 = (bf16[8,2,512,512]{3,2,1,0:T(8,128)(2,1)S(1)}, f32[2,64,512]{2,1,0:T(8,128)S(1)}, f32[2,64,512]{2,1,0:T(8,128)S(1)}, f32[2,64,512]{2,1,0:T(8,128)S(1)}, f32[2,2,64,512]{3,2,1,0:T(8,128)S(1)}) custom-call(s32[11]{0:T(128)S(1)} %convert_element_type.6.flags_ref, s32[4]{0:T(128)S(1)} %convert_element_type.7.far_ref, ...), custom_call_target="tpu_custom_call" | custom-call | flops 1000000000 | bytes 1000000 | tf_op jit(solution)/shard_map/pallas_call | solution.py:438
  35.5 0.8 collective-permute-start.6
  36.3 0.7 collective-permute-start.7
  37.0 0.9 collective-permute-done.6.parts_other
  37.9 3.0 %collective-permute-start.8 = (f32[2,64,512]{2,1,0:T(8,128)S(1)}, f32[2,64,512]{2,1,0:T(8,128)S(1)}, u32[]{:S(2)}, u32[]{:S(2)}) collective-permute-start(f32[2,64,512]{2,1,0:T(8,128)S(1)} %fusion.1), channel_id=1, source_target_pairs={{0,2},{2,0},{4,6},{6,4},{8,10},{10,8},{12,14},{14,12},{16,18},{18,... | collective-permute-start | bytes 786440 | tf_op jit(solution)/shard_map/ppermute | solution.py:317
  40.8 0.0 collective-permute-done.7.from_odd
  40.8 6.5 %collective-permute-done.8.from_even = f32[2,64,512]{2,1,0:T(8,128)S(1)} collective-permute-done((f32[2,64,512]{2,1,0:T(8,128)S(1)}, f32[2,64,512]{2,1,0:T(8,128)S(1)}, u32[]{:S(2)}, u32[]{:S(2)}) %collective-permute-start.8) | collective-permute-done | bytes 262176 | tf_op jit(solution)/shard_map/ppermute | solution.py:317
  47.3 0.1 shard_map.91
  47.4 1.2 collective-permute-start.9
  48.6 0.7 collective-permute-start.13
  49.3 1.5 %collective-permute-start.12 = (bf16[2,128,512]{2,1,0:T(8,128)(2,1)S(1)}, bf16[2,128,512]{2,1,0:T(8,128)(2,1)S(1)}, u32[]{:S(2)}, u32[]{:S(2)}) collective-permute-start(bf16[2,128,512]{2,1,0:T(8,128)(2,1)S(1)} %get-tuple-element.60.refs_1_.refs_2_), channel_id=1, source_target_pairs={{0,1},{1,0},{2,3},{3,2},{4,5},{5,4},{6,7},{7,6},{8,9},{9,8},{10,11... | collective-permute-start | bytes 786440 | tf_op jit(solution)/shard_map/ppermute | solution.py:329
  50.8 3.7 %collective-permute-done.9.refs_2_.refs_4_ = bf16[2,128,512]{2,1,0:T(8,128)(2,1)S(1)} collective-permute-done((bf16[2,128,512]{2,1,0:T(8,128)(2,1)S(1)}, bf16[2,128,512]{2,1,0:T(8,128)(2,1)S(1)}, u32[]{:S(2)}, u32[]{:S(2)}) %collective-permute-start.9) | collective-permute-done | bytes 262176 | tf_op jit(solution)/shard_map/ppermute | solution.py:317
  54.6 1.8 %collective-permute-start.10 = (bf16[128,512]{1,0:T(8,128)(2,1)S(1)}, bf16[128,512]{1,0:T(8,128)(2,1)S(1)}, u32[]{:S(2)}, u32[]{:S(2)}) collective-permute-start(bf16[128,512]{1,0:T(8,128)(2,1)S(1)} %get-tuple-element.82), channel_id=1, source_target_pairs={{0,1},{1,0},{2,3},{3,2},{4,5},{5,4},{6,7},{7,6},{8,9},{9,8},{10,11... | collective-permute-start | bytes 393224 | tf_op jit(solution)/shard_map/ppermute | solution.py:329
  56.3 0.3 collective-permute-start.11
  56.6 0.7 shard_map.93
  57.3 0.0 collective-permute-done.10
  57.3 0.4 collective-permute-done.11
  57.7 2.5 %shard_map.94 = (f32[2,64,512]{2,1,0:T(8,128)S(1)}, f32[2,64,512]{2,1,0:T(8,128)S(1)}, f32[2,64,512]{2,1,0:T(8,128)S(1)}) custom-call(s32[11]{0:T(128)S(1)} %convert_element_type.6.flags_ref, bf16[4,2,512,512]{3,2,1,0:T(8,128)(2,1)S(1)} %get-tuple-element.59.refs_0_, bf16[2,128,512]{2,1,0:T(8,128)(2,1)S(1)} %get-tuple-element.60.refs_1_.refs_2_, ...), custom_call_target="tpu_custom_call" | custom-call | flops 10000 | bytes 10000 | tf_op jit(solution)/shard_map/pallas_call | solution.py:458
  60.3 0.0 collective-permute-done.13.refs_1_
  60.3 0.8 shard_map.95
  61.0 0.4 collective-permute-start.14
  61.4 0.7 collective-permute-start.15
  62.1 1.0 collective-permute-done.14.parts_other
  63.1 3.6 %collective-permute-start.16 = (f32[2,64,512]{2,1,0:T(8,128)S(1)}, f32[2,64,512]{2,1,0:T(8,128)S(1)}, u32[]{:S(2)}, u32[]{:S(2)}) collective-permute-start(f32[2,64,512]{2,1,0:T(8,128)S(1)} %fusion), channel_id=1, source_target_pairs={{0,2},{2,0},{4,6},{6,4},{8,10},{10,8},{12,14},{14,12},{16,18},{18,... | collective-permute-start | bytes 786440 | tf_op jit(solution)/shard_map/ppermute | solution.py:317
  66.7 0.4 shard_map.92.first_ref
  67.1 6.0 %collective-permute-done.16.from_even = f32[2,64,512]{2,1,0:T(8,128)S(1)} collective-permute-done((f32[2,64,512]{2,1,0:T(8,128)S(1)}, f32[2,64,512]{2,1,0:T(8,128)S(1)}, u32[]{:S(2)}, u32[]{:S(2)}) %collective-permute-start.16) | collective-permute-done | bytes 262176 | tf_op jit(solution)/shard_map/ppermute | solution.py:317
  73.1 0.1 shard_map.96.value_ref
  73.2 0.4 shard_map.97
  73.6 0.9 collective-permute-start.17
  74.5 0.8 collective-permute-done.17.refs_1_
  75.4 29.8 %all_to_all.10.refs_0_ = f32[16,32,128]{2,1,0:T(8,128)S(1)} all-to-all(f32[16,32,128]{2,1,0:T(8,128)S(1)} %shard_map.98), channel_id=1, replica_groups={{0,2,4,6,64,66,68,70,128,130,132,134,192,194,196,198},{8,10,12,14,72,74..., dimensions={0} | all-to-all | bytes 524288 | tf_op jit(solution)/shard_map/all_to_all | solution.py:387
  105.2 0.7 shard_map.99
  105.9 5.3 %all-to-all-start.1 = ((f32[8,32,128]{2,1,0:T(8,128)}), f32[8,32,128]{2,1,0:T(8,128)S(1)}, u32[]{:S(2)}, u32[]{:S(2)}) async-start(f32[8,32,128]{2,1,0:T(8,128)} %shard_map.99), calls=%async_computation.1 | async-start | bytes 262144 | tf_op jit(solution)/shard_map/all_to_all | solution.py:387
  111.2 2.2 %collective-permute-start.19 = (f32[64,512]{1,0:T(8,128)S(1)}, f32[64,512]{1,0:T(8,128)S(1)}, u32[]{:S(2)}, u32[]{:S(2)}) collective-permute-start(f32[64,512]{1,0:T(8,128)S(1)} %get-tuple-element.77), channel_id=1, source_target_pairs={{0,1},{1,0},{2,3},{3,2},{4,5},{5,4},{6,7},{7,6},{8,9},{9,8},{10,11... | collective-permute-start | bytes 393224 | tf_op jit(solution)/shard_map/ppermute | solution.py:329
  113.4 5.9 %all-to-all-done.1 = f32[8,32,128]{2,1,0:T(8,128)S(1)} async-done(((f32[8,32,128]{2,1,0:T(8,128)}), f32[8,32,128]{2,1,0:T(8,128)S(1)}, u32[]{:S(2)}, u32[]{:S(2)}) %all-to-all-start.1) | async-done | bytes 131104 | tf_op jit(solution)/shard_map/all_to_all | solution.py:387
  119.3 3.3 %collective-permute-start.18 = (f32[32,128]{1,0:T(8,128)S(1)}, f32[32,128]{1,0:T(8,128)S(1)}, u32[]{:S(2)}, u32[]{:S(2)}) collective-permute-start(f32[32,128]{1,0:T(8,128)S(1)} %reduce_sum.9.mine_ref), channel_id=1, source_target_pairs={{0,1},{1,0},{2,3},{3,2},{4,5},{5,4},{6,7},{7,6},{8,9},{9,8},{10,11... | collective-permute-start | bytes 49160 | tf_op jit(solution)/shard_map/ppermute | solution.py:329
  122.5 0.0 collective-permute-done.19.got_ref
  122.5 0.8 collective-permute-done.18.other_ref
  123.4 3.0 %shard_map.100 = (f32[64,1024]{1,0:T(8,128)}, f32[64,64]{1,0:T(8,128)}) custom-call(s32[1]{0:T(128)} %bitcast.core_ref, f32[32,128]{1,0:T(8,128)S(1)} %reduce_sum.9.mine_ref, f32[32,128]{1,0:T(8,128)S(1)} %collective-permute-done.18.other_ref, f32[2,64,512]{2,1,0:T(8,128)S(1)} %shard_map.96.value_ref, f32[64,512]{1,0:T(8,128)S(1)} %collective-permute-done.19.got_ref), custom_call_target="tpu_custom_call" | custom-call | flops 100000000 | bytes 1000000 | tf_op jit(solution)/shard_map/pallas_call | solution.py:479
  (22 shorter events, 0.2 us)
Async XLA Ops:
  0.6 8.2 %copy-start.3 = (s32[11]{0:T(128)S(1)}, s32[11]{0:T(128)}, u32[]{:S(2)}) copy-start(s32[11]{0:T(128)} %constant.40.clone) | copy-start | bytes 136
  0.6 8.1 %copy-start.4 = (s32[11]{0:T(128)S(1)}, s32[11]{0:T(128)}, u32[]{:S(2)}) copy-start(s32[11]{0:T(128)} %constant.39.clone) | copy-start | bytes 136
  0.7 6.9 %copy-start = (s32[4,2]{0,1:T(2,128)S(1)}, s32[4,2]{0,1:T(2,128)}, u32[]{:S(2)}) copy-start(s32[4,2]{0,1:T(2,128)} %param.9) | copy-start | bytes 100
  0.7 25.3 %copy-start.1 = (s32[4]{0:T(128)S(1)}, s32[4]{0:T(128)}, u32[]{:S(2)}) copy-start(s32[4]{0:T(128)} %constant.42.clone) | copy-start | bytes 52
  0.7 25.3 %copy-start.2 = (s32[4]{0:T(128)S(1)}, s32[4]{0:T(128)}, u32[]{:S(2)}) copy-start(s32[4]{0:T(128)} %constant.41.clone) | copy-start | bytes 52
  2.2 21.0 %collective-permute-start.1 = (bf16[2,1792,128]{2,1,0:T(8,128)(2,1)S(1)}, bf16[2,1792,128]{2,1,0:T(8,128)(2,1)S(1)}, u32[]{:S(2)}, u32[]{:S(2)}) collective-permute-start(bf16[2,1792,128]{2,1,0:T(8,128)(2,1)S(1)} %shard_map.87.refs_0_.refs_1_), channel_id=1, source_target_pairs={{0,2},{2,0},{4,6},{6,4},{8,10},{10,8},{12,14},{14,12},{16,18},{18,... | collective-permute-start | bytes 2752520 | tf_op jit(solution)/shard_map/ppermute | solution.py:317
  4.4 29.4 %collective-permute-start.4 = (bf16[2,1792,128]{2,1,0:T(8,128)(2,1)S(1)}, bf16[2,1792,128]{2,1,0:T(8,128)(2,1)}, u32[]{:S(2)}, u32[]{:S(2)}) collective-permute-start(bf16[2,1792,128]{2,1,0:T(8,128)(2,1)S(1)} %shard_map.87.refs_0_.refs_1_), channel_id=1, source_target_pairs={{2,4},{4,2},{6,8},{8,6},{10,12},{12,10},{14,16},{16,14},{18,20},{2... | collective-permute-start | bytes 2752520 | tf_op jit(solution)/shard_map/ppermute | solution.py:317
  7.6 2.0 %collective-permute-start = (s32[4,2]{0,1:T(2,128)S(1)}, s32[4,2]{0,1:T(2,128)S(1)}, u32[]{:S(2)}, u32[]{:S(2)}) collective-permute-start(s32[4,2]{0,1:T(2,128)S(1)} %copy-done), channel_id=1, source_target_pairs={{0,1},{1,0},{2,3},{3,2},{4,5},{5,4},{6,7},{7,6},{8,9},{9,8},{10,11... | collective-permute-start | bytes 104 | tf_op jit(solution)/shard_map/ppermute | solution.py:329
  23.3 6.1 %collective-permute-start.2 = (bf16[1792,128]{1,0:T(8,128)(2,1)S(1)}, bf16[1792,128]{1,0:T(8,128)(2,1)S(1)}, u32[]{:S(2)}, u32[]{:S(2)}) collective-permute-start(bf16[1792,128]{1,0:T(8,128)(2,1)S(1)} %get-tuple-element.80), channel_id=1, source_target_pairs={{0,1},{1,0},{2,3},{3,2},{4,5},{5,4},{6,7},{7,6},{8,9},{9,8},{10,11... | collective-permute-start | bytes 1376264 | tf_op jit(solution)/shard_map/ppermute | solution.py:329
  25.9 3.5 %collective-permute-start.3 = (bf16[1792,128]{1,0:T(8,128)(2,1)S(1)}, bf16[1792,128]{1,0:T(8,128)(2,1)S(1)}, u32[]{:S(2)}, u32[]{:S(2)}) collective-permute-start(bf16[1792,128]{1,0:T(8,128)(2,1)S(1)} %get-tuple-element.81), channel_id=1, source_target_pairs={{0,1},{1,0},{2,3},{3,2},{4,5},{5,4},{6,7},{7,6},{8,9},{9,8},{10,11... | collective-permute-start | bytes 1376264 | tf_op jit(solution)/shard_map/ppermute | solution.py:329
  26.0 7.8 %collective-permute-start.5 = (s32[8,2]{0,1:T(2,128)S(1)}, s32[8,2]{0,1:T(2,128)S(1)}, u32[]{:S(2)}, u32[]{:S(2)}) collective-permute-start(s32[8,2]{0,1:T(2,128)S(1)} %pad_add_fusion), channel_id=1, source_target_pairs={{0,2},{2,4},{4,6},{6,8},{8,10},{10,12},{12,14},{14,16},{16,18},{18... | collective-permute-start | bytes 200 | tf_op jit(solution)/shard_map/ppermute | solution.py:354
  35.5 2.3 %collective-permute-start.6 = (f32[2,2,64,512]{3,2,1,0:T(8,128)S(1)}, f32[2,2,64,512]{3,2,1,0:T(8,128)S(1)}, u32[]{:S(2)}, u32[]{:S(2)}) collective-permute-start(f32[2,2,64,512]{3,2,1,0:T(8,128)S(1)} %get-tuple-element.55), channel_id=1, source_target_pairs={{0,1},{1,0},{2,3},{3,2},{4,5},{5,4},{6,7},{7,6},{8,9},{9,8},{10,11... | collective-permute-start | bytes 1572872 | tf_op jit(solution)/shard_map/ppermute | solution.py:329
  36.3 4.6 %collective-permute-start.7 = (f32[2,64,512]{2,1,0:T(8,128)S(1)}, f32[2,64,512]{2,1,0:T(8,128)S(1)}, u32[]{:S(2)}, u32[]{:S(2)}) collective-permute-start(f32[2,64,512]{2,1,0:T(8,128)S(1)} %get-tuple-element.56), channel_id=1, source_target_pairs={{2,4},{4,2},{6,8},{8,6},{10,12},{12,10},{14,16},{16,14},{18,20},{2... | collective-permute-start | bytes 786440 | tf_op jit(solution)/shard_map/ppermute | solution.py:317
  37.9 9.4 %collective-permute-start.8 = (f32[2,64,512]{2,1,0:T(8,128)S(1)}, f32[2,64,512]{2,1,0:T(8,128)S(1)}, u32[]{:S(2)}, u32[]{:S(2)}) collective-permute-start(f32[2,64,512]{2,1,0:T(8,128)S(1)} %fusion.1), channel_id=1, source_target_pairs={{0,2},{2,0},{4,6},{6,4},{8,10},{10,8},{12,14},{14,12},{16,18},{18,... | collective-permute-start | bytes 786440 | tf_op jit(solution)/shard_map/ppermute | solution.py:317
  47.4 7.1 %collective-permute-start.9 = (bf16[2,128,512]{2,1,0:T(8,128)(2,1)S(1)}, bf16[2,128,512]{2,1,0:T(8,128)(2,1)S(1)}, u32[]{:S(2)}, u32[]{:S(2)}) collective-permute-start(bf16[2,128,512]{2,1,0:T(8,128)(2,1)S(1)} %get-tuple-element.60.refs_1_.refs_2_), channel_id=1, source_target_pairs={{0,2},{2,0},{4,6},{6,4},{8,10},{10,8},{12,14},{14,12},{16,18},{18,... | collective-permute-start | bytes 786440 | tf_op jit(solution)/shard_map/ppermute | solution.py:317
  48.6 11.6 %collective-permute-start.13 = (bf16[2,128,512]{2,1,0:T(8,128)(2,1)S(1)}, bf16[2,128,512]{2,1,0:T(8,128)(2,1)S(1)}, u32[]{:S(2)}, u32[]{:S(2)}) collective-permute-start(bf16[2,128,512]{2,1,0:T(8,128)(2,1)S(1)} %get-tuple-element.60.refs_1_.refs_2_), channel_id=1, source_target_pairs={{2,4},{4,2},{6,8},{8,6},{10,12},{12,10},{14,16},{16,14},{18,20},{2... | collective-permute-start | bytes 786440 | tf_op jit(solution)/shard_map/ppermute | solution.py:317
  49.3 7.3 %collective-permute-start.12 = (bf16[2,128,512]{2,1,0:T(8,128)(2,1)S(1)}, bf16[2,128,512]{2,1,0:T(8,128)(2,1)S(1)}, u32[]{:S(2)}, u32[]{:S(2)}) collective-permute-start(bf16[2,128,512]{2,1,0:T(8,128)(2,1)S(1)} %get-tuple-element.60.refs_1_.refs_2_), channel_id=1, source_target_pairs={{0,1},{1,0},{2,3},{3,2},{4,5},{5,4},{6,7},{7,6},{8,9},{9,8},{10,11... | collective-permute-start | bytes 786440 | tf_op jit(solution)/shard_map/ppermute | solution.py:329
  54.6 2.8 %collective-permute-start.10 = (bf16[128,512]{1,0:T(8,128)(2,1)S(1)}, bf16[128,512]{1,0:T(8,128)(2,1)S(1)}, u32[]{:S(2)}, u32[]{:S(2)}) collective-permute-start(bf16[128,512]{1,0:T(8,128)(2,1)S(1)} %get-tuple-element.82), channel_id=1, source_target_pairs={{0,1},{1,0},{2,3},{3,2},{4,5},{5,4},{6,7},{7,6},{8,9},{9,8},{10,11... | collective-permute-start | bytes 393224 | tf_op jit(solution)/shard_map/ppermute | solution.py:329
  56.3 1.3 %collective-permute-start.11 = (bf16[128,512]{1,0:T(8,128)(2,1)S(1)}, bf16[128,512]{1,0:T(8,128)(2,1)S(1)}, u32[]{:S(2)}, u32[]{:S(2)}) collective-permute-start(bf16[128,512]{1,0:T(8,128)(2,1)S(1)} %get-tuple-element.83), channel_id=1, source_target_pairs={{0,1},{1,0},{2,3},{3,2},{4,5},{5,4},{6,7},{7,6},{8,9},{9,8},{10,11... | collective-permute-start | bytes 393224 | tf_op jit(solution)/shard_map/ppermute | solution.py:329
  61.0 2.0 %collective-permute-start.14 = (f32[2,2,64,512]{3,2,1,0:T(8,128)S(1)}, f32[2,2,64,512]{3,2,1,0:T(8,128)S(1)}, u32[]{:S(2)}, u32[]{:S(2)}) collective-permute-start(f32[2,2,64,512]{3,2,1,0:T(8,128)S(1)} %get-tuple-element.72), channel_id=1, source_target_pairs={{0,1},{1,0},{2,3},{3,2},{4,5},{5,4},{6,7},{7,6},{8,9},{9,8},{10,11... | collective-permute-start | bytes 1572872 | tf_op jit(solution)/shard_map/ppermute | solution.py:329
  61.4 5.7 %collective-permute-start.15 = (f32[2,64,512]{2,1,0:T(8,128)S(1)}, f32[2,64,512]{2,1,0:T(8,128)S(1)}, u32[]{:S(2)}, u32[]{:S(2)}) collective-permute-start(f32[2,64,512]{2,1,0:T(8,128)S(1)} %get-tuple-element.73), channel_id=1, source_target_pairs={{2,4},{4,2},{6,8},{8,6},{10,12},{12,10},{14,16},{16,14},{18,20},{2... | collective-permute-start | bytes 786440 | tf_op jit(solution)/shard_map/ppermute | solution.py:317
  63.1 10.0 %collective-permute-start.16 = (f32[2,64,512]{2,1,0:T(8,128)S(1)}, f32[2,64,512]{2,1,0:T(8,128)S(1)}, u32[]{:S(2)}, u32[]{:S(2)}) collective-permute-start(f32[2,64,512]{2,1,0:T(8,128)S(1)} %fusion), channel_id=1, source_target_pairs={{0,2},{2,0},{4,6},{6,4},{8,10},{10,8},{12,14},{14,12},{16,18},{18,... | collective-permute-start | bytes 786440 | tf_op jit(solution)/shard_map/ppermute | solution.py:317
  73.6 1.7 %collective-permute-start.17 = (f32[32,128]{1,0:T(8,128)S(1)}, f32[32,128]{1,0:T(8,128)S(1)}, u32[]{:S(2)}, u32[]{:S(2)}) collective-permute-start(f32[32,128]{1,0:T(8,128)S(1)} %get-tuple-element.76), channel_id=1, source_target_pairs={{0,1},{1,0},{2,3},{3,2},{4,5},{5,4},{6,7},{7,6},{8,9},{9,8},{10,11... | collective-permute-start | bytes 49160 | tf_op jit(solution)/shard_map/ppermute | solution.py:329
  105.9 13.4 %all-to-all-start.1 = ((f32[8,32,128]{2,1,0:T(8,128)}), f32[8,32,128]{2,1,0:T(8,128)S(1)}, u32[]{:S(2)}, u32[]{:S(2)}) async-start(f32[8,32,128]{2,1,0:T(8,128)} %shard_map.99), calls=%async_computation.1 | async-start | bytes 262144 | tf_op jit(solution)/shard_map/all_to_all | solution.py:387
  111.2 11.3 %collective-permute-start.19 = (f32[64,512]{1,0:T(8,128)S(1)}, f32[64,512]{1,0:T(8,128)S(1)}, u32[]{:S(2)}, u32[]{:S(2)}) collective-permute-start(f32[64,512]{1,0:T(8,128)S(1)} %get-tuple-element.77), channel_id=1, source_target_pairs={{0,1},{1,0},{2,3},{3,2},{4,5},{5,4},{6,7},{7,6},{8,9},{9,8},{10,11... | collective-permute-start | bytes 393224 | tf_op jit(solution)/shard_map/ppermute | solution.py:329
  119.3 4.1 %collective-permute-start.18 = (f32[32,128]{1,0:T(8,128)S(1)}, f32[32,128]{1,0:T(8,128)S(1)}, u32[]{:S(2)}, u32[]{:S(2)}) collective-permute-start(f32[32,128]{1,0:T(8,128)S(1)} %reduce_sum.9.mine_ref), channel_id=1, source_target_pairs={{0,1},{1,0},{2,3},{3,2},{4,5},{5,4},{6,7},{7,6},{8,9},{9,8},{10,11... | collective-permute-start | bytes 49160 | tf_op jit(solution)/shard_map/ppermute | solution.py:329

commit v8 on v7

--- a/solution.py
+++ b/solution.py
@@ -205,16 +205,28 @@
                 )
 
 
-def total_kernel(done, part_mine, parts_other, from_odd, from_even, sum_ref, pair_ref=None):
+def put_pair(pair_ref, block, value):
+    high = value.astype(jnp.bfloat16)
+    pair_ref[block, :64] = high
+    pair_ref[block, 64:] = (value - high.astype(jnp.float32)).astype(jnp.bfloat16)
+
+
+def partial_kernel(done, part_mine, parts_other, from_even, sum_ref):
     for block in range(2):
-        value = (
-            done[block] + part_mine[block] + parts_other[0, block] + from_odd[block] + from_even[block]
-        )
+        sum_ref[block] = done[block] + part_mine[block] + parts_other[0, block] + from_even[block]
+
+
+def pair_kernel(partial, ours, pair_ref):
+    for block in range(2):
+        put_pair(pair_ref, block, partial[block] + ours[block])
+
+
+def total_kernel(partial, from_odd, sum_ref, pair_ref=None):
+    for block in range(2):
+        value = partial[block] + from_odd[block]
         sum_ref[block] = value
         if pair_ref is not None:
-            high = value.astype(jnp.bfloat16)
-            pair_ref[block, :64] = high
-            pair_ref[block, 64:] = (value - high.astype(jnp.float32)).astype(jnp.bfloat16)
+            put_pair(pair_ref, block, value)
 
 
 def gram_of(value_ref, scale):
@@ -373,7 +385,10 @@
     from_odd = to_odd(out_odd)
     got = swap(give)
     from_even = to_even(even0 + got[1])
-    return done, own0, got, from_odd, from_even
+    partial = call(partial_kernel, shape((2, 64, HALF)), 10**4, 10**4)(in_specs=[VMEM] * 4)(
+        done, own0, got, from_even
+    )
+    return partial, from_odd
 
 
 def sum_over_chips(*values):
@@ -440,32 +455,35 @@
     )(in_specs=[SMEM] * 2 + [VMEM] * 9)(
         flags, far_flags, odd0, own0, own1, even0, even1, own_part0, own_part1, even_part0, even_part1
     )
-    sketch, pair0 = call(total_kernel, (sum_shape, shape((2, 128, HALF), bf16)), 10**6, 2 * 10**6)(
-        in_specs=[VMEM] * 5
-    )(*spread(done, own_part0, out_odd, even_part0, give))
-
+    partial, from_odd = spread(done, own_part0, out_odd, even_part0, give)
+    odd_partial, odd_ours = to_odd(partial), out_odd
+    sketch, pair0 = call(total_kernel, (sum_shape, shape((2, 128, HALF), bf16)), 10**4, 10**4)(
+        in_specs=[VMEM] * 2
+    )(partial, from_odd)
     even0 = to_even(pair0)
-    odd0 = to_odd(pair0)
     gram_shape = shape((32, 128))
     first_gram = call(functools.partial(gram_kernel, scale), gram_shape, 10**4, 10**4)(
         in_specs=[VMEM]
     )(sketch)
-    pair1 = swap(pair0)
+    odd0 = call(pair_kernel, shape((2, 128, HALF), bf16), 10**4, 10**4)(in_specs=[VMEM] * 2)(
+        odd_partial, odd_ours
+    )
+    pair1, odd0 = lax.optimization_barrier((swap(pair0), odd0))
     done, own_part0, own_part1 = call(
-        functools.partial(local_kernel, False), 3 * (sum_shape,), 10**4, 10**4
+        functools.partial(local_kernel, False), 3 * (sum_shape,), 10**11, 10**4
     )(in_specs=[SMEM] + [VMEM] * 3)(flags, tiles_own, pair0, pair1)
+    done, even0 = lax.optimization_barrier((done, even0))
     even1 = swap_blocks(even0)
     done, even_part0, even_part1 = call(
         functools.partial(early_kernel, False), 3 * (sum_shape,), 10**4, 10**4
     )(in_specs=[SMEM] + [VMEM] * 5)(flags, tiles_early, pair0, even0, even1, done)
-    done, odd0 = lax.optimization_barrier((done, odd0))
     out_odd, own_part0, even_part0, give = call(
         functools.partial(late_kernel, False), 3 * (sum_shape,) + (give_shape,), 10**9, 10**6
     )(in_specs=[SMEM] * 2 + [VMEM] * 10)(
         flags, far_flags, tiles_late, odd0, pair0, pair1, even0, even1,
         own_part0, own_part1, even_part0, even_part1,
     )
-    image = call(total_kernel, sum_shape, 10**6, 2 * 10**6)(in_specs=[VMEM] * 5)(
+    image = call(total_kernel, sum_shape, 10**4, 10**4)(in_specs=[VMEM] * 2)(
         *spread(done, own_part0, out_odd, even_part0, give)
     )
     keep, gram_give, half = call(

time: 125 us -> 124 us (level); the launches traced: 126 us -> 124 us
    ppermute x8, starting transfers between devices: 13.6 us -> 16.7 us  [exchange(): return lax.ppermute(value, 'rows', links)]
    ppermute x8, waiting for transfers between devices: 29 us -> 26.1 us  [exchange(): return lax.ppermute(value, 'rows', links)]
    pallas_call x1, Pallas kernels: 4.34 us -> 1.88 us  [local(): call(functools.partial(early_kernel, True), (tiles(4),) + 3 * (sum_shape,...]
    pallas_call x1, Pallas kernels: 0.65 us -> 3.05 us  [local(): call(functools.partial(local_kernel, True), (tiles(3),) + 3 * (sum_shape,...]
    ppermute x11, waiting for transfers between devices: 4.71 us -> 6.73 us  [swap(): return lax.ppermute(value, 'cols', [(0, 1), (1, 0)])]
    ppermute x11, starting transfers between devices: 15 us -> 12.9 us  [swap(): return lax.ppermute(value, 'cols', [(0, 1), (1, 0)])]
    all_to_all x1, starting transfers between devices: 5.32 us -> 3.37 us  [sum_over_chips(): lax.all_to_all(copies, 'rows', 0, 0, axis_index_groups=groups, tiled=True)]
    pallas_call x3 -> x6, Pallas kernels: 0.85 us -> 2.17 us  [the longest x1 1.9 us: local(): call(functools.partial(local_kernel, False), 3 * (sum_shape,), 10 ** 11,...]
  transfers between devices with their start and end apart: 21 -> 21, of which waited for: 11 -> 12; matrix products, arithmetic and copies ran while one was open for 0% -> 0% of each run, Pallas kernels for 8% -> 7%
where the time goes in v8:
time: 124 us
  waiting for transfers between devices  38.7 us (31%)
  starting transfers between devices  36.4 us (29%)
  blocking collectives  29 us (23%)
  Pallas kernels  18.1 us (15%)
    all_to_all x1, blocking collectives, sum_over_chips(): lax.all_to_all(copies, 'rows', 0, 0, axis_index_groups=groups, tiled=True)  29 us
    ppermute x8, waiting for transfers between devices, exchange(): return lax.ppermute(value, 'rows', links)  26.1 us
    ppermute x8, starting transfers between devices, exchange(): return lax.ppermute(value, 'rows', links)  16.7 us
    ppermute x11, starting transfers between devices, swap(): return lax.ppermute(value, 'cols', [(0, 1), (1, 0)])  12.9 us
    ppermute x11, waiting for transfers between devices, swap(): return lax.ppermute(value, 'cols', [(0, 1), (1, 0)])  6.73 us
    all_to_all x1, waiting for transfers between devices, sum_over_chips(): lax.all_to_all(copies, 'rows', 0, 0, axis_index_groups=groups, tiled=True)  5.91 us
    all_to_all x1, starting transfers between devices, sum_over_chips(): lax.all_to_all(copies, 'rows', 0, 0, axis_index_groups=groups, tiled=True)  3.37 us
    ppermute x1, starting transfers between devices, own_flags_and_list(): lax.ppermute(own, 'rows', [(r, r + 1) for r in range(lax.axis_size('rows'...  3.36 us
  transfers between devices with their start and end apart: 21, of which 12 were waited for; matrix products, arithmetic and copies ran while one was open for 0% of the time, Pallas kernels for 7%

profile of v8, /device:TPU:1, one launch (start us, length us, event | category | flops | bytes accessed | tf_op | source)
XLA Modules:
  0.0 123.9 jit_solution(10846226752074692728)
XLA Ops:
  0.6 0.0 copy-start.3
  0.6 0.0 copy-start.4
  0.7 0.0 copy-start.1
  0.7 0.0 copy-start.2
  0.7 1.5 %shard_map.87.refs_0_.refs_1_ = bf16[2,1792,128]{2,1,0:T(8,128)(2,1)S(1)} custom-call(s32[1]{0:T(128)} %bitcast.core_ref, bf16[2048,384]{1,0:T(8,128)(2,1)} %rows_ref.3, bf16[64,2048]{1,0:T(8,128)(2,1)} %bitcast.31), custom_call_target="tpu_custom_call" | custom-call | flops 10000 | bytes 10000 | tf_op jit(solution)/shard_map/pallas_call | solution.py:420
  2.2 2.2 %collective-permute-start.1 = (bf16[2,1792,128]{2,1,0:T(8,128)(2,1)S(1)}, bf16[2,1792,128]{2,1,0:T(8,128)(2,1)S(1)}, u32[]{:S(2)}, u32[]{:S(2)}) collective-permute-start(bf16[2,1792,128]{2,1,0:T(8,128)(2,1)S(1)} %shard_map.87.refs_0_.refs_1_), channel_id=1, source_target_pairs={{0,2},{2,0},{4,6},{6,4},{8,10},{10,8},{12,14},{14,12},{16,18},{18,... | collective-permute-start | bytes 2752520 | tf_op jit(solution)/shard_map/ppermute | solution.py:329
  4.4 1.6 %collective-permute-start.4 = (bf16[2,1792,128]{2,1,0:T(8,128)(2,1)S(1)}, bf16[2,1792,128]{2,1,0:T(8,128)(2,1)}, u32[]{:S(2)}, u32[]{:S(2)}) collective-permute-start(bf16[2,1792,128]{2,1,0:T(8,128)(2,1)S(1)} %shard_map.87.refs_0_.refs_1_), channel_id=1, source_target_pairs={{2,4},{4,2},{6,8},{8,6},{10,12},{12,10},{14,16},{16,14},{18,20},{2... | collective-permute-start | bytes 2752520 | tf_op jit(solution)/shard_map/ppermute | solution.py:329
  6.0 1.5 %shard_map.86.refs_1_.refs_2_ = bf16[2,1792,128]{2,1,0:T(8,128)(2,1)S(1)} custom-call(s32[1]{0:T(128)} %bitcast.core_ref, bf16[2048,384]{1,0:T(8,128)(2,1)} %rows_ref.3, bf16[64,2048]{1,0:T(8,128)(2,1)} %bitcast.32), custom_call_target="tpu_custom_call" | custom-call | flops 10000 | bytes 10000 | tf_op jit(solution)/shard_map/pallas_call | solution.py:420
  7.6 1.2 collective-permute-start
  8.8 0.8 collective-permute-done
  9.6 0.1 pad_add_fusion
  9.7 0.1 and_reduce_fusion
  9.8 3.0 %shard_map.88 = (bf16[3,2,512,512]{3,2,1,0:T(8,128)(2,1)S(1)}, f32[2,64,512]{2,1,0:T(8,128)S(1)}, f32[2,64,512]{2,1,0:T(8,128)S(1)}, f32[2,64,512]{2,1,0:T(8,128)S(1)}) custom-call(s32[11]{0:T(128)S(1)} %convert_element_type.6.flags_ref, bf16[2,1792,128]{2,1,0:T(8,128)(2,1)S(1)} %shard_map.87.refs_0_.refs_1_, bf16[2,1792,128]{2,1,0:T(8,128)(2,1)S(1)} %shard_map.86.refs_1_.refs_2_), custom_call_target="tpu_custom_call" | custom-call | flops 10000 | bytes 10000 | tf_op jit(solution)/shard_map/pallas_call | solution.py:442
  12.8 10.4 %collective-permute-done.1.refs_1_.refs_3_ = bf16[2,1792,128]{2,1,0:T(8,128)(2,1)S(1)} collective-permute-done((bf16[2,1792,128]{2,1,0:T(8,128)(2,1)S(1)}, bf16[2,1792,128]{2,1,0:T(8,128)(2,1)S(1)}, u32[]{:S(2)}, u32[]{:S(2)}) %collective-permute-start.1) | collective-permute-done | bytes 917536 | tf_op jit(solution)/shard_map/ppermute | solution.py:329
  23.3 0.1 slice_bitcast_fusion.1
  23.3 2.6 %collective-permute-start.2 = (bf16[1792,128]{1,0:T(8,128)(2,1)S(1)}, bf16[1792,128]{1,0:T(8,128)(2,1)S(1)}, u32[]{:S(2)}, u32[]{:S(2)}) collective-permute-start(bf16[1792,128]{1,0:T(8,128)(2,1)S(1)} %get-tuple-element.84), channel_id=1, source_target_pairs={{0,1},{1,0},{2,3},{3,2},{4,5},{5,4},{6,7},{7,6},{8,9},{9,8},{10,11... | collective-permute-start | bytes 1376264 | tf_op jit(solution)/shard_map/ppermute | solution.py:341
  25.9 0.1 collective-permute-start.3
  26.0 3.4 %collective-permute-start.5 = (s32[8,2]{0,1:T(2,128)S(1)}, s32[8,2]{0,1:T(2,128)S(1)}, u32[]{:S(2)}, u32[]{:S(2)}) collective-permute-start(s32[8,2]{0,1:T(2,128)S(1)} %pad_add_fusion), channel_id=1, source_target_pairs={{0,2},{2,4},{4,6},{6,8},{8,10},{10,12},{12,14},{14,16},{16,18},{18... | collective-permute-start | bytes 200 | tf_op jit(solution)/shard_map/ppermute | solution.py:366
  29.4 0.0 collective-permute-done.2
  29.4 0.0 collective-permute-done.3
  29.4 0.1 pad_maximum_fusion.refs_2_.refs_4_
  29.5 1.9 %shard_map.89 = (bf16[4,2,512,512]{3,2,1,0:T(8,128)(2,1)S(1)}, f32[2,64,512]{2,1,0:T(8,128)S(1)}, f32[2,64,512]{2,1,0:T(8,128)S(1)}, f32[2,64,512]{2,1,0:T(8,128)S(1)}) custom-call(s32[11]{0:T(128)S(1)} %convert_element_type.6.flags_ref, bf16[2,1792,128]{2,1,0:T(8,128)(2,1)S(1)} %shard_map.87.refs_0_.refs_1_, ...), custom_call_target="tpu_custom_call" | custom-call | flops 10000 | bytes 10000 | tf_op jit(solution)/shard_map/pallas_call | solution.py:447
  31.4 0.0 collective-permute-done.5
  31.4 0.2 and_reduce_fusion.1
  31.6 1.4 %shard_map.90 = (bf16[8,2,512,512]{3,2,1,0:T(8,128)(2,1)S(1)}, f32[2,64,512]{2,1,0:T(8,128)S(1)}, f32[2,64,512]{2,1,0:T(8,128)S(1)}, f32[2,64,512]{2,1,0:T(8,128)S(1)}, f32[2,2,64,512]{3,2,1,0:T(8,128)S(1)}) custom-call(s32[11]{0:T(128)S(1)} %convert_element_type.6.flags_ref, s32[4]{0:T(128)S(1)} %convert_element_type.7.far_ref, ...), custom_call_target="tpu_custom_call" | custom-call | flops 1000000000 | bytes 1000000 | tf_op jit(solution)/shard_map/pallas_call | solution.py:453
  33.1 0.8 collective-permute-start.6
  33.8 1.5 %collective-permute-done.6.parts_other = f32[2,2,64,512]{3,2,1,0:T(8,128)S(1)} collective-permute-done((f32[2,2,64,512]{3,2,1,0:T(8,128)S(1)}, f32[2,2,64,512]{3,2,1,0:T(8,128)S(1)}, u32[]{:S(2)}, u32[]{:S(2)}) %collective-permute-start.6) | collective-permute-done | bytes 524320 | tf_op jit(solution)/shard_map/ppermute | solution.py:341
  35.4 5.0 %collective-permute-start.7 = (f32[2,64,512]{2,1,0:T(8,128)S(1)}, f32[2,64,512]{2,1,0:T(8,128)S(1)}, u32[]{:S(2)}, u32[]{:S(2)}) collective-permute-start(f32[2,64,512]{2,1,0:T(8,128)S(1)} %fusion.1), channel_id=1, source_target_pairs={{0,2},{2,0},{4,6},{6,4},{8,10},{10,8},{12,14},{14,12},{16,18},{18,... | collective-permute-start | bytes 786440 | tf_op jit(solution)/shard_map/ppermute | solution.py:329
  40.4 0.7 collective-permute-start.8
  41.1 5.7 %collective-permute-done.7.from_even = f32[2,64,512]{2,1,0:T(8,128)S(1)} collective-permute-done((f32[2,64,512]{2,1,0:T(8,128)S(1)}, f32[2,64,512]{2,1,0:T(8,128)S(1)}, u32[]{:S(2)}, u32[]{:S(2)}) %collective-permute-start.7) | collective-permute-done | bytes 262176 | tf_op jit(solution)/shard_map/ppermute | solution.py:329
  46.8 0.7 collective-permute-start.10
  47.5 0.0 collective-permute-done.8.from_odd
  47.5 0.1 shard_map.92
  47.6 1.0 collective-permute-start.9
  48.6 3.1 %collective-permute-start.11 = (bf16[2,128,512]{2,1,0:T(8,128)(2,1)S(1)}, bf16[2,128,512]{2,1,0:T(8,128)(2,1)S(1)}, u32[]{:S(2)}, u32[]{:S(2)}) collective-permute-start(bf16[2,128,512]{2,1,0:T(8,128)(2,1)S(1)} %get-tuple-element.62.refs_1_.refs_2_), channel_id=1, source_target_pairs={{0,2},{2,0},{4,6},{6,4},{8,10},{10,8},{12,14},{14,12},{16,18},{18,... | collective-permute-start | bytes 786440 | tf_op jit(solution)/shard_map/ppermute | solution.py:329
  51.6 0.1 shard_map.94.refs_1_
  51.7 0.0 collective-permute-done.9.refs_2_.refs_3_
  51.7 1.9 %shard_map.95 = (f32[2,64,512]{2,1,0:T(8,128)S(1)}, f32[2,64,512]{2,1,0:T(8,128)S(1)}, f32[2,64,512]{2,1,0:T(8,128)S(1)}) custom-call(s32[11]{0:T(128)S(1)} %convert_element_type.6.flags_ref, bf16[3,2,512,512]{3,2,1,0:T(8,128)(2,1)S(1)} %get-tuple-element.63.refs_0_, bf16[2,128,512]{2,1,0:T(8,128)(2,1)S(1)} %get-tuple-element.62.refs_1_.refs_2_, ...), custom_call_target="tpu_custom_call" | custom-call | flops 99999997952 | bytes 10000 | tf_op jit(solution)/shard_map/pallas_call | solution.py:472
  53.6 4.6 %collective-permute-done.11.refs_2_.refs_4_ = bf16[2,128,512]{2,1,0:T(8,128)(2,1)S(1)} collective-permute-done((bf16[2,128,512]{2,1,0:T(8,128)(2,1)S(1)}, bf16[2,128,512]{2,1,0:T(8,128)(2,1)S(1)}, u32[]{:S(2)}, u32[]{:S(2)}) %collective-permute-start.11) | collective-permute-done | bytes 262176 | tf_op jit(solution)/shard_map/ppermute | solution.py:329
  58.2 0.8 collective-permute-start.12
  59.0 0.3 collective-permute-start.13
  59.3 0.7 collective-permute-done.12
  60.0 0.4 collective-permute-done.13
  60.4 1.3 %shard_map.96 = (f32[2,64,512]{2,1,0:T(8,128)S(1)}, f32[2,64,512]{2,1,0:T(8,128)S(1)}, f32[2,64,512]{2,1,0:T(8,128)S(1)}) custom-call(s32[11]{0:T(128)S(1)} %convert_element_type.6.flags_ref, bf16[4,2,512,512]{3,2,1,0:T(8,128)(2,1)S(1)} %get-tuple-element.61.refs_0_, bf16[2,128,512]{2,1,0:T(8,128)(2,1)S(1)} %get-tuple-element.62.refs_1_.refs_2_, ...), custom_call_target="tpu_custom_call" | custom-call | flops 10000 | bytes 10000 | tf_op jit(solution)/shard_map/pallas_call | solution.py:477
  61.7 0.8 shard_map.97
  62.4 0.4 collective-permute-start.14
  62.8 1.6 %collective-permute-done.14.parts_other = f32[2,2,64,512]{3,2,1,0:T(8,128)S(1)} collective-permute-done((f32[2,2,64,512]{3,2,1,0:T(8,128)S(1)}, f32[2,2,64,512]{3,2,1,0:T(8,128)S(1)}, u32[]{:S(2)}, u32[]{:S(2)}) %collective-permute-start.14) | collective-permute-done | bytes 524320 | tf_op jit(solution)/shard_map/ppermute | solution.py:341
  64.5 2.8 %collective-permute-start.15 = (f32[2,64,512]{2,1,0:T(8,128)S(1)}, f32[2,64,512]{2,1,0:T(8,128)S(1)}, u32[]{:S(2)}, u32[]{:S(2)}) collective-permute-start(f32[2,64,512]{2,1,0:T(8,128)S(1)} %fusion), channel_id=1, source_target_pairs={{0,2},{2,0},{4,6},{6,4},{8,10},{10,8},{12,14},{14,12},{16,18},{18,... | collective-permute-start | bytes 786440 | tf_op jit(solution)/shard_map/ppermute | solution.py:329
  67.3 0.7 collective-permute-start.16
  68.0 0.4 shard_map.93.first_ref
  68.4 5.4 %collective-permute-done.15.from_even = f32[2,64,512]{2,1,0:T(8,128)S(1)} collective-permute-done((f32[2,64,512]{2,1,0:T(8,128)S(1)}, f32[2,64,512]{2,1,0:T(8,128)S(1)}, u32[]{:S(2)}, u32[]{:S(2)}) %collective-permute-start.15) | collective-permute-done | bytes 262176 | tf_op jit(solution)/shard_map/ppermute | solution.py:329
  73.8 0.1 shard_map.98.partial
  73.8 0.0 collective-permute-done.16.from_odd
  73.9 0.4 shard_map.100
  74.3 0.9 collective-permute-start.17
  75.2 0.8 collective-permute-done.17.refs_1_
  76.0 29.0 %all_to_all.10.refs_0_ = f32[16,32,128]{2,1,0:T(8,128)S(1)} all-to-all(f32[16,32,128]{2,1,0:T(8,128)S(1)} %shard_map.101), channel_id=1, replica_groups={{0,2,4,6,64,66,68,70,128,130,132,134,192,194,196,198},{8,10,12,14,72,74..., dimensions={0} | all-to-all | bytes 524288 | tf_op jit(solution)/shard_map/all_to_all | solution.py:402
  105.0 0.7 shard_map.102
  105.7 3.4 %all-to-all-start.1 = ((f32[8,32,128]{2,1,0:T(8,128)}), f32[8,32,128]{2,1,0:T(8,128)S(1)}, u32[]{:S(2)}, u32[]{:S(2)}) async-start(f32[8,32,128]{2,1,0:T(8,128)} %shard_map.102), calls=%async_computation.1 | async-start | bytes 262144 | tf_op jit(solution)/shard_map/all_to_all | solution.py:402
  109.1 2.0 %collective-permute-start.19 = (f32[64,512]{1,0:T(8,128)S(1)}, f32[64,512]{1,0:T(8,128)S(1)}, u32[]{:S(2)}, u32[]{:S(2)}) collective-permute-start(f32[64,512]{1,0:T(8,128)S(1)} %get-tuple-element.81), channel_id=1, source_target_pairs={{0,1},{1,0},{2,3},{3,2},{4,5},{5,4},{6,7},{7,6},{8,9},{9,8},{10,11... | collective-permute-start | bytes 393224 | tf_op jit(solution)/shard_map/ppermute | solution.py:341
  111.0 5.9 %all-to-all-done.1 = f32[8,32,128]{2,1,0:T(8,128)S(1)} async-done(((f32[8,32,128]{2,1,0:T(8,128)}), f32[8,32,128]{2,1,0:T(8,128)S(1)}, u32[]{:S(2)}, u32[]{:S(2)}) %all-to-all-start.1) | async-done | bytes 131104 | tf_op jit(solution)/shard_map/all_to_all | solution.py:402
  117.0 3.1 %collective-permute-start.18 = (f32[32,128]{1,0:T(8,128)S(1)}, f32[32,128]{1,0:T(8,128)S(1)}, u32[]{:S(2)}, u32[]{:S(2)}) collective-permute-start(f32[32,128]{1,0:T(8,128)S(1)} %reduce_sum.9.mine_ref), channel_id=1, source_target_pairs={{0,1},{1,0},{2,3},{3,2},{4,5},{5,4},{6,7},{7,6},{8,9},{9,8},{10,11... | collective-permute-start | bytes 49160 | tf_op jit(solution)/shard_map/ppermute | solution.py:341
  120.0 0.8 collective-permute-done.18.other_ref
  120.9 3.0 %shard_map.103 = (f32[64,1024]{1,0:T(8,128)}, f32[64,64]{1,0:T(8,128)}) custom-call(s32[1]{0:T(128)} %bitcast.core_ref, f32[32,128]{1,0:T(8,128)S(1)} %reduce_sum.9.mine_ref, f32[32,128]{1,0:T(8,128)S(1)} %collective-permute-done.18.other_ref, f32[2,64,512]{2,1,0:T(8,128)S(1)} %shard_map.99.value_ref, f32[64,512]{1,0:T(8,128)S(1)} %collective-permute-done.19.got_ref), custom_call_target="tpu_custom_call" | custom-call | flops 100000000 | bytes 1000000 | tf_op jit(solution)/shard_map/pallas_call | solution.py:497
  (25 shorter events, 0.3 us)
Async XLA Ops:
  0.6 8.2 %copy-start.3 = (s32[11]{0:T(128)S(1)}, s32[11]{0:T(128)}, u32[]{:S(2)}) copy-start(s32[11]{0:T(128)} %constant.40.clone) | copy-start | bytes 136
  0.6 8.1 %copy-start.4 = (s32[11]{0:T(128)S(1)}, s32[11]{0:T(128)}, u32[]{:S(2)}) copy-start(s32[11]{0:T(128)} %constant.39.clone) | copy-start | bytes 136
  0.7 6.9 %copy-start = (s32[4,2]{0,1:T(2,128)S(1)}, s32[4,2]{0,1:T(2,128)}, u32[]{:S(2)}) copy-start(s32[4,2]{0,1:T(2,128)} %param.9) | copy-start | bytes 100
  0.7 25.3 %copy-start.1 = (s32[4]{0:T(128)S(1)}, s32[4]{0:T(128)}, u32[]{:S(2)}) copy-start(s32[4]{0:T(128)} %constant.42.clone) | copy-start | bytes 52
  0.7 25.3 %copy-start.2 = (s32[4]{0:T(128)S(1)}, s32[4]{0:T(128)}, u32[]{:S(2)}) copy-start(s32[4]{0:T(128)} %constant.41.clone) | copy-start | bytes 52
  2.2 21.0 %collective-permute-start.1 = (bf16[2,1792,128]{2,1,0:T(8,128)(2,1)S(1)}, bf16[2,1792,128]{2,1,0:T(8,128)(2,1)S(1)}, u32[]{:S(2)}, u32[]{:S(2)}) collective-permute-start(bf16[2,1792,128]{2,1,0:T(8,128)(2,1)S(1)} %shard_map.87.refs_0_.refs_1_), channel_id=1, source_target_pairs={{0,2},{2,0},{4,6},{6,4},{8,10},{10,8},{12,14},{14,12},{16,18},{18,... | collective-permute-start | bytes 2752520 | tf_op jit(solution)/shard_map/ppermute | solution.py:329
  4.4 27.0 %collective-permute-start.4 = (bf16[2,1792,128]{2,1,0:T(8,128)(2,1)S(1)}, bf16[2,1792,128]{2,1,0:T(8,128)(2,1)}, u32[]{:S(2)}, u32[]{:S(2)}) collective-permute-start(bf16[2,1792,128]{2,1,0:T(8,128)(2,1)S(1)} %shard_map.87.refs_0_.refs_1_), channel_id=1, source_target_pairs={{2,4},{4,2},{6,8},{8,6},{10,12},{12,10},{14,16},{16,14},{18,20},{2... | collective-permute-start | bytes 2752520 | tf_op jit(solution)/shard_map/ppermute | solution.py:329
  7.6 2.0 %collective-permute-start = (s32[4,2]{0,1:T(2,128)S(1)}, s32[4,2]{0,1:T(2,128)S(1)}, u32[]{:S(2)}, u32[]{:S(2)}) collective-permute-start(s32[4,2]{0,1:T(2,128)S(1)} %copy-done), channel_id=1, source_target_pairs={{0,1},{1,0},{2,3},{3,2},{4,5},{5,4},{6,7},{7,6},{8,9},{9,8},{10,11... | collective-permute-start | bytes 104 | tf_op jit(solution)/shard_map/ppermute | solution.py:341
  23.3 6.1 %collective-permute-start.2 = (bf16[1792,128]{1,0:T(8,128)(2,1)S(1)}, bf16[1792,128]{1,0:T(8,128)(2,1)S(1)}, u32[]{:S(2)}, u32[]{:S(2)}) collective-permute-start(bf16[1792,128]{1,0:T(8,128)(2,1)S(1)} %get-tuple-element.84), channel_id=1, source_target_pairs={{0,1},{1,0},{2,3},{3,2},{4,5},{5,4},{6,7},{7,6},{8,9},{9,8},{10,11... | collective-permute-start | bytes 1376264 | tf_op jit(solution)/shard_map/ppermute | solution.py:341
  25.9 3.5 %collective-permute-start.3 = (bf16[1792,128]{1,0:T(8,128)(2,1)S(1)}, bf16[1792,128]{1,0:T(8,128)(2,1)S(1)}, u32[]{:S(2)}, u32[]{:S(2)}) collective-permute-start(bf16[1792,128]{1,0:T(8,128)(2,1)S(1)} %get-tuple-element.85), channel_id=1, source_target_pairs={{0,1},{1,0},{2,3},{3,2},{4,5},{5,4},{6,7},{7,6},{8,9},{9,8},{10,11... | collective-permute-start | bytes 1376264 | tf_op jit(solution)/shard_map/ppermute | solution.py:341
  26.0 5.4 %collective-permute-start.5 = (s32[8,2]{0,1:T(2,128)S(1)}, s32[8,2]{0,1:T(2,128)S(1)}, u32[]{:S(2)}, u32[]{:S(2)}) collective-permute-start(s32[8,2]{0,1:T(2,128)S(1)} %pad_add_fusion), channel_id=1, source_target_pairs={{0,2},{2,4},{4,6},{6,8},{8,10},{10,12},{12,14},{14,16},{16,18},{18... | collective-permute-start | bytes 200 | tf_op jit(solution)/shard_map/ppermute | solution.py:366
  33.1 2.3 %collective-permute-start.6 = (f32[2,2,64,512]{3,2,1,0:T(8,128)S(1)}, f32[2,2,64,512]{3,2,1,0:T(8,128)S(1)}, u32[]{:S(2)}, u32[]{:S(2)}) collective-permute-start(f32[2,2,64,512]{3,2,1,0:T(8,128)S(1)} %get-tuple-element.57), channel_id=1, source_target_pairs={{0,1},{1,0},{2,3},{3,2},{4,5},{5,4},{6,7},{7,6},{8,9},{9,8},{10,11... | collective-permute-start | bytes 1572872 | tf_op jit(solution)/shard_map/ppermute | solution.py:341
  35.4 11.4 %collective-permute-start.7 = (f32[2,64,512]{2,1,0:T(8,128)S(1)}, f32[2,64,512]{2,1,0:T(8,128)S(1)}, u32[]{:S(2)}, u32[]{:S(2)}) collective-permute-start(f32[2,64,512]{2,1,0:T(8,128)S(1)} %fusion.1), channel_id=1, source_target_pairs={{0,2},{2,0},{4,6},{6,4},{8,10},{10,8},{12,14},{14,12},{16,18},{18,... | collective-permute-start | bytes 786440 | tf_op jit(solution)/shard_map/ppermute | solution.py:329
  40.4 7.1 %collective-permute-start.8 = (f32[2,64,512]{2,1,0:T(8,128)S(1)}, f32[2,64,512]{2,1,0:T(8,128)S(1)}, u32[]{:S(2)}, u32[]{:S(2)}) collective-permute-start(f32[2,64,512]{2,1,0:T(8,128)S(1)} %get-tuple-element.59.ours), channel_id=1, source_target_pairs={{2,4},{4,2},{6,8},{8,6},{10,12},{12,10},{14,16},{16,14},{18,20},{2... | collective-permute-start | bytes 786440 | tf_op jit(solution)/shard_map/ppermute | solution.py:329
  46.8 4.8 %collective-permute-start.10 = (f32[2,64,512]{2,1,0:T(8,128)S(1)}, f32[2,64,512]{2,1,0:T(8,128)S(1)}, u32[]{:S(2)}, u32[]{:S(2)}) collective-permute-start(f32[2,64,512]{2,1,0:T(8,128)S(1)} %shard_map.91.partial), channel_id=1, source_target_pairs={{2,4},{4,2},{6,8},{8,6},{10,12},{12,10},{14,16},{16,14},{18,20},{2... | collective-permute-start | bytes 786440 | tf_op jit(solution)/shard_map/ppermute | solution.py:329
  47.6 4.1 %collective-permute-start.9 = (bf16[2,128,512]{2,1,0:T(8,128)(2,1)S(1)}, bf16[2,128,512]{2,1,0:T(8,128)(2,1)S(1)}, u32[]{:S(2)}, u32[]{:S(2)}) collective-permute-start(bf16[2,128,512]{2,1,0:T(8,128)(2,1)S(1)} %get-tuple-element.62.refs_1_.refs_2_), channel_id=1, source_target_pairs={{0,1},{1,0},{2,3},{3,2},{4,5},{5,4},{6,7},{7,6},{8,9},{9,8},{10,11... | collective-permute-start | bytes 786440 | tf_op jit(solution)/shard_map/ppermute | solution.py:341
  48.6 9.6 %collective-permute-start.11 = (bf16[2,128,512]{2,1,0:T(8,128)(2,1)S(1)}, bf16[2,128,512]{2,1,0:T(8,128)(2,1)S(1)}, u32[]{:S(2)}, u32[]{:S(2)}) collective-permute-start(bf16[2,128,512]{2,1,0:T(8,128)(2,1)S(1)} %get-tuple-element.62.refs_1_.refs_2_), channel_id=1, source_target_pairs={{0,2},{2,0},{4,6},{6,4},{8,10},{10,8},{12,14},{14,12},{16,18},{18,... | collective-permute-start | bytes 786440 | tf_op jit(solution)/shard_map/ppermute | solution.py:329
  58.2 1.8 %collective-permute-start.12 = (bf16[128,512]{1,0:T(8,128)(2,1)S(1)}, bf16[128,512]{1,0:T(8,128)(2,1)S(1)}, u32[]{:S(2)}, u32[]{:S(2)}) collective-permute-start(bf16[128,512]{1,0:T(8,128)(2,1)S(1)} %get-tuple-element.86), channel_id=1, source_target_pairs={{0,1},{1,0},{2,3},{3,2},{4,5},{5,4},{6,7},{7,6},{8,9},{9,8},{10,11... | collective-permute-start | bytes 393224 | tf_op jit(solution)/shard_map/ppermute | solution.py:341
  59.0 1.3 %collective-permute-start.13 = (bf16[128,512]{1,0:T(8,128)(2,1)S(1)}, bf16[128,512]{1,0:T(8,128)(2,1)S(1)}, u32[]{:S(2)}, u32[]{:S(2)}) collective-permute-start(bf16[128,512]{1,0:T(8,128)(2,1)S(1)} %get-tuple-element.87), channel_id=1, source_target_pairs={{0,1},{1,0},{2,3},{3,2},{4,5},{5,4},{6,7},{7,6},{8,9},{9,8},{10,11... | collective-permute-start | bytes 393224 | tf_op jit(solution)/shard_map/ppermute | solution.py:341
  62.4 2.0 %collective-permute-start.14 = (f32[2,2,64,512]{3,2,1,0:T(8,128)S(1)}, f32[2,2,64,512]{3,2,1,0:T(8,128)S(1)}, u32[]{:S(2)}, u32[]{:S(2)}) collective-permute-start(f32[2,2,64,512]{3,2,1,0:T(8,128)S(1)} %get-tuple-element.76), channel_id=1, source_target_pairs={{0,1},{1,0},{2,3},{3,2},{4,5},{5,4},{6,7},{7,6},{8,9},{9,8},{10,11... | collective-permute-start | bytes 1572872 | tf_op jit(solution)/shard_map/ppermute | solution.py:341
  64.5 9.3 %collective-permute-start.15 = (f32[2,64,512]{2,1,0:T(8,128)S(1)}, f32[2,64,512]{2,1,0:T(8,128)S(1)}, u32[]{:S(2)}, u32[]{:S(2)}) collective-permute-start(f32[2,64,512]{2,1,0:T(8,128)S(1)} %fusion), channel_id=1, source_target_pairs={{0,2},{2,0},{4,6},{6,4},{8,10},{10,8},{12,14},{14,12},{16,18},{18,... | collective-permute-start | bytes 786440 | tf_op jit(solution)/shard_map/ppermute | solution.py:329
  67.3 6.5 %collective-permute-start.16 = (f32[2,64,512]{2,1,0:T(8,128)S(1)}, f32[2,64,512]{2,1,0:T(8,128)S(1)}, u32[]{:S(2)}, u32[]{:S(2)}) collective-permute-start(f32[2,64,512]{2,1,0:T(8,128)S(1)} %get-tuple-element.78), channel_id=1, source_target_pairs={{2,4},{4,2},{6,8},{8,6},{10,12},{12,10},{14,16},{16,14},{18,20},{2... | collective-permute-start | bytes 786440 | tf_op jit(solution)/shard_map/ppermute | solution.py:329
  74.3 1.7 %collective-permute-start.17 = (f32[32,128]{1,0:T(8,128)S(1)}, f32[32,128]{1,0:T(8,128)S(1)}, u32[]{:S(2)}, u32[]{:S(2)}) collective-permute-start(f32[32,128]{1,0:T(8,128)S(1)} %get-tuple-element.80), channel_id=1, source_target_pairs={{0,1},{1,0},{2,3},{3,2},{4,5},{5,4},{6,7},{7,6},{8,9},{9,8},{10,11... | collective-permute-start | bytes 49160 | tf_op jit(solution)/shard_map/ppermute | solution.py:341
  105.7 11.3 %all-to-all-start.1 = ((f32[8,32,128]{2,1,0:T(8,128)}), f32[8,32,128]{2,1,0:T(8,128)S(1)}, u32[]{:S(2)}, u32[]{:S(2)}) async-start(f32[8,32,128]{2,1,0:T(8,128)} %shard_map.102), calls=%async_computation.1 | async-start | bytes 262144 | tf_op jit(solution)/shard_map/all_to_all | solution.py:402
  109.1 11.0 %collective-permute-start.19 = (f32[64,512]{1,0:T(8,128)S(1)}, f32[64,512]{1,0:T(8,128)S(1)}, u32[]{:S(2)}, u32[]{:S(2)}) collective-permute-start(f32[64,512]{1,0:T(8,128)S(1)} %get-tuple-element.81), channel_id=1, source_target_pairs={{0,1},{1,0},{2,3},{3,2},{4,5},{5,4},{6,7},{7,6},{8,9},{9,8},{10,11... | collective-permute-start | bytes 393224 | tf_op jit(solution)/shard_map/ppermute | solution.py:341
  117.0 3.9 %collective-permute-start.18 = (f32[32,128]{1,0:T(8,128)S(1)}, f32[32,128]{1,0:T(8,128)S(1)}, u32[]{:S(2)}, u32[]{:S(2)}) collective-permute-start(f32[32,128]{1,0:T(8,128)S(1)} %reduce_sum.9.mine_ref), channel_id=1, source_target_pairs={{0,1},{1,0},{2,3},{3,2},{4,5},{5,4},{6,7},{7,6},{8,9},{9,8},{10,11... | collective-permute-start | bytes 49160 | tf_op jit(solution)/shard_map/ppermute | solution.py:341

commit v9 on v8

--- a/solution.py
+++ b/solution.py
@@ -180,11 +180,10 @@
 def late_kernel(make, flags_ref, far_ref, *refs):
     if make:
         odd0, own0, own1, even0, even1, *ins = refs[:9]
-        tile_ref, done_ref, own_part, even_part, give_ref = refs[9:]
+        tile_ref, done_ref, *parts = refs[9:]
     else:
         tile_ref, odd0, own0, own1, even0, even1, *ins = refs[:10]
-        done_ref, own_part, even_part, give_ref = refs[10:]
-    parts = (own_part, give_ref.at[0], even_part, give_ref.at[1])
+        done_ref, *parts = refs[10:]
     done_ref[...] = jnp.zeros_like(done_ref)
     for ref, value in zip(parts, ins):
         ref[...] = value[...]
@@ -211,9 +210,13 @@
     pair_ref[block, 64:] = (value - high.astype(jnp.float32)).astype(jnp.bfloat16)
 
 
-def partial_kernel(done, part_mine, parts_other, from_even, sum_ref):
+def sum_kernel(*refs):
+    *value_refs, sum_ref = refs
     for block in range(2):
-        sum_ref[block] = done[block] + part_mine[block] + parts_other[0, block] + from_even[block]
+        total = value_refs[0][block]
+        for ref in value_refs[1:]:
+            total = total + ref[block]
+        sum_ref[block] = total
 
 
 def pair_kernel(partial, ours, pair_ref):
@@ -221,12 +224,11 @@
         put_pair(pair_ref, block, partial[block] + ours[block])
 
 
-def total_kernel(partial, from_odd, sum_ref, pair_ref=None):
+def total_kernel(partial, from_odd, sum_ref, pair_ref):
     for block in range(2):
         value = partial[block] + from_odd[block]
         sum_ref[block] = value
-        if pair_ref is not None:
-            put_pair(pair_ref, block, value)
+        put_pair(pair_ref, block, value)
 
 
 def gram_of(value_ref, scale):
@@ -381,14 +383,10 @@
     )
 
 
-def spread(done, own0, out_odd, even0, give):
+def spread(done, own0, own1, out_odd, even0, even1):
     from_odd = to_odd(out_odd)
-    got = swap(give)
-    from_even = to_even(even0 + got[1])
-    partial = call(partial_kernel, shape((2, 64, HALF)), 10**4, 10**4)(in_specs=[VMEM] * 4)(
-        done, own0, got, from_even
-    )
-    return partial, from_odd
+    from_even = to_even(even0 + swap(even1))
+    return done, own0, swap(own1), from_even, from_odd
 
 
 def sum_over_chips(*values):
@@ -449,13 +447,13 @@
     )(in_specs=[SMEM] + [VMEM] * 4)(flags, own0, even0, even1, done)
     done, odd0, before = lax.optimization_barrier((done, odd0, before))
     far_flags = flags_of_far(before, base)
-    give_shape = shape((2, 2, 64, HALF))
-    tiles_late, out_odd, own_part0, even_part0, give = call(
-        functools.partial(late_kernel, True), (tiles(8),) + 3 * (sum_shape,) + (give_shape,), 10**9, 10**6
+    tiles_late, out_odd, own_part0, own_part1, even_part0, even_part1 = call(
+        functools.partial(late_kernel, True), (tiles(8),) + 5 * (sum_shape,), 10**9, 10**6
     )(in_specs=[SMEM] * 2 + [VMEM] * 9)(
         flags, far_flags, odd0, own0, own1, even0, even1, own_part0, own_part1, even_part0, even_part1
     )
-    partial, from_odd = spread(done, own_part0, out_odd, even_part0, give)
+    *known, from_odd = spread(done, own_part0, own_part1, out_odd, even_part0, even_part1)
+    partial = call(sum_kernel, sum_shape, 10**4, 10**4)(in_specs=[VMEM] * 4)(*known)
     odd_partial, odd_ours = to_odd(partial), out_odd
     sketch, pair0 = call(total_kernel, (sum_shape, shape((2, 128, HALF), bf16)), 10**4, 10**4)(
         in_specs=[VMEM] * 2
@@ -477,14 +475,14 @@
     done, even_part0, even_part1 = call(
         functools.partial(early_kernel, False), 3 * (sum_shape,), 10**4, 10**4
     )(in_specs=[SMEM] + [VMEM] * 5)(flags, tiles_early, pair0, even0, even1, done)
-    out_odd, own_part0, even_part0, give = call(
-        functools.partial(late_kernel, False), 3 * (sum_shape,) + (give_shape,), 10**9, 10**6
+    out_odd, own_part0, own_part1, even_part0, even_part1 = call(
+        functools.partial(late_kernel, False), 5 * (sum_shape,), 10**9, 10**6
     )(in_specs=[SMEM] * 2 + [VMEM] * 10)(
         flags, far_flags, tiles_late, odd0, pair0, pair1, even0, even1,
         own_part0, own_part1, even_part0, even_part1,
     )
-    image = call(total_kernel, sum_shape, 10**4, 10**4)(in_specs=[VMEM] * 2)(
-        *spread(done, own_part0, out_odd, even_part0, give)
+    image = call(sum_kernel, sum_shape, 10**6, 2 * 10**6)(in_specs=[VMEM] * 5)(
+        *spread(done, own_part0, own_part1, out_odd, even_part0, even_part1)
     )
     keep, gram_give, half = call(
         functools.partial(second_gram_kernel, scale),

time: 124 us -> 122 us (0.984)
  blocking collectives: 29 us -> 24.6 us
  starting transfers between devices: 36.4 us -> 40.1 us
  Pallas kernels: 18.1 us -> 16.6 us
    all_to_all x1, blocking collectives: 29 us -> 24.6 us  [sum_over_chips(): lax.all_to_all(copies, 'rows', 0, 0, axis_index_groups=groups, tiled=True)]
    ppermute x8, starting transfers between devices: 16.7 us -> 18.8 us  [exchange(): return lax.ppermute(value, 'rows', links)]
    ppermute x8, waiting for transfers between devices: 26.1 us -> 27.9 us  [exchange(): return lax.ppermute(value, 'rows', links)]
    ppermute x11 -> x13, waiting for transfers between devices: 6.73 us -> 4.98 us  [swap(): return lax.ppermute(value, 'cols', [(0, 1), (1, 0)])]
    ppermute x11 -> x13, starting transfers between devices: 12.9 us -> 14 us  [swap(): return lax.ppermute(value, 'cols', [(0, 1), (1, 0)])]
  transfers between devices with their start and end apart: 21 -> 23, of which waited for: 12 -> 12; matrix products, arithmetic and copies ran while one was open for 0% -> 0% of each run, Pallas kernels for 7% -> 6%
where the time goes in v9:
time: 122 us
  starting transfers between devices  40.1 us (33%)
  waiting for transfers between devices  38.8 us (32%)
  blocking collectives  24.6 us (20%)
  Pallas kernels  16.6 us (14%)
    ppermute x8, waiting for transfers between devices, exchange(): return lax.ppermute(value, 'rows', links)  27.9 us
    all_to_all x1, blocking collectives, sum_over_chips(): lax.all_to_all(copies, 'rows', 0, 0, axis_index_groups=groups, tiled=True)  24.6 us
    ppermute x8, starting transfers between devices, exchange(): return lax.ppermute(value, 'rows', links)  18.8 us
    ppermute x13, starting transfers between devices, swap(): return lax.ppermute(value, 'cols', [(0, 1), (1, 0)])  14 us
    all_to_all x1, waiting for transfers between devices, sum_over_chips(): lax.all_to_all(copies, 'rows', 0, 0, axis_index_groups=groups, tiled=True)  5.87 us
    ppermute x13, waiting for transfers between devices, swap(): return lax.ppermute(value, 'cols', [(0, 1), (1, 0)])  4.98 us
    all_to_all x1, starting transfers between devices, sum_over_chips(): lax.all_to_all(copies, 'rows', 0, 0, axis_index_groups=groups, tiled=True)  4.01 us
    ppermute x1, starting transfers between devices, own_flags_and_list(): lax.ppermute(own, 'rows', [(r, r + 1) for r in range(lax.axis_size('rows'...  3.36 us
  transfers between devices with their start and end apart: 23, of which 12 were waited for; matrix products, arithmetic and copies ran while one was open for 0% of the time, Pallas kernels for 6%

profile of v9, /device:TPU:1, one launch (start us, length us, event | category | flops | bytes accessed | tf_op | source)
XLA Modules:
  0.0 121.8 jit_solution(8827741024007100361)
XLA Ops:
  0.6 0.0 copy-start.3
  0.6 0.0 copy-start.4
  0.7 0.0 copy-start.1
  0.7 0.0 copy-start.2
  0.7 1.5 %shard_map.87.refs_0_.refs_1_ = bf16[2,1792,128]{2,1,0:T(8,128)(2,1)S(1)} custom-call(s32[1]{0:T(128)} %bitcast.core_ref, bf16[2048,384]{1,0:T(8,128)(2,1)} %rows_ref.3, bf16[64,2048]{1,0:T(8,128)(2,1)} %bitcast.23), custom_call_target="tpu_custom_call" | custom-call | flops 10000 | bytes 10000 | tf_op jit(solution)/shard_map/pallas_call | solution.py:418
  2.2 2.2 %collective-permute-start.1 = (bf16[2,1792,128]{2,1,0:T(8,128)(2,1)S(1)}, bf16[2,1792,128]{2,1,0:T(8,128)(2,1)S(1)}, u32[]{:S(2)}, u32[]{:S(2)}) collective-permute-start(bf16[2,1792,128]{2,1,0:T(8,128)(2,1)S(1)} %shard_map.87.refs_0_.refs_1_), channel_id=1, source_target_pairs={{0,2},{2,0},{4,6},{6,4},{8,10},{10,8},{12,14},{14,12},{16,18},{18,... | collective-permute-start | bytes 2752520 | tf_op jit(solution)/shard_map/ppermute | solution.py:331
  4.4 1.6 %collective-permute-start.4 = (bf16[2,1792,128]{2,1,0:T(8,128)(2,1)S(1)}, bf16[2,1792,128]{2,1,0:T(8,128)(2,1)}, u32[]{:S(2)}, u32[]{:S(2)}) collective-permute-start(bf16[2,1792,128]{2,1,0:T(8,128)(2,1)S(1)} %shard_map.87.refs_0_.refs_1_), channel_id=1, source_target_pairs={{2,4},{4,2},{6,8},{8,6},{10,12},{12,10},{14,16},{16,14},{18,20},{2... | collective-permute-start | bytes 2752520 | tf_op jit(solution)/shard_map/ppermute | solution.py:331
  6.0 1.5 %shard_map.86.refs_1_.refs_2_ = bf16[2,1792,128]{2,1,0:T(8,128)(2,1)S(1)} custom-call(s32[1]{0:T(128)} %bitcast.core_ref, bf16[2048,384]{1,0:T(8,128)(2,1)} %rows_ref.3, bf16[64,2048]{1,0:T(8,128)(2,1)} %bitcast.24), custom_call_target="tpu_custom_call" | custom-call | flops 10000 | bytes 10000 | tf_op jit(solution)/shard_map/pallas_call | solution.py:418
  7.6 1.2 %collective-permute-start = (s32[4,2]{0,1:T(2,128)S(1)}, s32[4,2]{0,1:T(2,128)S(1)}, u32[]{:S(2)}, u32[]{:S(2)}) collective-permute-start(s32[4,2]{0,1:T(2,128)S(1)} %copy-done), channel_id=1, source_target_pairs={{0,1},{1,0},{2,3},{3,2},{4,5},{5,4},{6,7},{7,6},{8,9},{9,8},{10,11... | collective-permute-start | bytes 104 | tf_op jit(solution)/shard_map/ppermute | solution.py:343
  8.8 0.8 collective-permute-done
  9.6 0.1 pad_add_fusion
  9.7 0.1 and_reduce_fusion
  9.8 2.0 %shard_map.88 = (bf16[3,2,512,512]{3,2,1,0:T(8,128)(2,1)S(1)}, f32[2,64,512]{2,1,0:T(8,128)S(1)}, f32[2,64,512]{2,1,0:T(8,128)S(1)}, f32[2,64,512]{2,1,0:T(8,128)S(1)}) custom-call(s32[11]{0:T(128)S(1)} %convert_element_type.6.flags_ref, bf16[2,1792,128]{2,1,0:T(8,128)(2,1)S(1)} %shard_map.87.refs_0_.refs_1_, bf16[2,1792,128]{2,1,0:T(8,128)(2,1)S(1)} %shard_map.86.refs_1_.refs_2_), custom_call_target="tpu_custom_call" | custom-call | flops 10000 | bytes 10000 | tf_op jit(solution)/shard_map/pallas_call | solution.py:440
  11.8 11.5 %collective-permute-done.1.refs_1_.refs_3_ = bf16[2,1792,128]{2,1,0:T(8,128)(2,1)S(1)} collective-permute-done((bf16[2,1792,128]{2,1,0:T(8,128)(2,1)S(1)}, bf16[2,1792,128]{2,1,0:T(8,128)(2,1)S(1)}, u32[]{:S(2)}, u32[]{:S(2)}) %collective-permute-start.1) | collective-permute-done | bytes 917536 | tf_op jit(solution)/shard_map/ppermute | solution.py:331
  23.3 0.1 slice_bitcast_fusion.1
  23.3 2.6 %collective-permute-start.2 = (bf16[1792,128]{1,0:T(8,128)(2,1)S(1)}, bf16[1792,128]{1,0:T(8,128)(2,1)S(1)}, u32[]{:S(2)}, u32[]{:S(2)}) collective-permute-start(bf16[1792,128]{1,0:T(8,128)(2,1)S(1)} %get-tuple-element.88), channel_id=1, source_target_pairs={{0,1},{1,0},{2,3},{3,2},{4,5},{5,4},{6,7},{7,6},{8,9},{9,8},{10,11... | collective-permute-start | bytes 1376264 | tf_op jit(solution)/shard_map/ppermute | solution.py:343
  25.9 0.1 collective-permute-start.3
  26.0 3.4 %collective-permute-start.5 = (s32[8,2]{0,1:T(2,128)S(1)}, s32[8,2]{0,1:T(2,128)S(1)}, u32[]{:S(2)}, u32[]{:S(2)}) collective-permute-start(s32[8,2]{0,1:T(2,128)S(1)} %pad_add_fusion), channel_id=1, source_target_pairs={{0,2},{2,4},{4,6},{6,8},{8,10},{10,12},{12,14},{14,16},{16,18},{18... | collective-permute-start | bytes 200 | tf_op jit(solution)/shard_map/ppermute | solution.py:368
  29.4 0.0 collective-permute-done.2
  29.4 0.0 collective-permute-done.3
  29.4 0.1 pad_maximum_fusion.refs_2_.refs_4_
  29.5 1.9 %shard_map.89 = (bf16[4,2,512,512]{3,2,1,0:T(8,128)(2,1)S(1)}, f32[2,64,512]{2,1,0:T(8,128)S(1)}, f32[2,64,512]{2,1,0:T(8,128)S(1)}, f32[2,64,512]{2,1,0:T(8,128)S(1)}) custom-call(s32[11]{0:T(128)S(1)} %convert_element_type.6.flags_ref, bf16[2,1792,128]{2,1,0:T(8,128)(2,1)S(1)} %shard_map.87.refs_0_.refs_1_, ...), custom_call_target="tpu_custom_call" | custom-call | flops 10000 | bytes 10000 | tf_op jit(solution)/shard_map/pallas_call | solution.py:445
  31.4 0.0 collective-permute-done.4.refs_0_
  31.5 0.2 and_reduce_fusion.1
  31.6 1.4 %shard_map.90 = (bf16[8,2,512,512]{3,2,1,0:T(8,128)(2,1)S(1)}, f32[2,64,512]{2,1,0:T(8,128)S(1)}, f32[2,64,512]{2,1,0:T(8,128)S(1)}, f32[2,64,512]{2,1,0:T(8,128...) custom-call(s32[11]{0:T(128)S(1)} %convert_element_type.6.flags_ref, s32[4]{0:T(128)S(1)} %convert_element_type.7.far_ref, ...), custom_call_target="tpu_custom_call" | custom-call | flops 1000000000 | bytes 1000000 | tf_op jit(solution)/shard_map/pallas_call | solution.py:450
  33.1 0.8 collective-permute-start.7
  33.8 0.1 collective-permute-start.6
  33.9 1.1 collective-permute-done.7
  35.1 3.7 %collective-permute-start.8 = (f32[2,64,512]{2,1,0:T(8,128)S(1)}, f32[2,64,512]{2,1,0:T(8,128)S(1)}, u32[]{:S(2)}, u32[]{:S(2)}) collective-permute-start(f32[2,64,512]{2,1,0:T(8,128)S(1)} %add.36), channel_id=1, source_target_pairs={{0,2},{2,0},{4,6},{6,4},{8,10},{10,8},{12,14},{14,12},{16,18},{18,... | collective-permute-start | bytes 786440 | tf_op jit(solution)/shard_map/ppermute | solution.py:331
  38.8 0.7 collective-permute-start.9
  39.5 0.0 collective-permute-done.6.refs_2_
  39.5 5.7 %collective-permute-done.8.refs_3_ = f32[2,64,512]{2,1,0:T(8,128)S(1)} collective-permute-done((f32[2,64,512]{2,1,0:T(8,128)S(1)}, f32[2,64,512]{2,1,0:T(8,128)S(1)}, u32[]{:S(2)}, u32[]{:S(2)}) %collective-permute-start.8) | collective-permute-done | bytes 262176 | tf_op jit(solution)/shard_map/ppermute | solution.py:331
  45.2 0.1 shard_map.91.partial
  45.3 0.7 collective-permute-start.11
  46.0 1.0 collective-permute-start.10
  47.0 5.1 %collective-permute-start.12 = (bf16[2,128,512]{2,1,0:T(8,128)(2,1)S(1)}, bf16[2,128,512]{2,1,0:T(8,128)(2,1)S(1)}, u32[]{:S(2)}, u32[]{:S(2)}) collective-permute-start(bf16[2,128,512]{2,1,0:T(8,128)(2,1)S(1)} %get-tuple-element.65.refs_1_.refs_2_), channel_id=1, source_target_pairs={{0,2},{2,0},{4,6},{6,4},{8,10},{10,8},{12,14},{14,12},{16,18},{18,... | collective-permute-start | bytes 786440 | tf_op jit(solution)/shard_map/ppermute | solution.py:331
  52.0 0.1 shard_map.94.refs_1_
  52.1 1.4 %shard_map.95 = (f32[2,64,512]{2,1,0:T(8,128)S(1)}, f32[2,64,512]{2,1,0:T(8,128)S(1)}, f32[2,64,512]{2,1,0:T(8,128)S(1)}) custom-call(s32[11]{0:T(128)S(1)} %convert_element_type.6.flags_ref, bf16[3,2,512,512]{3,2,1,0:T(8,128)(2,1)S(1)} %get-tuple-element.66.refs_0_, bf16[2,128,512]{2,1,0:T(8,128)(2,1)S(1)} %get-tuple-element.65.refs_1_.refs_2_, ...), custom_call_target="tpu_custom_call" | custom-call | flops 99999997952 | bytes 10000 | tf_op jit(solution)/shard_map/pallas_call | solution.py:470
  53.5 5.1 %collective-permute-done.12.refs_2_.refs_4_ = bf16[2,128,512]{2,1,0:T(8,128)(2,1)S(1)} collective-permute-done((bf16[2,128,512]{2,1,0:T(8,128)(2,1)S(1)}, bf16[2,128,512]{2,1,0:T(8,128)(2,1)S(1)}, u32[]{:S(2)}, u32[]{:S(2)}) %collective-permute-start.12) | collective-permute-done | bytes 262176 | tf_op jit(solution)/shard_map/ppermute | solution.py:331
  58.6 0.8 collective-permute-start.13
  59.4 0.3 collective-permute-start.14
  59.7 0.7 collective-permute-done.13
  60.4 0.4 collective-permute-done.14
  60.8 1.3 %shard_map.96 = (f32[2,64,512]{2,1,0:T(8,128)S(1)}, f32[2,64,512]{2,1,0:T(8,128)S(1)}, f32[2,64,512]{2,1,0:T(8,128)S(1)}) custom-call(s32[11]{0:T(128)S(1)} %convert_element_type.6.flags_ref, bf16[4,2,512,512]{3,2,1,0:T(8,128)(2,1)S(1)} %get-tuple-element.64.refs_0_, bf16[2,128,512]{2,1,0:T(8,128)(2,1)S(1)} %get-tuple-element.65.refs_1_.refs_2_, ...), custom_call_target="tpu_custom_call" | custom-call | flops 10000 | bytes 10000 | tf_op jit(solution)/shard_map/pallas_call | solution.py:475
  62.1 0.8 shard_map.97
  62.8 0.4 collective-permute-start.16
  63.2 0.2 collective-permute-start.15
  63.4 0.7 collective-permute-start.18
  64.1 0.4 collective-permute-done.16
  64.5 4.2 %collective-permute-start.17 = (f32[2,64,512]{2,1,0:T(8,128)S(1)}, f32[2,64,512]{2,1,0:T(8,128)S(1)}, u32[]{:S(2)}, u32[]{:S(2)}) collective-permute-start(f32[2,64,512]{2,1,0:T(8,128)S(1)} %add.37), channel_id=1, source_target_pairs={{0,2},{2,0},{4,6},{6,4},{8,10},{10,8},{12,14},{14,12},{16,18},{18,... | collective-permute-start | bytes 786440 | tf_op jit(solution)/shard_map/ppermute | solution.py:331
  68.7 0.4 shard_map.93.first_ref
  69.1 5.7 %collective-permute-done.17.refs_3_ = f32[2,64,512]{2,1,0:T(8,128)S(1)} collective-permute-done((f32[2,64,512]{2,1,0:T(8,128)S(1)}, f32[2,64,512]{2,1,0:T(8,128)S(1)}, u32[]{:S(2)}, u32[]{:S(2)}) %collective-permute-start.17) | collective-permute-done | bytes 262176 | tf_op jit(solution)/shard_map/ppermute | solution.py:331
  74.8 0.1 shard_map.98.value_ref
  74.9 0.4 shard_map.99
  75.3 1.2 collective-permute-start.19
  76.5 0.8 collective-permute-done.19.refs_1_
  77.3 24.6 %all_to_all.10.refs_0_ = f32[16,32,128]{2,1,0:T(8,128)S(1)} all-to-all(f32[16,32,128]{2,1,0:T(8,128)S(1)} %shard_map.100), channel_id=1, replica_groups={{0,2,4,6,64,66,68,70,128,130,132,134,192,194,196,198},{8,10,12,14,72,74..., dimensions={0} | all-to-all | bytes 524288 | tf_op jit(solution)/shard_map/all_to_all | solution.py:400
  101.9 0.7 shard_map.101
  102.6 4.0 %all-to-all-start.1 = ((f32[8,32,128]{2,1,0:T(8,128)}), f32[8,32,128]{2,1,0:T(8,128)S(1)}, u32[]{:S(2)}, u32[]{:S(2)}) async-start(f32[8,32,128]{2,1,0:T(8,128)} %shard_map.101), calls=%async_computation.1 | async-start | bytes 262144 | tf_op jit(solution)/shard_map/all_to_all | solution.py:400
  106.6 2.2 %collective-permute-start.21 = (f32[64,512]{1,0:T(8,128)S(1)}, f32[64,512]{1,0:T(8,128)S(1)}, u32[]{:S(2)}, u32[]{:S(2)}) collective-permute-start(f32[64,512]{1,0:T(8,128)S(1)} %get-tuple-element.85), channel_id=1, source_target_pairs={{0,1},{1,0},{2,3},{3,2},{4,5},{5,4},{6,7},{7,6},{8,9},{9,8},{10,11... | collective-permute-start | bytes 393224 | tf_op jit(solution)/shard_map/ppermute | solution.py:343
  108.8 5.9 %all-to-all-done.1 = f32[8,32,128]{2,1,0:T(8,128)S(1)} async-done(((f32[8,32,128]{2,1,0:T(8,128)}), f32[8,32,128]{2,1,0:T(8,128)S(1)}, u32[]{:S(2)}, u32[]{:S(2)}) %all-to-all-start.1) | async-done | bytes 131104 | tf_op jit(solution)/shard_map/all_to_all | solution.py:400
  114.7 3.3 %collective-permute-start.20 = (f32[32,128]{1,0:T(8,128)S(1)}, f32[32,128]{1,0:T(8,128)S(1)}, u32[]{:S(2)}, u32[]{:S(2)}) collective-permute-start(f32[32,128]{1,0:T(8,128)S(1)} %reduce_sum.9.mine_ref), channel_id=1, source_target_pairs={{0,1},{1,0},{2,3},{3,2},{4,5},{5,4},{6,7},{7,6},{8,9},{9,8},{10,11... | collective-permute-start | bytes 49160 | tf_op jit(solution)/shard_map/ppermute | solution.py:343
  118.0 0.8 collective-permute-done.20.other_ref
  118.8 3.0 %shard_map.102 = (f32[64,1024]{1,0:T(8,128)}, f32[64,64]{1,0:T(8,128)}) custom-call(s32[1]{0:T(128)} %bitcast.core_ref, f32[32,128]{1,0:T(8,128)S(1)} %reduce_sum.9.mine_ref, f32[32,128]{1,0:T(8,128)S(1)} %collective-permute-done.20.other_ref, f32[2,64,512]{2,1,0:T(8,128)S(1)} %shard_map.98.value_ref, f32[64,512]{1,0:T(8,128)S(1)} %collective-permute-done.21.got_ref), custom_call_target="tpu_custom_call" | custom-call | flops 100000000 | bytes 1000000 | tf_op jit(solution)/shard_map/pallas_call | solution.py:495
  (28 shorter events, 0.3 us)
Async XLA Ops:
  0.6 8.2 %copy-start.3 = (s32[11]{0:T(128)S(1)}, s32[11]{0:T(128)}, u32[]{:S(2)}) copy-start(s32[11]{0:T(128)} %constant.40.clone) | copy-start | bytes 136
  0.6 8.1 %copy-start.4 = (s32[11]{0:T(128)S(1)}, s32[11]{0:T(128)}, u32[]{:S(2)}) copy-start(s32[11]{0:T(128)} %constant.39.clone) | copy-start | bytes 136
  0.7 6.9 %copy-start = (s32[4,2]{0,1:T(2,128)S(1)}, s32[4,2]{0,1:T(2,128)}, u32[]{:S(2)}) copy-start(s32[4,2]{0,1:T(2,128)} %param.9) | copy-start | bytes 100
  0.7 25.3 %copy-start.1 = (s32[4]{0:T(128)S(1)}, s32[4]{0:T(128)}, u32[]{:S(2)}) copy-start(s32[4]{0:T(128)} %constant.42.clone) | copy-start | bytes 52
  0.7 25.3 %copy-start.2 = (s32[4]{0:T(128)S(1)}, s32[4]{0:T(128)}, u32[]{:S(2)}) copy-start(s32[4]{0:T(128)} %constant.41.clone) | copy-start | bytes 52
  2.2 21.0 %collective-permute-start.1 = (bf16[2,1792,128]{2,1,0:T(8,128)(2,1)S(1)}, bf16[2,1792,128]{2,1,0:T(8,128)(2,1)S(1)}, u32[]{:S(2)}, u32[]{:S(2)}) collective-permute-start(bf16[2,1792,128]{2,1,0:T(8,128)(2,1)S(1)} %shard_map.87.refs_0_.refs_1_), channel_id=1, source_target_pairs={{0,2},{2,0},{4,6},{6,4},{8,10},{10,8},{12,14},{14,12},{16,18},{18,... | collective-permute-start | bytes 2752520 | tf_op jit(solution)/shard_map/ppermute | solution.py:331
  4.4 27.0 %collective-permute-start.4 = (bf16[2,1792,128]{2,1,0:T(8,128)(2,1)S(1)}, bf16[2,1792,128]{2,1,0:T(8,128)(2,1)}, u32[]{:S(2)}, u32[]{:S(2)}) collective-permute-start(bf16[2,1792,128]{2,1,0:T(8,128)(2,1)S(1)} %shard_map.87.refs_0_.refs_1_), channel_id=1, source_target_pairs={{2,4},{4,2},{6,8},{8,6},{10,12},{12,10},{14,16},{16,14},{18,20},{2... | collective-permute-start | bytes 2752520 | tf_op jit(solution)/shard_map/ppermute | solution.py:331
  7.6 2.0 %collective-permute-start = (s32[4,2]{0,1:T(2,128)S(1)}, s32[4,2]{0,1:T(2,128)S(1)}, u32[]{:S(2)}, u32[]{:S(2)}) collective-permute-start(s32[4,2]{0,1:T(2,128)S(1)} %copy-done), channel_id=1, source_target_pairs={{0,1},{1,0},{2,3},{3,2},{4,5},{5,4},{6,7},{7,6},{8,9},{9,8},{10,11... | collective-permute-start | bytes 104 | tf_op jit(solution)/shard_map/ppermute | solution.py:343
  23.3 6.1 %collective-permute-start.2 = (bf16[1792,128]{1,0:T(8,128)(2,1)S(1)}, bf16[1792,128]{1,0:T(8,128)(2,1)S(1)}, u32[]{:S(2)}, u32[]{:S(2)}) collective-permute-start(bf16[1792,128]{1,0:T(8,128)(2,1)S(1)} %get-tuple-element.88), channel_id=1, source_target_pairs={{0,1},{1,0},{2,3},{3,2},{4,5},{5,4},{6,7},{7,6},{8,9},{9,8},{10,11... | collective-permute-start | bytes 1376264 | tf_op jit(solution)/shard_map/ppermute | solution.py:343
  25.9 3.5 %collective-permute-start.3 = (bf16[1792,128]{1,0:T(8,128)(2,1)S(1)}, bf16[1792,128]{1,0:T(8,128)(2,1)S(1)}, u32[]{:S(2)}, u32[]{:S(2)}) collective-permute-start(bf16[1792,128]{1,0:T(8,128)(2,1)S(1)} %get-tuple-element.89), channel_id=1, source_target_pairs={{0,1},{1,0},{2,3},{3,2},{4,5},{5,4},{6,7},{7,6},{8,9},{9,8},{10,11... | collective-permute-start | bytes 1376264 | tf_op jit(solution)/shard_map/ppermute | solution.py:343
  26.0 5.4 %collective-permute-start.5 = (s32[8,2]{0,1:T(2,128)S(1)}, s32[8,2]{0,1:T(2,128)S(1)}, u32[]{:S(2)}, u32[]{:S(2)}) collective-permute-start(s32[8,2]{0,1:T(2,128)S(1)} %pad_add_fusion), channel_id=1, source_target_pairs={{0,2},{2,4},{4,6},{6,8},{8,10},{10,12},{12,14},{14,16},{16,18},{18... | collective-permute-start | bytes 200 | tf_op jit(solution)/shard_map/ppermute | solution.py:368
  33.1 1.9 %collective-permute-start.7 = (f32[2,64,512]{2,1,0:T(8,128)S(1)}, f32[2,64,512]{2,1,0:T(8,128)S(1)}, u32[]{:S(2)}, u32[]{:S(2)}) collective-permute-start(f32[2,64,512]{2,1,0:T(8,128)S(1)} %get-tuple-element.61), channel_id=1, source_target_pairs={{0,1},{1,0},{2,3},{3,2},{4,5},{5,4},{6,7},{7,6},{8,9},{9,8},{10,11... | collective-permute-start | bytes 786440 | tf_op jit(solution)/shard_map/ppermute | solution.py:343
  33.8 5.6 %collective-permute-start.6 = (f32[2,64,512]{2,1,0:T(8,128)S(1)}, f32[2,64,512]{2,1,0:T(8,128)S(1)}, u32[]{:S(2)}, u32[]{:S(2)}) collective-permute-start(f32[2,64,512]{2,1,0:T(8,128)S(1)} %get-tuple-element.59), channel_id=1, source_target_pairs={{0,1},{1,0},{2,3},{3,2},{4,5},{5,4},{6,7},{7,6},{8,9},{9,8},{10,11... | collective-permute-start | bytes 786440 | tf_op jit(solution)/shard_map/ppermute | solution.py:343
  35.1 10.1 %collective-permute-start.8 = (f32[2,64,512]{2,1,0:T(8,128)S(1)}, f32[2,64,512]{2,1,0:T(8,128)S(1)}, u32[]{:S(2)}, u32[]{:S(2)}) collective-permute-start(f32[2,64,512]{2,1,0:T(8,128)S(1)} %add.36), channel_id=1, source_target_pairs={{0,2},{2,0},{4,6},{6,4},{8,10},{10,8},{12,14},{14,12},{16,18},{18,... | collective-permute-start | bytes 786440 | tf_op jit(solution)/shard_map/ppermute | solution.py:331
  38.8 7.2 %collective-permute-start.9 = (f32[2,64,512]{2,1,0:T(8,128)S(1)}, f32[2,64,512]{2,1,0:T(8,128)S(1)}, u32[]{:S(2)}, u32[]{:S(2)}) collective-permute-start(f32[2,64,512]{2,1,0:T(8,128)S(1)} %get-tuple-element.62.ours), channel_id=1, source_target_pairs={{2,4},{4,2},{6,8},{8,6},{10,12},{12,10},{14,16},{16,14},{18,20},{2... | collective-permute-start | bytes 786440 | tf_op jit(solution)/shard_map/ppermute | solution.py:331
  45.3 6.8 %collective-permute-start.11 = (f32[2,64,512]{2,1,0:T(8,128)S(1)}, f32[2,64,512]{2,1,0:T(8,128)S(1)}, u32[]{:S(2)}, u32[]{:S(2)}) collective-permute-start(f32[2,64,512]{2,1,0:T(8,128)S(1)} %shard_map.91.partial), channel_id=1, source_target_pairs={{2,4},{4,2},{6,8},{8,6},{10,12},{12,10},{14,16},{16,14},{18,20},{2... | collective-permute-start | bytes 786440 | tf_op jit(solution)/shard_map/ppermute | solution.py:331
  46.0 6.1 %collective-permute-start.10 = (bf16[2,128,512]{2,1,0:T(8,128)(2,1)S(1)}, bf16[2,128,512]{2,1,0:T(8,128)(2,1)S(1)}, u32[]{:S(2)}, u32[]{:S(2)}) collective-permute-start(bf16[2,128,512]{2,1,0:T(8,128)(2,1)S(1)} %get-tuple-element.65.refs_1_.refs_2_), channel_id=1, source_target_pairs={{0,1},{1,0},{2,3},{3,2},{4,5},{5,4},{6,7},{7,6},{8,9},{9,8},{10,11... | collective-permute-start | bytes 786440 | tf_op jit(solution)/shard_map/ppermute | solution.py:343
  47.0 11.6 %collective-permute-start.12 = (bf16[2,128,512]{2,1,0:T(8,128)(2,1)S(1)}, bf16[2,128,512]{2,1,0:T(8,128)(2,1)S(1)}, u32[]{:S(2)}, u32[]{:S(2)}) collective-permute-start(bf16[2,128,512]{2,1,0:T(8,128)(2,1)S(1)} %get-tuple-element.65.refs_1_.refs_2_), channel_id=1, source_target_pairs={{0,2},{2,0},{4,6},{6,4},{8,10},{10,8},{12,14},{14,12},{16,18},{18,... | collective-permute-start | bytes 786440 | tf_op jit(solution)/shard_map/ppermute | solution.py:331
  58.6 1.8 %collective-permute-start.13 = (bf16[128,512]{1,0:T(8,128)(2,1)S(1)}, bf16[128,512]{1,0:T(8,128)(2,1)S(1)}, u32[]{:S(2)}, u32[]{:S(2)}) collective-permute-start(bf16[128,512]{1,0:T(8,128)(2,1)S(1)} %get-tuple-element.90), channel_id=1, source_target_pairs={{0,1},{1,0},{2,3},{3,2},{4,5},{5,4},{6,7},{7,6},{8,9},{9,8},{10,11... | collective-permute-start | bytes 393224 | tf_op jit(solution)/shard_map/ppermute | solution.py:343
  59.4 1.3 %collective-permute-start.14 = (bf16[128,512]{1,0:T(8,128)(2,1)S(1)}, bf16[128,512]{1,0:T(8,128)(2,1)S(1)}, u32[]{:S(2)}, u32[]{:S(2)}) collective-permute-start(bf16[128,512]{1,0:T(8,128)(2,1)S(1)} %get-tuple-element.91), channel_id=1, source_target_pairs={{0,1},{1,0},{2,3},{3,2},{4,5},{5,4},{6,7},{7,6},{8,9},{9,8},{10,11... | collective-permute-start | bytes 393224 | tf_op jit(solution)/shard_map/ppermute | solution.py:343
  62.8 1.6 %collective-permute-start.16 = (f32[2,64,512]{2,1,0:T(8,128)S(1)}, f32[2,64,512]{2,1,0:T(8,128)S(1)}, u32[]{:S(2)}, u32[]{:S(2)}) collective-permute-start(f32[2,64,512]{2,1,0:T(8,128)S(1)} %get-tuple-element.81), channel_id=1, source_target_pairs={{0,1},{1,0},{2,3},{3,2},{4,5},{5,4},{6,7},{7,6},{8,9},{9,8},{10,11... | collective-permute-start | bytes 786440 | tf_op jit(solution)/shard_map/ppermute | solution.py:343
  63.2 5.9 %collective-permute-start.15 = (f32[2,64,512]{2,1,0:T(8,128)S(1)}, f32[2,64,512]{2,1,0:T(8,128)S(1)}, u32[]{:S(2)}, u32[]{:S(2)}) collective-permute-start(f32[2,64,512]{2,1,0:T(8,128)S(1)} %get-tuple-element.79), channel_id=1, source_target_pairs={{0,1},{1,0},{2,3},{3,2},{4,5},{5,4},{6,7},{7,6},{8,9},{9,8},{10,11... | collective-permute-start | bytes 786440 | tf_op jit(solution)/shard_map/ppermute | solution.py:343
  63.4 5.7 %collective-permute-start.18 = (f32[2,64,512]{2,1,0:T(8,128)S(1)}, f32[2,64,512]{2,1,0:T(8,128)S(1)}, u32[]{:S(2)}, u32[]{:S(2)}) collective-permute-start(f32[2,64,512]{2,1,0:T(8,128)S(1)} %get-tuple-element.82), channel_id=1, source_target_pairs={{2,4},{4,2},{6,8},{8,6},{10,12},{12,10},{14,16},{16,14},{18,20},{2... | collective-permute-start | bytes 786440 | tf_op jit(solution)/shard_map/ppermute | solution.py:331
  64.5 10.3 %collective-permute-start.17 = (f32[2,64,512]{2,1,0:T(8,128)S(1)}, f32[2,64,512]{2,1,0:T(8,128)S(1)}, u32[]{:S(2)}, u32[]{:S(2)}) collective-permute-start(f32[2,64,512]{2,1,0:T(8,128)S(1)} %add.37), channel_id=1, source_target_pairs={{0,2},{2,0},{4,6},{6,4},{8,10},{10,8},{12,14},{14,12},{16,18},{18,... | collective-permute-start | bytes 786440 | tf_op jit(solution)/shard_map/ppermute | solution.py:331
  75.3 2.0 %collective-permute-start.19 = (f32[32,128]{1,0:T(8,128)S(1)}, f32[32,128]{1,0:T(8,128)S(1)}, u32[]{:S(2)}, u32[]{:S(2)}) collective-permute-start(f32[32,128]{1,0:T(8,128)S(1)} %get-tuple-element.84), channel_id=1, source_target_pairs={{0,1},{1,0},{2,3},{3,2},{4,5},{5,4},{6,7},{7,6},{8,9},{9,8},{10,11... | collective-permute-start | bytes 49160 | tf_op jit(solution)/shard_map/ppermute | solution.py:343
  102.6 12.0 %all-to-all-start.1 = ((f32[8,32,128]{2,1,0:T(8,128)}), f32[8,32,128]{2,1,0:T(8,128)S(1)}, u32[]{:S(2)}, u32[]{:S(2)}) async-start(f32[8,32,128]{2,1,0:T(8,128)} %shard_map.101), calls=%async_computation.1 | async-start | bytes 262144 | tf_op jit(solution)/shard_map/all_to_all | solution.py:400
  106.6 11.3 %collective-permute-start.21 = (f32[64,512]{1,0:T(8,128)S(1)}, f32[64,512]{1,0:T(8,128)S(1)}, u32[]{:S(2)}, u32[]{:S(2)}) collective-permute-start(f32[64,512]{1,0:T(8,128)S(1)} %get-tuple-element.85), channel_id=1, source_target_pairs={{0,1},{1,0},{2,3},{3,2},{4,5},{5,4},{6,7},{7,6},{8,9},{9,8},{10,11... | collective-permute-start | bytes 393224 | tf_op jit(solution)/shard_map/ppermute | solution.py:343
  114.7 4.1 %collective-permute-start.20 = (f32[32,128]{1,0:T(8,128)S(1)}, f32[32,128]{1,0:T(8,128)S(1)}, u32[]{:S(2)}, u32[]{:S(2)}) collective-permute-start(f32[32,128]{1,0:T(8,128)S(1)} %reduce_sum.9.mine_ref), channel_id=1, source_target_pairs={{0,1},{1,0},{2,3},{3,2},{4,5},{5,4},{6,7},{7,6},{8,9},{9,8},{10,11... | collective-permute-start | bytes 49160 | tf_op jit(solution)/shard_map/ppermute | solution.py:343

commit v10 on v6

--- a/solution.py
+++ b/solution.py
@@ -91,12 +91,13 @@
 
 
 def make_tiles(left, rights, tile_ref, slot):
-    whole = unit_rows(left, 0, HALF)
     for side in range(2):
         for at in range(0, HALF, 256):
-            tile_ref[slot, side, :, at : at + 256] = affinity_tile(
-                whole, unit_rows(rights[side], at, 256)
-            )
+            right = unit_rows(rights[side], at, 256)
+            for row in range(0, HALF, 256):
+                tile_ref[slot, side, row : row + 256, at : at + 256] = affinity_tile(
+                    unit_rows(left, row, 256), right
+                )
 
 
 def use_tiles(tile_ref, slot, rights, left, done_ref, done_at, part_refs, part_at, partial):

time: 124 us -> 124 us (level); the launches traced: 124 us -> 126 us
  blocking collectives: 27.6 us -> 30.9 us
    all_to_all x1, blocking collectives: 27.6 us -> 30.9 us  [sum_over_chips(): lax.all_to_all(copies, 'rows', 0, 0, axis_index_groups=groups, tiled=True)]
    all_to_all x1, starting transfers between devices: 5.33 us -> 3.83 us  [sum_over_chips(): lax.all_to_all(copies, 'rows', 0, 0, axis_index_groups=groups, tiled=True)]
  transfers between devices with their start and end apart: 23 -> 23, of which waited for: 10 -> 10; matrix products, arithmetic and copies ran while one was open for 0% -> 0% of each run, Pallas kernels for 8% -> 7%
where the time goes in v10:
time: 124 us; the launch traced here: 126 us
  starting transfers between devices  42 us (34%)
  waiting for transfers between devices  34.6 us (28%)
  blocking collectives  30.9 us (25%)
  Pallas kernels  17.2 us (14%)
    all_to_all x1, blocking collectives, sum_over_chips(): lax.all_to_all(copies, 'rows', 0, 0, axis_index_groups=groups, tiled=True)  30.9 us
    ppermute x8, waiting for transfers between devices, exchange(): return lax.ppermute(value, 'rows', links)  25.5 us
    ppermute x8, starting transfers between devices, exchange(): return lax.ppermute(value, 'rows', links)  18.4 us
    ppermute x13, starting transfers between devices, swap(): return lax.ppermute(value, 'cols', [(0, 1), (1, 0)])  16.4 us
    all_to_all x1, waiting for transfers between devices, sum_over_chips(): lax.all_to_all(copies, 'rows', 0, 0, axis_index_groups=groups, tiled=True)  5.87 us
    all_to_all x1, starting transfers between devices, sum_over_chips(): lax.all_to_all(copies, 'rows', 0, 0, axis_index_groups=groups, tiled=True)  3.83 us
    ppermute x1, starting transfers between devices, own_flags_and_list(): lax.ppermute(own, 'rows', [(r, r + 1) for r in range(lax.axis_size('rows'...  3.36 us
    ppermute x13, waiting for transfers between devices, swap(): return lax.ppermute(value, 'cols', [(0, 1), (1, 0)])  3.24 us
  transfers between devices with their start and end apart: 23, of which 10 were waited for; matrix products, arithmetic and copies ran while one was open for 0% of the time, Pallas kernels for 7%

profile of v10, /device:TPU:1, one launch (start us, length us, event | category | flops | bytes accessed | tf_op | source)
XLA Modules:
  0.0 126.3 jit_solution(18118175872650646131)
XLA Ops:
  0.6 0.0 copy-start.3
  0.6 0.0 copy-start.4
  0.7 0.0 copy-start.1
  0.7 0.0 copy-start.2
  0.7 1.4 %shard_map.87.refs_0_.refs_1_ = bf16[2,1792,128]{2,1,0:T(8,128)(2,1)S(1)} custom-call(s32[1]{0:T(128)} %bitcast.core_ref, bf16[2048,384]{1,0:T(8,128)(2,1)} %rows_ref.3, bf16[64,2048]{1,0:T(8,128)(2,1)} %bitcast.23), custom_call_target="tpu_custom_call" | custom-call | flops 10000 | bytes 10000 | tf_op jit(solution)/shard_map/pallas_call | solution.py:391
  2.1 2.2 %collective-permute-start.1 = (bf16[2,1792,128]{2,1,0:T(8,128)(2,1)S(1)}, bf16[2,1792,128]{2,1,0:T(8,128)(2,1)S(1)}, u32[]{:S(2)}, u32[]{:S(2)}) collective-permute-start(bf16[2,1792,128]{2,1,0:T(8,128)(2,1)S(1)} %shard_map.87.refs_0_.refs_1_), channel_id=1, source_target_pairs={{0,2},{2,0},{4,6},{6,4},{8,10},{10,8},{12,14},{14,12},{16,18},{18,... | collective-permute-start | bytes 2752520 | tf_op jit(solution)/shard_map/ppermute | solution.py:304
  4.3 1.6 %collective-permute-start.4 = (bf16[2,1792,128]{2,1,0:T(8,128)(2,1)S(1)}, bf16[2,1792,128]{2,1,0:T(8,128)(2,1)}, u32[]{:S(2)}, u32[]{:S(2)}) collective-permute-start(bf16[2,1792,128]{2,1,0:T(8,128)(2,1)S(1)} %shard_map.87.refs_0_.refs_1_), channel_id=1, source_target_pairs={{2,4},{4,2},{6,8},{8,6},{10,12},{12,10},{14,16},{16,14},{18,20},{2... | collective-permute-start | bytes 2752520 | tf_op jit(solution)/shard_map/ppermute | solution.py:304
  5.9 1.4 %shard_map.86.refs_1_.refs_2_ = bf16[2,1792,128]{2,1,0:T(8,128)(2,1)S(1)} custom-call(s32[1]{0:T(128)} %bitcast.core_ref, bf16[2048,384]{1,0:T(8,128)(2,1)} %rows_ref.3, bf16[64,2048]{1,0:T(8,128)(2,1)} %bitcast.24), custom_call_target="tpu_custom_call" | custom-call | flops 10000 | bytes 10000 | tf_op jit(solution)/shard_map/pallas_call | solution.py:391
  7.3 1.2 collective-permute-start
  8.5 0.8 collective-permute-done
  9.4 0.1 pad_add_fusion
  9.4 0.1 and_reduce_fusion
  9.5 2.7 %shard_map.88 = (bf16[3,2,512,512]{3,2,1,0:T(8,128)(2,1)S(1)}, f32[2,64,512]{2,1,0:T(8,128)S(1)}, f32[2,64,512]{2,1,0:T(8,128)S(1)}, f32[2,64,512]{2,1,0:T(8,128)S(1)}) custom-call(s32[11]{0:T(128)S(1)} %convert_element_type.6.flags_ref, bf16[2,1792,128]{2,1,0:T(8,128)(2,1)S(1)} %shard_map.87.refs_0_.refs_1_, bf16[2,1792,128]{2,1,0:T(8,128)(2,1)S(1)} %shard_map.86.refs_1_.refs_2_), custom_call_target="tpu_custom_call" | custom-call | flops 10000 | bytes 10000 | tf_op jit(solution)/shard_map/pallas_call | solution.py:413
  12.3 10.9 %collective-permute-done.1.refs_1_.refs_3_ = bf16[2,1792,128]{2,1,0:T(8,128)(2,1)S(1)} collective-permute-done((bf16[2,1792,128]{2,1,0:T(8,128)(2,1)S(1)}, bf16[2,1792,128]{2,1,0:T(8,128)(2,1)S(1)}, u32[]{:S(2)}, u32[]{:S(2)}) %collective-permute-start.1) | collective-permute-done | bytes 917536 | tf_op jit(solution)/shard_map/ppermute | solution.py:304
  23.1 0.1 slice_bitcast_fusion.1
  23.2 2.6 %collective-permute-start.2 = (bf16[1792,128]{1,0:T(8,128)(2,1)S(1)}, bf16[1792,128]{1,0:T(8,128)(2,1)S(1)}, u32[]{:S(2)}, u32[]{:S(2)}) collective-permute-start(bf16[1792,128]{1,0:T(8,128)(2,1)S(1)} %get-tuple-element.84), channel_id=1, source_target_pairs={{0,1},{1,0},{2,3},{3,2},{4,5},{5,4},{6,7},{7,6},{8,9},{9,8},{10,11... | collective-permute-start | bytes 1376264 | tf_op jit(solution)/shard_map/ppermute | solution.py:316
  25.8 0.1 collective-permute-start.3
  25.9 3.4 %collective-permute-start.5 = (s32[8,2]{0,1:T(2,128)S(1)}, s32[8,2]{0,1:T(2,128)S(1)}, u32[]{:S(2)}, u32[]{:S(2)}) collective-permute-start(s32[8,2]{0,1:T(2,128)S(1)} %pad_add_fusion), channel_id=1, source_target_pairs={{0,2},{2,4},{4,6},{6,8},{8,10},{10,12},{12,14},{14,16},{16,18},{18... | collective-permute-start | bytes 200 | tf_op jit(solution)/shard_map/ppermute | solution.py:341
  29.3 0.0 collective-permute-done.2
  29.3 0.1 pad_maximum_fusion.refs_2_.refs_4_
  29.4 1.9 %shard_map.89 = (bf16[4,2,512,512]{3,2,1,0:T(8,128)(2,1)S(1)}, f32[2,64,512]{2,1,0:T(8,128)S(1)}, f32[2,64,512]{2,1,0:T(8,128)S(1)}, f32[2,64,512]{2,1,0:T(8,128)S(1)}) custom-call(s32[11]{0:T(128)S(1)} %convert_element_type.6.flags_ref, bf16[2,1792,128]{2,1,0:T(8,128)(2,1)S(1)} %shard_map.87.refs_0_.refs_1_, ...), custom_call_target="tpu_custom_call" | custom-call | flops 10000 | bytes 10000 | tf_op jit(solution)/shard_map/pallas_call | solution.py:418
  31.3 0.0 collective-permute-done.4.refs_0_
  31.3 0.2 and_reduce_fusion.1
  31.5 1.4 %shard_map.90 = (bf16[8,2,512,512]{3,2,1,0:T(8,128)(2,1)S(1)}, f32[2,64,512]{2,1,0:T(8,128)S(1)}, f32[2,64,512]{2,1,0:T(8,128)S(1)}, f32[2,64,512]{2,1,0:T(8,128...) custom-call(s32[11]{0:T(128)S(1)} %convert_element_type.6.flags_ref, s32[4]{0:T(128)S(1)} %convert_element_type.7.far_ref, ...), custom_call_target="tpu_custom_call" | custom-call | flops 1000000000 | bytes 1000000 | tf_op jit(solution)/shard_map/pallas_call | solution.py:423
  32.9 0.8 collective-permute-start.8
  33.7 0.1 collective-permute-start.6
  33.8 0.7 collective-permute-start.7
  34.5 0.4 collective-permute-done.8
  34.9 5.9 %collective-permute-start.9 = (f32[2,64,512]{2,1,0:T(8,128)S(1)}, f32[2,64,512]{2,1,0:T(8,128)S(1)}, u32[]{:S(2)}, u32[]{:S(2)}) collective-permute-start(f32[2,64,512]{2,1,0:T(8,128)S(1)} %add.36), channel_id=1, source_target_pairs={{0,2},{2,0},{4,6},{6,4},{8,10},{10,8},{12,14},{14,12},{16,18},{18,... | collective-permute-start | bytes 786440 | tf_op jit(solution)/shard_map/ppermute | solution.py:304
  40.8 0.0 collective-permute-done.7.from_odd
  40.8 6.0 %collective-permute-done.9.from_even = f32[2,64,512]{2,1,0:T(8,128)S(1)} collective-permute-done((f32[2,64,512]{2,1,0:T(8,128)S(1)}, f32[2,64,512]{2,1,0:T(8,128)S(1)}, u32[]{:S(2)}, u32[]{:S(2)}) %collective-permute-start.9) | collective-permute-done | bytes 262176 | tf_op jit(solution)/shard_map/ppermute | solution.py:304
  46.8 0.1 shard_map.91
  46.9 1.2 collective-permute-start.10
  48.2 0.7 collective-permute-start.14
  48.8 1.9 %collective-permute-start.13 = (bf16[2,128,512]{2,1,0:T(8,128)(2,1)S(1)}, bf16[2,128,512]{2,1,0:T(8,128)(2,1)S(1)}, u32[]{:S(2)}, u32[]{:S(2)}) collective-permute-start(bf16[2,128,512]{2,1,0:T(8,128)(2,1)S(1)} %get-tuple-element.63.refs_1_.refs_2_), channel_id=1, source_target_pairs={{0,1},{1,0},{2,3},{3,2},{4,5},{5,4},{6,7},{7,6},{8,9},{9,8},{10,11... | collective-permute-start | bytes 786440 | tf_op jit(solution)/shard_map/ppermute | solution.py:316
  50.8 2.8 %collective-permute-done.10.refs_2_.refs_4_ = bf16[2,128,512]{2,1,0:T(8,128)(2,1)S(1)} collective-permute-done((bf16[2,128,512]{2,1,0:T(8,128)(2,1)S(1)}, bf16[2,128,512]{2,1,0:T(8,128)(2,1)S(1)}, u32[]{:S(2)}, u32[]{:S(2)}) %collective-permute-start.10) | collective-permute-done | bytes 262176 | tf_op jit(solution)/shard_map/ppermute | solution.py:304
  53.6 2.3 %collective-permute-start.11 = (bf16[128,512]{1,0:T(8,128)(2,1)S(1)}, bf16[128,512]{1,0:T(8,128)(2,1)S(1)}, u32[]{:S(2)}, u32[]{:S(2)}) collective-permute-start(bf16[128,512]{1,0:T(8,128)(2,1)S(1)} %get-tuple-element.86), channel_id=1, source_target_pairs={{0,1},{1,0},{2,3},{3,2},{4,5},{5,4},{6,7},{7,6},{8,9},{9,8},{10,11... | collective-permute-start | bytes 393224 | tf_op jit(solution)/shard_map/ppermute | solution.py:316
  55.9 0.3 collective-permute-start.12
  56.1 0.0 collective-permute-done.13.refs_2_.refs_3_
  56.1 1.6 %shard_map.93 = (f32[2,64,512]{2,1,0:T(8,128)S(1)}, f32[2,64,512]{2,1,0:T(8,128)S(1)}, f32[2,64,512]{2,1,0:T(8,128)S(1)}) custom-call(s32[11]{0:T(128)S(1)} %convert_element_type.6.flags_ref, bf16[3,2,512,512]{3,2,1,0:T(8,128)(2,1)S(1)} %get-tuple-element.64.refs_0_, bf16[2,128,512]{2,1,0:T(8,128)(2,1)S(1)} %get-tuple-element.63.refs_1_.refs_2_, ...), custom_call_target="tpu_custom_call" | custom-call | flops 10000 | bytes 10000 | tf_op jit(solution)/shard_map/pallas_call | solution.py:439
  57.8 0.0 collective-permute-done.12
  57.8 1.3 %shard_map.94 = (f32[2,64,512]{2,1,0:T(8,128)S(1)}, f32[2,64,512]{2,1,0:T(8,128)S(1)}, f32[2,64,512]{2,1,0:T(8,128)S(1)}) custom-call(s32[11]{0:T(128)S(1)} %convert_element_type.6.flags_ref, bf16[4,2,512,512]{3,2,1,0:T(8,128)(2,1)S(1)} %get-tuple-element.62.refs_0_, bf16[2,128,512]{2,1,0:T(8,128)(2,1)S(1)} %get-tuple-element.63.refs_1_.refs_2_, ...), custom_call_target="tpu_custom_call" | custom-call | flops 10000 | bytes 10000 | tf_op jit(solution)/shard_map/pallas_call | solution.py:443
  59.1 0.0 collective-permute-done.14.refs_1_
  59.1 0.8 shard_map.95
  59.9 0.3 collective-permute-start.17
  60.2 0.3 collective-permute-start.15
  60.5 0.7 collective-permute-start.16
  61.2 0.4 collective-permute-done.17
  61.6 5.5 %collective-permute-start.18 = (f32[2,64,512]{2,1,0:T(8,128)S(1)}, f32[2,64,512]{2,1,0:T(8,128)S(1)}, u32[]{:S(2)}, u32[]{:S(2)}) collective-permute-start(f32[2,64,512]{2,1,0:T(8,128)S(1)} %add.37), channel_id=1, source_target_pairs={{0,2},{2,0},{4,6},{6,4},{8,10},{10,8},{12,14},{14,12},{16,18},{18,... | collective-permute-start | bytes 786440 | tf_op jit(solution)/shard_map/ppermute | solution.py:304
  67.0 0.4 shard_map.92.first_ref
  67.5 0.0 collective-permute-done.16.from_odd
  67.5 5.8 %collective-permute-done.18.from_even = f32[2,64,512]{2,1,0:T(8,128)S(1)} collective-permute-done((f32[2,64,512]{2,1,0:T(8,128)S(1)}, f32[2,64,512]{2,1,0:T(8,128)S(1)}, u32[]{:S(2)}, u32[]{:S(2)}) %collective-permute-start.18) | collective-permute-done | bytes 262176 | tf_op jit(solution)/shard_map/ppermute | solution.py:304
  73.3 0.1 shard_map.96.value_ref
  73.4 0.4 shard_map.97
  73.8 1.1 collective-permute-start.19
  74.9 0.8 collective-permute-done.19.refs_1_
  75.8 30.9 %all_to_all.10.refs_0_ = f32[16,32,128]{2,1,0:T(8,128)S(1)} all-to-all(f32[16,32,128]{2,1,0:T(8,128)S(1)} %shard_map.98), channel_id=1, replica_groups={{0,2,4,6,64,66,68,70,128,130,132,134,192,194,196,198},{8,10,12,14,72,74..., dimensions={0} | all-to-all | bytes 524288 | tf_op jit(solution)/shard_map/all_to_all | solution.py:373
  106.6 0.7 shard_map.99
  107.3 3.8 %all-to-all-start.1 = ((f32[8,32,128]{2,1,0:T(8,128)}), f32[8,32,128]{2,1,0:T(8,128)S(1)}, u32[]{:S(2)}, u32[]{:S(2)}) async-start(f32[8,32,128]{2,1,0:T(8,128)} %shard_map.99), calls=%async_computation.1 | async-start | bytes 262144 | tf_op jit(solution)/shard_map/all_to_all | solution.py:373
  111.1 2.2 %collective-permute-start.21 = (f32[64,512]{1,0:T(8,128)S(1)}, f32[64,512]{1,0:T(8,128)S(1)}, u32[]{:S(2)}, u32[]{:S(2)}) collective-permute-start(f32[64,512]{1,0:T(8,128)S(1)} %get-tuple-element.81), channel_id=1, source_target_pairs={{0,1},{1,0},{2,3},{3,2},{4,5},{5,4},{6,7},{7,6},{8,9},{9,8},{10,11... | collective-permute-start | bytes 393224 | tf_op jit(solution)/shard_map/ppermute | solution.py:316
  113.3 5.9 %all-to-all-done.1 = f32[8,32,128]{2,1,0:T(8,128)S(1)} async-done(((f32[8,32,128]{2,1,0:T(8,128)}), f32[8,32,128]{2,1,0:T(8,128)S(1)}, u32[]{:S(2)}, u32[]{:S(2)}) %all-to-all-start.1) | async-done | bytes 131104 | tf_op jit(solution)/shard_map/all_to_all | solution.py:373
  119.2 3.3 %collective-permute-start.20 = (f32[32,128]{1,0:T(8,128)S(1)}, f32[32,128]{1,0:T(8,128)S(1)}, u32[]{:S(2)}, u32[]{:S(2)}) collective-permute-start(f32[32,128]{1,0:T(8,128)S(1)} %reduce_sum.9.mine_ref), channel_id=1, source_target_pairs={{0,1},{1,0},{2,3},{3,2},{4,5},{5,4},{6,7},{7,6},{8,9},{9,8},{10,11... | collective-permute-start | bytes 49160 | tf_op jit(solution)/shard_map/ppermute | solution.py:316
  122.5 0.8 collective-permute-done.20.other_ref
  123.3 3.0 %shard_map.100 = (f32[64,1024]{1,0:T(8,128)}, f32[64,64]{1,0:T(8,128)}) custom-call(s32[1]{0:T(128)} %bitcast.core_ref, f32[32,128]{1,0:T(8,128)S(1)} %reduce_sum.9.mine_ref, f32[32,128]{1,0:T(8,128)S(1)} %collective-permute-done.20.other_ref, f32[2,64,512]{2,1,0:T(8,128)S(1)} %shard_map.96.value_ref, f32[64,512]{1,0:T(8,128)S(1)} %collective-permute-done.21.got_ref), custom_call_target="tpu_custom_call" | custom-call | flops 100000000 | bytes 1000000 | tf_op jit(solution)/shard_map/pallas_call | solution.py:464
  (26 shorter events, 0.2 us)
Async XLA Ops:
  0.6 7.9 %copy-start.3 = (s32[11]{0:T(128)S(1)}, s32[11]{0:T(128)}, u32[]{:S(2)}) copy-start(s32[11]{0:T(128)} %constant.40.clone) | copy-start | bytes 136
  0.6 7.9 %copy-start.4 = (s32[11]{0:T(128)S(1)}, s32[11]{0:T(128)}, u32[]{:S(2)}) copy-start(s32[11]{0:T(128)} %constant.39.clone) | copy-start | bytes 136
  0.7 6.6 %copy-start = (s32[4,2]{0,1:T(2,128)S(1)}, s32[4,2]{0,1:T(2,128)}, u32[]{:S(2)}) copy-start(s32[4,2]{0,1:T(2,128)} %param.9) | copy-start | bytes 100
  0.7 25.2 %copy-start.1 = (s32[4]{0:T(128)S(1)}, s32[4]{0:T(128)}, u32[]{:S(2)}) copy-start(s32[4]{0:T(128)} %constant.42.clone) | copy-start | bytes 52
  0.7 25.2 %copy-start.2 = (s32[4]{0:T(128)S(1)}, s32[4]{0:T(128)}, u32[]{:S(2)}) copy-start(s32[4]{0:T(128)} %constant.41.clone) | copy-start | bytes 52
  2.1 21.0 %collective-permute-start.1 = (bf16[2,1792,128]{2,1,0:T(8,128)(2,1)S(1)}, bf16[2,1792,128]{2,1,0:T(8,128)(2,1)S(1)}, u32[]{:S(2)}, u32[]{:S(2)}) collective-permute-start(bf16[2,1792,128]{2,1,0:T(8,128)(2,1)S(1)} %shard_map.87.refs_0_.refs_1_), channel_id=1, source_target_pairs={{0,2},{2,0},{4,6},{6,4},{8,10},{10,8},{12,14},{14,12},{16,18},{18,... | collective-permute-start | bytes 2752520 | tf_op jit(solution)/shard_map/ppermute | solution.py:304
  4.3 27.0 %collective-permute-start.4 = (bf16[2,1792,128]{2,1,0:T(8,128)(2,1)S(1)}, bf16[2,1792,128]{2,1,0:T(8,128)(2,1)}, u32[]{:S(2)}, u32[]{:S(2)}) collective-permute-start(bf16[2,1792,128]{2,1,0:T(8,128)(2,1)S(1)} %shard_map.87.refs_0_.refs_1_), channel_id=1, source_target_pairs={{2,4},{4,2},{6,8},{8,6},{10,12},{12,10},{14,16},{16,14},{18,20},{2... | collective-permute-start | bytes 2752520 | tf_op jit(solution)/shard_map/ppermute | solution.py:304
  7.3 2.0 %collective-permute-start = (s32[4,2]{0,1:T(2,128)S(1)}, s32[4,2]{0,1:T(2,128)S(1)}, u32[]{:S(2)}, u32[]{:S(2)}) collective-permute-start(s32[4,2]{0,1:T(2,128)S(1)} %copy-done), channel_id=1, source_target_pairs={{0,1},{1,0},{2,3},{3,2},{4,5},{5,4},{6,7},{7,6},{8,9},{9,8},{10,11... | collective-permute-start | bytes 104 | tf_op jit(solution)/shard_map/ppermute | solution.py:316
  23.2 6.1 %collective-permute-start.2 = (bf16[1792,128]{1,0:T(8,128)(2,1)S(1)}, bf16[1792,128]{1,0:T(8,128)(2,1)S(1)}, u32[]{:S(2)}, u32[]{:S(2)}) collective-permute-start(bf16[1792,128]{1,0:T(8,128)(2,1)S(1)} %get-tuple-element.84), channel_id=1, source_target_pairs={{0,1},{1,0},{2,3},{3,2},{4,5},{5,4},{6,7},{7,6},{8,9},{9,8},{10,11... | collective-permute-start | bytes 1376264 | tf_op jit(solution)/shard_map/ppermute | solution.py:316
  25.8 3.5 %collective-permute-start.3 = (bf16[1792,128]{1,0:T(8,128)(2,1)S(1)}, bf16[1792,128]{1,0:T(8,128)(2,1)S(1)}, u32[]{:S(2)}, u32[]{:S(2)}) collective-permute-start(bf16[1792,128]{1,0:T(8,128)(2,1)S(1)} %get-tuple-element.85), channel_id=1, source_target_pairs={{0,1},{1,0},{2,3},{3,2},{4,5},{5,4},{6,7},{7,6},{8,9},{9,8},{10,11... | collective-permute-start | bytes 1376264 | tf_op jit(solution)/shard_map/ppermute | solution.py:316
  25.9 5.4 %collective-permute-start.5 = (s32[8,2]{0,1:T(2,128)S(1)}, s32[8,2]{0,1:T(2,128)S(1)}, u32[]{:S(2)}, u32[]{:S(2)}) collective-permute-start(s32[8,2]{0,1:T(2,128)S(1)} %pad_add_fusion), channel_id=1, source_target_pairs={{0,2},{2,4},{4,6},{6,8},{8,10},{10,12},{12,14},{14,16},{16,18},{18... | collective-permute-start | bytes 200 | tf_op jit(solution)/shard_map/ppermute | solution.py:341
  32.9 1.9 %collective-permute-start.8 = (f32[2,64,512]{2,1,0:T(8,128)S(1)}, f32[2,64,512]{2,1,0:T(8,128)S(1)}, u32[]{:S(2)}, u32[]{:S(2)}) collective-permute-start(f32[2,64,512]{2,1,0:T(8,128)S(1)} %get-tuple-element.60), channel_id=1, source_target_pairs={{0,1},{1,0},{2,3},{3,2},{4,5},{5,4},{6,7},{7,6},{8,9},{9,8},{10,11... | collective-permute-start | bytes 786440 | tf_op jit(solution)/shard_map/ppermute | solution.py:316
  33.7 7.1 %collective-permute-start.6 = (f32[2,64,512]{2,1,0:T(8,128)S(1)}, f32[2,64,512]{2,1,0:T(8,128)S(1)}, u32[]{:S(2)}, u32[]{:S(2)}) collective-permute-start(f32[2,64,512]{2,1,0:T(8,128)S(1)} %get-tuple-element.57), channel_id=1, source_target_pairs={{0,1},{1,0},{2,3},{3,2},{4,5},{5,4},{6,7},{7,6},{8,9},{9,8},{10,11... | collective-permute-start | bytes 786440 | tf_op jit(solution)/shard_map/ppermute | solution.py:316
  33.8 7.0 %collective-permute-start.7 = (f32[2,64,512]{2,1,0:T(8,128)S(1)}, f32[2,64,512]{2,1,0:T(8,128)S(1)}, u32[]{:S(2)}, u32[]{:S(2)}) collective-permute-start(f32[2,64,512]{2,1,0:T(8,128)S(1)} %get-tuple-element.58), channel_id=1, source_target_pairs={{2,4},{4,2},{6,8},{8,6},{10,12},{12,10},{14,16},{16,14},{18,20},{2... | collective-permute-start | bytes 786440 | tf_op jit(solution)/shard_map/ppermute | solution.py:304
  34.9 11.9 %collective-permute-start.9 = (f32[2,64,512]{2,1,0:T(8,128)S(1)}, f32[2,64,512]{2,1,0:T(8,128)S(1)}, u32[]{:S(2)}, u32[]{:S(2)}) collective-permute-start(f32[2,64,512]{2,1,0:T(8,128)S(1)} %add.36), channel_id=1, source_target_pairs={{0,2},{2,0},{4,6},{6,4},{8,10},{10,8},{12,14},{14,12},{16,18},{18,... | collective-permute-start | bytes 786440 | tf_op jit(solution)/shard_map/ppermute | solution.py:304
  46.9 6.6 %collective-permute-start.10 = (bf16[2,128,512]{2,1,0:T(8,128)(2,1)S(1)}, bf16[2,128,512]{2,1,0:T(8,128)(2,1)S(1)}, u32[]{:S(2)}, u32[]{:S(2)}) collective-permute-start(bf16[2,128,512]{2,1,0:T(8,128)(2,1)S(1)} %get-tuple-element.63.refs_1_.refs_2_), channel_id=1, source_target_pairs={{0,2},{2,0},{4,6},{6,4},{8,10},{10,8},{12,14},{14,12},{16,18},{18,... | collective-permute-start | bytes 786440 | tf_op jit(solution)/shard_map/ppermute | solution.py:304
  48.2 10.9 %collective-permute-start.14 = (bf16[2,128,512]{2,1,0:T(8,128)(2,1)S(1)}, bf16[2,128,512]{2,1,0:T(8,128)(2,1)S(1)}, u32[]{:S(2)}, u32[]{:S(2)}) collective-permute-start(bf16[2,128,512]{2,1,0:T(8,128)(2,1)S(1)} %get-tuple-element.63.refs_1_.refs_2_), channel_id=1, source_target_pairs={{2,4},{4,2},{6,8},{8,6},{10,12},{12,10},{14,16},{16,14},{18,20},{2... | collective-permute-start | bytes 786440 | tf_op jit(solution)/shard_map/ppermute | solution.py:304
  48.8 7.3 %collective-permute-start.13 = (bf16[2,128,512]{2,1,0:T(8,128)(2,1)S(1)}, bf16[2,128,512]{2,1,0:T(8,128)(2,1)S(1)}, u32[]{:S(2)}, u32[]{:S(2)}) collective-permute-start(bf16[2,128,512]{2,1,0:T(8,128)(2,1)S(1)} %get-tuple-element.63.refs_1_.refs_2_), channel_id=1, source_target_pairs={{0,1},{1,0},{2,3},{3,2},{4,5},{5,4},{6,7},{7,6},{8,9},{9,8},{10,11... | collective-permute-start | bytes 786440 | tf_op jit(solution)/shard_map/ppermute | solution.py:316
  53.6 4.1 %collective-permute-start.11 = (bf16[128,512]{1,0:T(8,128)(2,1)S(1)}, bf16[128,512]{1,0:T(8,128)(2,1)S(1)}, u32[]{:S(2)}, u32[]{:S(2)}) collective-permute-start(bf16[128,512]{1,0:T(8,128)(2,1)S(1)} %get-tuple-element.86), channel_id=1, source_target_pairs={{0,1},{1,0},{2,3},{3,2},{4,5},{5,4},{6,7},{7,6},{8,9},{9,8},{10,11... | collective-permute-start | bytes 393224 | tf_op jit(solution)/shard_map/ppermute | solution.py:316
  55.9 1.9 %collective-permute-start.12 = (bf16[128,512]{1,0:T(8,128)(2,1)S(1)}, bf16[128,512]{1,0:T(8,128)(2,1)S(1)}, u32[]{:S(2)}, u32[]{:S(2)}) collective-permute-start(bf16[128,512]{1,0:T(8,128)(2,1)S(1)} %get-tuple-element.87), channel_id=1, source_target_pairs={{0,1},{1,0},{2,3},{3,2},{4,5},{5,4},{6,7},{7,6},{8,9},{9,8},{10,11... | collective-permute-start | bytes 393224 | tf_op jit(solution)/shard_map/ppermute | solution.py:316
  59.9 1.6 %collective-permute-start.17 = (f32[2,64,512]{2,1,0:T(8,128)S(1)}, f32[2,64,512]{2,1,0:T(8,128)S(1)}, u32[]{:S(2)}, u32[]{:S(2)}) collective-permute-start(f32[2,64,512]{2,1,0:T(8,128)S(1)} %get-tuple-element.78), channel_id=1, source_target_pairs={{0,1},{1,0},{2,3},{3,2},{4,5},{5,4},{6,7},{7,6},{8,9},{9,8},{10,11... | collective-permute-start | bytes 786440 | tf_op jit(solution)/shard_map/ppermute | solution.py:316
  60.2 7.3 %collective-permute-start.15 = (f32[2,64,512]{2,1,0:T(8,128)S(1)}, f32[2,64,512]{2,1,0:T(8,128)S(1)}, u32[]{:S(2)}, u32[]{:S(2)}) collective-permute-start(f32[2,64,512]{2,1,0:T(8,128)S(1)} %get-tuple-element.75), channel_id=1, source_target_pairs={{0,1},{1,0},{2,3},{3,2},{4,5},{5,4},{6,7},{7,6},{8,9},{9,8},{10,11... | collective-permute-start | bytes 786440 | tf_op jit(solution)/shard_map/ppermute | solution.py:316
  60.5 7.0 %collective-permute-start.16 = (f32[2,64,512]{2,1,0:T(8,128)S(1)}, f32[2,64,512]{2,1,0:T(8,128)S(1)}, u32[]{:S(2)}, u32[]{:S(2)}) collective-permute-start(f32[2,64,512]{2,1,0:T(8,128)S(1)} %get-tuple-element.76), channel_id=1, source_target_pairs={{2,4},{4,2},{6,8},{8,6},{10,12},{12,10},{14,16},{16,14},{18,20},{2... | collective-permute-start | bytes 786440 | tf_op jit(solution)/shard_map/ppermute | solution.py:304
  61.6 11.7 %collective-permute-start.18 = (f32[2,64,512]{2,1,0:T(8,128)S(1)}, f32[2,64,512]{2,1,0:T(8,128)S(1)}, u32[]{:S(2)}, u32[]{:S(2)}) collective-permute-start(f32[2,64,512]{2,1,0:T(8,128)S(1)} %add.37), channel_id=1, source_target_pairs={{0,2},{2,0},{4,6},{6,4},{8,10},{10,8},{12,14},{14,12},{16,18},{18,... | collective-permute-start | bytes 786440 | tf_op jit(solution)/shard_map/ppermute | solution.py:304
  73.8 1.9 %collective-permute-start.19 = (f32[32,128]{1,0:T(8,128)S(1)}, f32[32,128]{1,0:T(8,128)S(1)}, u32[]{:S(2)}, u32[]{:S(2)}) collective-permute-start(f32[32,128]{1,0:T(8,128)S(1)} %get-tuple-element.80), channel_id=1, source_target_pairs={{0,1},{1,0},{2,3},{3,2},{4,5},{5,4},{6,7},{7,6},{8,9},{9,8},{10,11... | collective-permute-start | bytes 49160 | tf_op jit(solution)/shard_map/ppermute | solution.py:316
  107.3 11.9 %all-to-all-start.1 = ((f32[8,32,128]{2,1,0:T(8,128)}), f32[8,32,128]{2,1,0:T(8,128)S(1)}, u32[]{:S(2)}, u32[]{:S(2)}) async-start(f32[8,32,128]{2,1,0:T(8,128)} %shard_map.99), calls=%async_computation.1 | async-start | bytes 262144 | tf_op jit(solution)/shard_map/all_to_all | solution.py:373
  111.1 11.3 %collective-permute-start.21 = (f32[64,512]{1,0:T(8,128)S(1)}, f32[64,512]{1,0:T(8,128)S(1)}, u32[]{:S(2)}, u32[]{:S(2)}) collective-permute-start(f32[64,512]{1,0:T(8,128)S(1)} %get-tuple-element.81), channel_id=1, source_target_pairs={{0,1},{1,0},{2,3},{3,2},{4,5},{5,4},{6,7},{7,6},{8,9},{9,8},{10,11... | collective-permute-start | bytes 393224 | tf_op jit(solution)/shard_map/ppermute | solution.py:316
  119.2 4.1 %collective-permute-start.20 = (f32[32,128]{1,0:T(8,128)S(1)}, f32[32,128]{1,0:T(8,128)S(1)}, u32[]{:S(2)}, u32[]{:S(2)}) collective-permute-start(f32[32,128]{1,0:T(8,128)S(1)} %reduce_sum.9.mine_ref), channel_id=1, source_target_pairs={{0,1},{1,0},{2,3},{3,2},{4,5},{5,4},{6,7},{7,6},{8,9},{9,8},{10,11... | collective-permute-start | bytes 49160 | tf_op jit(solution)/shard_map/ppermute | solution.py:316

commit v11 on v10

--- a/solution.py
+++ b/solution.py
@@ -365,7 +365,7 @@
 def sum_over_chips(*values):
     planes = [[(x * PLANES + z) * RING + y for x in range(ACROSS) for y in range(RING)] for z in range(PLANES)]
     lines = [[(x * PLANES + z) * RING + y for z in range(PLANES)] for x in range(ACROSS) for y in range(RING)]
-    for groups in (planes, lines):
+    for groups in (lines, planes):
         copies = call(copies_kernel, shape((len(groups[0]), 32, 128)), 10**5, 10**5)(
             in_specs=[VMEM] * len(values)
         )(*values)

time: 124 us -> 122 us (0.984); the launches traced: 126 us -> 121 us
  blocking collectives: 30.9 us -> 23.6 us
  starting transfers between devices: 42 us -> 45 us
    all_to_all x1, blocking collectives: 30.9 us -> 23.6 us  [sum_over_chips(): lax.all_to_all(copies, 'rows', 0, 0, axis_index_groups=groups, tiled=True)]
    all_to_all x1, starting transfers between devices: 3.83 us -> 5.45 us  [sum_over_chips(): lax.all_to_all(copies, 'rows', 0, 0, axis_index_groups=groups, tiled=True)]
where the time goes in v11:
time: 122 us; the launch traced here: 121 us
  starting transfers between devices  45 us (37%)
  waiting for transfers between devices  34.2 us (28%)
  blocking collectives  23.6 us (19%)
  Pallas kernels  16.4 us (13%)
    ppermute x8, waiting for transfers between devices, exchange(): return lax.ppermute(value, 'rows', links)  26 us
    all_to_all x1, blocking collectives, sum_over_chips(): lax.all_to_all(copies, 'rows', 0, 0, axis_index_groups=groups, tiled=True)  23.6 us
    ppermute x8, starting transfers between devices, exchange(): return lax.ppermute(value, 'rows', links)  19.1 us
    ppermute x13, starting transfers between devices, swap(): return lax.ppermute(value, 'cols', [(0, 1), (1, 0)])  17 us
    all_to_all x1, starting transfers between devices, sum_over_chips(): lax.all_to_all(copies, 'rows', 0, 0, axis_index_groups=groups, tiled=True)  5.45 us
    all_to_all x1, waiting for transfers between devices, sum_over_chips(): lax.all_to_all(copies, 'rows', 0, 0, axis_index_groups=groups, tiled=True)  4.96 us
    ppermute x1, starting transfers between devices, own_flags_and_list(): lax.ppermute(own, 'rows', [(r, r + 1) for r in range(lax.axis_size('rows'...  3.36 us
    ppermute x13, waiting for transfers between devices, swap(): return lax.ppermute(value, 'cols', [(0, 1), (1, 0)])  3.24 us
  transfers between devices with their start and end apart: 23, of which 10 were waited for; matrix products, arithmetic and copies ran while one was open for 0% of the time, Pallas kernels for 7%

profile of v11, /device:TPU:1, one launch (start us, length us, event | category | flops | bytes accessed | tf_op | source)
XLA Modules:
  0.0 120.8 jit_solution(13254931908951975704)
XLA Ops:
  0.6 0.0 copy-start.3
  0.6 0.0 copy-start.4
  0.7 0.0 copy-start.1
  0.7 0.0 copy-start.2
  0.7 1.4 %shard_map.87.refs_0_.refs_1_ = bf16[2,1792,128]{2,1,0:T(8,128)(2,1)S(1)} custom-call(s32[1]{0:T(128)} %bitcast.core_ref, bf16[2048,384]{1,0:T(8,128)(2,1)} %rows_ref.3, bf16[64,2048]{1,0:T(8,128)(2,1)} %bitcast.23), custom_call_target="tpu_custom_call" | custom-call | flops 10000 | bytes 10000 | tf_op jit(solution)/shard_map/pallas_call | solution.py:391
  2.1 2.2 %collective-permute-start.1 = (bf16[2,1792,128]{2,1,0:T(8,128)(2,1)S(1)}, bf16[2,1792,128]{2,1,0:T(8,128)(2,1)S(1)}, u32[]{:S(2)}, u32[]{:S(2)}) collective-permute-start(bf16[2,1792,128]{2,1,0:T(8,128)(2,1)S(1)} %shard_map.87.refs_0_.refs_1_), channel_id=1, source_target_pairs={{0,2},{2,0},{4,6},{6,4},{8,10},{10,8},{12,14},{14,12},{16,18},{18,... | collective-permute-start | bytes 2752520 | tf_op jit(solution)/shard_map/ppermute | solution.py:304
  4.3 1.6 %collective-permute-start.4 = (bf16[2,1792,128]{2,1,0:T(8,128)(2,1)S(1)}, bf16[2,1792,128]{2,1,0:T(8,128)(2,1)}, u32[]{:S(2)}, u32[]{:S(2)}) collective-permute-start(bf16[2,1792,128]{2,1,0:T(8,128)(2,1)S(1)} %shard_map.87.refs_0_.refs_1_), channel_id=1, source_target_pairs={{2,4},{4,2},{6,8},{8,6},{10,12},{12,10},{14,16},{16,14},{18,20},{2... | collective-permute-start | bytes 2752520 | tf_op jit(solution)/shard_map/ppermute | solution.py:304
  5.9 1.4 %shard_map.86.refs_1_.refs_2_ = bf16[2,1792,128]{2,1,0:T(8,128)(2,1)S(1)} custom-call(s32[1]{0:T(128)} %bitcast.core_ref, bf16[2048,384]{1,0:T(8,128)(2,1)} %rows_ref.3, bf16[64,2048]{1,0:T(8,128)(2,1)} %bitcast.24), custom_call_target="tpu_custom_call" | custom-call | flops 10000 | bytes 10000 | tf_op jit(solution)/shard_map/pallas_call | solution.py:391
  7.3 1.2 %collective-permute-start = (s32[4,2]{0,1:T(2,128)S(1)}, s32[4,2]{0,1:T(2,128)S(1)}, u32[]{:S(2)}, u32[]{:S(2)}) collective-permute-start(s32[4,2]{0,1:T(2,128)S(1)} %copy-done), channel_id=1, source_target_pairs={{0,1},{1,0},{2,3},{3,2},{4,5},{5,4},{6,7},{7,6},{8,9},{9,8},{10,11... | collective-permute-start | bytes 104 | tf_op jit(solution)/shard_map/ppermute | solution.py:316
  8.5 0.8 collective-permute-done
  9.4 0.1 pad_add_fusion
  9.4 0.1 and_reduce_fusion
  9.5 2.0 %shard_map.88 = (bf16[3,2,512,512]{3,2,1,0:T(8,128)(2,1)S(1)}, f32[2,64,512]{2,1,0:T(8,128)S(1)}, f32[2,64,512]{2,1,0:T(8,128)S(1)}, f32[2,64,512]{2,1,0:T(8,128)S(1)}) custom-call(s32[11]{0:T(128)S(1)} %convert_element_type.6.flags_ref, bf16[2,1792,128]{2,1,0:T(8,128)(2,1)S(1)} %shard_map.87.refs_0_.refs_1_, bf16[2,1792,128]{2,1,0:T(8,128)(2,1)S(1)} %shard_map.86.refs_1_.refs_2_), custom_call_target="tpu_custom_call" | custom-call | flops 10000 | bytes 10000 | tf_op jit(solution)/shard_map/pallas_call | solution.py:413
  11.5 11.6 %collective-permute-done.1.refs_1_.refs_3_ = bf16[2,1792,128]{2,1,0:T(8,128)(2,1)S(1)} collective-permute-done((bf16[2,1792,128]{2,1,0:T(8,128)(2,1)S(1)}, bf16[2,1792,128]{2,1,0:T(8,128)(2,1)S(1)}, u32[]{:S(2)}, u32[]{:S(2)}) %collective-permute-start.1) | collective-permute-done | bytes 917536 | tf_op jit(solution)/shard_map/ppermute | solution.py:304
  23.1 0.1 slice_bitcast_fusion.1
  23.2 2.6 %collective-permute-start.2 = (bf16[1792,128]{1,0:T(8,128)(2,1)S(1)}, bf16[1792,128]{1,0:T(8,128)(2,1)S(1)}, u32[]{:S(2)}, u32[]{:S(2)}) collective-permute-start(bf16[1792,128]{1,0:T(8,128)(2,1)S(1)} %get-tuple-element.84), channel_id=1, source_target_pairs={{0,1},{1,0},{2,3},{3,2},{4,5},{5,4},{6,7},{7,6},{8,9},{9,8},{10,11... | collective-permute-start | bytes 1376264 | tf_op jit(solution)/shard_map/ppermute | solution.py:316
  25.8 0.1 collective-permute-start.3
  25.9 3.4 %collective-permute-start.5 = (s32[8,2]{0,1:T(2,128)S(1)}, s32[8,2]{0,1:T(2,128)S(1)}, u32[]{:S(2)}, u32[]{:S(2)}) collective-permute-start(s32[8,2]{0,1:T(2,128)S(1)} %pad_add_fusion), channel_id=1, source_target_pairs={{0,2},{2,4},{4,6},{6,8},{8,10},{10,12},{12,14},{14,16},{16,18},{18... | collective-permute-start | bytes 200 | tf_op jit(solution)/shard_map/ppermute | solution.py:341
  29.3 0.0 collective-permute-done.2
  29.3 0.1 pad_maximum_fusion.refs_2_.refs_4_
  29.4 1.9 %shard_map.89 = (bf16[4,2,512,512]{3,2,1,0:T(8,128)(2,1)S(1)}, f32[2,64,512]{2,1,0:T(8,128)S(1)}, f32[2,64,512]{2,1,0:T(8,128)S(1)}, f32[2,64,512]{2,1,0:T(8,128)S(1)}) custom-call(s32[11]{0:T(128)S(1)} %convert_element_type.6.flags_ref, bf16[2,1792,128]{2,1,0:T(8,128)(2,1)S(1)} %shard_map.87.refs_0_.refs_1_, ...), custom_call_target="tpu_custom_call" | custom-call | flops 10000 | bytes 10000 | tf_op jit(solution)/shard_map/pallas_call | solution.py:418
  31.3 0.0 collective-permute-done.4.refs_0_
  31.3 0.2 and_reduce_fusion.1
  31.5 1.4 %shard_map.90 = (bf16[8,2,512,512]{3,2,1,0:T(8,128)(2,1)S(1)}, f32[2,64,512]{2,1,0:T(8,128)S(1)}, f32[2,64,512]{2,1,0:T(8,128)S(1)}, f32[2,64,512]{2,1,0:T(8,128...) custom-call(s32[11]{0:T(128)S(1)} %convert_element_type.6.flags_ref, s32[4]{0:T(128)S(1)} %convert_element_type.7.far_ref, ...), custom_call_target="tpu_custom_call" | custom-call | flops 1000000000 | bytes 1000000 | tf_op jit(solution)/shard_map/pallas_call | solution.py:423
  32.9 0.8 collective-permute-start.8
  33.7 0.1 collective-permute-start.6
  33.8 0.7 collective-permute-start.7
  34.5 0.4 collective-permute-done.8
  34.9 5.9 %collective-permute-start.9 = (f32[2,64,512]{2,1,0:T(8,128)S(1)}, f32[2,64,512]{2,1,0:T(8,128)S(1)}, u32[]{:S(2)}, u32[]{:S(2)}) collective-permute-start(f32[2,64,512]{2,1,0:T(8,128)S(1)} %add.36), channel_id=1, source_target_pairs={{0,2},{2,0},{4,6},{6,4},{8,10},{10,8},{12,14},{14,12},{16,18},{18,... | collective-permute-start | bytes 786440 | tf_op jit(solution)/shard_map/ppermute | solution.py:304
  40.8 0.0 collective-permute-done.7.from_odd
  40.8 6.0 %collective-permute-done.9.from_even = f32[2,64,512]{2,1,0:T(8,128)S(1)} collective-permute-done((f32[2,64,512]{2,1,0:T(8,128)S(1)}, f32[2,64,512]{2,1,0:T(8,128)S(1)}, u32[]{:S(2)}, u32[]{:S(2)}) %collective-permute-start.9) | collective-permute-done | bytes 262176 | tf_op jit(solution)/shard_map/ppermute | solution.py:304
  46.8 0.1 shard_map.91
  46.9 1.3 %collective-permute-start.10 = (bf16[2,128,512]{2,1,0:T(8,128)(2,1)S(1)}, bf16[2,128,512]{2,1,0:T(8,128)(2,1)S(1)}, u32[]{:S(2)}, u32[]{:S(2)}) collective-permute-start(bf16[2,128,512]{2,1,0:T(8,128)(2,1)S(1)} %get-tuple-element.63.refs_1_.refs_2_), channel_id=1, source_target_pairs={{0,2},{2,0},{4,6},{6,4},{8,10},{10,8},{12,14},{14,12},{16,18},{18,... | collective-permute-start | bytes 786440 | tf_op jit(solution)/shard_map/ppermute | solution.py:304
  48.3 0.7 collective-permute-start.14
  48.9 1.9 %collective-permute-start.13 = (bf16[2,128,512]{2,1,0:T(8,128)(2,1)S(1)}, bf16[2,128,512]{2,1,0:T(8,128)(2,1)S(1)}, u32[]{:S(2)}, u32[]{:S(2)}) collective-permute-start(bf16[2,128,512]{2,1,0:T(8,128)(2,1)S(1)} %get-tuple-element.63.refs_1_.refs_2_), channel_id=1, source_target_pairs={{0,1},{1,0},{2,3},{3,2},{4,5},{5,4},{6,7},{7,6},{8,9},{9,8},{10,11... | collective-permute-start | bytes 786440 | tf_op jit(solution)/shard_map/ppermute | solution.py:316
  50.8 2.8 %collective-permute-done.10.refs_2_.refs_4_ = bf16[2,128,512]{2,1,0:T(8,128)(2,1)S(1)} collective-permute-done((bf16[2,128,512]{2,1,0:T(8,128)(2,1)S(1)}, bf16[2,128,512]{2,1,0:T(8,128)(2,1)S(1)}, u32[]{:S(2)}, u32[]{:S(2)}) %collective-permute-start.10) | collective-permute-done | bytes 262176 | tf_op jit(solution)/shard_map/ppermute | solution.py:304
  53.6 2.3 %collective-permute-start.11 = (bf16[128,512]{1,0:T(8,128)(2,1)S(1)}, bf16[128,512]{1,0:T(8,128)(2,1)S(1)}, u32[]{:S(2)}, u32[]{:S(2)}) collective-permute-start(bf16[128,512]{1,0:T(8,128)(2,1)S(1)} %get-tuple-element.86), channel_id=1, source_target_pairs={{0,1},{1,0},{2,3},{3,2},{4,5},{5,4},{6,7},{7,6},{8,9},{9,8},{10,11... | collective-permute-start | bytes 393224 | tf_op jit(solution)/shard_map/ppermute | solution.py:316
  55.9 0.3 collective-permute-start.12
  56.1 0.0 collective-permute-done.13.refs_2_.refs_3_
  56.1 1.4 %shard_map.93 = (f32[2,64,512]{2,1,0:T(8,128)S(1)}, f32[2,64,512]{2,1,0:T(8,128)S(1)}, f32[2,64,512]{2,1,0:T(8,128)S(1)}) custom-call(s32[11]{0:T(128)S(1)} %convert_element_type.6.flags_ref, bf16[3,2,512,512]{3,2,1,0:T(8,128)(2,1)S(1)} %get-tuple-element.64.refs_0_, bf16[2,128,512]{2,1,0:T(8,128)(2,1)S(1)} %get-tuple-element.63.refs_1_.refs_2_, ...), custom_call_target="tpu_custom_call" | custom-call | flops 10000 | bytes 10000 | tf_op jit(solution)/shard_map/pallas_call | solution.py:439
  57.6 0.0 collective-permute-done.11
  57.6 1.3 %shard_map.94 = (f32[2,64,512]{2,1,0:T(8,128)S(1)}, f32[2,64,512]{2,1,0:T(8,128)S(1)}, f32[2,64,512]{2,1,0:T(8,128)S(1)}) custom-call(s32[11]{0:T(128)S(1)} %convert_element_type.6.flags_ref, bf16[4,2,512,512]{3,2,1,0:T(8,128)(2,1)S(1)} %get-tuple-element.62.refs_0_, bf16[2,128,512]{2,1,0:T(8,128)(2,1)S(1)} %get-tuple-element.63.refs_1_.refs_2_, ...), custom_call_target="tpu_custom_call" | custom-call | flops 10000 | bytes 10000 | tf_op jit(solution)/shard_map/pallas_call | solution.py:443
  58.9 0.0 collective-permute-done.14.refs_1_
  58.9 0.8 shard_map.95
  59.7 0.3 collective-permute-start.17
  60.0 0.3 collective-permute-start.15
  60.3 0.7 collective-permute-start.16
  61.0 0.4 collective-permute-done.17
  61.4 6.1 %collective-permute-start.18 = (f32[2,64,512]{2,1,0:T(8,128)S(1)}, f32[2,64,512]{2,1,0:T(8,128)S(1)}, u32[]{:S(2)}, u32[]{:S(2)}) collective-permute-start(f32[2,64,512]{2,1,0:T(8,128)S(1)} %add.37), channel_id=1, source_target_pairs={{0,2},{2,0},{4,6},{6,4},{8,10},{10,8},{12,14},{14,12},{16,18},{18,... | collective-permute-start | bytes 786440 | tf_op jit(solution)/shard_map/ppermute | solution.py:304
  67.5 0.4 shard_map.92.first_ref
  68.0 0.0 collective-permute-done.15.part_other
  68.0 5.6 %collective-permute-done.18.from_even = f32[2,64,512]{2,1,0:T(8,128)S(1)} collective-permute-done((f32[2,64,512]{2,1,0:T(8,128)S(1)}, f32[2,64,512]{2,1,0:T(8,128)S(1)}, u32[]{:S(2)}, u32[]{:S(2)}) %collective-permute-start.18) | collective-permute-done | bytes 262176 | tf_op jit(solution)/shard_map/ppermute | solution.py:304
  73.5 0.1 shard_map.96.value_ref
  73.6 0.4 shard_map.97
  74.1 1.3 %collective-permute-start.19 = (f32[32,128]{1,0:T(8,128)S(1)}, f32[32,128]{1,0:T(8,128)S(1)}, u32[]{:S(2)}, u32[]{:S(2)}) collective-permute-start(f32[32,128]{1,0:T(8,128)S(1)} %get-tuple-element.80), channel_id=1, source_target_pairs={{0,1},{1,0},{2,3},{3,2},{4,5},{5,4},{6,7},{7,6},{8,9},{9,8},{10,11... | collective-permute-start | bytes 49160 | tf_op jit(solution)/shard_map/ppermute | solution.py:316
  75.4 0.8 collective-permute-done.19.refs_1_
  76.2 23.6 %all_to_all.10.refs_0_ = f32[8,32,128]{2,1,0:T(8,128)S(1)} all-to-all(f32[8,32,128]{2,1,0:T(8,128)S(1)} %shard_map.98), channel_id=1, replica_groups={{0,8,16,24,32,40,48,56},{2,10,18,26,34,42,50,58},{4,12,20,28,36,44,52,6..., dimensions={0} | all-to-all | bytes 262144 | tf_op jit(solution)/shard_map/all_to_all | solution.py:373
  99.8 0.7 shard_map.99
  100.6 5.5 %all-to-all-start.1 = ((f32[16,32,128]{2,1,0:T(8,128)}), f32[16,32,128]{2,1,0:T(8,128)S(1)}, u32[]{:S(2)}, u32[]{:S(2)}) async-start(f32[16,32,128]{2,1,0:T(8,128)} %shard_map.99), calls=%async_computation.1 | async-start | bytes 524288 | tf_op jit(solution)/shard_map/all_to_all | solution.py:373
  106.0 2.5 %collective-permute-start.21 = (f32[64,512]{1,0:T(8,128)S(1)}, f32[64,512]{1,0:T(8,128)S(1)}, u32[]{:S(2)}, u32[]{:S(2)}) collective-permute-start(f32[64,512]{1,0:T(8,128)S(1)} %get-tuple-element.81), channel_id=1, source_target_pairs={{0,1},{1,0},{2,3},{3,2},{4,5},{5,4},{6,7},{7,6},{8,9},{9,8},{10,11... | collective-permute-start | bytes 393224 | tf_op jit(solution)/shard_map/ppermute | solution.py:316
  108.5 5.0 %all-to-all-done.1 = f32[16,32,128]{2,1,0:T(8,128)S(1)} async-done(((f32[16,32,128]{2,1,0:T(8,128)}), f32[16,32,128]{2,1,0:T(8,128)S(1)}, u32[]{:S(2)}, u32[]{:S(2)}) %all-to-all-start.1) | async-done | bytes 262176 | tf_op jit(solution)/shard_map/all_to_all | solution.py:373
  113.5 3.5 %collective-permute-start.20 = (f32[32,128]{1,0:T(8,128)S(1)}, f32[32,128]{1,0:T(8,128)S(1)}, u32[]{:S(2)}, u32[]{:S(2)}) collective-permute-start(f32[32,128]{1,0:T(8,128)S(1)} %reduce_sum.9.mine_ref), channel_id=1, source_target_pairs={{0,1},{1,0},{2,3},{3,2},{4,5},{5,4},{6,7},{7,6},{8,9},{9,8},{10,11... | collective-permute-start | bytes 49160 | tf_op jit(solution)/shard_map/ppermute | solution.py:316
  117.0 0.8 collective-permute-done.20.other_ref
  117.8 3.0 %shard_map.100 = (f32[64,1024]{1,0:T(8,128)}, f32[64,64]{1,0:T(8,128)}) custom-call(s32[1]{0:T(128)} %bitcast.core_ref, f32[32,128]{1,0:T(8,128)S(1)} %reduce_sum.9.mine_ref, f32[32,128]{1,0:T(8,128)S(1)} %collective-permute-done.20.other_ref, f32[2,64,512]{2,1,0:T(8,128)S(1)} %shard_map.96.value_ref, f32[64,512]{1,0:T(8,128)S(1)} %collective-permute-done.21.got_ref), custom_call_target="tpu_custom_call" | custom-call | flops 100000000 | bytes 1000000 | tf_op jit(solution)/shard_map/pallas_call | solution.py:464
  (26 shorter events, 0.2 us)
Async XLA Ops:
  0.6 7.9 %copy-start.3 = (s32[11]{0:T(128)S(1)}, s32[11]{0:T(128)}, u32[]{:S(2)}) copy-start(s32[11]{0:T(128)} %constant.40.clone) | copy-start | bytes 136
  0.6 7.9 %copy-start.4 = (s32[11]{0:T(128)S(1)}, s32[11]{0:T(128)}, u32[]{:S(2)}) copy-start(s32[11]{0:T(128)} %constant.39.clone) | copy-start | bytes 136
  0.7 6.6 %copy-start = (s32[4,2]{0,1:T(2,128)S(1)}, s32[4,2]{0,1:T(2,128)}, u32[]{:S(2)}) copy-start(s32[4,2]{0,1:T(2,128)} %param.9) | copy-start | bytes 100
  0.7 25.2 %copy-start.1 = (s32[4]{0:T(128)S(1)}, s32[4]{0:T(128)}, u32[]{:S(2)}) copy-start(s32[4]{0:T(128)} %constant.42.clone) | copy-start | bytes 52
  0.7 25.2 %copy-start.2 = (s32[4]{0:T(128)S(1)}, s32[4]{0:T(128)}, u32[]{:S(2)}) copy-start(s32[4]{0:T(128)} %constant.41.clone) | copy-start | bytes 52
  2.1 21.0 %collective-permute-start.1 = (bf16[2,1792,128]{2,1,0:T(8,128)(2,1)S(1)}, bf16[2,1792,128]{2,1,0:T(8,128)(2,1)S(1)}, u32[]{:S(2)}, u32[]{:S(2)}) collective-permute-start(bf16[2,1792,128]{2,1,0:T(8,128)(2,1)S(1)} %shard_map.87.refs_0_.refs_1_), channel_id=1, source_target_pairs={{0,2},{2,0},{4,6},{6,4},{8,10},{10,8},{12,14},{14,12},{16,18},{18,... | collective-permute-start | bytes 2752520 | tf_op jit(solution)/shard_map/ppermute | solution.py:304
  4.3 27.0 %collective-permute-start.4 = (bf16[2,1792,128]{2,1,0:T(8,128)(2,1)S(1)}, bf16[2,1792,128]{2,1,0:T(8,128)(2,1)}, u32[]{:S(2)}, u32[]{:S(2)}) collective-permute-start(bf16[2,1792,128]{2,1,0:T(8,128)(2,1)S(1)} %shard_map.87.refs_0_.refs_1_), channel_id=1, source_target_pairs={{2,4},{4,2},{6,8},{8,6},{10,12},{12,10},{14,16},{16,14},{18,20},{2... | collective-permute-start | bytes 2752520 | tf_op jit(solution)/shard_map/ppermute | solution.py:304
  7.3 2.0 %collective-permute-start = (s32[4,2]{0,1:T(2,128)S(1)}, s32[4,2]{0,1:T(2,128)S(1)}, u32[]{:S(2)}, u32[]{:S(2)}) collective-permute-start(s32[4,2]{0,1:T(2,128)S(1)} %copy-done), channel_id=1, source_target_pairs={{0,1},{1,0},{2,3},{3,2},{4,5},{5,4},{6,7},{7,6},{8,9},{9,8},{10,11... | collective-permute-start | bytes 104 | tf_op jit(solution)/shard_map/ppermute | solution.py:316
  23.2 6.1 %collective-permute-start.2 = (bf16[1792,128]{1,0:T(8,128)(2,1)S(1)}, bf16[1792,128]{1,0:T(8,128)(2,1)S(1)}, u32[]{:S(2)}, u32[]{:S(2)}) collective-permute-start(bf16[1792,128]{1,0:T(8,128)(2,1)S(1)} %get-tuple-element.84), channel_id=1, source_target_pairs={{0,1},{1,0},{2,3},{3,2},{4,5},{5,4},{6,7},{7,6},{8,9},{9,8},{10,11... | collective-permute-start | bytes 1376264 | tf_op jit(solution)/shard_map/ppermute | solution.py:316
  25.8 3.5 %collective-permute-start.3 = (bf16[1792,128]{1,0:T(8,128)(2,1)S(1)}, bf16[1792,128]{1,0:T(8,128)(2,1)S(1)}, u32[]{:S(2)}, u32[]{:S(2)}) collective-permute-start(bf16[1792,128]{1,0:T(8,128)(2,1)S(1)} %get-tuple-element.85), channel_id=1, source_target_pairs={{0,1},{1,0},{2,3},{3,2},{4,5},{5,4},{6,7},{7,6},{8,9},{9,8},{10,11... | collective-permute-start | bytes 1376264 | tf_op jit(solution)/shard_map/ppermute | solution.py:316
  25.9 5.4 %collective-permute-start.5 = (s32[8,2]{0,1:T(2,128)S(1)}, s32[8,2]{0,1:T(2,128)S(1)}, u32[]{:S(2)}, u32[]{:S(2)}) collective-permute-start(s32[8,2]{0,1:T(2,128)S(1)} %pad_add_fusion), channel_id=1, source_target_pairs={{0,2},{2,4},{4,6},{6,8},{8,10},{10,12},{12,14},{14,16},{16,18},{18... | collective-permute-start | bytes 200 | tf_op jit(solution)/shard_map/ppermute | solution.py:341
  32.9 1.9 %collective-permute-start.8 = (f32[2,64,512]{2,1,0:T(8,128)S(1)}, f32[2,64,512]{2,1,0:T(8,128)S(1)}, u32[]{:S(2)}, u32[]{:S(2)}) collective-permute-start(f32[2,64,512]{2,1,0:T(8,128)S(1)} %get-tuple-element.60), channel_id=1, source_target_pairs={{0,1},{1,0},{2,3},{3,2},{4,5},{5,4},{6,7},{7,6},{8,9},{9,8},{10,11... | collective-permute-start | bytes 786440 | tf_op jit(solution)/shard_map/ppermute | solution.py:316
  33.7 7.1 %collective-permute-start.6 = (f32[2,64,512]{2,1,0:T(8,128)S(1)}, f32[2,64,512]{2,1,0:T(8,128)S(1)}, u32[]{:S(2)}, u32[]{:S(2)}) collective-permute-start(f32[2,64,512]{2,1,0:T(8,128)S(1)} %get-tuple-element.57), channel_id=1, source_target_pairs={{0,1},{1,0},{2,3},{3,2},{4,5},{5,4},{6,7},{7,6},{8,9},{9,8},{10,11... | collective-permute-start | bytes 786440 | tf_op jit(solution)/shard_map/ppermute | solution.py:316
  33.8 7.0 %collective-permute-start.7 = (f32[2,64,512]{2,1,0:T(8,128)S(1)}, f32[2,64,512]{2,1,0:T(8,128)S(1)}, u32[]{:S(2)}, u32[]{:S(2)}) collective-permute-start(f32[2,64,512]{2,1,0:T(8,128)S(1)} %get-tuple-element.58), channel_id=1, source_target_pairs={{2,4},{4,2},{6,8},{8,6},{10,12},{12,10},{14,16},{16,14},{18,20},{2... | collective-permute-start | bytes 786440 | tf_op jit(solution)/shard_map/ppermute | solution.py:304
  34.9 11.9 %collective-permute-start.9 = (f32[2,64,512]{2,1,0:T(8,128)S(1)}, f32[2,64,512]{2,1,0:T(8,128)S(1)}, u32[]{:S(2)}, u32[]{:S(2)}) collective-permute-start(f32[2,64,512]{2,1,0:T(8,128)S(1)} %add.36), channel_id=1, source_target_pairs={{0,2},{2,0},{4,6},{6,4},{8,10},{10,8},{12,14},{14,12},{16,18},{18,... | collective-permute-start | bytes 786440 | tf_op jit(solution)/shard_map/ppermute | solution.py:304
  46.9 6.6 %collective-permute-start.10 = (bf16[2,128,512]{2,1,0:T(8,128)(2,1)S(1)}, bf16[2,128,512]{2,1,0:T(8,128)(2,1)S(1)}, u32[]{:S(2)}, u32[]{:S(2)}) collective-permute-start(bf16[2,128,512]{2,1,0:T(8,128)(2,1)S(1)} %get-tuple-element.63.refs_1_.refs_2_), channel_id=1, source_target_pairs={{0,2},{2,0},{4,6},{6,4},{8,10},{10,8},{12,14},{14,12},{16,18},{18,... | collective-permute-start | bytes 786440 | tf_op jit(solution)/shard_map/ppermute | solution.py:304
  48.3 10.7 %collective-permute-start.14 = (bf16[2,128,512]{2,1,0:T(8,128)(2,1)S(1)}, bf16[2,128,512]{2,1,0:T(8,128)(2,1)S(1)}, u32[]{:S(2)}, u32[]{:S(2)}) collective-permute-start(bf16[2,128,512]{2,1,0:T(8,128)(2,1)S(1)} %get-tuple-element.63.refs_1_.refs_2_), channel_id=1, source_target_pairs={{2,4},{4,2},{6,8},{8,6},{10,12},{12,10},{14,16},{16,14},{18,20},{2... | collective-permute-start | bytes 786440 | tf_op jit(solution)/shard_map/ppermute | solution.py:304
  48.9 7.2 %collective-permute-start.13 = (bf16[2,128,512]{2,1,0:T(8,128)(2,1)S(1)}, bf16[2,128,512]{2,1,0:T(8,128)(2,1)S(1)}, u32[]{:S(2)}, u32[]{:S(2)}) collective-permute-start(bf16[2,128,512]{2,1,0:T(8,128)(2,1)S(1)} %get-tuple-element.63.refs_1_.refs_2_), channel_id=1, source_target_pairs={{0,1},{1,0},{2,3},{3,2},{4,5},{5,4},{6,7},{7,6},{8,9},{9,8},{10,11... | collective-permute-start | bytes 786440 | tf_op jit(solution)/shard_map/ppermute | solution.py:316
  53.6 4.0 %collective-permute-start.11 = (bf16[128,512]{1,0:T(8,128)(2,1)S(1)}, bf16[128,512]{1,0:T(8,128)(2,1)S(1)}, u32[]{:S(2)}, u32[]{:S(2)}) collective-permute-start(bf16[128,512]{1,0:T(8,128)(2,1)S(1)} %get-tuple-element.86), channel_id=1, source_target_pairs={{0,1},{1,0},{2,3},{3,2},{4,5},{5,4},{6,7},{7,6},{8,9},{9,8},{10,11... | collective-permute-start | bytes 393224 | tf_op jit(solution)/shard_map/ppermute | solution.py:316
  55.9 1.7 %collective-permute-start.12 = (bf16[128,512]{1,0:T(8,128)(2,1)S(1)}, bf16[128,512]{1,0:T(8,128)(2,1)S(1)}, u32[]{:S(2)}, u32[]{:S(2)}) collective-permute-start(bf16[128,512]{1,0:T(8,128)(2,1)S(1)} %get-tuple-element.87), channel_id=1, source_target_pairs={{0,1},{1,0},{2,3},{3,2},{4,5},{5,4},{6,7},{7,6},{8,9},{9,8},{10,11... | collective-permute-start | bytes 393224 | tf_op jit(solution)/shard_map/ppermute | solution.py:316
  59.7 1.6 %collective-permute-start.17 = (f32[2,64,512]{2,1,0:T(8,128)S(1)}, f32[2,64,512]{2,1,0:T(8,128)S(1)}, u32[]{:S(2)}, u32[]{:S(2)}) collective-permute-start(f32[2,64,512]{2,1,0:T(8,128)S(1)} %get-tuple-element.78), channel_id=1, source_target_pairs={{0,1},{1,0},{2,3},{3,2},{4,5},{5,4},{6,7},{7,6},{8,9},{9,8},{10,11... | collective-permute-start | bytes 786440 | tf_op jit(solution)/shard_map/ppermute | solution.py:316
  60.0 7.9 %collective-permute-start.15 = (f32[2,64,512]{2,1,0:T(8,128)S(1)}, f32[2,64,512]{2,1,0:T(8,128)S(1)}, u32[]{:S(2)}, u32[]{:S(2)}) collective-permute-start(f32[2,64,512]{2,1,0:T(8,128)S(1)} %get-tuple-element.75), channel_id=1, source_target_pairs={{0,1},{1,0},{2,3},{3,2},{4,5},{5,4},{6,7},{7,6},{8,9},{9,8},{10,11... | collective-permute-start | bytes 786440 | tf_op jit(solution)/shard_map/ppermute | solution.py:316
  60.3 7.6 %collective-permute-start.16 = (f32[2,64,512]{2,1,0:T(8,128)S(1)}, f32[2,64,512]{2,1,0:T(8,128)S(1)}, u32[]{:S(2)}, u32[]{:S(2)}) collective-permute-start(f32[2,64,512]{2,1,0:T(8,128)S(1)} %get-tuple-element.76), channel_id=1, source_target_pairs={{2,4},{4,2},{6,8},{8,6},{10,12},{12,10},{14,16},{16,14},{18,20},{2... | collective-permute-start | bytes 786440 | tf_op jit(solution)/shard_map/ppermute | solution.py:304
  61.4 12.2 %collective-permute-start.18 = (f32[2,64,512]{2,1,0:T(8,128)S(1)}, f32[2,64,512]{2,1,0:T(8,128)S(1)}, u32[]{:S(2)}, u32[]{:S(2)}) collective-permute-start(f32[2,64,512]{2,1,0:T(8,128)S(1)} %add.37), channel_id=1, source_target_pairs={{0,2},{2,0},{4,6},{6,4},{8,10},{10,8},{12,14},{14,12},{16,18},{18,... | collective-permute-start | bytes 786440 | tf_op jit(solution)/shard_map/ppermute | solution.py:304
  74.1 2.1 %collective-permute-start.19 = (f32[32,128]{1,0:T(8,128)S(1)}, f32[32,128]{1,0:T(8,128)S(1)}, u32[]{:S(2)}, u32[]{:S(2)}) collective-permute-start(f32[32,128]{1,0:T(8,128)S(1)} %get-tuple-element.80), channel_id=1, source_target_pairs={{0,1},{1,0},{2,3},{3,2},{4,5},{5,4},{6,7},{7,6},{8,9},{9,8},{10,11... | collective-permute-start | bytes 49160 | tf_op jit(solution)/shard_map/ppermute | solution.py:316
  100.6 12.9 %all-to-all-start.1 = ((f32[16,32,128]{2,1,0:T(8,128)}), f32[16,32,128]{2,1,0:T(8,128)S(1)}, u32[]{:S(2)}, u32[]{:S(2)}) async-start(f32[16,32,128]{2,1,0:T(8,128)} %shard_map.99), calls=%async_computation.1 | async-start | bytes 524288 | tf_op jit(solution)/shard_map/all_to_all | solution.py:373
  106.0 11.0 %collective-permute-start.21 = (f32[64,512]{1,0:T(8,128)S(1)}, f32[64,512]{1,0:T(8,128)S(1)}, u32[]{:S(2)}, u32[]{:S(2)}) collective-permute-start(f32[64,512]{1,0:T(8,128)S(1)} %get-tuple-element.81), channel_id=1, source_target_pairs={{0,1},{1,0},{2,3},{3,2},{4,5},{5,4},{6,7},{7,6},{8,9},{9,8},{10,11... | collective-permute-start | bytes 393224 | tf_op jit(solution)/shard_map/ppermute | solution.py:316
  113.5 4.4 %collective-permute-start.20 = (f32[32,128]{1,0:T(8,128)S(1)}, f32[32,128]{1,0:T(8,128)S(1)}, u32[]{:S(2)}, u32[]{:S(2)}) collective-permute-start(f32[32,128]{1,0:T(8,128)S(1)} %reduce_sum.9.mine_ref), channel_id=1, source_target_pairs={{0,1},{1,0},{2,3},{3,2},{4,5},{5,4},{6,7},{7,6},{8,9},{9,8},{10,11... | collective-permute-start | bytes 49160 | tf_op jit(solution)/shard_map/ppermute | solution.py:316
